TPU v7x, 32 devices: a whole 2x2x4 slice. The times are simulated.
32 devices in a mesh: fsdp: 8 (over y, x, core), tp: 4 (over z).
Axes of the slice: x: 2, y: 2, z: 4, core: 2. Of those that a mesh axis runs over, the one named last changes fastest.
Arguments:
- block_in: bfloat16 [4096, 2048], P(('fsdp', 'tp')), may hold values from -6 to 6
- out_cotan: bfloat16 [4096, 2048], P(('fsdp', 'tp')), may hold values from -6 to 6
- segment_ids: int32 [4096], P('fsdp'), may hold values from 0 to 63, never falling along the last dimension, each value on 1 to 256 neighbouring positions
- expert_ids: int32 [4096, 6], P('fsdp'), may hold values from 0 to 15, all different within a row; in each aligned block of 128 rows (0 to 127, 128 to 255, ...) at most 64 rows name the same one
- expert_wts: float32 [4096, 6], P('fsdp'), may hold values from 0.5 to 1.5
- attn_gain: bfloat16 [2048], P('fsdp'), may hold values from 0.5 to 1.5
- query_proj: bfloat16 [2048, 3072], P('fsdp', 'tp'), may hold values from -0.125 to 0.125
- latent_proj: bfloat16 [2048, 576], P('fsdp'), may hold values from -0.125 to 0.125
- latent_gain: bfloat16 [512], P('fsdp'), may hold values from 0.5 to 1.5
- latent_up: bfloat16 [512, 4096], P('fsdp', 'tp'), may hold values from -0.25 to 0.25
- out_proj: bfloat16 [2048, 2048], P('tp', 'fsdp'), may hold values from -0.5 to 0.5
- ffn_gain: bfloat16 [2048], P('fsdp'), may hold values from 0.5 to 1.5
- shared_gate: bfloat16 [2048, 2816], P('fsdp', 'tp'), may hold values from -0.125 to 0.125
- shared_up: bfloat16 [2048, 2816], P('fsdp', 'tp'), may hold values from -0.125 to 0.125
- shared_down: bfloat16 [2816, 2048], P('tp', 'fsdp'), may hold values from -0.109375 to 0.109375
- routed_gate: bfloat16 [16, 1408, 2048], P('fsdp', 'tp'), may hold values from -0.125 to 0.125
- routed_up: bfloat16 [16, 1408, 2048], P('fsdp', 'tp'), may hold values from -0.125 to 0.125
- routed_down: bfloat16 [16, 1408, 2048], P('fsdp', 'tp'), may hold values from -0.15625 to 0.15625
Outputs:
- block_out: bfloat16 [4096, 2048], P(('fsdp', 'tp'))
- block_in_grad: float32 [4096, 2048], P(('fsdp', 'tp'))
- attn_gain_grad: float32 [2048], P(('fsdp', 'tp'))
- query_proj_grad: float32 [2048, 3072], P('fsdp', 'tp')
- latent_proj_grad: float32 [2048, 576], P(('fsdp', 'tp'))
- latent_gain_grad: float32 [512], P(('fsdp', 'tp'))
- latent_up_grad: float32 [512, 4096], P('fsdp', 'tp')
- out_proj_grad: float32 [2048, 2048], P('tp', 'fsdp')
- ffn_gain_grad: float32 [2048], P(('fsdp', 'tp'))
- shared_gate_grad: float32 [2048, 2816], P('fsdp', 'tp')
- shared_up_grad: float32 [2048, 2816], P('fsdp', 'tp')
- shared_down_grad: float32 [2816, 2048], P('tp', 'fsdp')
- routed_gate_grad: float32 [16, 1408, 2048], P('fsdp', 'tp')
- routed_up_grad: float32 [16, 1408, 2048], P('fsdp', 'tp')
- routed_down_grad: float32 [16, 1408, 2048], P('fsdp', 'tp')
Inputs may be any that keep to these rules, and one draw needn't show every extreme that they name: `expert_ids`: each row names 6 different experts; among the 128 rows of one device no expert is named more than 64 times. `segment_ids`: never falls along the tokens.
All inputs are finite; a program needn't handle non-finite values.
Results may differ from a plain program's by a relative error of at most 0.024.
Values may be sent and summed in bfloat16 or wider, within the bound.
A program may use at most 320 MiB of HBM per device.

v0:
```python
import jax
import jax.numpy as jnp
from jax import lax
from jax.sharding import PartitionSpec as P

H = 16
NOPE = 128
ROPE = 64
DV = 128
LAT = 512
TOPK = 6
SEQ = 512


EPSILON = 1e-06
THETA_BASE = 10000.0
MASK_FILL = -1e30


def rope_tables(positions, width_rope):
    middle = width_rope // 2
    frequency = THETA_BASE ** (-(jnp.arange(middle) * 2).astype(jnp.float32) / width_rope)
    angles = positions.astype(jnp.float32)[:, None] * frequency[None, :]
    return (jnp.cos(angles), jnp.sin(angles))


def rotate(values, cosine, sine_part):
    middle = values.shape[-1] // 2
    first_half = values[..., :middle]
    second_half = values[..., middle:]
    return jnp.concatenate(
        [
            first_half * cosine - second_half * sine_part,
            second_half * cosine + first_half * sine_part,
        ],
        axis=-1,
    )


def unrotate(values, cosine, sine_part):
    middle = values.shape[-1] // 2
    first_half = values[..., :middle]
    second_half = values[..., middle:]
    return jnp.concatenate(
        [
            first_half * cosine + second_half * sine_part,
            second_half * cosine - first_half * sine_part,
        ],
        axis=-1,
    )


def norm_parts(values):
    inverse = lax.rsqrt(jnp.mean(values * values, axis=-1, keepdims=True) + EPSILON)
    return (values * inverse, inverse)


def norm_back(upstream, unit_rows, inverse, scaling):
    scaled = upstream * scaling
    gain_grad = jnp.sum(upstream * unit_rows, axis=0)
    input_grad = inverse * (
        scaled - unit_rows * jnp.mean(scaled * unit_rows, axis=-1, keepdims=True)
    )
    return (gain_grad, input_grad)


def silu_back(grad_hidden, gate_pre, up_pre):
    sigmoid = jax.nn.sigmoid(gate_pre)
    gate_grad = grad_hidden * up_pre * (sigmoid * (1.0 + gate_pre * (1.0 - sigmoid)))
    up_grad = grad_hidden * (gate_pre * sigmoid)
    return (gate_grad.astype(jnp.bfloat16), up_grad.astype(jnp.bfloat16))


def slot_numbers(expert_rows, blocks_count, cap_rows, expert_count):
    per_block = expert_rows.reshape(blocks_count, -1)
    onehot = (
        per_block[:, :, None] == jnp.arange(expert_count, dtype=jnp.int32)[None, None, :]
    ).astype(jnp.int32)
    running = jnp.cumsum(onehot, axis=1)
    slot_rank = jnp.sum((running - 1) * onehot, axis=2)
    block_ids = jnp.arange(blocks_count, dtype=jnp.int32)[:, None]
    return (per_block * (blocks_count * cap_rows) + block_ids * cap_rows + slot_rank, slot_rank)


def per_device(
    block_in,
    out_cotan,
    segment_ids,
    expert_ids,
    expert_wts,
    attn_gain,
    query_proj,
    latent_proj,
    latent_gain,
    latent_up,
    out_proj,
    ffn_gain,
    shared_gate,
    shared_up,
    shared_down,
    routed_gate,
    routed_up,
    routed_down,
):
    tp_count = lax.axis_size("tp")
    fsdp_count = lax.axis_size("fsdp")
    tp_rank = lax.axis_index("tp")
    tok_rows = block_in.shape[0]
    model_width = block_in.shape[1]
    local_experts = routed_gate.shape[0]
    expert_count = local_experts * fsdp_count
    cap_rows = tok_rows * TOPK * 4 // (3 * expert_count)
    slot_rows = tp_count * cap_rows
    heads_local = H // tp_count
    head_width = NOPE + ROPE
    score_scale = head_width ** (-0.5)
    (
        gain_attn,
        query_weight,
        latent_weight,
        gain_latent,
        latent_up_weight,
        out_weight,
        gain_ffn,
        shared_gate_weight,
        shared_up_weight,
        shared_down_weight,
    ) = (
        lax.all_gather(attn_gain, "fsdp", axis=0, tiled=True),
        lax.all_gather(query_proj, "fsdp", axis=0, tiled=True),
        lax.all_gather(latent_proj, "fsdp", axis=0, tiled=True),
        lax.all_gather(latent_gain, "fsdp", axis=0, tiled=True),
        lax.all_gather(latent_up, "fsdp", axis=0, tiled=True),
        lax.all_gather(out_proj, "fsdp", axis=1, tiled=True),
        lax.all_gather(ffn_gain, "fsdp", axis=0, tiled=True),
        lax.all_gather(shared_gate, "fsdp", axis=0, tiled=True),
        lax.all_gather(shared_up, "fsdp", axis=0, tiled=True),
        lax.all_gather(shared_down, "fsdp", axis=1, tiled=True),
    )
    tokens = block_in.astype(jnp.float32)
    unit_one, inverse_one = norm_parts(tokens)
    normed = (unit_one * gain_attn.astype(jnp.float32)).astype(jnp.bfloat16)
    latent = jnp.dot(normed, latent_weight, preferred_element_type=jnp.float32)
    unit_lat, inverse_lat = norm_parts(latent[:, :LAT])
    local_positions = tp_rank * tok_rows + jnp.arange(tok_rows, dtype=jnp.int32)
    cosine_local, sine_local = rope_tables(local_positions, ROPE)
    keys_local = jnp.concatenate(
        [
            unit_lat * gain_latent.astype(jnp.float32),
            rotate(latent[:, LAT:], cosine_local, sine_local),
        ],
        axis=1,
    ).astype(jnp.bfloat16)
    normed_all, keys_all, cotan_all = (
        lax.all_gather(normed, "tp", axis=0, tiled=True),
        lax.all_gather(keys_local, "tp", axis=0, tiled=True),
        lax.all_gather(out_cotan, "tp", axis=0, tiled=True),
    )
    positions = jnp.arange(SEQ, dtype=jnp.int32)
    cosine, sine_part = rope_tables(positions, ROPE)
    queries = jnp.dot(normed_all, query_weight, preferred_element_type=jnp.float32).reshape(
        SEQ, heads_local, head_width
    )
    query_cat = jnp.concatenate(
        [
            queries[:, :, :NOPE],
            rotate(queries[:, :, NOPE:], cosine[:, None, :], sine_part[:, None, :]),
        ],
        axis=2,
    ).astype(jnp.bfloat16)
    compressed_all = keys_all[:, :LAT]
    key_rope_all = keys_all[:, LAT:]
    key_value = (
        jnp.dot(compressed_all, latent_up_weight, preferred_element_type=jnp.float32)
        .reshape(SEQ, heads_local, NOPE + DV)
        .astype(jnp.bfloat16)
    )
    key_cat = jnp.concatenate(
        [
            key_value[:, :, :NOPE],
            jnp.broadcast_to(key_rope_all[:, None, :], (SEQ, heads_local, ROPE)),
        ],
        axis=2,
    )
    values = key_value[:, :, NOPE:]
    block_rows = min(512, SEQ)
    block_count = SEQ // block_rows
    starts = jnp.arange(block_count, dtype=jnp.int32) * block_rows

    def masked_scores(start):
        raw_scores = (
            jnp.einsum("qhd,khd->hqk", query_cat, key_cat, preferred_element_type=jnp.float32)
            * score_scale
        )
        row_index = start + jnp.arange(block_rows, dtype=jnp.int32)
        allowed = (positions[None, :] <= row_index[:, None]) & (
            segment_ids[None, :] == segment_ids[:, None]
        )
        return jnp.where(allowed[None], raw_scores, MASK_FILL)

    def attend(start):
        masked = masked_scores(start)
        top_score = jnp.max(masked, axis=2, keepdims=True)
        exponent = jnp.exp(masked - top_score)
        row_total = jnp.sum(exponent, axis=2, keepdims=True)
        probabilities = (exponent / row_total).astype(jnp.bfloat16)
        outputs = jnp.einsum(
            "hqk,khd->qhd", probabilities, values, preferred_element_type=jnp.float32
        )
        return (outputs, (top_score + jnp.log(row_total))[:, :, 0])

    attended_blocks, log_totals = lax.map(attend, starts)
    attended = attended_blocks.reshape(SEQ, heads_local * DV).astype(jnp.bfloat16)
    attn_rows = lax.psum_scatter(
        jnp.dot(attended, out_weight, preferred_element_type=jnp.float32).astype(jnp.bfloat16),
        "tp",
        scatter_dimension=0,
        tiled=True,
    ).astype(jnp.float32)
    mixed_rows = tokens + attn_rows
    unit_two, inverse_two = norm_parts(mixed_rows)
    normed_ffn = (unit_two * gain_ffn.astype(jnp.float32)).astype(jnp.bfloat16)
    normed_ffn_all = lax.all_gather(normed_ffn, "tp", axis=0, tiled=True)
    shared_gate_pre = jnp.dot(
        normed_ffn_all, shared_gate_weight, preferred_element_type=jnp.float32
    )
    shared_up_pre = jnp.dot(normed_ffn_all, shared_up_weight, preferred_element_type=jnp.float32)
    shared_hidden = (jax.nn.silu(shared_gate_pre) * shared_up_pre).astype(jnp.bfloat16)
    shared_rows = jnp.dot(shared_hidden, shared_down_weight, preferred_element_type=jnp.float32)
    shared_down_part = jnp.dot(shared_hidden.T, cotan_all, preferred_element_type=jnp.float32)
    d_shared_hidden = jnp.dot(cotan_all, shared_down_weight.T, preferred_element_type=jnp.float32)
    d_shared_gate, d_shared_up = silu_back(d_shared_hidden, shared_gate_pre, shared_up_pre)
    shared_gate_part = jnp.dot(normed_ffn_all.T, d_shared_gate, preferred_element_type=jnp.float32)
    shared_up_part = jnp.dot(normed_ffn_all.T, d_shared_up, preferred_element_type=jnp.float32)
    d_shared_in = jnp.dot(
        d_shared_gate, shared_gate_weight.T, preferred_element_type=jnp.float32
    ) + jnp.dot(d_shared_up, shared_up_weight.T, preferred_element_type=jnp.float32)
    slot_index, slot_rank = slot_numbers(expert_ids, tp_count, cap_rows, expert_count)
    slot_table = slot_index.reshape(SEQ, TOPK)
    zero_row = jnp.zeros((1, model_width), jnp.bfloat16)
    owners = jnp.arange(SEQ * TOPK, dtype=jnp.int32) // TOPK
    slot_owner = (
        jnp.full((expert_count * slot_rows,), SEQ, jnp.int32).at[slot_index.reshape(-1)].set(owners)
    )
    slot_gate = (
        jnp.zeros((expert_count * slot_rows,), jnp.float32)
        .at[slot_index.reshape(-1)]
        .set(expert_wts.reshape(-1))
    )
    padded_in = jnp.concatenate([normed_ffn_all, zero_row], axis=0)
    padded_cotan = jnp.concatenate([cotan_all, zero_row], axis=0)
    send_in = padded_in[slot_owner].reshape(fsdp_count, local_experts, slot_rows, model_width)
    send_grad = (
        (slot_gate[:, None] * padded_cotan[slot_owner].astype(jnp.float32))
        .astype(jnp.bfloat16)
        .reshape(fsdp_count, local_experts, slot_rows, model_width)
    )
    expert_in, expert_grad = (
        lax.all_to_all(send_in, "fsdp", split_axis=0, concat_axis=0, tiled=True),
        lax.all_to_all(send_grad, "fsdp", split_axis=0, concat_axis=0, tiled=True),
    )
    gate_pre = jnp.einsum(
        "fesd,ehd->fesh", expert_in, routed_gate, preferred_element_type=jnp.float32
    )
    up_pre = jnp.einsum("fesd,ehd->fesh", expert_in, routed_up, preferred_element_type=jnp.float32)
    hidden = (jax.nn.silu(gate_pre) * up_pre).astype(jnp.bfloat16)
    expert_part = jnp.einsum(
        "fesh,ehd->fesd", hidden, routed_down, preferred_element_type=jnp.float32
    ).astype(jnp.bfloat16)
    routed_down_grad = jnp.einsum(
        "fesh,fesd->ehd", hidden, expert_grad, preferred_element_type=jnp.float32
    )
    d_hidden = jnp.einsum(
        "fesd,ehd->fesh", expert_grad, routed_down, preferred_element_type=jnp.float32
    )
    d_gate, d_up = silu_back(d_hidden, gate_pre, up_pre)
    routed_gate_grad = jnp.einsum(
        "fesh,fesd->ehd", d_gate, expert_in, preferred_element_type=jnp.float32
    )
    routed_up_grad = jnp.einsum(
        "fesh,fesd->ehd", d_up, expert_in, preferred_element_type=jnp.float32
    )
    d_expert_in = jnp.einsum(
        "fesh,ehd->fesd", d_gate, routed_gate, preferred_element_type=jnp.float32
    ) + jnp.einsum("fesh,ehd->fesd", d_up, routed_up, preferred_element_type=jnp.float32)
    back_part = lax.all_to_all(expert_part, "fsdp", split_axis=0, concat_axis=0, tiled=True)
    back_grad = lax.all_to_all(
        d_expert_in.astype(jnp.bfloat16), "fsdp", split_axis=0, concat_axis=0, tiled=True
    ).astype(d_expert_in.dtype)
    part_flat = back_part.reshape(expert_count * slot_rows, model_width)
    grad_flat = back_grad.reshape(expert_count * slot_rows, model_width)
    routed_rows = jnp.zeros((SEQ, model_width), jnp.float32)
    d_routed_in = jnp.zeros((SEQ, model_width), jnp.float32)
    for pick_index in range(TOPK):
        column = slot_table[:, pick_index]
        routed_rows = routed_rows + expert_wts[:, pick_index : pick_index + 1] * part_flat[
            column
        ].astype(jnp.float32)
        d_routed_in = d_routed_in + grad_flat[column]
    ffn_rows, d_normed_ffn = (
        lax.psum_scatter(
            (shared_rows + routed_rows).astype(jnp.bfloat16), "tp", scatter_dimension=0, tiled=True
        ).astype(jnp.float32),
        lax.psum_scatter(
            (d_shared_in + d_routed_in).astype(jnp.bfloat16), "tp", scatter_dimension=0, tiled=True
        ).astype(jnp.float32),
    )
    block_out = (mixed_rows + ffn_rows).astype(jnp.bfloat16)
    ffn_gain_part, d_mixed_norm = norm_back(
        d_normed_ffn, unit_two, inverse_two, gain_ffn.astype(jnp.float32)
    )
    d_mixed = out_cotan.astype(jnp.float32) + d_mixed_norm
    d_proj_all = lax.all_gather(d_mixed.astype(jnp.bfloat16), "tp", axis=0, tiled=True)
    out_part = jnp.dot(attended.T, d_proj_all, preferred_element_type=jnp.float32)
    d_attended = (
        jnp.dot(d_proj_all, out_weight.T, preferred_element_type=jnp.float32)
        .astype(jnp.bfloat16)
        .reshape(SEQ, heads_local, DV)
    )

    def attend_back(carry, pieces):
        key_grad, value_grad = carry
        start, log_total = pieces
        masked = masked_scores(start)
        probs_full = jnp.exp(masked - log_total[:, :, None])
        probs_low = probs_full.astype(jnp.bfloat16)
        prob_grad = jnp.einsum(
            "qhd,khd->hqk", d_attended, values, preferred_element_type=jnp.float32
        )
        score_grad = (
            probs_full * (prob_grad - jnp.sum(probs_full * prob_grad, axis=2, keepdims=True))
        ).astype(jnp.bfloat16)
        query_grad = (
            jnp.einsum("hqk,khd->qhd", score_grad, key_cat, preferred_element_type=jnp.float32)
            * score_scale
        )
        key_grad = (
            key_grad
            + jnp.einsum("hqk,qhd->khd", score_grad, query_cat, preferred_element_type=jnp.float32)
            * score_scale
        )
        value_grad = value_grad + jnp.einsum(
            "hqk,qhd->khd", probs_low, d_attended, preferred_element_type=jnp.float32
        )
        return ((key_grad, value_grad), query_grad)

    start_grads = (
        jnp.zeros((SEQ, heads_local, head_width), jnp.float32),
        jnp.zeros((SEQ, heads_local, DV), jnp.float32),
    )
    (key_grad, value_grad), query_grads = lax.scan(attend_back, start_grads, (starts, log_totals))
    query_grad_all = query_grads.reshape(SEQ, heads_local, head_width)
    d_queries = (
        jnp.concatenate(
            [
                query_grad_all[:, :, :NOPE],
                unrotate(query_grad_all[:, :, NOPE:], cosine[:, None, :], sine_part[:, None, :]),
            ],
            axis=2,
        )
        .reshape(SEQ, heads_local * head_width)
        .astype(jnp.bfloat16)
    )
    query_part = jnp.dot(normed_all.T, d_queries, preferred_element_type=jnp.float32)
    d_normed_query = jnp.dot(d_queries, query_weight.T, preferred_element_type=jnp.float32)
    d_key_value = (
        jnp.concatenate([key_grad[:, :, :NOPE], value_grad], axis=2)
        .reshape(SEQ, heads_local * (NOPE + DV))
        .astype(jnp.bfloat16)
    )
    latent_up_part = jnp.dot(compressed_all.T, d_key_value, preferred_element_type=jnp.float32)
    d_compressed = jnp.dot(d_key_value, latent_up_weight.T, preferred_element_type=jnp.float32)
    d_key_rope = jnp.sum(key_grad[:, :, NOPE:], axis=1)
    d_normed_local, d_keys_local = (
        lax.psum_scatter(
            d_normed_query.astype(jnp.bfloat16), "tp", scatter_dimension=0, tiled=True
        ).astype(jnp.float32),
        lax.psum_scatter(
            jnp.concatenate([d_compressed, d_key_rope], axis=1).astype(jnp.bfloat16),
            "tp",
            scatter_dimension=0,
            tiled=True,
        ).astype(jnp.float32),
    )
    latent_gain_part, d_latent_main = norm_back(
        d_keys_local[:, :LAT], unit_lat, inverse_lat, gain_latent.astype(jnp.float32)
    )
    d_latent = jnp.concatenate(
        [d_latent_main, unrotate(d_keys_local[:, LAT:], cosine_local, sine_local)], axis=1
    ).astype(jnp.bfloat16)
    latent_proj_part = jnp.dot(normed.T, d_latent, preferred_element_type=jnp.float32)
    d_normed = d_normed_local + jnp.dot(
        d_latent, latent_weight.T, preferred_element_type=jnp.float32
    )
    attn_gain_part, d_tokens_norm = norm_back(
        d_normed, unit_one, inverse_one, gain_attn.astype(jnp.float32)
    )
    block_in_grad = d_mixed + d_tokens_norm
    (
        query_proj_grad,
        latent_up_grad,
        out_proj_grad,
        shared_gate_grad,
        shared_up_grad,
        shared_down_grad,
    ) = (
        lax.psum_scatter(
            query_part.astype(jnp.bfloat16), "fsdp", scatter_dimension=0, tiled=True
        ).astype(jnp.float32),
        lax.psum_scatter(
            latent_up_part.astype(jnp.bfloat16), "fsdp", scatter_dimension=0, tiled=True
        ).astype(jnp.float32),
        lax.psum_scatter(
            out_part.astype(jnp.bfloat16), "fsdp", scatter_dimension=1, tiled=True
        ).astype(jnp.float32),
        lax.psum_scatter(
            shared_gate_part.astype(jnp.bfloat16), "fsdp", scatter_dimension=0, tiled=True
        ).astype(jnp.float32),
        lax.psum_scatter(
            shared_up_part.astype(jnp.bfloat16), "fsdp", scatter_dimension=0, tiled=True
        ).astype(jnp.float32),
        lax.psum_scatter(
            shared_down_part.astype(jnp.bfloat16), "fsdp", scatter_dimension=1, tiled=True
        ).astype(jnp.float32),
    )
    attn_gain_grad, latent_proj_grad, latent_gain_grad, ffn_gain_grad = (
        lax.psum_scatter(attn_gain_part, ("fsdp", "tp"), scatter_dimension=0, tiled=True),
        lax.psum_scatter(latent_proj_part, ("fsdp", "tp"), scatter_dimension=0, tiled=True),
        lax.psum_scatter(latent_gain_part, ("fsdp", "tp"), scatter_dimension=0, tiled=True),
        lax.psum_scatter(ffn_gain_part, ("fsdp", "tp"), scatter_dimension=0, tiled=True),
    )
    return (
        block_out,
        block_in_grad,
        attn_gain_grad,
        query_proj_grad,
        latent_proj_grad,
        latent_gain_grad,
        latent_up_grad,
        out_proj_grad,
        ffn_gain_grad,
        shared_gate_grad,
        shared_up_grad,
        shared_down_grad,
        routed_gate_grad,
        routed_up_grad,
        routed_down_grad,
    )


def solution(mesh):
    placed = (
        P(("fsdp", "tp"), None),
        P(("fsdp", "tp"), None),
        P("fsdp"),
        P("fsdp", None),
        P("fsdp", None),
        P("fsdp"),
        P("fsdp", "tp"),
        P("fsdp", None),
        P("fsdp"),
        P("fsdp", "tp"),
        P("tp", "fsdp"),
        P("fsdp"),
        P("fsdp", "tp"),
        P("fsdp", "tp"),
        P("tp", "fsdp"),
        P("fsdp", "tp", None),
        P("fsdp", "tp", None),
        P("fsdp", "tp", None),
    )
    return jax.shard_map(
        per_device,
        mesh=mesh,
        in_specs=placed,
        out_specs=(
            P(("fsdp", "tp"), None),
            P(("fsdp", "tp"), None),
            P(("fsdp", "tp")),
            P("fsdp", "tp"),
            P(("fsdp", "tp"), None),
            P(("fsdp", "tp")),
            P("fsdp", "tp"),
            P("tp", "fsdp"),
            P(("fsdp", "tp")),
            P("fsdp", "tp"),
            P("fsdp", "tp"),
            P("tp", "fsdp"),
            P("fsdp", "tp", None),
            P("fsdp", "tp", None),
            P("fsdp", "tp", None),
        ),
        check_vma=False,
    )
```

profile of v0, /device:TPU:0, one launch (start us, length us, event | category | flops | bytes accessed | tf_op | source)
XLA Modules:
  0.0 1880.1 jit_solution(14042285583306871164)
XLA Ops:
  26.4 13.5 all-reduce.2
  45.7 16.4 all_gather.48
  73.8 41.8 %all-gather.18.cloned.1.call-done = bf16[512,2048]{1,0:T(8,128)(2,1)} async-done(((bf16[128,2048]{1,0:T(8,128)(2,1)}), bf16[512,2048]{1,0:T(8,128)(2,1)}) %all-gather.18.cloned.1.call-update) | async-done | bytes 2097168 | tf_op jit(solution)/shard_map/all_gather | solution.py:155
  115.6 32.8 %all-gather.20.cloned.1.call-done = bf16[2048,768]{1,0:T(8,128)(2,1)} async-done(((bf16[256,768]{1,0:T(8,128)(2,1)}), bf16[2048,768]{1,0:T(8,128)(2,1)}) %all-gather.20.cloned.1.call-update) | async-done | bytes 3145744 | tf_op jit(solution)/shard_map/all_gather | solution.py:130
  159.3 19.1 %all-gather.22.cloned.1.call-done = bf16[512,2048]{1,0:T(8,128)(2,1)} async-done(((bf16[512,256]{1,0:T(8,128)(2,1)}), bf16[512,2048]{1,0:T(8,128)(2,1)}) %all-gather.22.cloned.1.call-update) | async-done | bytes 2097168 | tf_op jit(solution)/shard_map/all_gather | solution.py:134
  192.2 34.6 %reduce-scatter.15.cloned.1.call-done = bf16[128,2048]{1,0:T(8,128)(2,1)} async-done(((bf16[512,2048]{1,0:T(8,128)(2,1)}), bf16[128,2048]{1,0:T(8,128)(2,1)}) %reduce-scatter.15.cloned.1.call-update) | async-done | bytes 524304 | tf_op jit(solution)/shard_map/reduce_scatter | solution.py:214
  243.7 11.8 scatter_custom_fusion
  255.5 20.7 %all-gather.24.cloned.1.call-done = bf16[512,2048]{1,0:T(8,128)(2,1)} async-done(((bf16[128,2048]{1,0:T(8,128)(2,1)}), bf16[512,2048]{1,0:T(8,128)(2,1)}) %all-gather.24.cloned.1.call-update) | async-done | bytes 2097168 | tf_op jit(solution)/shard_map/all_gather | solution.py:223
  279.4 33.2 %gather_fusion = bf16[4096,2048]{1,0:T(8,128)(2,1)} fusion(bf16[513,2048]{1,0:T(8,128)(2,1)} %concatenate.36, s32[4096]{0:T(1024)S(1)} %fusion.103), kind=kCustom, calls=%fused_computation | custom fusion | bytes 33570816 | tf_op jit(solution)/shard_map/gather | solution.py:252
  319.6 11.8 scatter_custom_fusion.1
  331.4 34.7 %all-gather.32.cloned.1.call-done = bf16[512,2048]{1,0:T(8,128)(2,1)} async-done(((bf16[128,2048]{1,0:T(8,128)(2,1)}), bf16[512,2048]{1,0:T(8,128)(2,1)}) %all-gather.32.cloned.1.call-update) | async-done | bytes 2097168 | tf_op jit(solution)/shard_map/all_gather | solution.py:157
  369.3 33.2 %gather_fusion.7 = bf16[4096,2048]{1,0:T(8,128)(2,1)} fusion(bf16[513,2048]{1,0:T(8,128)(2,1)} %concatenate.37, s32[4096]{0:T(1024)S(1)} %fusion.103), kind=kCustom, calls=%fused_computation.7 | custom fusion | bytes 33570816 | tf_op jit(solution)/shard_map/gather | solution.py:254
  402.5 14.6 fusion
  417.1 85.3 %all-to-all-done = bf16[8,2,256,2048]{3,2,1,0:T(8,128)(2,1)} async-done(((bf16[8,2,256,2048]{3,2,1,0:T(8,128)(2,1)}), bf16[8,2,256,2048]{3,2,1,0:T(8,128)(2,1)}, u32[]{:S(2)}, u32[]{:S(2)}) %all-to-all-start) | async-done | bytes 16777248 | tf_op jit(solution)/shard_map/all_to_all | solution.py:259
  508.9 12.3 fusion.10
  532.5 171.2 %all-to-all-done.2 = bf16[8,2,256,2048]{3,2,1,0:T(8,128)(2,1)} async-done(((bf16[8,2,256,2048]{3,2,1,0:T(8,128)(2,1)}), bf16[8,2,256,2048]{3,2,1,0:T(8,128)(2,1)}, u32[]{:S(2)}, u32[]{:S(2)}) %all-to-all-start.2) | async-done | bytes 16777248 | tf_op jit(solution)/shard_map/all_to_all | solution.py:260
  703.7 15.3 fusion.16
  719.0 18.0 fusion.36
  736.9 19.0 %fusion.1 = bf16[8,2,256,2048]{3,2,0,1:T(8,128)(2,1)} fusion(f32[2,8,256,2048]{3,2,1,0:T(8,128)} %fusion.36, bf16[8,2,256,352]{2,3,0,1:T(8,128)(2,1)S(1)} %copy-done.11, bf16[2,352,2048]{2,1,0:T(8,128)(2,1)S(1)} %copy-done.16), kind=kOutput, calls=%fused_computation.19 | convolution fusion | flops 5922357248 | bytes 56098816 | tf_op jit(solution)/shard_map/fesh,ehd->fesd/dot_general | solution.py:285
  755.9 14.1 copy.101
  783.7 107.8 %all-gather.26.cloned.1.call-done = bf16[2048,704]{0,1:T(8,128)(2,1)} async-done(((bf16[256,704]{0,1:T(8,128)(2,1)}), bf16[2048,704]{0,1:T(8,128)(2,1)}) %all-gather.26.cloned.1.call-update) | async-done | bytes 2883600 | tf_op jit(solution)/shard_map/all_gather | solution.py:136
  896.8 60.7 %all-gather.30.cloned.1.call-done = bf16[704,2048]{1,0:T(8,128)(2,1)} async-done(((bf16[704,256]{1,0:T(8,128)(2,1)}), bf16[704,2048]{1,0:T(8,128)(2,1)}) %all-gather.30.cloned.1.call-update) | async-done | bytes 2883600 | tf_op jit(solution)/shard_map/all_gather | solution.py:138
  969.0 14.1 all-to-all-done.3
  983.0 19.2 %bitcast_convert_fusion = f32[4096,2048]{1,0:T(8,128)} fusion(bf16[8,2,256,2048]{3,2,1,0:T(8,128)(2,1)} %all-to-all-done.3), kind=kLoop, calls=%fused_computation.20 | loop fusion | flops 8388608 | bytes 50331648 | tf_op jit(solution)/shard_map/reshape | solution.py:291
  1002.2 15.9 gather_fusion.13
  1018.1 15.9 gather_fusion.12
  1034.1 16.0 gather_fusion.11
  1050.1 16.0 gather_fusion.10
  1066.1 16.0 gather_fusion.9
  1082.1 16.3 gather_fusion.8
  1098.4 14.8 add_convert_fusion.1
  1113.2 40.9 %reduce-scatter.19.cloned.1.call-done = bf16[128,2048]{1,0:T(8,128)(2,1)} async-done(((bf16[512,2048]{1,0:T(8,128)(2,1)}), bf16[128,2048]{1,0:T(8,128)(2,1)}) %reduce-scatter.19.cloned.1.call-update) | async-done | bytes 524304 | tf_op jit(solution)/shard_map/reduce_scatter | solution.py:304
  1159.1 45.4 %all-gather.34.cloned.1.call-done = bf16[512,2048]{1,0:T(8,128)(2,1)} async-done(((bf16[128,2048]{1,0:T(8,128)(2,1)}), bf16[512,2048]{1,0:T(8,128)(2,1)}) %all-gather.34.cloned.1.call-update) | async-done | bytes 2097168 | tf_op jit(solution)/shard_map/all_gather | solution.py:313
  1226.1 14.4 convert_bitcast_fusion
  1240.5 14.5 copy.98
  1282.8 184.2 %all-to-all-done.1 = bf16[8,2,256,2048]{3,2,1,0:T(8,128)(2,1)} async-done(((bf16[8,2,256,2048]{3,2,1,0:T(8,128)(2,1)}), bf16[8,2,256,2048]{3,2,1,0:T(8,128)(2,1)}, u32[]{:S(2)}, u32[]{:S(2)}) %all-to-all-start.1) | async-done | bytes 16777248 | tf_op jit(solution)/shard_map/all_to_all | solution.py:286
  1467.0 13.3 gather_fusion.6
  1480.3 13.4 gather_fusion.5
  1493.7 13.4 gather_fusion.4
  1507.2 13.2 gather_fusion.3
  1520.3 13.3 gather_fusion.2
  1533.6 13.5 gather_fusion.1
  1577.7 12.5 fusion.30
  1590.2 11.7 fusion.27
  1601.9 11.6 fusion.24
  1624.6 43.0 %all-reduce.6 = (f32[2048]{0:T(1024)S(1)}, f32[512]{0:T(512)S(1)}, f32[2048]{0:T(1024)S(1)}) all-reduce(f32[2048]{0:T(1024)} %get-tuple-element.63, f32[512]{0:T(512)} %get-tuple-element.76, f32[2048]{0:T(1024)} %get-tuple-element.61), channel_id=7, replica_groups=mesh['fsdp'=8,'tp'=4] {'fsdp','tp'}, use_global_device_ids=true, to_apply=%region_21.22.clone | all-reduce | flops 4608 | bytes 36864
  1673.8 42.2 %reduce-scatter.23.cloned.1.call-done = bf16[256,768]{1,0:T(8,128)(2,1)} async-done(((bf16[2048,768]{1,0:T(8,128)(2,1)}), bf16[256,768]{1,0:T(8,128)(2,1)}) %reduce-scatter.23.cloned.1.call-update) | async-done | bytes 393232 | tf_op jit(solution)/shard_map/reduce_scatter | solution.py:407
  1718.0 155.2 %reduce-scatter.25.cloned.1.call-done = f32[64,576]{1,0:T(8,128)} async-done(((f32[2048,576]{1,0:T(8,128)}), f32[64,576]{1,0:T(8,128)}) %reduce-scatter.25.cloned.1.call-update) | async-done | bytes 147472 | tf_op jit(solution)/shard_map/reduce_scatter | solution.py:428
  (322 shorter events, 242.1 us)
Async XLA Ops:
  7.2 696.5 %copy-start = (bf16[2,352,2048]{2,1,0:T(8,128)(2,1)S(1)}, bf16[2,352,2048]{2,1,0:T(8,128)(2,1)}, u32[]{:S(2)}) copy-start(bf16[2,352,2048]{2,1,0:T(8,128)(2,1)} %param.35) | copy-start | bytes 8650756
  7.2 18.9 %copy-start.66 = (bf16[64]{0:T(256)(128)(2,1)S(1)}, bf16[64]{0:T(256)(128)(2,1)}, u32[]{:S(2)}) copy-start(bf16[64]{0:T(256)(128)(2,1)} %param.26) | copy-start | bytes 388
  7.2 32.7 %copy-start.56 = (s32[512]{0:T(512)S(1)}, s32[512]{0:T(512)}, u32[]{:S(2)}) copy-start(s32[512]{0:T(512)} %param.20) | copy-start | bytes 6148
  7.2 34.9 %all-gather.14.cloned.1.call-start = ((), (), s32[]{:S(2)}) async-start(), calls=%async_computation.16 | async-start | bytes 2654208 | tf_op jit(solution)/shard_map/all_gather | solution.py:131
  8.0 59.6 %all-gather.16.cloned.1.call-start = ((), (), s32[]{:S(2)}) async-start(), calls=%async_computation.17 | async-start | bytes 1179648 | tf_op jit(solution)/shard_map/all_gather | solution.py:133
  8.7 106.9 %all-gather.18.cloned.1.call-start = ((), (), s32[]{:S(2)}) async-start(), calls=%async_computation.18 | async-start | bytes 2621440 | tf_op jit(solution)/shard_map/all_gather | solution.py:155
  23.6 124.8 %all-gather.20.cloned.1.call-start = ((), (), s32[]{:S(2)}) async-start(), calls=%async_computation.19 | async-start | bytes 3538944 | tf_op jit(solution)/shard_map/all_gather | solution.py:130
  24.2 154.2 %all-gather.22.cloned.1.call-start = ((), (), s32[]{:S(2)}) async-start(), calls=%async_computation.20 | async-start | bytes 2359296 | tf_op jit(solution)/shard_map/all_gather | solution.py:134
  24.8 202.1 %reduce-scatter.15.cloned.1.call-start = ((), (), s32[]{:S(2)}) async-start(), calls=%async_computation.21 | async-start | bytes 2621440 | tf_op jit(solution)/shard_map/reduce_scatter | solution.py:214
  24.8 20.8 %copy-start.60 = (f32[32]{0:T(128)}, f32[32]{0:T(128)S(1)}, u32[]{:S(2)}) copy-start(f32[32]{0:T(128)S(1)} %multiply_power_fusion) | copy-start | bytes 388
  24.9 20.8 %copy-start.62 = (f32[128]{0:T(128)}, f32[128]{0:T(128)S(1)}, u32[]{:S(2)}) copy-start(f32[128]{0:T(128)S(1)} %add_convert_fusion.6) | copy-start | bytes 1540
  41.8 111.1 %copy-start.26 = (f32[512,32]{0,1:T(8,128)}, f32[512,32]{0,1:T(8,128)S(1)}, u32[]{:S(2)}) copy-start(f32[512,32]{0,1:T(8,128)S(1)} %get-tuple-element.111) | copy-start | bytes 196612
  73.8 79.3 %copy-start.18 = (bf16[512,4,128]{0,2,1:T(8,128)(2,1)}, bf16[512,4,128]{0,2,1:T(8,128)(2,1)S(1)}, u32[]{:S(2)}) copy-start(bf16[512,4,128]{0,2,1:T(8,128)(2,1)S(1)} %slice.179) | copy-start | bytes 1572868
  73.8 79.2 %slice-start = ((bf16[512,576]{0,1:T(8,128)(2,1)}), bf16[512,64]{0,1:T(8,128)(2,1)S(1)}, s32[]{:S(2)}) async-start(bf16[512,576]{0,1:T(8,128)(2,1)} %copy-done.23), calls=%async_computation.39 | async-start | bytes 131072 | tf_op jit(solution)/shard_map/slice | solution.py:172
  178.4 48.4 %copy-start.3 = (bf16[128,2048]{1,0:T(8,128)(2,1)S(1)}, bf16[128,2048]{1,0:T(8,128)(2,1)}, u32[]{:S(2)}) copy-start(bf16[128,2048]{1,0:T(8,128)(2,1)} %param.18) | copy-start | bytes 1572868
  182.8 47.9 %copy-start.55 = (s32[512,6]{0,1:T(8,128)S(1)}, s32[512,6]{0,1:T(8,128)}, u32[]{:S(2)}) copy-start(s32[512,6]{0,1:T(8,128)} %param.21) | copy-start | bytes 36868
  182.8 93.4 %all-gather.24.cloned.1.call-start = ((), (), s32[]{:S(2)}) async-start(), calls=%async_computation.22 | async-start | bytes 2621440 | tf_op jit(solution)/shard_map/all_gather | solution.py:223
  192.2 39.1 %copy-start.33 = (f32[8,1,256]{2,1,0:T(1,128)}, f32[8,1,256]{2,1,0:T(1,128)S(1)}, u32[]{:S(2)}) copy-start(f32[8,1,256]{2,1,0:T(1,128)S(1)} %convert_element_type.318) | copy-start | bytes 24580
  312.6 189.8 %all-to-all-start = ((bf16[8,2,256,2048]{3,2,1,0:T(8,128)(2,1)}), bf16[8,2,256,2048]{3,2,1,0:T(8,128)(2,1)}, u32[]{:S(2)}, u32[]{:S(2)}) async-start(bf16[8,2,256,2048]{3,2,1,0:T(8,128)(2,1)} %bitcast.185), calls=%async_computation.1 | async-start | bytes 33554432 | tf_op jit(solution)/shard_map/all_to_all | solution.py:259
  318.5 47.6 %all-gather.32.cloned.1.call-start = ((), (), s32[]{:S(2)}) async-start(), calls=%async_computation.27 | async-start | bytes 2621440 | tf_op jit(solution)/shard_map/all_gather | solution.py:157
  502.4 201.3 %all-to-all-start.2 = ((bf16[8,2,256,2048]{3,2,1,0:T(8,128)(2,1)}), bf16[8,2,256,2048]{3,2,1,0:T(8,128)(2,1)}, u32[]{:S(2)}, u32[]{:S(2)}) async-start(bf16[8,2,256,2048]{3,2,1,0:T(8,128)(2,1)} %fusion), calls=%async_computation.4 | async-start | bytes 33554432 | tf_op jit(solution)/shard_map/all_to_all | solution.py:260
  508.2 270.3 %all-gather.28.cloned.1.call-start = ((), (), s32[]{:S(2)}) async-start(), calls=%async_computation.24 | async-start | bytes 3244032 | tf_op jit(solution)/shard_map/all_gather | solution.py:137
  770.0 213.0 %all-to-all-start.3 = ((bf16[8,2,256,2048]{3,2,1,0:T(8,128)(2,1)}), bf16[8,2,256,2048]{3,2,1,0:T(8,128)(2,1)}, u32[]{:S(2)}, u32[]{:S(2)}) async-start(bf16[8,2,256,2048]{3,2,1,0:T(8,128)(2,1)} %copy.101), calls=%async_computation.5 | async-start | bytes 33554432 | tf_op jit(solution)/shard_map/all_to_all | solution.py:287
  775.9 115.6 %all-gather.26.cloned.1.call-start = ((), (), s32[]{:S(2)}) async-start(), calls=%async_computation.23 | async-start | bytes 3244032 | tf_op jit(solution)/shard_map/all_gather | solution.py:136
  776.5 181.0 %all-gather.30.cloned.1.call-start = ((), (), s32[]{:S(2)}) async-start(), calls=%async_computation.25 | async-start | bytes 3244032 | tf_op jit(solution)/shard_map/all_gather | solution.py:138
  777.2 376.9 %reduce-scatter.19.cloned.1.call-start = ((), (), s32[]{:S(2)}) async-start(), calls=%async_computation.28 | async-start | bytes 2621440 | tf_op jit(solution)/shard_map/reduce_scatter | solution.py:304
  778.4 255.6 %copy-start.53 = (s32[1024]{0:T(1024)}, s32[1024]{0:T(1024)S(1)}, u32[]{:S(2)}) copy-start(s32[1024]{0:T(1024)S(1)} %get-tuple-element.120) | copy-start | bytes 12292
  778.5 271.6 %copy-start.51 = (s32[1024]{0:T(1024)}, s32[1024]{0:T(1024)S(1)}, u32[]{:S(2)}) copy-start(s32[1024]{0:T(1024)S(1)} %get-tuple-element.121) | copy-start | bytes 12292
  1098.3 55.8 %copy-start.4 = (bf16[128,2048]{1,0:T(8,128)(2,1)S(1)}, bf16[128,2048]{1,0:T(8,128)(2,1)}, u32[]{:S(2)}) copy-start(bf16[128,2048]{1,0:T(8,128)(2,1)} %param.18) | copy-start | bytes 1572868
  1098.3 55.8 %copy-start.34 = (f32[8,1,256]{2,1,0:T(1,128)S(1)}, f32[8,1,256]{2,1,0:T(1,128)}, u32[]{:S(2)}) copy-start(f32[8,1,256]{2,1,0:T(1,128)} %copy-done.33) | copy-start | bytes 24580
  1098.3 55.8 %copy-start.58 = (f32[128]{0:T(128)S(1)}, f32[128]{0:T(128)}, u32[]{:S(2)}) copy-start(f32[128]{0:T(128)} %copy-done.57) | copy-start | bytes 1540
  1113.2 45.9 %copy-start.48 = (f32[4,512]{1,0:T(4,128)S(1)}, f32[4,512]{1,0:T(4,128)}, u32[]{:S(2)}) copy-start(f32[4,512]{1,0:T(4,128)} %copy-done.47) | copy-start | bytes 24580
  1113.2 45.9 %copy-start.50 = (f32[4,512]{1,0:T(4,128)S(1)}, f32[4,512]{1,0:T(4,128)}, u32[]{:S(2)}) copy-start(f32[4,512]{1,0:T(4,128)} %copy-done.49) | copy-start | bytes 24580
  1113.2 91.3 %all-gather.34.cloned.1.call-start = ((), (), s32[]{:S(2)}) async-start(), calls=%async_computation.29 | async-start | bytes 2621440 | tf_op jit(solution)/shard_map/all_gather | solution.py:313
  1156.4 51.7 %copy-start.63 = (f32[128]{0:T(128)}, f32[128]{0:T(128)S(1)}, u32[]{:S(2)}) copy-start(f32[128]{0:T(128)S(1)} %broadcast_multiply_fusion.3) | copy-start | bytes 1540
  1159.0 404.7 %reduce-scatter.37.cloned.1.call-start = ((), (), s32[]{:S(2)}) async-start(), calls=%async_computation.38 | async-start | bytes 819200
  1215.8 356.1 %reduce-scatter.35.cloned.1.call-start = ((), (), s32[]{:S(2)}) async-start(), calls=%async_computation.37 | async-start | bytes 3244032 | tf_op jit(solution)/shard_map/reduce_scatter | solution.py:422
  1221.0 352.9 %reduce-scatter.31.cloned.1.call-start = ((), (), s32[]{:S(2)}) async-start(), calls=%async_computation.35 | async-start | bytes 3244032 | tf_op jit(solution)/shard_map/reduce_scatter | solution.py:416
  1255.0 212.0 %all-to-all-start.1 = ((bf16[8,2,256,2048]{3,2,1,0:T(8,128)(2,1)}), bf16[8,2,256,2048]{3,2,1,0:T(8,128)(2,1)}, u32[]{:S(2)}, u32[]{:S(2)}) async-start(bf16[8,2,256,2048]{3,2,1,0:T(8,128)(2,1)} %copy.98), calls=%async_computation.2 | async-start | bytes 33554432 | tf_op jit(solution)/shard_map/all_to_all | solution.py:286
  1260.8 315.0 %reduce-scatter.33.cloned.1.call-start = ((), (), s32[]{:S(2)}) async-start(), calls=%async_computation.36 | async-start | bytes 3244032 | tf_op jit(solution)/shard_map/reduce_scatter | solution.py:419
  1266.0 347.5 %reduce-scatter.27.cloned.1.call-start = ((), (), s32[]{:S(2)}) async-start(), calls=%async_computation.33 | async-start | bytes 1179648 | tf_op jit(solution)/shard_map/reduce_scatter | solution.py:410
  1270.0 345.1 %reduce-scatter.29.cloned.1.call-start = ((), (), s32[]{:S(2)}) async-start(), calls=%async_computation.34 | async-start | bytes 2359296 | tf_op jit(solution)/shard_map/reduce_scatter | solution.py:413
  1274.5 346.0 %reduce-scatter.21.cloned.1.call-start = ((), (), s32[]{:S(2)}) async-start(), calls=%async_computation.30 | async-start | bytes 2621440 | tf_op jit(solution)/shard_map/reduce_scatter | solution.py:375
  1282.3 387.7 %reduce-scatter.17.cloned.1.call-start = ((), (), s32[]{:S(2)}) async-start(), calls=%async_computation.26 | async-start | bytes 2621440 | tf_op jit(solution)/shard_map/reduce_scatter | solution.py:301
  1558.2 157.8 %reduce-scatter.23.cloned.1.call-start = ((), (), s32[]{:S(2)}) async-start(), calls=%async_computation.31 | async-start | bytes 3538944 | tf_op jit(solution)/shard_map/reduce_scatter | solution.py:407
  1563.7 309.4 %reduce-scatter.25.cloned.1.call-start = ((), (), s32[]{:S(2)}) async-start(), calls=%async_computation.32 | async-start | bytes 5406720 | tf_op jit(solution)/shard_map/reduce_scatter | solution.py:428
  1601.9 18.6 copy-start.37
  1613.5 56.5 %copy-start.35 = (f32[8,1,256]{2,1,0:T(1,128)S(1)}, f32[8,1,256]{2,1,0:T(1,128)}, u32[]{:S(2)}) copy-start(f32[8,1,256]{2,1,0:T(1,128)} %copy-done.33) | copy-start | bytes 24580
  (49 other events, 242.4 us)
Sparse Core Ops, SparseCore 0:
  9.9 32.1 all-gather.13
  44.0 23.4 all-gather.15
  69.7 45.9 all-gather.17
  117.4 31.0 all-gather.19
  150.2 28.1 all-gather.21
  183.0 43.8 reduce-scatter.14
  230.9 45.2 all-gather.23
  321.0 45.0 all-gather.31
  511.0 112.7 all-gather.27
  778.5 113.0 all-gather.25
  893.6 63.8 all-gather.29
  1113.3 40.7 reduce-scatter.18
  1159.1 45.2 all-gather.33
  1215.9 20.8 reduce-scatter.36
  1240.6 129.9 reduce-scatter.34
  1374.8 67.3 reduce-scatter.30
  1446.0 44.0 reduce-scatter.32
  1493.4 36.0 reduce-scatter.26
  1533.1 41.2 reduce-scatter.28
  1576.5 43.9 reduce-scatter.20
  1622.9 44.1 reduce-scatter.16
  1670.5 45.4 reduce-scatter.22
  1719.0 154.0 reduce-scatter.24
where the time goes:
time: 1890 us; the launch traced here: 1880 us
  waiting for transfers between devices  1110 us (59%)
  local copies, waits for them, and re-layouts  324 us (17%)
  matrix products  238 us (13%)
  blocking collectives  92.5 us (5%)
  other arithmetic  79.1 us (4%)
  starting transfers between devices  25 us (1%)
    all_to_all x1, waiting for transfers between devices, per_device(): lax.all_to_all(expert_part, 'fsdp', split_axis=0, concat_axis=0, tiled=True)  184 us
    all_to_all x1, waiting for transfers between devices, per_device(): lax.all_to_all(send_grad, 'fsdp', split_axis=0, concat_axis=0, tiled=True)  171 us
    reduce_scatter x1, waiting for transfers between devices, per_device(): lax.psum_scatter(latent_proj_part, ('fsdp', 'tp'), scatter_dimension=0, t...  155 us
    all_gather x1, waiting for transfers between devices, per_device(): lax.all_gather(shared_gate, 'fsdp', axis=0, tiled=True)  108 us
    gather x6, local copies, waits for them, and re-layouts, per_device(): d_routed_in = d_routed_in + grad_flat[column]  96.1 us
    all_to_all x1, waiting for transfers between devices, per_device(): lax.all_to_all(send_in, 'fsdp', split_axis=0, concat_axis=0, tiled=True)  85.3 us
    gather x6, local copies, waits for them, and re-layouts, per_device(): part_flat[column].astype(jnp.float32)  80.1 us
    all_gather x1, waiting for transfers between devices, per_device(): lax.all_gather(shared_down, 'fsdp', axis=1, tiled=True)  60.7 us
  transfers between devices with their start and end apart: 27, of which 19 were waited for; matrix products, arithmetic and copies ran while one was open for 24% of the time, Pallas kernels for 0%

commit v1 on v0

v1 whole, which is shorter than its diff:
```python
import functools

import jax
import jax.numpy as jnp
from jax import lax
from jax.experimental import pallas as pl
from jax.experimental.pallas import tpu as pltpu
from jax.sharding import PartitionSpec as P

H = 16
NOPE = 128
ROPE = 64
DV = 128
LAT = 512
TOPK = 6
SEQ = 512
HALF = 256
QUARTET = 4


EPSILON = 1e-06
THETA_BASE = 10000.0
MASK_FILL = -1e30
NO_SLOT = -1e6

BF = jnp.bfloat16
F32 = jnp.float32


def rope_tables(positions, width_rope):
    middle = width_rope // 2
    frequency = THETA_BASE ** (-(jnp.arange(middle) * 2).astype(jnp.float32) / width_rope)
    angles = positions.astype(jnp.float32)[:, None] * frequency[None, :]
    return (jnp.cos(angles), jnp.sin(angles))


def rotate(values, cosine, sine_part):
    middle = values.shape[-1] // 2
    first_half = values[..., :middle]
    second_half = values[..., middle:]
    return jnp.concatenate(
        [
            first_half * cosine - second_half * sine_part,
            second_half * cosine + first_half * sine_part,
        ],
        axis=-1,
    )


def unrotate(values, cosine, sine_part):
    middle = values.shape[-1] // 2
    first_half = values[..., :middle]
    second_half = values[..., middle:]
    return jnp.concatenate(
        [
            first_half * cosine + second_half * sine_part,
            second_half * cosine - first_half * sine_part,
        ],
        axis=-1,
    )


def norm_parts(values):
    inverse = lax.rsqrt(jnp.mean(values * values, axis=-1, keepdims=True) + EPSILON)
    return (values * inverse, inverse)


def norm_back(upstream, unit_rows, inverse, scaling):
    scaled = upstream * scaling
    gain_grad = jnp.sum(upstream * unit_rows, axis=0)
    input_grad = inverse * (
        scaled - unit_rows * jnp.mean(scaled * unit_rows, axis=-1, keepdims=True)
    )
    return (gain_grad, input_grad)


def silu_back(grad_hidden, gate_pre, up_pre):
    sigmoid = jax.nn.sigmoid(gate_pre)
    gate_grad = grad_hidden * up_pre * (sigmoid * (1.0 + gate_pre * (1.0 - sigmoid)))
    up_grad = grad_hidden * (gate_pre * sigmoid)
    return (gate_grad.astype(jnp.bfloat16), up_grad.astype(jnp.bfloat16))


def is_power(count):
    return count & (count - 1) == 0


def swap(values, axis_name, bit):
    count = lax.axis_size(axis_name)
    return lax.ppermute(values, axis_name, [(i, i ^ bit) for i in range(count)])


def dot_rows(left, right):
    return lax.dot_general(left, right, (((1,), (1,)), ((), ())), preferred_element_type=F32)


def dot_plain(left, right):
    return lax.dot_general(left, right, (((1,), (0,)), ((), ())), preferred_element_type=F32)


def dot_first(left, right):
    return lax.dot_general(left, right, (((0,), (0,)), ((), ())), preferred_element_type=F32)


def select_rows(slot_rows, experts, cap):
    row = lax.broadcasted_iota(jnp.int32, (experts * cap, HALF), 0).astype(F32)
    hit = row == slot_rows[0:1, :]
    for e in range(1, experts):
        hit = hit | (row == slot_rows[e : e + 1, :] + float(e * cap))
    return hit


def select_cols(slot_cols, experts, cap):
    lane = lax.broadcasted_iota(jnp.int32, (HALF, experts * cap), 1).astype(F32)
    hit = lane == slot_cols[:, 0:1]
    for e in range(1, experts):
        hit = hit | (lane == slot_cols[:, e : e + 1] + float(e * cap))
    return hit


def slot_weights(hit, weight_rows, experts, cap):
    pieces = []
    for e in range(experts):
        part = hit[e * cap : (e + 1) * cap, :]
        pieces.append(
            jnp.sum(jnp.where(part, weight_rows[e : e + 1, :], 0.0), axis=1, keepdims=True)
        )
    return jnp.concatenate(pieces, axis=0)


def expert_front_kernel(step, experts, cap, aliased, *refs):
    count = QUARTET
    x_in, dy_in = refs[:count], refs[count : 2 * count]
    gate_up_in, down_in, slot_row_ref, weight_row_ref, slot_col_ref = refs[
        2 * count : 2 * count + 5
    ]
    base = 2 * count + 5 + aliased
    dx_out = refs[base : base + count]
    x_all, d_all, hid_all, dgu_all = refs[base + count : base + count + 4]
    (xb, db, gate_up, down, xs, ds, dxs, dxo, hid, dgu, sem_in, sem_w, sem_out, sem_dx) = refs[
        base + count + 4 :
    ]
    width = xb.shape[2]
    pad = down.shape[1]
    tile = min(1024, width)
    x_copies = [pltpu.make_async_copy(x_in[q], xb.at[q], sem_in.at[q]) for q in range(count)]
    d_copies = [
        pltpu.make_async_copy(dy_in[q], db.at[q], sem_in.at[count + q]) for q in range(count)
    ]
    w_copies = [
        pltpu.make_async_copy(gate_up_in, gate_up, sem_w.at[0]),
        pltpu.make_async_copy(down_in, down, sem_w.at[1]),
    ]
    for q in range(count):
        x_copies[q].start()
        d_copies[q].start()
    for copy in w_copies:
        copy.start()
    for q in range(count):
        x_copies[q].wait()
        d_copies[q].wait()

        hit = select_rows(slot_row_ref[q], experts, cap)
        weights = slot_weights(hit, weight_row_ref[q], experts, cap)
        choose = jnp.where(hit, 1.0, 0.0).astype(BF)

        def spread(n, carry, q=q, choose=choose, weights=weights):
            cols = pl.ds(pl.multiple_of(n * tile, tile), tile)
            rows = dot_plain(choose, xb[q, :, cols])
            grads = dot_plain(choose, db[q, :, cols]) * weights
            for e in range(experts):
                xs[e, q * cap : (q + 1) * cap, cols] = rows[e * cap : (e + 1) * cap].astype(BF)
                ds[e, q * cap : (q + 1) * cap, cols] = grads[e * cap : (e + 1) * cap].astype(BF)
            return carry

        lax.fori_loop(0, width // tile, spread, 0)
    out_copies = [
        pltpu.make_async_copy(xs, x_all.at[step], sem_out.at[0]),
        pltpu.make_async_copy(ds, d_all.at[step], sem_out.at[1]),
        pltpu.make_async_copy(hid, hid_all.at[step], sem_out.at[2]),
        pltpu.make_async_copy(dgu, dgu_all.at[step], sem_out.at[3]),
    ]
    out_copies[0].start()
    out_copies[1].start()
    for copy in w_copies:
        copy.wait()

    def one_expert(e, carry):
        both = dot_rows(xs[e], gate_up[e])
        gate_pre, up_pre = both[:, :pad], both[:, pad:]
        d_hidden = dot_rows(ds[e], down[e])
        sigmoid = jax.nn.sigmoid(gate_pre)
        silu = gate_pre * sigmoid
        hid[e] = (silu * up_pre).astype(BF)
        gate_grad = d_hidden * up_pre * (sigmoid * (1.0 + gate_pre * (1.0 - sigmoid)))
        grads = jnp.concatenate([gate_grad, d_hidden * silu], axis=1).astype(BF)
        dgu[e] = grads

        def back(n, inner):
            cols = pl.ds(pl.multiple_of(n * tile, tile), tile)
            part = dot_plain(dgu[e], gate_up[e, :, cols]).astype(BF)
            for q in range(count):
                dxs[q, pl.ds(pl.multiple_of(e * cap, cap), cap), cols] = part[
                    q * cap : (q + 1) * cap
                ]
            return inner

        lax.fori_loop(0, width // tile, back, 0)
        return carry

    lax.fori_loop(0, experts, one_expert, 0)
    out_copies[2].start()
    out_copies[3].start()
    dx_copies = [pltpu.make_async_copy(dxo.at[q], dx_out[q], sem_dx.at[q]) for q in range(count)]
    for q in range(count):
        choose = jnp.where(select_cols(slot_col_ref[q], experts, cap), 1.0, 0.0).astype(BF)

        def gather(n, carry, q=q, choose=choose):
            cols = pl.ds(pl.multiple_of(n * tile, tile), tile)
            dxo[q, :, cols] = dot_plain(choose, dxs[q, :, cols]).astype(BF)
            return carry

        lax.fori_loop(0, width // tile, gather, 0)
        dx_copies[q].start()
    for copy in out_copies:
        copy.wait()
    for copy in dx_copies:
        copy.wait()


def expert_front(step, steps, x_parts, dy_parts, gate_up, down, tables, kept, cap):
    experts, wide, width = gate_up.shape
    pad = wide // 2
    slots = QUARTET * cap
    slot_row, weight_row, slot_col = (t[step] for t in tables)
    any_spec = pl.BlockSpec(memory_space=pl.ANY)
    vmem_spec = pl.BlockSpec(memory_space=pltpu.VMEM)
    half_shape = jax.ShapeDtypeStruct((HALF, width), BF)
    kept_shapes = [
        jax.ShapeDtypeStruct((steps, experts, slots, columns), BF)
        for columns in (width, width, pad, wide)
    ]
    results = pl.pallas_call(
        functools.partial(expert_front_kernel, step, experts, cap, len(kept)),
        out_shape=[half_shape] * QUARTET + kept_shapes,
        in_specs=[any_spec] * (2 * QUARTET + 2) + [vmem_spec] * 3 + [any_spec] * len(kept),
        out_specs=[any_spec] * (QUARTET + 4),
        input_output_aliases={2 * QUARTET + 5 + i: QUARTET + i for i in range(len(kept))},
        scratch_shapes=[
            pltpu.VMEM((QUARTET, HALF, width), BF),
            pltpu.VMEM((QUARTET, HALF, width), BF),
            pltpu.VMEM((experts, wide, width), BF),
            pltpu.VMEM((experts, pad, width), BF),
            pltpu.VMEM((experts, slots, width), BF),
            pltpu.VMEM((experts, slots, width), BF),
            pltpu.VMEM((QUARTET, experts * cap, width), BF),
            pltpu.VMEM((QUARTET, HALF, width), BF),
            pltpu.VMEM((experts, slots, pad), BF),
            pltpu.VMEM((experts, slots, wide), BF),
            pltpu.SemaphoreType.DMA((2 * QUARTET,)),
            pltpu.SemaphoreType.DMA((2,)),
            pltpu.SemaphoreType.DMA((4,)),
            pltpu.SemaphoreType.DMA((QUARTET,)),
        ],
        compiler_params=pltpu.CompilerParams(vmem_limit_bytes=62 * 1024 * 1024),
        cost_estimate=pl.CostEstimate(
            flops=2 * slots * experts * width * pad * 5
            + 6 * QUARTET * HALF * experts * cap * width,
            bytes_accessed=2 * width * (3 * QUARTET * HALF + experts * 3 * pad + 2 * experts * slots),
            transcendentals=slots * experts * pad,
        ),
        name="expert_front",
    )(*x_parts, *dy_parts, gate_up, down, slot_row, weight_row, slot_col, *kept)
    return list(results[:QUARTET]), list(results[QUARTET:])


def expert_out_kernel(experts, cap, hid, down, slot_row, weight_row, slot_col, out, parts):
    width = down.shape[2]
    tile = min(1024, width)
    for q in range(QUARTET):
        hit = select_rows(slot_row[0, q], experts, cap)
        weights = slot_weights(hit, weight_row[0, q], experts, cap)

        def front(n, carry, q=q, weights=weights):
            cols = pl.ds(pl.multiple_of(n * tile, tile), tile)
            for e in range(experts):
                rows = dot_plain(hid[0, e, q * cap : (q + 1) * cap, :], down[e, :, cols])
                parts[q, e * cap : (e + 1) * cap, cols] = (
                    rows * weights[e * cap : (e + 1) * cap]
                ).astype(BF)
            return carry

        lax.fori_loop(0, width // tile, front, 0)
    for q in range(QUARTET):
        choose = jnp.where(select_cols(slot_col[0, q], experts, cap), 1.0, 0.0).astype(BF)

        def gather(n, carry, q=q, choose=choose):
            cols = pl.ds(pl.multiple_of(n * tile, tile), tile)
            out[0, q, :, cols] = dot_plain(choose, parts[q, :, cols]).astype(BF)
            return carry

        lax.fori_loop(0, width // tile, gather, 0)


def expert_out(hid_all, down, tables, cap):
    steps, experts, slots, pad = hid_all.shape
    width = down.shape[2]
    slot_row, weight_row, slot_col = tables
    return pl.pallas_call(
        functools.partial(expert_out_kernel, experts, cap),
        grid=(steps,),
        out_shape=jax.ShapeDtypeStruct((steps, QUARTET, HALF, width), BF),
        in_specs=[
            pl.BlockSpec((1, experts, slots, pad), lambda i: (i, 0, 0, 0)),
            pl.BlockSpec((experts, pad, width), lambda i: (0, 0, 0)),
            pl.BlockSpec((1,) + slot_row.shape[1:], lambda i: (i, 0, 0, 0)),
            pl.BlockSpec((1,) + weight_row.shape[1:], lambda i: (i, 0, 0, 0)),
            pl.BlockSpec((1,) + slot_col.shape[1:], lambda i: (i, 0, 0, 0)),
        ],
        out_specs=pl.BlockSpec((1, QUARTET, HALF, width), lambda i: (i, 0, 0, 0)),
        scratch_shapes=[pltpu.VMEM((QUARTET, experts * cap, width), BF)],
        compiler_params=pltpu.CompilerParams(vmem_limit_bytes=48 * 1024 * 1024),
        cost_estimate=pl.CostEstimate(
            flops=steps * (2 * slots * experts * width * pad + 2 * QUARTET * HALF * experts * cap * width),
            bytes_accessed=2 * steps * QUARTET * HALF * width + 2 * hid_all.size + 2 * down.size,
            transcendentals=0,
        ),
        name="expert_out",
    )(hid_all, down, slot_row, weight_row, slot_col)


def expert_grads_kernel(dgu, x, hid, d, gate_grad, up_grad, down_grad):
    local = gate_grad.shape[1]
    pad = hid.shape[3]
    width = x.shape[3]
    tile = min(1024, width)

    @pl.when(pl.program_id(1) == 0)
    def _():
        gate_grad[...] = jnp.zeros_like(gate_grad)
        up_grad[...] = jnp.zeros_like(up_grad)
        down_grad[...] = jnp.zeros_like(down_grad)

    def part(n, carry):
        cols = pl.ds(pl.multiple_of(n * tile, tile), tile)
        gate_grad[0, :, cols] += dot_first(dgu[0, 0, :, :pad], x[0, 0, :, cols])[:local]
        up_grad[0, :, cols] += dot_first(dgu[0, 0, :, pad:], x[0, 0, :, cols])[:local]
        down_grad[0, :, cols] += dot_first(hid[0, 0], d[0, 0, :, cols])[:local]
        return carry

    lax.fori_loop(0, width // tile, part, 0)


def expert_grads(kept, local):
    x_all, d_all, hid_all, dgu_all = kept
    steps, experts, slots, width = x_all.shape
    pad = hid_all.shape[3]

    def block(array):
        return pl.BlockSpec((1, 1) + array.shape[2:], lambda e, i: (i, e, 0, 0))

    grad = jax.ShapeDtypeStruct((experts, local, width), F32)
    return pl.pallas_call(
        expert_grads_kernel,
        grid=(experts, steps),
        out_shape=[grad] * 3,
        in_specs=[block(dgu_all), block(x_all), block(hid_all), block(d_all)],
        out_specs=[pl.BlockSpec((1, local, width), lambda e, i: (e, 0, 0))] * 3,
        compiler_params=pltpu.CompilerParams(vmem_limit_bytes=48 * 1024 * 1024),
        cost_estimate=pl.CostEstimate(
            flops=2 * 3 * steps * experts * slots * width * pad,
            bytes_accessed=2 * (x_all.size + d_all.size + hid_all.size + dgu_all.size)
            + 12 * experts * local * width,
            transcendentals=0,
        ),
        name="expert_grads",
    )(dgu_all, x_all, hid_all, d_all)


def plane_units(count):
    if count == 8:
        return [
            [(0, 0), (0, 1), (1, 0), (1, 1)],
            [(2, 0), (4, 1), (3, 0), (5, 1)],
            [(2, 1), (4, 0), (3, 1), (5, 0)],
            [(6, 0), (6, 1), (7, 0), (7, 1)],
        ]
    return [[(2 * i + j // 2, j % 2) for j in range(4)] for i in range(count // 2)]


def plane_gather(rows, count):
    top, bottom = rows[:HALF], rows[HALF:]
    blocks = {}
    if count == 8:
        own = {0: top, 1: bottom}
        for h in (0, 1):
            blocks[0, h] = own[h]
            blocks[1, h] = swap(own[h], "fsdp", 1)
        blocks[2, 0] = swap(top, "fsdp", 2)
        blocks[4, 1] = swap(bottom, "fsdp", 4)
        blocks[2, 1] = swap(bottom, "fsdp", 2)
        blocks[4, 0] = swap(top, "fsdp", 4)
        blocks[6, 0] = swap(blocks[2, 0], "fsdp", 4)
        blocks[6, 1] = swap(blocks[4, 1], "fsdp", 2)
        for r in (2, 4, 6):
            for h in (0, 1):
                blocks[r + 1, h] = swap(blocks[r, h], "fsdp", 1)
        return blocks
    gathered = lax.all_gather(rows, "fsdp", axis=0)
    for r in range(count):
        blocks[r, 0] = gathered[r, :HALF]
        blocks[r, 1] = gathered[r, HALF:]
    return blocks


def plane_scatter(parts, count):
    if count == 8:

        def add(left, right):
            return left.astype(F32) + right.astype(F32)

        chip = {}
        for r in (2, 4, 6, 0):
            for h in (0, 1):
                chip[r, h] = add(parts[r, h], swap(parts[r + 1, h], "fsdp", 1))
        top = add(chip[0, 0], swap(chip[2, 0].astype(BF), "fsdp", 2))
        bottom = add(chip[0, 1], swap(chip[4, 1].astype(BF), "fsdp", 4))
        over_top = add(chip[4, 0], swap(chip[6, 0].astype(BF), "fsdp", 2)).astype(BF)
        over_bottom = add(chip[2, 1], swap(chip[6, 1].astype(BF), "fsdp", 4)).astype(BF)
        top = add(top, swap(over_top, "fsdp", 4))
        bottom = add(bottom, swap(over_bottom, "fsdp", 2))
        return jnp.concatenate([top, bottom], axis=0)
    stacked = jnp.concatenate([parts[r, h] for r in range(count) for h in (0, 1)], axis=0)
    return lax.psum_scatter(stacked, "fsdp", scatter_dimension=0, tiled=True).astype(F32)


def sum_everywhere(values):
    for axis_name in ("fsdp", "tp"):
        count = lax.axis_size(axis_name)
        if is_power(count):
            bit = 1
            while bit < count:
                values = values + swap(values, axis_name, bit)
                bit *= 2
        else:
            values = lax.psum(values, axis_name)
    return values


def expert_tables(expert_ids, expert_wts, local_experts, units, cap):
    fsdp_count = lax.axis_size("fsdp")
    fsdp_rank = lax.axis_index("fsdp")
    expert_count = local_experts * fsdp_count
    names = jnp.arange(expert_count, dtype=jnp.int32)[:, None]
    member = jnp.zeros((expert_count, SEQ), jnp.bool_)
    weight = jnp.zeros((expert_count, SEQ), F32)
    ids_rows, wts_rows = expert_ids.T, expert_wts.T
    for pick in range(TOPK):
        same = ids_rows[pick : pick + 1] == names
        member = member | same
        weight = weight + jnp.where(same, wts_rows[pick : pick + 1], 0.0)
    position = jnp.arange(HALF)
    before = (position[:, None] < position[None, :]).astype(BF)
    rank = jnp.dot(
        member.astype(BF).reshape(expert_count * 2, HALF), before, preferred_element_type=F32
    ).reshape(expert_count, SEQ)
    slot = jnp.where(member, rank, NO_SLOT)
    table = jnp.concatenate([slot, weight], axis=0)
    table = lax.all_gather(table, "fsdp", axis=0).reshape(
        fsdp_count, 2, fsdp_count, local_experts, 2, HALF
    )
    table = lax.dynamic_index_in_dim(table, fsdp_rank, axis=2, keepdims=False)
    relative = jnp.arange(fsdp_count, dtype=jnp.int32)
    order = relative ^ fsdp_rank if fsdp_count == 8 else relative
    table = jnp.take(table, order, axis=0)
    slot_steps, weight_steps = [], []
    for unit in units:
        slot_steps.append(jnp.stack([table[r, 0, :, h] for r, h in unit]))
        weight_steps.append(jnp.stack([table[r, 1, :, h] for r, h in unit]))
    slot_row, weight_row = jnp.stack(slot_steps), jnp.stack(weight_steps)
    return (slot_row, weight_row, jnp.swapaxes(slot_row, 2, 3))


def per_device(
    block_in,
    out_cotan,
    segment_ids,
    expert_ids,
    expert_wts,
    attn_gain,
    query_proj,
    latent_proj,
    latent_gain,
    latent_up,
    out_proj,
    ffn_gain,
    shared_gate,
    shared_up,
    shared_down,
    routed_gate,
    routed_up,
    routed_down,
):
    tp_count = lax.axis_size("tp")
    fsdp_count = lax.axis_size("fsdp")
    tp_rank = lax.axis_index("tp")
    fsdp_rank = lax.axis_index("fsdp")
    tok_rows, model_width = block_in.shape
    local_experts, local_hidden = routed_gate.shape[:2]
    expert_count = local_experts * fsdp_count
    cap_rows = tok_rows * TOPK * 4 // (3 * expert_count)
    cap = cap_rows * (HALF // tok_rows)
    heads_local = H // tp_count
    head_width = NOPE + ROPE
    score_scale = head_width ** (-0.5)
    shard_rows, query_cols = query_proj.shape
    latent_cols = latent_proj.shape[1]
    up_cols = latent_up.shape[1]
    out_rows = out_proj.shape[0]
    units = plane_units(fsdp_count)

    joint = query_cols + latent_cols
    spare = (-joint) % 128
    spare = spare + 128 if spare < 3 else spare
    gains = jnp.concatenate(
        [
            attn_gain[:, None],
            ffn_gain[:, None],
            jnp.pad(latent_gain, (0, shard_rows - latent_gain.shape[0]))[:, None],
            jnp.zeros((shard_rows, spare - 3), BF),
        ],
        axis=1,
    )
    packed = jnp.concatenate(
        [query_proj, latent_proj, gains, latent_up.reshape(shard_rows, -1)], axis=1
    )
    packed_all = lax.all_gather(packed, "fsdp", axis=0, tiled=True)
    joint_weight = packed_all[:, :joint]
    gain_attn = packed_all[:, joint].astype(F32)
    gain_ffn = packed_all[:, joint + 1].astype(F32)
    gain_latent = (
        packed_all[:, joint + 2]
        .reshape(fsdp_count, shard_rows)[:, : latent_gain.shape[0]]
        .reshape(LAT)
        .astype(F32)
    )
    latent_up_weight = packed_all[:, joint + spare :].reshape(LAT, up_cols)
    tokens_all = lax.all_gather(block_in, "tp", axis=0, tiled=True)
    out_down = lax.all_gather(
        jnp.concatenate([out_proj, shared_down], axis=0), "fsdp", axis=1, tiled=True
    )
    out_weight, shared_down_weight = out_down[:out_rows], out_down[out_rows:]
    cotan_all = lax.all_gather(out_cotan, "tp", axis=0, tiled=True)
    shared_weight = lax.all_gather(
        jnp.concatenate([shared_gate, shared_up], axis=1), "fsdp", axis=0, tiled=True
    )
    shared_cols = shared_gate.shape[1]
    tables = expert_tables(expert_ids, expert_wts, local_experts, units, cap)
    hidden_pad = -(-local_hidden // 128) * 128
    lift = ((0, 0), (0, hidden_pad - local_hidden), (0, 0))
    routed_gate_up = jnp.concatenate([jnp.pad(routed_gate, lift), jnp.pad(routed_up, lift)], axis=1)
    routed_down_pad = jnp.pad(routed_down, lift)

    unit_all, inverse_all = norm_parts(tokens_all.astype(F32))
    normed_all = (unit_all * gain_attn).astype(BF)
    joint_rows = jnp.dot(normed_all, joint_weight, preferred_element_type=F32)
    queries = joint_rows[:, :query_cols].reshape(SEQ, heads_local, head_width)
    latent = joint_rows[:, query_cols:]
    unit_lat, inverse_lat = norm_parts(latent[:, :LAT])
    positions = jnp.arange(SEQ, dtype=jnp.int32)
    cosine, sine_part = rope_tables(positions, ROPE)
    compressed_all = (unit_lat * gain_latent).astype(BF)
    key_rope_all = rotate(latent[:, LAT:], cosine, sine_part).astype(BF)
    query_cat = jnp.concatenate(
        [
            queries[:, :, :NOPE],
            rotate(queries[:, :, NOPE:], cosine[:, None, :], sine_part[:, None, :]),
        ],
        axis=2,
    ).astype(BF)
    key_value = (
        jnp.dot(compressed_all, latent_up_weight, preferred_element_type=F32)
        .reshape(SEQ, heads_local, NOPE + DV)
        .astype(BF)
    )
    key_cat = jnp.concatenate(
        [
            key_value[:, :, :NOPE],
            jnp.broadcast_to(key_rope_all[:, None, :], (SEQ, heads_local, ROPE)),
        ],
        axis=2,
    )
    values = key_value[:, :, NOPE:]
    allowed = (positions[None, :] <= positions[:, None]) & (
        segment_ids[None, :] == segment_ids[:, None]
    )
    raw_scores = (
        jnp.einsum("qhd,khd->hqk", query_cat, key_cat, preferred_element_type=F32) * score_scale
    )
    masked = jnp.where(allowed[None], raw_scores, MASK_FILL)
    top_score = jnp.max(masked, axis=2, keepdims=True)
    exponent = jnp.exp(masked - top_score)
    row_total = jnp.sum(exponent, axis=2, keepdims=True)
    probabilities = exponent / row_total
    probs_low = probabilities.astype(BF)
    attended = (
        jnp.einsum("hqk,khd->qhd", probs_low, values, preferred_element_type=F32)
        .reshape(SEQ, heads_local * DV)
        .astype(BF)
    )
    attn_rows = lax.psum_scatter(
        jnp.dot(attended, out_weight, preferred_element_type=F32).astype(BF),
        "tp",
        scatter_dimension=0,
        tiled=True,
    ).astype(F32)
    mixed_rows = block_in.astype(F32) + attn_rows
    unit_two, inverse_two = norm_parts(mixed_rows)
    normed_ffn = (unit_two * gain_ffn).astype(BF)
    normed_ffn_all = lax.all_gather(normed_ffn, "tp", axis=0, tiled=True)

    x_blocks = plane_gather(normed_ffn_all, fsdp_count)
    dy_blocks = plane_gather(cotan_all, fsdp_count)
    kept = []
    dx_parts = {}
    for step, unit in enumerate(units):
        dx_list, kept = expert_front(
            step,
            len(units),
            [x_blocks[key] for key in unit],
            [dy_blocks[key] for key in unit],
            routed_gate_up,
            routed_down_pad,
            tables,
            kept,
            cap,
        )
        for key, part in zip(unit, dx_list):
            dx_parts[key] = part
    d_routed_in = plane_scatter(dx_parts, fsdp_count)
    out_array = expert_out(kept[2], routed_down_pad, tables, cap)
    out_parts = {
        key: out_array[step, q] for step, unit in enumerate(units) for q, key in enumerate(unit)
    }
    routed_rows = plane_scatter(out_parts, fsdp_count)
    routed_gate_grad, routed_up_grad, routed_down_grad = expert_grads(kept, local_hidden)

    shared_pre = jnp.dot(normed_ffn_all, shared_weight, preferred_element_type=F32)
    shared_gate_pre, shared_up_pre = shared_pre[:, :shared_cols], shared_pre[:, shared_cols:]
    shared_hidden = (jax.nn.silu(shared_gate_pre) * shared_up_pre).astype(BF)
    shared_rows = jnp.dot(shared_hidden, shared_down_weight, preferred_element_type=F32)
    shared_down_part = jnp.dot(shared_hidden.T, cotan_all, preferred_element_type=F32)
    d_shared_hidden = jnp.dot(cotan_all, shared_down_weight.T, preferred_element_type=F32)
    d_shared = jnp.concatenate(silu_back(d_shared_hidden, shared_gate_pre, shared_up_pre), axis=1)
    shared_part = jnp.dot(normed_ffn_all.T, d_shared, preferred_element_type=F32)
    d_shared_in = jnp.dot(d_shared, shared_weight.T, preferred_element_type=F32)

    d_normed_ffn = lax.psum_scatter(
        (d_shared_in + d_routed_in).astype(BF), "tp", scatter_dimension=0, tiled=True
    ).astype(F32)
    ffn_rows = lax.psum_scatter(
        (shared_rows + routed_rows).astype(BF), "tp", scatter_dimension=0, tiled=True
    ).astype(F32)
    block_out = (mixed_rows + ffn_rows).astype(BF)
    ffn_gain_part, d_mixed_norm = norm_back(d_normed_ffn, unit_two, inverse_two, gain_ffn)
    d_mixed = out_cotan.astype(F32) + d_mixed_norm
    d_proj_all = lax.all_gather(d_mixed.astype(BF), "tp", axis=0, tiled=True)

    out_part = jnp.dot(attended.T, d_proj_all, preferred_element_type=F32)
    d_attended = (
        jnp.dot(d_proj_all, out_weight.T, preferred_element_type=F32)
        .astype(BF)
        .reshape(SEQ, heads_local, DV)
    )
    prob_grad = jnp.einsum("qhd,khd->hqk", d_attended, values, preferred_element_type=F32)
    score_grad = (
        probabilities
        * (prob_grad - jnp.sum(probabilities * prob_grad, axis=2, keepdims=True))
    ).astype(BF)
    query_grad = (
        jnp.einsum("hqk,khd->qhd", score_grad, key_cat, preferred_element_type=F32) * score_scale
    )
    key_grad = (
        jnp.einsum("hqk,qhd->khd", score_grad, query_cat, preferred_element_type=F32) * score_scale
    )
    value_grad = jnp.einsum("hqk,qhd->khd", probs_low, d_attended, preferred_element_type=F32)
    d_queries = (
        jnp.concatenate(
            [
                query_grad[:, :, :NOPE],
                unrotate(query_grad[:, :, NOPE:], cosine[:, None, :], sine_part[:, None, :]),
            ],
            axis=2,
        )
        .reshape(SEQ, heads_local * head_width)
        .astype(BF)
    )
    d_key_value = (
        jnp.concatenate([key_grad[:, :, :NOPE], value_grad], axis=2)
        .reshape(SEQ, heads_local * (NOPE + DV))
        .astype(BF)
    )
    latent_up_part = jnp.dot(compressed_all.T, d_key_value, preferred_element_type=F32)
    d_compressed = jnp.dot(d_key_value, latent_up_weight.T, preferred_element_type=F32)
    d_key_rope = jnp.sum(key_grad[:, :, NOPE:], axis=1)
    latent_gain_part, d_latent_main = norm_back(d_compressed, unit_lat, inverse_lat, gain_latent)
    d_latent = jnp.concatenate(
        [d_latent_main, unrotate(d_key_rope, cosine, sine_part)], axis=1
    ).astype(BF)
    d_joint = jnp.concatenate([d_queries, d_latent], axis=1)
    joint_part = jnp.dot(normed_all.T, d_joint, preferred_element_type=F32)
    d_normed_part = jnp.dot(d_joint, joint_weight.T, preferred_element_type=F32)
    attn_gain_part = jnp.sum(d_normed_part * unit_all, axis=0)
    d_normed = lax.psum_scatter(
        d_normed_part.astype(BF), "tp", scatter_dimension=0, tiled=True
    ).astype(F32)
    unit_one, inverse_one = norm_parts(block_in.astype(F32))
    _, d_tokens_norm = norm_back(d_normed, unit_one, inverse_one, gain_attn)
    block_in_grad = d_mixed + d_tokens_norm

    def scatter(part, dimension):
        return lax.psum_scatter(
            part.astype(BF), "fsdp", scatter_dimension=dimension, tiled=True
        )

    joint_grad = scatter(joint_part, 0)
    query_proj_grad = joint_grad[:, :query_cols].astype(F32)
    latent_proj_grad = lax.psum_scatter(
        joint_grad[:, query_cols:], "tp", scatter_dimension=0, tiled=True
    ).astype(F32)
    latent_up_grad = scatter(latent_up_part, 0).astype(F32)
    out_proj_grad = scatter(out_part, 1).astype(F32)
    shared_grad = scatter(shared_part, 0).astype(F32)
    shared_gate_grad, shared_up_grad = shared_grad[:, :shared_cols], shared_grad[:, shared_cols:]
    shared_down_grad = scatter(shared_down_part, 1).astype(F32)
    gain_sums = sum_everywhere(
        jnp.concatenate([attn_gain_part, latent_gain_part, ffn_gain_part]).reshape(-1, 128)
    ).reshape(-1)
    device = fsdp_rank * tp_count + tp_rank
    devices = tp_count * fsdp_count

    def own_gain(start, size):
        return lax.dynamic_slice(gain_sums, (start + device * (size // devices),), (size // devices,))

    attn_gain_grad = own_gain(0, model_width)
    latent_gain_grad = own_gain(model_width, LAT)
    ffn_gain_grad = own_gain(model_width + LAT, model_width)
    return (
        block_out,
        block_in_grad,
        attn_gain_grad,
        query_proj_grad,
        latent_proj_grad,
        latent_gain_grad,
        latent_up_grad,
        out_proj_grad,
        ffn_gain_grad,
        shared_gate_grad,
        shared_up_grad,
        shared_down_grad,
        routed_gate_grad,
        routed_up_grad,
        routed_down_grad,
    )


def solution(mesh):
    placed = (
        P(("fsdp", "tp"), None),
        P(("fsdp", "tp"), None),
        P("fsdp"),
        P("fsdp", None),
        P("fsdp", None),
        P("fsdp"),
        P("fsdp", "tp"),
        P("fsdp", None),
        P("fsdp"),
        P("fsdp", "tp"),
        P("tp", "fsdp"),
        P("fsdp"),
        P("fsdp", "tp"),
        P("fsdp", "tp"),
        P("tp", "fsdp"),
        P("fsdp", "tp", None),
        P("fsdp", "tp", None),
        P("fsdp", "tp", None),
    )
    return jax.shard_map(
        per_device,
        mesh=mesh,
        in_specs=placed,
        out_specs=(
            P(("fsdp", "tp"), None),
            P(("fsdp", "tp"), None),
            P(("fsdp", "tp")),
            P("fsdp", "tp"),
            P(("fsdp", "tp"), None),
            P(("fsdp", "tp")),
            P("fsdp", "tp"),
            P("tp", "fsdp"),
            P(("fsdp", "tp")),
            P("fsdp", "tp"),
            P("fsdp", "tp"),
            P("tp", "fsdp"),
            P("fsdp", "tp", None),
            P("fsdp", "tp", None),
            P("fsdp", "tp", None),
        ),
        check_vma=False,
    )
```

time: 1890 us -> 1100 us (0.58)
  waiting for transfers between devices: 1110 us -> 612 us
  local copies, waits for them, and re-layouts: 324 us -> 67.2 us
  Pallas kernels: 0 us -> 162 us
  matrix products: 238 us -> 79.2 us
  blocking collectives: 92.5 us -> 50 us
  other arithmetic: 79.1 us -> 59.5 us
    all_to_all x4 -> x0, waiting for transfers between devices: 455 us -> none  [the longest x1 184 us: per_device(): lax.all_to_all(expert_part, 'fsdp', split_axis=0, concat_axis=0, tiled=True)]
    gather x14 -> x1, local copies, waits for them, and re-layouts: 243 us -> 0.62 us  [expert_tables(): table = jnp.take(table, order, axis=0)]
    ppermute x0 -> x61, waiting for transfers between devices: none -> 235 us  [swap(): return lax.ppermute(values, axis_name, [(i, i ^ bit) for i in range(count)])]
    all_gather x10 -> x6, waiting for transfers between devices: 348 us -> 176 us  [the longest x1 46.9 us: per_device(): packed_all = lax.all_gather(packed, 'fsdp', axis=0, tiled=True)]
    pallas_call x0 -> x6, Pallas kernels: none -> 162 us  [the longest x4 98.1 us: expert_front(): pl.pallas_call(functools.partial(expert_front_kernel, step, experts, cap,...]
    dot_general x36 -> x22, matrix products: 238 us -> 79.2 us  [the longest x1 8.41 us: per_device(): d_normed_part = jnp.dot(d_joint, joint_weight.T, preferred_element_type=F32)]
    reduce_scatter x11 -> x9, waiting for transfers between devices: 276 us -> 183 us  [the longest x5 51.2 us: scatter(): lax.psum_scatter(part.astype(BF), 'fsdp', scatter_dimension=dimension, ti...]
    unnamed x2 -> x0, blocking collectives: 56.5 us -> none
  transfers between devices with their start and end apart: 27 -> 78, of which waited for: 19 -> 27; matrix products, arithmetic and copies ran while one was open for 24% -> 16% of each run, Pallas kernels for 0% -> 15%
where the time goes in v1:
time: 1100 us; the launch traced here: 1090 us
  waiting for transfers between devices  612 us (56%)
  Pallas kernels  162 us (15%)
  matrix products  79.2 us (7%)
  local copies, waits for them, and re-layouts  67.2 us (6%)
  other arithmetic  59.5 us (5%)
  blocking collectives  50 us (5%)
  starting transfers between devices  38.7 us (4%)
  between operations  16.2 us (1%)
    ppermute x61, waiting for transfers between devices, swap(): return lax.ppermute(values, axis_name, [(i, i ^ bit) for i in range(count)])  235 us
    pallas_call x4, Pallas kernels, expert_front(): pl.pallas_call(functools.partial(expert_front_kernel, step, experts, cap,...  98.1 us
    reduce_scatter x5, waiting for transfers between devices, scatter(): lax.psum_scatter(part.astype(BF), 'fsdp', scatter_dimension=dimension, ti...  51.2 us
    all_gather x1, blocking collectives, expert_tables(): lax.all_gather(table, 'fsdp', axis=0)  50 us
    all_gather x1, waiting for transfers between devices, per_device(): packed_all = lax.all_gather(packed, 'fsdp', axis=0, tiled=True)  46.9 us
    reduce_scatter x1, waiting for transfers between devices, per_device(): lax.psum_scatter((shared_rows + routed_rows).astype(BF), 'tp', scatter_di...  44.2 us
    reduce_scatter x1, waiting for transfers between devices, per_device(): lax.psum_scatter((d_shared_in + d_routed_in).astype(BF), 'tp', scatter_di...  44 us
    reduce_scatter x1, waiting for transfers between devices, per_device(): lax.psum_scatter(jnp.dot(attended, out_weight, preferred_element_type=F32...  43.3 us
  transfers between devices with their start and end apart: 78, of which 27 were waited for; matrix products, arithmetic and copies ran while one was open for 16% of the time, Pallas kernels for 15%

profile of v1, /device:TPU:0, one launch (start us, length us, event | category | flops | bytes accessed | tf_op | source)
XLA Modules:
  0.0 1085.3 jit_solution(1906918856378155628)
XLA Ops:
  16.5 41.8 %all-gather.9.cloned.1.call-done = bf16[512,2048]{1,0:T(8,128)(2,1)} async-done(((bf16[128,2048]{1,0:T(8,128)(2,1)}), bf16[512,2048]{1,0:T(8,128)(2,1)}) %all-gather.9.cloned.1.call-update) | async-done | bytes 2097168 | tf_op jit(solution)/shard_map/all_gather | solution.py:548
  60.3 46.9 %all-gather.11.cloned.1.call-done = bf16[2048,1664]{1,0:T(8,128)(2,1)} async-done(((bf16[256,1664]{1,0:T(8,128)(2,1)}), bf16[2048,1664]{1,0:T(8,128)(2,1)}) %all-gather.11.cloned.1.call-update) | async-done | bytes 6815760 | tf_op jit(solution)/shard_map/all_gather | solution.py:537
  109.5 6.4 fusion.6
  136.0 14.6 %all-gather.13.cloned.1.call-done = bf16[1216,2048]{1,0:T(8,128)(2,1)} async-done(((bf16[1216,256]{1,0:T(8,128)(2,1)}), bf16[1216,2048]{1,0:T(8,128)(2,1)}) %all-gather.13.cloned.1.call-update) | async-done | bytes 4980752 | tf_op jit(solution)/shard_map/all_gather | solution.py:549
  150.6 4.2 convolution_convert_fusion.4
  155.5 43.3 %reduce-scatter.13.cloned.1.call-done = bf16[128,2048]{1,0:T(8,128)(2,1)} async-done(((bf16[512,2048]{1,0:T(8,128)(2,1)}), bf16[128,2048]{1,0:T(8,128)(2,1)}) %reduce-scatter.13.cloned.1.call-update) | async-done | bytes 524304 | tf_op jit(solution)/shard_map/reduce_scatter | solution.py:611
  204.9 40.8 %all-gather.19.cloned.1.call-done = bf16[512,2048]{1,0:T(8,128)(2,1)} async-done(((bf16[128,2048]{1,0:T(8,128)(2,1)}), bf16[512,2048]{1,0:T(8,128)(2,1)}) %all-gather.19.cloned.1.call-update) | async-done | bytes 2097168 | tf_op jit(solution)/shard_map/all_gather | solution.py:553
  245.6 3.2 fusion.127
  252.3 50.0 %all-gather = f32[256,512]{1,0:T(8,128)S(1)} all-gather(f32[32,512]{1,0:T(8,128)S(1)} %pad_maximum_fusion.18), channel_id=2, replica_groups=mesh['fsdp'=8,'tp'=4] {'fsdp'}, dimensions={0}, use_global_device_ids=true | all-gather | bytes 589824 | tf_op jit(solution)/shard_map/all_gather | solution.py:469
  308.6 3.1 fusion.128
  311.7 30.9 %collective-permute-done.17.refs_5_ = bf16[256,2048]{1,0:T(8,128)(2,1)} collective-permute-done((bf16[256,2048]{1,0:T(8,128)(2,1)}, bf16[256,2048]{1,0:T(8,128)(2,1)}, u32[]{:S(2)}, u32[]{:S(2)}) %collective-permute-start.17) | collective-permute-done | bytes 1048608 | tf_op jit(solution)/shard_map/ppermute | solution.py:90
  349.9 4.1 pad.17.refs_9_.down
  360.2 6.8 fusion.3.refs_8_
  369.4 3.4 collective-permute-done.2.refs_1_
  372.8 22.2 %expert_front.4 = (bf16[256,2048]{1,0:T(8,128)(2,1)}, bf16[256,2048]{1,0:T(8,128)(2,1)}, bf16[256,2048]{1,0:T(8,128)(2,1)}, bf16[256,2048]{1,0:T(8,128)(2,1)}, b...) custom-call(bf16[256,2048]{1,0:T(8,128)(2,1)} %get-tuple-element.170, ...), custom_call_target="tpu_custom_call" | custom-call | flops 11274289152 | bytes 30408704 | tf_op jit(solution)/shard_map/expert_front/pallas_call | solution.py:243
  397.3 20.5 %collective-permute-done.13.refs_1_ = bf16[256,2048]{1,0:T(8,128)(2,1)} collective-permute-done((bf16[256,2048]{1,0:T(8,128)(2,1)}, bf16[256,2048]{1,0:T(8,128)(2,1)}, u32[]{:S(2)}, u32[]{:S(2)}) %collective-permute-start.13) | collective-permute-done | bytes 1048608 | tf_op jit(solution)/shard_map/ppermute | solution.py:90
  419.7 30.8 %expert_front.5 = (bf16[256,2048]{1,0:T(8,128)(2,1)}, bf16[256,2048]{1,0:T(8,128)(2,1)}, bf16[256,2048]{1,0:T(8,128)(2,1)}, bf16[256,2048]{1,0:T(8,128)(2,1)}, b...) custom-call(bf16[256,2048]{1,0:T(8,128)(2,1)} %collective-permute-do, ...), custom_call_target="tpu_custom_call", output_to_operand_aliasing={{4}: (13, {}), {5}: (14, {}), {6}: (15, {}), {7}: (16, {})} | custom-call | flops 11274289152 | bytes 30408704 | tf_op jit(solution)/shard_map/expert_front/pallas_call | solution.py:243
  451.8 22.4 %expert_front.6 = (bf16[256,2048]{1,0:T(8,128)(2,1)}, bf16[256,2048]{1,0:T(8,128)(2,1)}, bf16[256,2048]{1,0:T(8,128)(2,1)}, bf16[256,2048]{1,0:T(8,128)(2,1)}, b...) custom-call(bf16[256,2048]{1,0:T(8,128)(2,1)} %collective-permute-do, ...), custom_call_target="tpu_custom_call", output_to_operand_aliasing={{4}: (13, {}), {5}: (14, {}), {6}: (15, {}), {7}: (16, {})} | custom-call | flops 11274289152 | bytes 30408704 | tf_op jit(solution)/shard_map/expert_front/pallas_call | solution.py:243
  474.3 22.6 %expert_front.7 = (bf16[256,2048]{1,0:T(8,128)(2,1)}, bf16[256,2048]{1,0:T(8,128)(2,1)}, bf16[256,2048]{1,0:T(8,128)(2,1)}, bf16[256,2048]{1,0:T(8,128)(2,1)}, b...) custom-call(bf16[256,2048]{1,0:T(8,128)(2,1)} %collective-permute-do, ...), custom_call_target="tpu_custom_call", output_to_operand_aliasing={{4}: (13, {}), {5}: (14, {}), {6}: (15, {}), {7}: (16, {})} | custom-call | flops 11274289152 | bytes 30408704 | tf_op jit(solution)/shard_map/expert_front/pallas_call | solution.py:243
  497.4 6.5 fusion.133
  508.5 4.3 collective-permute-done.53
  515.0 23.0 %collective-permute-done.47 = bf16[256,2048]{1,0:T(8,128)(2,1)S(1)} collective-permute-done((bf16[256,2048]{1,0:T(8,128)(2,1)S(1)}, bf16[256,2048]{1,0:T(8,128)(2,1)S(1)}, u32[]{:S(2)}, u32[]{:S(2)}) %collective-permute-start.47) | collective-permute-done | bytes 1048608 | tf_op jit(solution)/shard_map/ppermute | solution.py:90
  543.4 5.4 fusion.41
  548.8 15.3 %collective-permute-done.44 = bf16[256,2048]{1,0:T(8,128)(2,1)S(1)} collective-permute-done((bf16[256,2048]{1,0:T(8,128)(2,1)S(1)}, bf16[256,2048]{1,0:T(8,128)(2,1)S(1)}, u32[]{:S(2)}, u32[]{:S(2)}) %collective-permute-start.44) | collective-permute-done | bytes 1048608 | tf_op jit(solution)/shard_map/ppermute | solution.py:90
  564.1 21.7 %collective-permute-done.48 = bf16[256,2048]{1,0:T(8,128)(2,1)S(1)} collective-permute-done((bf16[256,2048]{1,0:T(8,128)(2,1)S(1)}, bf16[256,2048]{1,0:T(8,128)(2,1)S(1)}, u32[]{:S(2)}, u32[]{:S(2)}) %collective-permute-start.48) | collective-permute-done | bytes 1048608 | tf_op jit(solution)/shard_map/ppermute | solution.py:90
  587.7 4.8 fusion.14
  592.6 44.0 %reduce-scatter.17.cloned.1.call-done = bf16[128,2048]{1,0:T(8,128)(2,1)} async-done(((bf16[512,2048]{1,0:T(8,128)(2,1)}), bf16[128,2048]{1,0:T(8,128)(2,1)}) %reduce-scatter.17.cloned.1.call-update) | async-done | bytes 524304 | tf_op jit(solution)/shard_map/reduce_scatter | solution.py:658
  641.0 5.0 convolution_convert_fusion.2
  647.7 7.0 convolution_convert_fusion.1
  654.8 31.6 %all-gather.21.cloned.1.call-done = bf16[512,2048]{1,0:T(8,128)(2,1)} async-done(((bf16[128,2048]{1,0:T(8,128)(2,1)}), bf16[512,2048]{1,0:T(8,128)(2,1)}) %all-gather.21.cloned.1.call-update) | async-done | bytes 2097168 | tf_op jit(solution)/shard_map/all_gather | solution.py:667
  686.4 3.6 fusion.44
  697.6 4.5 convolution_convert_fusion.3
  708.9 8.4 fusion.11
  719.8 32.0 %expert_out.1 = bf16[4,4,256,2048]{3,2,1,0:T(8,128)(2,1)} custom-call(bf16[4,2,512,384]{3,2,1,0:T(8,128)(2,1)S(1)} %copy-done, bf16[2,384,2048]{2,1,0:T(8,128)(2,1)} %pad.17.refs_9_.down, f32[4,4,2,256]{3,2,1,0:T(2,128)S(1)} %copy.115.slot_row, f32[4,4,2,256]{3,2,1,0:T(2,128)S(1)} %copy.116.weight_row, f32[4,4,256,2]{3,2,1,0:T(8,128)S(1)} %bitcast.223), custom_call_target="tpu_custom_call" | custom-call | flops 10737418240 | bytes 23068672 | tf_op jit(solution)/shard_map/expert_out/pallas_call | solution.py:309
  751.8 6.5 slice_bitcast_fusion.14
  759.0 7.4 convolution_convert_fusion
  766.9 3.3 fusion.31
  773.2 34.1 %collective-permute-done.33 = bf16[256,2048]{1,0:T(8,128)(2,1)S(1)} collective-permute-done((bf16[256,2048]{1,0:T(8,128)(2,1)S(1)}, bf16[256,2048]{1,0:T(8,128)(2,1)S(1)}, u32[]{:S(2)}, u32[]{:S(2)}) %collective-permute-start.33) | collective-permute-done | bytes 1048608 | tf_op jit(solution)/shard_map/ppermute | solution.py:90
  810.7 20.0 %collective-permute-done.30 = bf16[256,2048]{1,0:T(8,128)(2,1)S(1)} collective-permute-done((bf16[256,2048]{1,0:T(8,128)(2,1)S(1)}, bf16[256,2048]{1,0:T(8,128)(2,1)S(1)}, u32[]{:S(2)}, u32[]{:S(2)}) %collective-permute-start.30) | collective-permute-done | bytes 1048608 | tf_op jit(solution)/shard_map/ppermute | solution.py:90
  830.6 3.3 collective-permute-done.34
  833.9 3.6 fusion.33
  839.7 25.5 %collective-permute-done.40 = bf16[256,2048]{1,0:T(8,128)(2,1)S(1)} collective-permute-done((bf16[256,2048]{1,0:T(8,128)(2,1)S(1)}, bf16[256,2048]{1,0:T(8,128)(2,1)S(1)}, u32[]{:S(2)}, u32[]{:S(2)}) %collective-permute-start.40) | collective-permute-done | bytes 1048608 | tf_op jit(solution)/shard_map/ppermute | solution.py:90
  867.5 23.8 %collective-permute-done.37 = bf16[256,2048]{1,0:T(8,128)(2,1)S(1)} collective-permute-done((bf16[256,2048]{1,0:T(8,128)(2,1)S(1)}, bf16[256,2048]{1,0:T(8,128)(2,1)S(1)}, u32[]{:S(2)}, u32[]{:S(2)}) %collective-permute-start.37) | collective-permute-done | bytes 1048608 | tf_op jit(solution)/shard_map/ppermute | solution.py:90
  895.7 5.0 fusion.13
  907.4 32.1 %expert_grads.1 = (f32[2,352,2048]{2,1,0:T(8,128)}, f32[2,352,2048]{2,1,0:T(8,128)}, f32[2,352,2048]{2,1,0:T(8,128)}) custom-call(bf16[4,2,512,768]{3,2,1,0:T(8,128)(2,1)} %get-tuple-element.79.dgu, bf16[4,2,512,2048]{3,2,1,0:T(8,128)(2,1)} %get-tuple-element.80.x, bf16[4,2,512,384]{3,2,1,0:T(8,128)(2,1)S(1)} %copy-done, ...), custom_call_target="tpu_custom_call" | custom-call | flops 19327352832 | bytes 60293120 | tf_op jit(solution)/shard_map/expert_grads/pallas_call | solution.py:363
  957.6 51.2 %reduce-scatter.21.cloned.1.call-done = bf16[256,1344]{0,1:T(8,128)(2,1)} async-done(((bf16[2048,1344]{0,1:T(8,128)(2,1)}), bf16[256,1344]{0,1:T(8,128)(2,1)}) %reduce-scatter.21.cloned.1.call-update) | async-done | bytes 688144 | tf_op jit(solution)/shard_map/reduce_scatter | solution.py:722
  1010.8 44.2 %reduce-scatter.15.cloned.1.call-done = bf16[128,2048]{1,0:T(8,128)(2,1)} async-done(((bf16[512,2048]{1,0:T(8,128)(2,1)}), bf16[128,2048]{1,0:T(8,128)(2,1)}) %reduce-scatter.15.cloned.1.call-update) | async-done | bytes 524304 | tf_op jit(solution)/shard_map/reduce_scatter | solution.py:661
  1059.2 17.2 %reduce-scatter.31.cloned.1.call-done = bf16[64,576]{1,0:T(8,128)(2,1)} async-done(((bf16[256,576]{1,0:T(8,128)(2,1)}), bf16[64,576]{1,0:T(8,128)(2,1)}) %reduce-scatter.31.cloned.1.call-update) | async-done | bytes 73744
  (510 shorter events, 156.7 us)
Async XLA Ops:
  7.2 51.1 %all-gather.9.cloned.1.call-start = ((), (), s32[]{:S(2)}) async-start(), calls=%async_computation.10 | async-start | bytes 2621440 | tf_op jit(solution)/shard_map/all_gather | solution.py:548
  7.9 99.3 %all-gather.11.cloned.1.call-start = ((), (), s32[]{:S(2)}) async-start(), calls=%async_computation.11 | async-start | bytes 7667712 | tf_op jit(solution)/shard_map/all_gather | solution.py:537
  14.5 136.1 %all-gather.13.cloned.1.call-start = ((), (), s32[]{:S(2)}) async-start(), calls=%async_computation.12 | async-start | bytes 5603328 | tf_op jit(solution)/shard_map/all_gather | solution.py:549
  15.4 183.4 %reduce-scatter.13.cloned.1.call-start = ((), (), s32[]{:S(2)}) async-start(), calls=%async_computation.13 | async-start | bytes 2621440 | tf_op jit(solution)/shard_map/reduce_scatter | solution.py:611
  154.8 90.8 %all-gather.19.cloned.1.call-start = ((), (), s32[]{:S(2)}) async-start(), calls=%async_computation.16 | async-start | bytes 2621440 | tf_op jit(solution)/shard_map/all_gather | solution.py:553
  155.4 153.2 %all-gather.15.cloned.1.call-start = ((), (), s32[]{:S(2)}) async-start(), calls=%async_computation.14 | async-start | bytes 2621440 | tf_op jit(solution)/shard_map/all_gather | solution.py:620
  202.7 294.7 %all-gather.17.cloned.1.call-start = ((), (), s32[]{:S(2)}) async-start(), calls=%async_computation.15 | async-start | bytes 6488064 | tf_op jit(solution)/shard_map/all_gather | solution.py:554
  203.7 432.9 %reduce-scatter.17.cloned.1.call-start = ((), (), s32[]{:S(2)}) async-start(), calls=%async_computation.18 | async-start | bytes 2621440 | tf_op jit(solution)/shard_map/reduce_scatter | solution.py:658
  248.8 55.7 %collective-permute-start.26 = (bf16[256,2048]{1,0:T(8,128)(2,1)}, bf16[256,2048]{1,0:T(8,128)(2,1)}, u32[]{:S(2)}, u32[]{:S(2)}) collective-permute-start(bf16[256,2048]{1,0:T(8,128)(2,1)} %get-tuple-element.168.refs_4_), channel_id=1, source_target_pairs={{0,4},{4,0},{8,12},{12,8},{16,20},{20,16},{24,28},{28,24},{1,5},{5... | collective-permute-start | bytes 3145736 | tf_op jit(solution)/shard_map/ppermute | solution.py:90
  248.8 57.1 %collective-permute-start.6 = (bf16[256,2048]{1,0:T(8,128)(2,1)}, bf16[256,2048]{1,0:T(8,128)(2,1)}, u32[]{:S(2)}, u32[]{:S(2)}) collective-permute-start(bf16[256,2048]{1,0:T(8,128)(2,1)} %get-tuple-element.168.refs_4_), channel_id=1, source_target_pairs={{0,8},{4,12},{8,0},{12,4},{16,24},{20,28},{24,16},{28,20},{1,9},{5... | collective-permute-start | bytes 3145736 | tf_op jit(solution)/shard_map/ppermute | solution.py:90
  250.3 55.7 %collective-permute-start.8 = (bf16[256,2048]{1,0:T(8,128)(2,1)}, bf16[256,2048]{1,0:T(8,128)(2,1)}, u32[]{:S(2)}, u32[]{:S(2)}) collective-permute-start(bf16[256,2048]{1,0:T(8,128)(2,1)} %get-tuple-element.167.refs_5_), channel_id=1, source_target_pairs={{0,16},{4,20},{8,24},{12,28},{16,0},{20,4},{24,8},{28,12},{1,17},{... | collective-permute-start | bytes 3145736 | tf_op jit(solution)/shard_map/ppermute | solution.py:90
  251.7 54.7 %collective-permute-start.16 = (bf16[256,2048]{1,0:T(8,128)(2,1)}, bf16[256,2048]{1,0:T(8,128)(2,1)S(1)}, u32[]{:S(2)}, u32[]{:S(2)}) collective-permute-start(bf16[256,2048]{1,0:T(8,128)(2,1)} %get-tuple-element.167.refs_5_), channel_id=1, source_target_pairs={{0,8},{4,12},{8,0},{12,4},{16,24},{20,28},{24,16},{28,20},{1,9},{5... | collective-permute-start | bytes 3145736 | tf_op jit(solution)/shard_map/ppermute | solution.py:90
  304.1 38.5 %collective-permute-start.27 = (bf16[256,2048]{1,0:T(8,128)(2,1)}, bf16[256,2048]{1,0:T(8,128)(2,1)}, u32[]{:S(2)}, u32[]{:S(2)}) collective-permute-start(bf16[256,2048]{1,0:T(8,128)(2,1)} %get-tuple-element.167.refs_5_), channel_id=1, source_target_pairs={{0,4},{4,0},{8,12},{12,8},{16,20},{20,16},{24,28},{28,24},{1,5},{5... | collective-permute-start | bytes 3145736 | tf_op jit(solution)/shard_map/ppermute | solution.py:90
  304.5 38.1 %collective-permute-start.17 = (bf16[256,2048]{1,0:T(8,128)(2,1)}, bf16[256,2048]{1,0:T(8,128)(2,1)}, u32[]{:S(2)}, u32[]{:S(2)}) collective-permute-start(bf16[256,2048]{1,0:T(8,128)(2,1)} %get-tuple-element.168.refs_4_), channel_id=1, source_target_pairs={{0,16},{4,20},{8,24},{12,28},{16,0},{20,4},{24,8},{28,12},{1,17},{... | collective-permute-start | bytes 3145736 | tf_op jit(solution)/shard_map/ppermute | solution.py:90
  305.9 37.2 %collective-permute-start.22 = (bf16[256,2048]{1,0:T(8,128)(2,1)}, bf16[256,2048]{1,0:T(8,128)(2,1)}, u32[]{:S(2)}, u32[]{:S(2)}) collective-permute-start(bf16[256,2048]{1,0:T(8,128)(2,1)} %collective-permute-done.6.refs_4_), channel_id=1, source_target_pairs={{0,4},{4,0},{8,12},{12,8},{16,20},{20,16},{24,28},{28,24},{1,5},{5... | collective-permute-start | bytes 3145736 | tf_op jit(solution)/shard_map/ppermute | solution.py:90
  306.0 38.7 %collective-permute-start.23 = (bf16[256,2048]{1,0:T(8,128)(2,1)}, bf16[256,2048]{1,0:T(8,128)(2,1)}, u32[]{:S(2)}, u32[]{:S(2)}) collective-permute-start(bf16[256,2048]{1,0:T(8,128)(2,1)} %collective-permute-done.8.refs_5_), channel_id=1, source_target_pairs={{0,4},{4,0},{8,12},{12,8},{16,20},{20,16},{24,28},{28,24},{1,5},{5... | collective-permute-start | bytes 3145736 | tf_op jit(solution)/shard_map/ppermute | solution.py:90
  306.5 38.2 %collective-permute-start.18 = (bf16[256,2048]{1,0:T(8,128)(2,1)S(1)}, bf16[256,2048]{1,0:T(8,128)(2,1)}, u32[]{:S(2)}, u32[]{:S(2)}) collective-permute-start(bf16[256,2048]{1,0:T(8,128)(2,1)S(1)} %collective-permute-done.16.refs_4_), channel_id=1, source_target_pairs={{0,4},{4,0},{8,12},{12,8},{16,20},{20,16},{24,28},{28,24},{1,5},{5... | collective-permute-start | bytes 3145736 | tf_op jit(solution)/shard_map/ppermute | solution.py:90
  369.1 48.6 %collective-permute-start.13 = (bf16[256,2048]{1,0:T(8,128)(2,1)}, bf16[256,2048]{1,0:T(8,128)(2,1)}, u32[]{:S(2)}, u32[]{:S(2)}) collective-permute-start(bf16[256,2048]{1,0:T(8,128)(2,1)} %get-tuple-element.170.refs_0_), channel_id=1, source_target_pairs={{0,16},{4,20},{8,24},{12,28},{16,0},{20,4},{24,8},{28,12},{1,17},{... | collective-permute-start | bytes 3145736 | tf_op jit(solution)/shard_map/ppermute | solution.py:90
  369.4 49.8 %collective-permute-start.20 = (bf16[256,2048]{1,0:T(8,128)(2,1)}, bf16[256,2048]{1,0:T(8,128)(2,1)}, u32[]{:S(2)}, u32[]{:S(2)}) collective-permute-start(bf16[256,2048]{1,0:T(8,128)(2,1)} %collective-permute-done.refs_0_), channel_id=1, source_target_pairs={{0,4},{4,0},{8,12},{12,8},{16,20},{20,16},{24,28},{28,24},{1,5},{5... | collective-permute-start | bytes 3145736 | tf_op jit(solution)/shard_map/ppermute | solution.py:90
  372.8 46.4 %collective-permute-start.21 = (bf16[256,2048]{1,0:T(8,128)(2,1)}, bf16[256,2048]{1,0:T(8,128)(2,1)}, u32[]{:S(2)}, u32[]{:S(2)}) collective-permute-start(bf16[256,2048]{1,0:T(8,128)(2,1)} %collective-permute-done.2.refs_1_), channel_id=1, source_target_pairs={{0,4},{4,0},{8,12},{12,8},{16,20},{20,16},{24,28},{28,24},{1,5},{5... | collective-permute-start | bytes 3145736 | tf_op jit(solution)/shard_map/ppermute | solution.py:90
  395.3 55.3 %collective-permute-start.9 = (bf16[256,2048]{1,0:T(8,128)(2,1)}, bf16[256,2048]{1,0:T(8,128)(2,1)}, u32[]{:S(2)}, u32[]{:S(2)}) collective-permute-start(bf16[256,2048]{1,0:T(8,128)(2,1)} %collective-permute-done.8.refs_5_), channel_id=1, source_target_pairs={{0,8},{4,12},{8,0},{12,4},{16,24},{20,28},{24,16},{28,20},{1,9},{5... | collective-permute-start | bytes 3145736 | tf_op jit(solution)/shard_map/ppermute | solution.py:90
  396.7 54.5 %collective-permute-start.1 = (bf16[256,2048]{1,0:T(8,128)(2,1)}, bf16[256,2048]{1,0:T(8,128)(2,1)}, u32[]{:S(2)}, u32[]{:S(2)}) collective-permute-start(bf16[256,2048]{1,0:T(8,128)(2,1)} %collective-permute-done.refs_0_), channel_id=1, source_target_pairs={{0,16},{4,20},{8,24},{12,28},{16,0},{20,4},{24,8},{28,12},{1,17},{... | collective-permute-start | bytes 3145736 | tf_op jit(solution)/shard_map/ppermute | solution.py:90
  417.7 34.0 %collective-permute-start.3 = (bf16[256,2048]{1,0:T(8,128)(2,1)}, bf16[256,2048]{1,0:T(8,128)(2,1)}, u32[]{:S(2)}, u32[]{:S(2)}) collective-permute-start(bf16[256,2048]{1,0:T(8,128)(2,1)} %collective-permute-done.2.refs_1_), channel_id=1, source_target_pairs={{0,8},{4,12},{8,0},{12,4},{16,24},{20,28},{24,16},{28,20},{1,9},{5... | collective-permute-start | bytes 3145736 | tf_op jit(solution)/shard_map/ppermute | solution.py:90
  419.2 31.5 %collective-permute-start.14 = (bf16[256,2048]{1,0:T(8,128)(2,1)}, bf16[256,2048]{1,0:T(8,128)(2,1)}, u32[]{:S(2)}, u32[]{:S(2)}) collective-permute-start(bf16[256,2048]{1,0:T(8,128)(2,1)} %collective-permute-done.12.refs_0_), channel_id=1, source_target_pairs={{0,4},{4,0},{8,12},{12,8},{16,20},{20,16},{24,28},{28,24},{1,5},{5... | collective-permute-start | bytes 3145736 | tf_op jit(solution)/shard_map/ppermute | solution.py:90
  419.2 32.0 %collective-permute-start.15 = (bf16[256,2048]{1,0:T(8,128)(2,1)}, bf16[256,2048]{1,0:T(8,128)(2,1)}, u32[]{:S(2)}, u32[]{:S(2)}) collective-permute-start(bf16[256,2048]{1,0:T(8,128)(2,1)} %collective-permute-done.13.refs_1_), channel_id=1, source_target_pairs={{0,4},{4,0},{8,12},{12,8},{16,20},{20,16},{24,28},{28,24},{1,5},{5... | collective-permute-start | bytes 3145736 | tf_op jit(solution)/shard_map/ppermute | solution.py:90
  451.2 53.4 %collective-permute-start.43 = (bf16[256,2048]{1,0:T(8,128)(2,1)}, bf16[256,2048]{1,0:T(8,128)(2,1)}, u32[]{:S(2)}, u32[]{:S(2)}) collective-permute-start(bf16[256,2048]{1,0:T(8,128)(2,1)} %get-tuple-element.66), channel_id=1, source_target_pairs={{0,4},{4,0},{8,12},{12,8},{16,20},{20,16},{24,28},{28,24},{1,5},{5... | collective-permute-start | bytes 3145736 | tf_op jit(solution)/shard_map/ppermute | solution.py:90
  503.9 37.9 %collective-permute-start.42 = (bf16[256,2048]{1,0:T(8,128)(2,1)}, bf16[256,2048]{1,0:T(8,128)(2,1)S(1)}, u32[]{:S(2)}, u32[]{:S(2)}) collective-permute-start(bf16[256,2048]{1,0:T(8,128)(2,1)} %get-tuple-element.64), channel_id=1, source_target_pairs={{0,4},{4,0},{8,12},{12,8},{16,20},{20,16},{24,28},{28,24},{1,5},{5... | collective-permute-start | bytes 3145736 | tf_op jit(solution)/shard_map/ppermute | solution.py:90
  506.6 32.5 %collective-permute-start.52 = (bf16[256,2048]{1,0:T(8,128)(2,1)S(1)}, bf16[256,2048]{1,0:T(8,128)(2,1)S(1)}, u32[]{:S(2)}, u32[]{:S(2)}) collective-permute-start(bf16[256,2048]{1,0:T(8,128)(2,1)S(1)} %copy-done.98), channel_id=1, source_target_pairs={{0,4},{4,0},{8,12},{12,8},{16,20},{20,16},{24,28},{28,24},{1,5},{5... | collective-permute-start | bytes 3145736 | tf_op jit(solution)/shard_map/ppermute | solution.py:90
  515.0 71.5 %collective-permute-start.49 = (bf16[256,2048]{1,0:T(8,128)(2,1)S(1)}, bf16[256,2048]{1,0:T(8,128)(2,1)S(1)}, u32[]{:S(2)}, u32[]{:S(2)}) collective-permute-start(bf16[256,2048]{1,0:T(8,128)(2,1)S(1)} %copy-done.97), channel_id=1, source_target_pairs={{0,4},{4,0},{8,12},{12,8},{16,20},{20,16},{24,28},{28,24},{1,5},{5... | collective-permute-start | bytes 3145736 | tf_op jit(solution)/shard_map/ppermute | solution.py:90
  539.2 47.3 %collective-permute-start.51 = (bf16[256,2048]{1,0:T(8,128)(2,1)S(1)}, bf16[256,2048]{1,0:T(8,128)(2,1)S(1)}, u32[]{:S(2)}, u32[]{:S(2)}) collective-permute-start(bf16[256,2048]{1,0:T(8,128)(2,1)S(1)} %add_convert_fusion.2), channel_id=1, source_target_pairs={{0,16},{4,20},{8,24},{12,28},{16,0},{20,4},{24,8},{28,12},{1,17},{... | collective-permute-start | bytes 3145736 | tf_op jit(solution)/shard_map/ppermute | solution.py:90
  539.5 46.3 %collective-permute-start.48 = (bf16[256,2048]{1,0:T(8,128)(2,1)S(1)}, bf16[256,2048]{1,0:T(8,128)(2,1)S(1)}, u32[]{:S(2)}, u32[]{:S(2)}) collective-permute-start(bf16[256,2048]{1,0:T(8,128)(2,1)S(1)} %add_convert_fusion.3), channel_id=1, source_target_pairs={{0,16},{4,20},{8,24},{12,28},{16,0},{20,4},{24,8},{28,12},{1,17},{... | collective-permute-start | bytes 3145736 | tf_op jit(solution)/shard_map/ppermute | solution.py:90
  541.8 44.7 %collective-permute-start.55 = (bf16[256,2048]{1,0:T(8,128)(2,1)S(1)}, bf16[256,2048]{1,0:T(8,128)(2,1)S(1)}, u32[]{:S(2)}, u32[]{:S(2)}) collective-permute-start(bf16[256,2048]{1,0:T(8,128)(2,1)S(1)} %add_convert_fusion), channel_id=1, source_target_pairs={{0,8},{4,12},{8,0},{12,4},{16,24},{20,28},{24,16},{28,20},{1,9},{5... | collective-permute-start | bytes 3145736 | tf_op jit(solution)/shard_map/ppermute | solution.py:90
  592.6 93.8 %all-gather.21.cloned.1.call-start = ((), (), s32[]{:S(2)}) async-start(), calls=%async_computation.19 | async-start | bytes 2621440 | tf_op jit(solution)/shard_map/all_gather | solution.py:667
  641.0 298.5 %reduce-scatter.29.cloned.1.call-start = ((), (), s32[]{:S(2)}) async-start(), calls=%async_computation.25 | async-start | bytes 3244032 | tf_op jit(solution)/shard_map/reduce_scatter | solution.py:722
  646.0 297.0 %reduce-scatter.27.cloned.1.call-start = ((), (), s32[]{:S(2)}) async-start(), calls=%async_computation.24 | async-start | bytes 6488064 | tf_op jit(solution)/shard_map/reduce_scatter | solution.py:722
  654.8 298.0 %reduce-scatter.23.cloned.1.call-start = ((), (), s32[]{:S(2)}) async-start(), calls=%async_computation.22 | async-start | bytes 1179648 | tf_op jit(solution)/shard_map/reduce_scatter | solution.py:722
  697.6 256.8 %reduce-scatter.25.cloned.1.call-start = ((), (), s32[]{:S(2)}) async-start(), calls=%async_computation.23 | async-start | bytes 2359296 | tf_op jit(solution)/shard_map/reduce_scatter | solution.py:722
  702.2 253.9 %reduce-scatter.19.cloned.1.call-start = ((), (), s32[]{:S(2)}) async-start(), calls=%async_computation.20 | async-start | bytes 2621440 | tf_op jit(solution)/shard_map/reduce_scatter | solution.py:714
  717.3 291.5 %reduce-scatter.21.cloned.1.call-start = ((), (), s32[]{:S(2)}) async-start(), calls=%async_computation.21 | async-start | bytes 6193152 | tf_op jit(solution)/shard_map/reduce_scatter | solution.py:722
  766.5 288.5 %reduce-scatter.15.cloned.1.call-start = ((), (), s32[]{:S(2)}) async-start(), calls=%async_computation.17 | async-start | bytes 2621440 | tf_op jit(solution)/shard_map/reduce_scatter | solution.py:661
  770.2 37.0 %collective-permute-start.33 = (bf16[256,2048]{1,0:T(8,128)(2,1)S(1)}, bf16[256,2048]{1,0:T(8,128)(2,1)S(1)}, u32[]{:S(2)}, u32[]{:S(2)}) collective-permute-start(bf16[256,2048]{1,0:T(8,128)(2,1)S(1)} %get-tuple-element.155), channel_id=1, source_target_pairs={{0,8},{4,12},{8,0},{12,4},{16,24},{20,28},{24,16},{28,20},{1,9},{5... | collective-permute-start | bytes 3145736 | tf_op jit(solution)/shard_map/ppermute | solution.py:90
  771.8 38.8 %collective-permute-start.28 = (bf16[256,2048]{1,0:T(8,128)(2,1)S(1)}, bf16[256,2048]{1,0:T(8,128)(2,1)S(1)}, u32[]{:S(2)}, u32[]{:S(2)}) collective-permute-start(bf16[256,2048]{1,0:T(8,128)(2,1)S(1)} %copy-done.37), channel_id=1, source_target_pairs={{0,4},{4,0},{8,12},{12,8},{16,20},{20,16},{24,28},{28,24},{1,5},{5... | collective-permute-start | bytes 3145736 | tf_op jit(solution)/shard_map/ppermute | solution.py:90
  772.2 38.5 %collective-permute-start.36 = (bf16[256,2048]{1,0:T(8,128)(2,1)S(1)}, bf16[256,2048]{1,0:T(8,128)(2,1)S(1)}, u32[]{:S(2)}, u32[]{:S(2)}) collective-permute-start(bf16[256,2048]{1,0:T(8,128)(2,1)S(1)} %copy-done.36), channel_id=1, source_target_pairs={{0,4},{4,0},{8,12},{12,8},{16,20},{20,16},{24,28},{28,24},{1,5},{5... | collective-permute-start | bytes 3145736 | tf_op jit(solution)/shard_map/ppermute | solution.py:90
  772.3 38.3 %collective-permute-start.39 = (bf16[256,2048]{1,0:T(8,128)(2,1)S(1)}, bf16[256,2048]{1,0:T(8,128)(2,1)S(1)}, u32[]{:S(2)}, u32[]{:S(2)}) collective-permute-start(bf16[256,2048]{1,0:T(8,128)(2,1)S(1)} %copy-done.35), channel_id=1, source_target_pairs={{0,4},{4,0},{8,12},{12,8},{16,20},{20,16},{24,28},{28,24},{1,5},{5... | collective-permute-start | bytes 3145736 | tf_op jit(solution)/shard_map/ppermute | solution.py:90
  772.7 58.0 %collective-permute-start.30 = (bf16[256,2048]{1,0:T(8,128)(2,1)S(1)}, bf16[256,2048]{1,0:T(8,128)(2,1)S(1)}, u32[]{:S(2)}, u32[]{:S(2)}) collective-permute-start(bf16[256,2048]{1,0:T(8,128)(2,1)S(1)} %get-tuple-element.154), channel_id=1, source_target_pairs={{0,8},{4,12},{8,0},{12,4},{16,24},{20,28},{24,16},{28,20},{1,9},{5... | collective-permute-start | bytes 3145736 | tf_op jit(solution)/shard_map/ppermute | solution.py:90
  839.1 52.1 %collective-permute-start.37 = (bf16[256,2048]{1,0:T(8,128)(2,1)S(1)}, bf16[256,2048]{1,0:T(8,128)(2,1)S(1)}, u32[]{:S(2)}, u32[]{:S(2)}) collective-permute-start(bf16[256,2048]{1,0:T(8,128)(2,1)S(1)} %get-tuple-element.145), channel_id=1, source_target_pairs={{0,16},{4,20},{8,24},{12,28},{16,0},{20,4},{24,8},{28,12},{1,17},{... | collective-permute-start | bytes 3145736 | tf_op jit(solution)/shard_map/ppermute | solution.py:90
  900.8 175.7 %reduce-scatter.31.cloned.1.call-start = ((), (), s32[]{:S(2)}) async-start(), calls=%async_computation.26 | async-start | bytes 409600
  906.0 35.4 %collective-permute-start.58 = (f32[36,128]{1,0:T(8,128)S(1)}, f32[36,128]{1,0:T(8,128)S(1)}, u32[]{:S(2)}, u32[]{:S(2)}) collective-permute-start(f32[36,128]{1,0:T(8,128)S(1)} %fusion.154), channel_id=1, source_target_pairs={{0,16},{4,20},{8,24},{12,28},{16,0},{20,4},{24,8},{28,12},{1,17},{... | collective-permute-start | bytes 55304 | tf_op jit(solution)/shard_map/ppermute | solution.py:90
  (136 other events, 2565.9 us)
Sparse Core Ops, SparseCore 0:
  9.6 48.6 all-gather.8
  60.7 46.4 all-gather.10
  109.7 40.8 all-gather.12
  154.9 43.8 reduce-scatter.12
  200.3 45.2 all-gather.18
  247.7 44.6 all-gather.14
  295.0 59.9 all-gather.16
  592.7 43.8 reduce-scatter.16
  641.1 45.2 all-gather.20
  689.6 43.5 reduce-scatter.28
  737.1 73.4 reduce-scatter.26
  813.6 37.8 reduce-scatter.22
  854.8 46.7 reduce-scatter.24
  903.8 44.0 reduce-scatter.18
  951.2 57.5 reduce-scatter.20
  1011.1 43.8 reduce-scatter.14
  1057.1 19.3 reduce-scatter.30

commit v2 on v1

--- a/solution.py
+++ b/solution.py
@@ -90,6 +90,30 @@
     return lax.ppermute(values, axis_name, [(i, i ^ bit) for i in range(count)])
 
 
+def after(values, *earlier):
+    return lax.optimization_barrier((values,) + earlier)[0]
+
+
+def column_gather(rows):
+    count = lax.axis_size("tp")
+    pieces = [rows]
+    for s in range(1, count):
+        pieces.append(lax.ppermute(rows, "tp", [((i + s) % count, i) for i in range(count)]))
+    return jnp.concatenate(pieces, axis=0)
+
+
+def column_scatter(values):
+    count = lax.axis_size("tp")
+    size = values.shape[0] // count
+    total = values[:size].astype(F32)
+    for s in range(1, count):
+        piece = values[s * size : (s + 1) * size].astype(BF)
+        total = total + lax.ppermute(
+            piece, "tp", [(i, (i + s) % count) for i in range(count)]
+        ).astype(F32)
+    return total
+
+
 def dot_rows(left, right):
     return lax.dot_general(left, right, (((1,), (1,)), ((), ())), preferred_element_type=F32)
 
@@ -135,10 +159,10 @@
         2 * count : 2 * count + 5
     ]
     base = 2 * count + 5 + aliased
-    dx_out = refs[base : base + count]
-    x_all, d_all, hid_all, dgu_all = refs[base + count : base + count + 4]
+    dx_out = refs[base : base + 2]
+    x_all, d_all, hid_all, dgu_all = refs[base + 2 : base + 6]
     (xb, db, gate_up, down, xs, ds, dxs, dxo, hid, dgu, sem_in, sem_w, sem_out, sem_dx) = refs[
-        base + count + 4 :
+        base + 6 :
     ]
     width = xb.shape[2]
     pad = down.shape[1]
@@ -211,7 +235,10 @@
     lax.fori_loop(0, experts, one_expert, 0)
     out_copies[2].start()
     out_copies[3].start()
-    dx_copies = [pltpu.make_async_copy(dxo.at[q], dx_out[q], sem_dx.at[q]) for q in range(count)]
+    dx_copies = [
+        pltpu.make_async_copy(dxo.at[q], dx_out[q // 2].at[q % 2], sem_dx.at[q])
+        for q in range(count)
+    ]
     for q in range(count):
         choose = jnp.where(select_cols(slot_col_ref[q], experts, cap), 1.0, 0.0).astype(BF)
 
@@ -235,17 +262,17 @@
     slot_row, weight_row, slot_col = (t[step] for t in tables)
     any_spec = pl.BlockSpec(memory_space=pl.ANY)
     vmem_spec = pl.BlockSpec(memory_space=pltpu.VMEM)
-    half_shape = jax.ShapeDtypeStruct((HALF, width), BF)
+    pair_shape = jax.ShapeDtypeStruct((2, HALF, width), BF)
     kept_shapes = [
         jax.ShapeDtypeStruct((steps, experts, slots, columns), BF)
         for columns in (width, width, pad, wide)
     ]
     results = pl.pallas_call(
         functools.partial(expert_front_kernel, step, experts, cap, len(kept)),
-        out_shape=[half_shape] * QUARTET + kept_shapes,
+        out_shape=[pair_shape] * 2 + kept_shapes,
         in_specs=[any_spec] * (2 * QUARTET + 2) + [vmem_spec] * 3 + [any_spec] * len(kept),
-        out_specs=[any_spec] * (QUARTET + 4),
-        input_output_aliases={2 * QUARTET + 5 + i: QUARTET + i for i in range(len(kept))},
+        out_specs=[any_spec] * 6,
+        input_output_aliases={2 * QUARTET + 5 + i: 2 + i for i in range(len(kept))},
         scratch_shapes=[
             pltpu.VMEM((QUARTET, HALF, width), BF),
             pltpu.VMEM((QUARTET, HALF, width), BF),
@@ -271,32 +298,37 @@
         ),
         name="expert_front",
     )(*x_parts, *dy_parts, gate_up, down, slot_row, weight_row, slot_col, *kept)
-    return list(results[:QUARTET]), list(results[QUARTET:])
-
-
-def expert_out_kernel(experts, cap, hid, down, slot_row, weight_row, slot_col, out, parts):
+    return list(results[:2]), list(results[2:])
+
+
+def expert_out_kernel(experts, cap, hid, down, slot_row, weight_row, slot_col, near, far, parts):
     width = down.shape[2]
     tile = min(1024, width)
-    for q in range(QUARTET):
-        hit = select_rows(slot_row[0, q], experts, cap)
-        weights = slot_weights(hit, weight_row[0, q], experts, cap)
-
-        def front(n, carry, q=q, weights=weights):
+    weights = [
+        slot_weights(
+            select_rows(slot_row[0, q], experts, cap), weight_row[0, q], experts, cap
+        )
+        for q in range(QUARTET)
+    ]
+    for e in range(experts):
+
+        def front(n, carry, e=e):
             cols = pl.ds(pl.multiple_of(n * tile, tile), tile)
-            for e in range(experts):
-                rows = dot_plain(hid[0, e, q * cap : (q + 1) * cap, :], down[e, :, cols])
+            rows = dot_plain(hid[0, e], down[e, :, cols])
+            for q in range(QUARTET):
                 parts[q, e * cap : (e + 1) * cap, cols] = (
-                    rows * weights[e * cap : (e + 1) * cap]
+                    rows[q * cap : (q + 1) * cap] * weights[q][e * cap : (e + 1) * cap]
                 ).astype(BF)
             return carry
 
         lax.fori_loop(0, width // tile, front, 0)
     for q in range(QUARTET):
         choose = jnp.where(select_cols(slot_col[0, q], experts, cap), 1.0, 0.0).astype(BF)
-
-        def gather(n, carry, q=q, choose=choose):
+        out = (near, far)[q // 2]
+
+        def gather(n, carry, q=q, choose=choose, out=out):
             cols = pl.ds(pl.multiple_of(n * tile, tile), tile)
-            out[0, q, :, cols] = dot_plain(choose, parts[q, :, cols]).astype(BF)
+            out[0, q % 2, :, cols] = dot_plain(choose, parts[q, :, cols]).astype(BF)
             return carry
 
         lax.fori_loop(0, width // tile, gather, 0)
@@ -309,7 +341,7 @@
     return pl.pallas_call(
         functools.partial(expert_out_kernel, experts, cap),
         grid=(steps,),
-        out_shape=jax.ShapeDtypeStruct((steps, QUARTET, HALF, width), BF),
+        out_shape=[jax.ShapeDtypeStruct((steps, 2, HALF, width), BF)] * 2,
         in_specs=[
             pl.BlockSpec((1, experts, slots, pad), lambda i: (i, 0, 0, 0)),
             pl.BlockSpec((experts, pad, width), lambda i: (0, 0, 0)),
@@ -317,7 +349,7 @@
             pl.BlockSpec((1,) + weight_row.shape[1:], lambda i: (i, 0, 0, 0)),
             pl.BlockSpec((1,) + slot_col.shape[1:], lambda i: (i, 0, 0, 0)),
         ],
-        out_specs=pl.BlockSpec((1, QUARTET, HALF, width), lambda i: (i, 0, 0, 0)),
+        out_specs=[pl.BlockSpec((1, 2, HALF, width), lambda i: (i, 0, 0, 0))] * 2,
         scratch_shapes=[pltpu.VMEM((QUARTET, experts * cap, width), BF)],
         compiler_params=pltpu.CompilerParams(vmem_limit_bytes=48 * 1024 * 1024),
         cost_estimate=pl.CostEstimate(
@@ -388,23 +420,26 @@
     return [[(2 * i + j // 2, j % 2) for j in range(4)] for i in range(count // 2)]
 
 
+def partner(block):
+    return swap(block, "fsdp", 1)
+
+
 def plane_gather(rows, count):
-    top, bottom = rows[:HALF], rows[HALF:]
     blocks = {}
     if count == 8:
-        own = {0: top, 1: bottom}
+        other = partner(rows)
         for h in (0, 1):
-            blocks[0, h] = own[h]
-            blocks[1, h] = swap(own[h], "fsdp", 1)
-        blocks[2, 0] = swap(top, "fsdp", 2)
-        blocks[4, 1] = swap(bottom, "fsdp", 4)
-        blocks[2, 1] = swap(bottom, "fsdp", 2)
-        blocks[4, 0] = swap(top, "fsdp", 4)
+            blocks[0, h] = rows[h * HALF : (h + 1) * HALF]
+            blocks[1, h] = other[h * HALF : (h + 1) * HALF]
+        blocks[2, 0] = swap(blocks[0, 0], "fsdp", 2)
+        blocks[4, 1] = swap(blocks[0, 1], "fsdp", 4)
+        blocks[2, 1] = swap(blocks[0, 1], "fsdp", 2)
+        blocks[4, 0] = swap(blocks[0, 0], "fsdp", 4)
         blocks[6, 0] = swap(blocks[2, 0], "fsdp", 4)
         blocks[6, 1] = swap(blocks[4, 1], "fsdp", 2)
         for r in (2, 4, 6):
             for h in (0, 1):
-                blocks[r + 1, h] = swap(blocks[r, h], "fsdp", 1)
+                blocks[r + 1, h] = partner(blocks[r, h])
         return blocks
     gathered = lax.all_gather(rows, "fsdp", axis=0)
     for r in range(count):
@@ -413,23 +448,55 @@
     return blocks
 
 
-def plane_scatter(parts, count):
+def whole_gather_first(rows, count):
     if count == 8:
-
-        def add(left, right):
-            return left.astype(F32) + right.astype(F32)
-
-        chip = {}
-        for r in (2, 4, 6, 0):
-            for h in (0, 1):
-                chip[r, h] = add(parts[r, h], swap(parts[r + 1, h], "fsdp", 1))
-        top = add(chip[0, 0], swap(chip[2, 0].astype(BF), "fsdp", 2))
-        bottom = add(chip[0, 1], swap(chip[4, 1].astype(BF), "fsdp", 4))
-        over_top = add(chip[4, 0], swap(chip[6, 0].astype(BF), "fsdp", 2)).astype(BF)
-        over_bottom = add(chip[2, 1], swap(chip[6, 1].astype(BF), "fsdp", 4)).astype(BF)
-        top = add(top, swap(over_top, "fsdp", 4))
-        bottom = add(bottom, swap(over_bottom, "fsdp", 2))
-        return jnp.concatenate([top, bottom], axis=0)
+        return [rows, partner(rows), swap(rows, "fsdp", 2), swap(rows, "fsdp", 4)]
+    gathered = lax.all_gather(rows, "fsdp", axis=0)
+    return [gathered[r] for r in range(count)]
+
+
+def whole_gather_rest(first, count):
+    blocks = {}
+    if count == 8:
+        whole = {0: first[0], 1: first[1], 2: first[2], 4: first[3]}
+        blocks[6, 0] = swap(whole[2][:HALF], "fsdp", 4)
+        blocks[6, 1] = swap(whole[4][HALF:], "fsdp", 2)
+        whole[3] = partner(whole[2])
+        whole[5] = partner(whole[4])
+        for h in (0, 1):
+            blocks[7, h] = partner(blocks[6, h])
+    else:
+        whole = dict(enumerate(first))
+    for r, rows in whole.items():
+        for h in (0, 1):
+            blocks[r, h] = rows[h * HALF : (h + 1) * HALF]
+    return blocks
+
+
+def add_pairs(left, right):
+    return left.astype(F32) + right.astype(F32)
+
+
+def chip_sums(unit, pair):
+    theirs = partner(pair[1])
+    return {unit[h]: add_pairs(pair[0][h], theirs[h]) for h in (0, 1)}
+
+
+def plane_scatter(chip):
+    top = add_pairs(chip[0, 0], swap(chip[2, 0].astype(BF), "fsdp", 2))
+    bottom = add_pairs(chip[0, 1], swap(chip[4, 1].astype(BF), "fsdp", 4))
+    over_top = add_pairs(chip[4, 0], swap(chip[6, 0].astype(BF), "fsdp", 2)).astype(BF)
+    over_bottom = add_pairs(chip[2, 1], swap(chip[6, 1].astype(BF), "fsdp", 4)).astype(BF)
+    top = add_pairs(top, swap(over_top, "fsdp", 4))
+    bottom = add_pairs(bottom, swap(over_bottom, "fsdp", 2))
+    return jnp.concatenate([top, bottom], axis=0)
+
+
+def plane_scatter_whole(pairs, units, count):
+    parts = {}
+    for unit, pair in zip(units, pairs):
+        for q, key in enumerate(unit):
+            parts[key] = pair[q // 2][q % 2]
     stacked = jnp.concatenate([parts[r, h] for r in range(count) for h in (0, 1)], axis=0)
     return lax.psum_scatter(stacked, "fsdp", scatter_dimension=0, tiled=True).astype(F32)
 
@@ -450,7 +517,14 @@
 def expert_tables(expert_ids, expert_wts, local_experts, units, cap):
     fsdp_count = lax.axis_size("fsdp")
     fsdp_rank = lax.axis_index("fsdp")
+    tp_count = lax.axis_size("tp")
     expert_count = local_experts * fsdp_count
+    places = (lax.axis_index("tp") + jnp.arange(tp_count, dtype=jnp.int32)) % tp_count
+
+    def reorder(rows):
+        return jnp.take(rows.reshape(tp_count, -1, TOPK), places, axis=0).reshape(SEQ, TOPK)
+
+    expert_ids, expert_wts = reorder(expert_ids), reorder(expert_wts)
     names = jnp.arange(expert_count, dtype=jnp.int32)[:, None]
     member = jnp.zeros((expert_count, SEQ), jnp.bool_)
     weight = jnp.zeros((expert_count, SEQ), F32)
@@ -466,13 +540,13 @@
     ).reshape(expert_count, SEQ)
     slot = jnp.where(member, rank, NO_SLOT)
     table = jnp.concatenate([slot, weight], axis=0)
-    table = lax.all_gather(table, "fsdp", axis=0).reshape(
-        fsdp_count, 2, fsdp_count, local_experts, 2, HALF
-    )
+    if fsdp_count == 8:
+        for bit in (1, 2, 4):
+            table = jnp.concatenate([table, swap(table, "fsdp", bit)], axis=0)
+    else:
+        table = lax.all_gather(table, "fsdp", axis=0, tiled=True)
+    table = table.reshape(fsdp_count, 2, fsdp_count, local_experts, 2, HALF)
     table = lax.dynamic_index_in_dim(table, fsdp_rank, axis=2, keepdims=False)
-    relative = jnp.arange(fsdp_count, dtype=jnp.int32)
-    order = relative ^ fsdp_rank if fsdp_count == 8 else relative
-    table = jnp.take(table, order, axis=0)
     slot_steps, weight_steps = [], []
     for unit in units:
         slot_steps.append(jnp.stack([table[r, 0, :, h] for r, h in unit]))
@@ -534,6 +608,7 @@
     packed = jnp.concatenate(
         [query_proj, latent_proj, gains, latent_up.reshape(shard_rows, -1)], axis=1
     )
+    lift_cols = packed.shape[1] - joint - spare
     packed_all = lax.all_gather(packed, "fsdp", axis=0, tiled=True)
     joint_weight = packed_all[:, :joint]
     gain_attn = packed_all[:, joint].astype(F32)
@@ -545,14 +620,17 @@
         .astype(F32)
     )
     latent_up_weight = packed_all[:, joint + spare :].reshape(LAT, up_cols)
-    tokens_all = lax.all_gather(block_in, "tp", axis=0, tiled=True)
-    out_down = lax.all_gather(
-        jnp.concatenate([out_proj, shared_down], axis=0), "fsdp", axis=1, tiled=True
-    )
-    out_weight, shared_down_weight = out_down[:out_rows], out_down[out_rows:]
-    cotan_all = lax.all_gather(out_cotan, "tp", axis=0, tiled=True)
+    tokens_all = column_gather(block_in)
+    out_weight = lax.all_gather(after(out_proj, packed_all), "fsdp", axis=1, tiled=True)
+    cotan_all = column_gather(after(out_cotan, tokens_all))
     shared_weight = lax.all_gather(
-        jnp.concatenate([shared_gate, shared_up], axis=1), "fsdp", axis=0, tiled=True
+        after(jnp.concatenate([shared_gate, shared_up], axis=1), out_weight),
+        "fsdp",
+        axis=0,
+        tiled=True,
+    )
+    shared_down_weight = lax.all_gather(
+        after(shared_down, shared_weight), "fsdp", axis=1, tiled=True
     )
     shared_cols = shared_gate.shape[1]
     tables = expert_tables(expert_ids, expert_wts, local_experts, units, cap)
@@ -567,7 +645,11 @@
     queries = joint_rows[:, :query_cols].reshape(SEQ, heads_local, head_width)
     latent = joint_rows[:, query_cols:]
     unit_lat, inverse_lat = norm_parts(latent[:, :LAT])
-    positions = jnp.arange(SEQ, dtype=jnp.int32)
+    places = (tp_rank + jnp.arange(tp_count, dtype=jnp.int32)) % tp_count
+    positions = (
+        places[:, None] * tok_rows + jnp.arange(tok_rows, dtype=jnp.int32)[None, :]
+    ).reshape(SEQ)
+    segments = jnp.take(segment_ids.reshape(tp_count, tok_rows), places, axis=0).reshape(SEQ)
     cosine, sine_part = rope_tables(positions, ROPE)
     compressed_all = (unit_lat * gain_latent).astype(BF)
     key_rope_all = rotate(latent[:, LAT:], cosine, sine_part).astype(BF)
@@ -592,7 +674,7 @@
     )
     values = key_value[:, :, NOPE:]
     allowed = (positions[None, :] <= positions[:, None]) & (
-        segment_ids[None, :] == segment_ids[:, None]
+        segments[None, :] == segments[:, None]
     )
     raw_scores = (
         jnp.einsum("qhd,khd->hqk", query_cat, key_cat, preferred_element_type=F32) * score_scale
@@ -608,26 +690,33 @@
         .reshape(SEQ, heads_local * DV)
         .astype(BF)
     )
-    attn_rows = lax.psum_scatter(
-        jnp.dot(attended, out_weight, preferred_element_type=F32).astype(BF),
-        "tp",
-        scatter_dimension=0,
-        tiled=True,
-    ).astype(F32)
+    attended = after(attended, cotan_all)
+    dy_first = whole_gather_first(cotan_all, fsdp_count)
+    attn_rows = column_scatter(jnp.dot(attended, out_weight, preferred_element_type=F32))
     mixed_rows = block_in.astype(F32) + attn_rows
     unit_two, inverse_two = norm_parts(mixed_rows)
-    normed_ffn = (unit_two * gain_ffn).astype(BF)
-    normed_ffn_all = lax.all_gather(normed_ffn, "tp", axis=0, tiled=True)
-
+    normed_ffn, dy_first, shared_weight = after(
+        ((unit_two * gain_ffn).astype(BF), dy_first, shared_weight)
+    )
+    normed_ffn_all = column_gather(normed_ffn)
+
+    dy_blocks = whole_gather_rest(dy_first, fsdp_count)
+    normed_ffn_all, dy_blocks = after((normed_ffn_all, dy_blocks))
     x_blocks = plane_gather(normed_ffn_all, fsdp_count)
-    dy_blocks = plane_gather(cotan_all, fsdp_count)
+    paired = fsdp_count == 8
     kept = []
-    dx_parts = {}
+    dx_pairs = []
+    dx_chip = {}
     for step, unit in enumerate(units):
-        dx_list, kept = expert_front(
+        x_list = [x_blocks[key] for key in unit]
+        if paired and step == 2:
+            x_list = after(x_list, dx_pairs[0])
+        if paired and step == 3:
+            x_list, dx_chip = after((x_list, dx_chip))
+        pair, kept = expert_front(
             step,
             len(units),
-            [x_blocks[key] for key in unit],
+            x_list,
             [dy_blocks[key] for key in unit],
             routed_gate_up,
             routed_down_pad,
@@ -635,14 +724,14 @@
             kept,
             cap,
         )
-        for key, part in zip(unit, dx_list):
-            dx_parts[key] = part
-    d_routed_in = plane_scatter(dx_parts, fsdp_count)
-    out_array = expert_out(kept[2], routed_down_pad, tables, cap)
-    out_parts = {
-        key: out_array[step, q] for step, unit in enumerate(units) for q, key in enumerate(unit)
-    }
-    routed_rows = plane_scatter(out_parts, fsdp_count)
+        dx_pairs.append(pair)
+        if paired:
+            dx_chip.update(chip_sums(unit, pair))
+    near, far = expert_out(kept[2], routed_down_pad, tables, cap)
+    if paired:
+        d_routed_in = plane_scatter(dx_chip)
+    else:
+        d_routed_in = plane_scatter_whole(dx_pairs, units, fsdp_count)
     routed_gate_grad, routed_up_grad, routed_down_grad = expert_grads(kept, local_hidden)
 
     shared_pre = jnp.dot(normed_ffn_all, shared_weight, preferred_element_type=F32)
@@ -655,16 +744,29 @@
     shared_part = jnp.dot(normed_ffn_all.T, d_shared, preferred_element_type=F32)
     d_shared_in = jnp.dot(d_shared, shared_weight.T, preferred_element_type=F32)
 
-    d_normed_ffn = lax.psum_scatter(
-        (d_shared_in + d_routed_in).astype(BF), "tp", scatter_dimension=0, tiled=True
-    ).astype(F32)
-    ffn_rows = lax.psum_scatter(
-        (shared_rows + routed_rows).astype(BF), "tp", scatter_dimension=0, tiled=True
-    ).astype(F32)
+    d_ffn_rows, shared_part, shared_down_part, near, far = after(
+        (
+            d_shared_in + d_routed_in,
+            shared_part.astype(BF),
+            shared_down_part.astype(BF),
+            near,
+            far,
+        )
+    )
+    d_normed_ffn = column_scatter(d_ffn_rows)
+    out_pairs = [(near[step], far[step]) for step in range(len(units))]
+    if paired:
+        out_chip = {}
+        for unit, pair in zip(units, out_pairs):
+            out_chip.update(chip_sums(unit, pair))
+        routed_rows = plane_scatter(out_chip)
+    else:
+        routed_rows = plane_scatter_whole(out_pairs, units, fsdp_count)
+    ffn_rows = column_scatter(shared_rows + routed_rows)
     block_out = (mixed_rows + ffn_rows).astype(BF)
     ffn_gain_part, d_mixed_norm = norm_back(d_normed_ffn, unit_two, inverse_two, gain_ffn)
     d_mixed = out_cotan.astype(F32) + d_mixed_norm
-    d_proj_all = lax.all_gather(d_mixed.astype(BF), "tp", axis=0, tiled=True)
+    d_proj_all = after(column_gather(d_mixed.astype(BF)), routed_rows)
 
     out_part = jnp.dot(attended.T, d_proj_all, preferred_element_type=F32)
     d_attended = (
@@ -711,9 +813,7 @@
     joint_part = jnp.dot(normed_all.T, d_joint, preferred_element_type=F32)
     d_normed_part = jnp.dot(d_joint, joint_weight.T, preferred_element_type=F32)
     attn_gain_part = jnp.sum(d_normed_part * unit_all, axis=0)
-    d_normed = lax.psum_scatter(
-        d_normed_part.astype(BF), "tp", scatter_dimension=0, tiled=True
-    ).astype(F32)
+    d_normed = column_scatter(d_normed_part)
     unit_one, inverse_one = norm_parts(block_in.astype(F32))
     _, d_tokens_norm = norm_back(d_normed, unit_one, inverse_one, gain_attn)
     block_in_grad = d_mixed + d_tokens_norm
@@ -723,12 +823,26 @@
             part.astype(BF), "fsdp", scatter_dimension=dimension, tiled=True
         )
 
-    joint_grad = scatter(joint_part, 0)
+    lift_part = latent_up_part.astype(BF).reshape(model_width, lift_cols)
+    joint_grad = scatter(
+        jnp.concatenate(
+            [
+                joint_part.astype(BF),
+                jnp.zeros((model_width, (-joint) % 128), BF),
+                lift_part,
+            ],
+            axis=1,
+        ),
+        0,
+    )
     query_proj_grad = joint_grad[:, :query_cols].astype(F32)
-    latent_proj_grad = lax.psum_scatter(
-        joint_grad[:, query_cols:], "tp", scatter_dimension=0, tiled=True
-    ).astype(F32)
-    latent_up_grad = scatter(latent_up_part, 0).astype(F32)
+    latent_grad = joint_grad[:, query_cols:joint].reshape(tp_count, -1, latent_cols)
+    latent_proj_grad = column_scatter(
+        jnp.take(latent_grad, places, axis=0).reshape(-1, latent_cols)
+    )
+    latent_up_grad = (
+        joint_grad[:, joint_grad.shape[1] - lift_cols :].reshape(latent_up.shape).astype(F32)
+    )
     out_proj_grad = scatter(out_part, 1).astype(F32)
     shared_grad = scatter(shared_part, 0).astype(F32)
     shared_gate_grad, shared_up_grad = shared_grad[:, :shared_cols], shared_grad[:, shared_cols:]

time: 1100 us -> 916 us (0.83)
  waiting for transfers between devices: 612 us -> 406 us
  blocking collectives: 50 us -> 0 us
  starting transfers between devices: 38.7 us -> 82.3 us
  local copies, waits for them, and re-layouts: 67.2 us -> 102 us
  other arithmetic: 59.5 us -> 77.4 us
  Pallas kernels: 162 us -> 150 us
    ppermute x0 -> x27, waiting for transfers between devices: none -> 235 us  [the longest x12 132 us: column_gather(): lax.ppermute(rows, 'tp', [((i + s) % count, i) for i in range(count)])]
    ppermute x61 -> x50, waiting for transfers between devices: 235 us -> 85.6 us  [swap(): return lax.ppermute(values, axis_name, [(i, i ^ bit) for i in range(count)])]
    reduce_scatter x4 -> x0, waiting for transfers between devices: 132 us -> none  [the longest x1 44.2 us: per_device(): lax.psum_scatter((shared_rows + routed_rows).astype(BF), 'tp', scatter_di...]
    all_gather x6 -> x3, waiting for transfers between devices: 129 us -> 16.9 us  [the longest x1 16.9 us: per_device(): lax.all_gather(after(out_proj, packed_all), 'fsdp', axis=1, tiled=True)]
    ppermute x0 -> x27, starting transfers between devices: none -> 50.8 us  [the longest x12 29.1 us: column_gather(): lax.ppermute(rows, 'tp', [((i + s) % count, i) for i in range(count)])]
    all_gather x1 -> x0, blocking collectives: 50 us -> none  [expert_tables(): lax.all_gather(table, 'fsdp', axis=0)]
    reduce_scatter x5 -> x4, waiting for transfers between devices: 51.2 us -> 16.7 us  [scatter(): lax.psum_scatter(part.astype(BF), 'fsdp', scatter_dimension=dimension, ti...]
    unnamed x18 -> x8, waiting for transfers between devices: 18.7 us -> 1.32 us
  transfers between devices with their start and end apart: 78 -> 85, of which waited for: 27 -> 32; matrix products, arithmetic and copies ran while one was open for 16% -> 24% of each run, Pallas kernels for 15% -> 16%
where the time goes in v2:
time: 916 us; the launch traced here: 912 us
  waiting for transfers between devices  406 us (44%)
  Pallas kernels  150 us (16%)
  local copies, waits for them, and re-layouts  102 us (11%)
  starting transfers between devices  82.3 us (9%)
  matrix products  78.1 us (9%)
  other arithmetic  77.4 us (8%)
  between operations  16.2 us (2%)
    ppermute x12, waiting for transfers between devices, column_gather(): lax.ppermute(rows, 'tp', [((i + s) % count, i) for i in range(count)])  132 us
    ppermute x15, waiting for transfers between devices, column_scatter(): lax.ppermute(piece, 'tp', [(i, (i + s) % count) for i in range(count)])  103 us
    pallas_call x4, Pallas kernels, expert_front(): pl.pallas_call(functools.partial(expert_front_kernel, step, experts, cap,...  88.5 us
    ppermute x50, waiting for transfers between devices, swap(): return lax.ppermute(values, axis_name, [(i, i ^ bit) for i in range(count)])  85.6 us
    all_gather x1, waiting for transfers between devices, per_device(): packed_all = lax.all_gather(packed, 'fsdp', axis=0, tiled=True)  50.5 us
    pallas_call x1, Pallas kernels, expert_grads(): pl.pallas_call(expert_grads_kernel, grid=(experts, steps), out_shape=[gra...  32.8 us
    ppermute x50, starting transfers between devices, swap(): return lax.ppermute(values, axis_name, [(i, i ^ bit) for i in range(count)])  31.2 us
    ppermute x12, starting transfers between devices, column_gather(): lax.ppermute(rows, 'tp', [((i + s) % count, i) for i in range(count)])  29.1 us
  transfers between devices with their start and end apart: 85, of which 32 were waited for; matrix products, arithmetic and copies ran while one was open for 24% of the time, Pallas kernels for 16%

profile of v2, /device:TPU:0, one launch (start us, length us, event | category | flops | bytes accessed | tf_op | source)
XLA Modules:
  0.0 911.5 jit_solution(10800179422130845940)
XLA Ops:
  13.8 50.5 %all-gather.5.cloned.1.call-done = bf16[2048,1664]{1,0:T(8,128)(2,1)} async-done(((bf16[256,1664]{1,0:T(8,128)(2,1)}), bf16[2048,1664]{1,0:T(8,128)(2,1)}) %all-gather.5.cloned.1.call-update) | async-done | bytes 6815760 | tf_op jit(solution)/shard_map/all_gather | solution.py:612
  77.6 16.9 %all-gather.7.cloned.1.call-done = bf16[512,2048]{1,0:T(8,128)(2,1)} async-done(((bf16[512,256]{1,0:T(8,128)(2,1)}), bf16[512,2048]{1,0:T(8,128)(2,1)}) %all-gather.7.cloned.1.call-update) | async-done | bytes 2097168 | tf_op jit(solution)/shard_map/all_gather | solution.py:624
  99.5 13.8 %collective-permute-done.1 = bf16[128,2048]{1,0:T(8,128)(2,1)} collective-permute-done((bf16[128,2048]{1,0:T(8,128)(2,1)S(1)}, bf16[128,2048]{1,0:T(8,128)(2,1)}, u32[]{:S(2)}, u32[]{:S(2)}) %collective-permute-start.1) | collective-permute-done | bytes 524320 | tf_op jit(solution)/shard_map/ppermute | solution.py:101
  120.8 9.4 %collective-permute-done.3 = bf16[128,2048]{1,0:T(8,128)(2,1)S(1)} collective-permute-done((bf16[128,2048]{1,0:T(8,128)(2,1)S(1)}, bf16[128,2048]{1,0:T(8,128)(2,1)S(1)}, u32[]{:S(2)}, u32[]{:S(2)}) %collective-permute-start.3) | collective-permute-done | bytes 524320 | tf_op jit(solution)/shard_map/ppermute | solution.py:101
  131.0 31.3 %collective-permute-done.4 = bf16[128,2048]{1,0:T(8,128)(2,1)S(1)} collective-permute-done((bf16[128,2048]{1,0:T(8,128)(2,1)S(1)}, bf16[128,2048]{1,0:T(8,128)(2,1)S(1)}, u32[]{:S(2)}, u32[]{:S(2)}) %collective-permute-start.4) | collective-permute-done | bytes 524320 | tf_op jit(solution)/shard_map/ppermute | solution.py:101
  199.7 9.5 %collective-permute-done.6 = bf16[128,2048]{1,0:T(8,128)(2,1)} collective-permute-done((bf16[128,2048]{1,0:T(8,128)(2,1)}, bf16[128,2048]{1,0:T(8,128)(2,1)}, u32[]{:S(2)}, u32[]{:S(2)}) %collective-permute-start.6) | collective-permute-done | bytes 524320 | tf_op jit(solution)/shard_map/ppermute | solution.py:111
  209.3 5.8 fusion.3.refs_8_
  215.1 14.2 %collective-permute-done.7 = bf16[128,2048]{1,0:T(8,128)(2,1)S(1)} collective-permute-done((bf16[128,2048]{1,0:T(8,128)(2,1)}, bf16[128,2048]{1,0:T(8,128)(2,1)S(1)}, u32[]{:S(2)}, u32[]{:S(2)}) %collective-permute-start.7) | collective-permute-done | bytes 524320 | tf_op jit(solution)/shard_map/ppermute | solution.py:111
  230.8 5.4 collective-permute-done.8
  240.3 7.0 collective-permute-start.12
  254.3 5.4 collective-permute-done.12
  260.9 18.3 %collective-permute-done.13 = bf16[128,2048]{1,0:T(8,128)(2,1)S(1)} collective-permute-done((bf16[128,2048]{1,0:T(8,128)(2,1)S(1)}, bf16[128,2048]{1,0:T(8,128)(2,1)S(1)}, u32[]{:S(2)}, u32[]{:S(2)}) %collective-permute-start.13) | collective-permute-done | bytes 524320 | tf_op jit(solution)/shard_map/ppermute | solution.py:101
  281.0 4.4 fusion.129
  285.4 9.3 %collective-permute-done.14 = bf16[128,2048]{1,0:T(8,128)(2,1)S(1)} collective-permute-done((bf16[128,2048]{1,0:T(8,128)(2,1)S(1)}, bf16[128,2048]{1,0:T(8,128)(2,1)S(1)}, u32[]{:S(2)}, u32[]{:S(2)}) %collective-permute-start.14) | collective-permute-done | bytes 524320 | tf_op jit(solution)/shard_map/ppermute | solution.py:101
  318.0 16.3 %collective-permute-done.21.refs_0_ = bf16[256,2048]{1,0:T(8,128)(2,1)} collective-permute-done((bf16[256,2048]{1,0:T(8,128)(2,1)}, bf16[256,2048]{1,0:T(8,128)(2,1)}, u32[]{:S(2)}, u32[]{:S(2)}) %collective-permute-start.21) | collective-permute-done | bytes 1048608 | tf_op jit(solution)/shard_map/ppermute | solution.py:90
  339.4 21.3 %expert_front.4 = (bf16[2,256,2048]{2,1,0:T(8,128)(2,1)}, bf16[2,256,2048]{2,1,0:T(8,128)(2,1)}, bf16[4,2,512,2048]{3,2,1,0:T(8,128)(2,1)}, bf16[4,2,512,2048]{3...) custom-call(bf16[256,2048]{1,0:T(8,128)(2,1)} %get-tuple-element.306.refs_0_, ...), custom_call_target="tpu_custom_call" | custom-call | flops 11274289152 | bytes 30408704 | tf_op jit(solution)/shard_map/expert_front/pallas_call | solution.py:270
  362.9 22.2 %expert_front.5 = (bf16[2,256,2048]{2,1,0:T(8,128)(2,1)}, bf16[2,256,2048]{2,1,0:T(8,128)(2,1)}, bf16[4,2,512,2048]{3,2,1,0:T(8,128)(2,1)}, bf16[4,2,512,2048]{3...) custom-call(bf16[256,2048]{1,0:T(8,128)(2,1)} %collective-permute-do, ...), custom_call_target="tpu_custom_call", output_to_operand_aliasing={{2}: (13, {}), {3}: (14, {}), {4}: (15, {}), {5}: (16, {})} | custom-call | flops 11274289152 | bytes 30408704 | tf_op jit(solution)/shard_map/expert_front/pallas_call | solution.py:270
  385.5 22.2 %expert_front.6 = (bf16[2,256,2048]{2,1,0:T(8,128)(2,1)}, bf16[2,256,2048]{2,1,0:T(8,128)(2,1)}, bf16[4,2,512,2048]{3,2,1,0:T(8,128)(2,1)}, bf16[4,2,512,2048]{3...) custom-call(bf16[256,2048]{1,0:T(8,128)(2,1)} %collective-permute-do, ...), custom_call_target="tpu_custom_call", output_to_operand_aliasing={{2}: (13, {}), {3}: (14, {}), {4}: (15, {}), {5}: (16, {})} | custom-call | flops 11274289152 | bytes 30408704 | tf_op jit(solution)/shard_map/expert_front/pallas_call | solution.py:270
  409.9 5.0 add_bitcast_fusion.4
  414.9 3.9 add_bitcast_fusion
  418.8 4.3 add_bitcast_fusion.1
  424.1 22.8 %expert_front.7 = (bf16[2,256,2048]{2,1,0:T(8,128)(2,1)}, bf16[2,256,2048]{2,1,0:T(8,128)(2,1)}, bf16[4,2,512,2048]{3,2,1,0:T(8,128)(2,1)}, bf16[4,2,512,2048]{3...) custom-call(bf16[256,2048]{1,0:T(8,128)(2,1)} %collective-permute-do, ...), custom_call_target="tpu_custom_call", output_to_operand_aliasing={{2}: (13, {}), {3}: (14, {}), {4}: (15, {}), {5}: (16, {})} | custom-call | flops 11274289152 | bytes 30408704 | tf_op jit(solution)/shard_map/expert_front/pallas_call | solution.py:270
  447.3 8.4 fusion.138
  458.2 6.7 multiply_convert_fusion.2
  465.7 4.9 convolution_convert_fusion.2
  471.7 8.2 convolution_convert_fusion.1
  485.4 11.6 %collective-permute-done.45 = bf16[256,2048]{1,0:T(8,128)(2,1)} collective-permute-done((bf16[256,2048]{1,0:T(8,128)(2,1)}, bf16[256,2048]{1,0:T(8,128)(2,1)}, u32[]{:S(2)}, u32[]{:S(2)}) %collective-permute-start.45) | collective-permute-done | bytes 1048608 | tf_op jit(solution)/shard_map/ppermute | solution.py:90
  499.9 28.7 %expert_out.1 = (bf16[4,2,256,2048]{3,2,1,0:T(8,128)(2,1)}, bf16[4,2,256,2048]{3,2,1,0:T(8,128)(2,1)}) custom-call(bf16[4,2,512,384]{3,2,1,0:T(8,128)(2,1)S(1)} %copy-done.2, bf16[2,384,2048]{2,1,0:T(8,128)(2,1)} %pad.17.refs_9_.down, f32[4,4,2,256]{3,2,1,0:T(2,128)S(1)} %copy.181.slot_row, f32[4,4,2,256]{3,2,1,0:T(2,128)S(1)} %copy.182.weight_row, ...), custom_call_target="tpu_custom_call" | custom-call | flops 10737418240 | bytes 23068672 | tf_op jit(solution)/shard_map/expert_out/pallas_call | solution.py:341
  528.7 12.1 %collective-permute-done.43 = bf16[256,2048]{1,0:T(8,128)(2,1)S(1)} collective-permute-done((bf16[256,2048]{1,0:T(8,128)(2,1)S(1)}, bf16[256,2048]{1,0:T(8,128)(2,1)S(1)}, u32[]{:S(2)}, u32[]{:S(2)}) %collective-permute-start.43) | collective-permute-done | bytes 1048608 | tf_op jit(solution)/shard_map/ppermute | solution.py:90
  542.6 5.5 maximum_add_fusion
  552.6 12.9 %collective-permute-done.60 = bf16[128,2048]{1,0:T(8,128)(2,1)S(1)} collective-permute-done((bf16[128,2048]{1,0:T(8,128)(2,1)S(1)}, bf16[128,2048]{1,0:T(8,128)(2,1)S(1)}, u32[]{:S(2)}, u32[]{:S(2)}) %collective-permute-start.60) | collective-permute-done | bytes 524320 | tf_op jit(solution)/shard_map/ppermute | solution.py:111
  565.5 20.6 %collective-permute-done.61 = bf16[128,2048]{1,0:T(8,128)(2,1)S(1)} collective-permute-done((bf16[128,2048]{1,0:T(8,128)(2,1)S(1)}, bf16[128,2048]{1,0:T(8,128)(2,1)S(1)}, u32[]{:S(2)}, u32[]{:S(2)}) %collective-permute-start.61) | collective-permute-done | bytes 524320 | tf_op jit(solution)/shard_map/ppermute | solution.py:111
  587.8 9.6 %collective-permute-start.63 = (bf16[128,2048]{1,0:T(8,128)(2,1)S(1)}, bf16[128,2048]{1,0:T(8,128)(2,1)S(1)}, u32[]{:S(2)}, u32[]{:S(2)}) collective-permute-start(bf16[128,2048]{1,0:T(8,128)(2,1)S(1)} %fusion.118), channel_id=1, source_target_pairs={{1,0},{2,1},{3,2},{0,3},{5,4},{6,5},{7,6},{4,7},{9,8},{10,9},{11,1... | collective-permute-start | bytes 1572872 | tf_op jit(solution)/shard_map/ppermute | solution.py:101
  600.0 9.8 %collective-permute-done.63 = bf16[128,2048]{1,0:T(8,128)(2,1)S(1)} collective-permute-done((bf16[128,2048]{1,0:T(8,128)(2,1)S(1)}, bf16[128,2048]{1,0:T(8,128)(2,1)S(1)}, u32[]{:S(2)}, u32[]{:S(2)}) %collective-permute-start.63) | collective-permute-done | bytes 524320 | tf_op jit(solution)/shard_map/ppermute | solution.py:101
  609.8 34.9 %collective-permute-done.64 = bf16[128,2048]{1,0:T(8,128)(2,1)S(1)} collective-permute-done((bf16[128,2048]{1,0:T(8,128)(2,1)S(1)}, bf16[128,2048]{1,0:T(8,128)(2,1)S(1)}, u32[]{:S(2)}, u32[]{:S(2)}) %collective-permute-start.64) | collective-permute-done | bytes 524320 | tf_op jit(solution)/shard_map/ppermute | solution.py:101
  650.4 7.3 slice_bitcast_fusion.3
  683.7 7.3 convolution_convert_fusion
  691.1 6.8 pad_maximum_fusion
  698.4 6.2 fusion.23
  706.7 9.6 %fusion.11 = (f32[2048]{0:T(1024)S(1)}, bf16[512,2048]{1,0:T(8,128)(2,1)}, f32[512,2048]{1,0:T(8,128)}) fusion(bf16[512,2048]{1,0:T(8,128)(2,1)S(1)} %copy-done.34, f32[512]{0:T(512)S(1)} %copy-done.106, bf16[2048,1664]{1,0:T(8,128)(2,1)} %all-gather.5.cloned.1.call-done, bf16[512,32]{0,1:T(8,128)(2,1)S(1)} %get-tuple-element.335, ...), kind=kOutput, calls=%fused_computation.22 | convolution fusion | flops 2829318144 | bytes 15542272 | tf_op jit(solution)/shard_map/dot_general | solution.py:814
  718.6 19.5 %collective-permute-done.70 = f32[36,128]{1,0:T(8,128)S(1)} collective-permute-done((f32[36,128]{1,0:T(8,128)S(1)}, f32[36,128]{1,0:T(8,128)S(1)}, u32[]{:S(2)}, u32[]{:S(2)}) %collective-permute-start.70) | collective-permute-done | bytes 18464 | tf_op jit(solution)/shard_map/ppermute | solution.py:90
  748.1 4.2 fusion.22
  754.4 32.8 %expert_grads.1 = (f32[2,352,2048]{2,1,0:T(8,128)}, f32[2,352,2048]{2,1,0:T(8,128)}, f32[2,352,2048]{2,1,0:T(8,128)}) custom-call(bf16[4,2,512,768]{3,2,1,0:T(8,128)(2,1)} %get-tuple-element.163.dgu, bf16[4,2,512,2048]{3,2,1,0:T(8,128)(2,1)} %get-tuple-element.164.x, bf16[4,2,512,384]{3,2,1,0:T(8,128)(2,1)S(1)} %copy-done.2, ...), custom_call_target="tpu_custom_call" | custom-call | flops 19327352832 | bytes 60293120 | tf_op jit(solution)/shard_map/expert_grads/pallas_call | solution.py:395
  793.2 14.4 %collective-permute-done.53 = bf16[256,2048]{1,0:T(8,128)(2,1)S(1)} collective-permute-done((bf16[256,2048]{1,0:T(8,128)(2,1)S(1)}, bf16[256,2048]{1,0:T(8,128)(2,1)S(1)}, u32[]{:S(2)}, u32[]{:S(2)}) %collective-permute-start.53) | collective-permute-done | bytes 1048608 | tf_op jit(solution)/shard_map/ppermute | solution.py:90
  822.9 17.0 %collective-permute-done.67 = bf16[128,2048]{1,0:T(8,128)(2,1)S(1)} collective-permute-done((bf16[128,2048]{1,0:T(8,128)(2,1)S(1)}, bf16[128,2048]{1,0:T(8,128)(2,1)S(1)}, u32[]{:S(2)}, u32[]{:S(2)}) %collective-permute-start.67) | collective-permute-done | bytes 524320 | tf_op jit(solution)/shard_map/ppermute | solution.py:111
  846.1 20.6 %collective-permute-done.58 = bf16[128,2048]{1,0:T(8,128)(2,1)} collective-permute-done((bf16[128,2048]{1,0:T(8,128)(2,1)}, bf16[128,2048]{1,0:T(8,128)(2,1)}, u32[]{:S(2)}, u32[]{:S(2)}) %collective-permute-start.58) | collective-permute-done | bytes 524320 | tf_op jit(solution)/shard_map/ppermute | solution.py:111
  866.7 4.8 fusion.35
  875.1 16.6 %reduce-scatter.5.cloned.1.call-done = bf16[256,1664]{0,1:T(8,128)(2,1)} async-done(((bf16[2048,1664]{0,1:T(8,128)(2,1)}), bf16[256,1664]{0,1:T(8,128)(2,1)}) %reduce-scatter.5.cloned.1.call-update) | async-done | bytes 851984 | tf_op jit(solution)/shard_map/reduce_scatter | solution.py:822
  (570 shorter events, 234.9 us)
Async XLA Ops:
  7.2 57.2 %all-gather.5.cloned.1.call-start = ((), (), s32[]{:S(2)}) async-start(), calls=%async_computation.4 | async-start | bytes 7667712 | tf_op jit(solution)/shard_map/all_gather | solution.py:612
  13.8 80.7 %all-gather.7.cloned.1.call-start = ((), (), s32[]{:S(2)}) async-start(), calls=%async_computation.5 | async-start | bytes 2359296 | tf_op jit(solution)/shard_map/all_gather | solution.py:624
  64.4 175.9 %all-gather.9.cloned.1.call-start = ((), (), s32[]{:S(2)}) async-start(), calls=%async_computation.6 | async-start | bytes 6488064 | tf_op jit(solution)/shard_map/all_gather | solution.py:626
  64.4 34.0 %collective-permute-start = (bf16[128,2048]{1,0:T(8,128)(2,1)S(1)}, bf16[128,2048]{1,0:T(8,128)(2,1)}, u32[]{:S(2)}, u32[]{:S(2)}) collective-permute-start(bf16[128,2048]{1,0:T(8,128)(2,1)S(1)} %copy-done.12), channel_id=1, source_target_pairs={{1,0},{2,1},{3,2},{0,3},{5,4},{6,5},{7,6},{4,7},{9,8},{10,9},{11,1... | collective-permute-start | bytes 1572872 | tf_op jit(solution)/shard_map/ppermute | solution.py:101
  67.8 45.5 %collective-permute-start.1 = (bf16[128,2048]{1,0:T(8,128)(2,1)S(1)}, bf16[128,2048]{1,0:T(8,128)(2,1)}, u32[]{:S(2)}, u32[]{:S(2)}) collective-permute-start(bf16[128,2048]{1,0:T(8,128)(2,1)S(1)} %copy-done.12), channel_id=1, source_target_pairs={{2,0},{3,1},{0,2},{1,3},{6,4},{7,5},{4,6},{5,7},{10,8},{11,9},{8,1... | collective-permute-start | bytes 1572872 | tf_op jit(solution)/shard_map/ppermute | solution.py:101
  67.8 46.7 %collective-permute-start.2 = (bf16[128,2048]{1,0:T(8,128)(2,1)S(1)}, bf16[128,2048]{1,0:T(8,128)(2,1)}, u32[]{:S(2)}, u32[]{:S(2)}) collective-permute-start(bf16[128,2048]{1,0:T(8,128)(2,1)S(1)} %copy-done.12), channel_id=1, source_target_pairs={{3,0},{0,1},{1,2},{2,3},{7,4},{4,5},{5,6},{6,7},{11,8},{8,9},{9,10... | collective-permute-start | bytes 1572872 | tf_op jit(solution)/shard_map/ppermute | solution.py:101
  94.5 363.7 %all-gather.11.cloned.1.call-start = ((), (), s32[]{:S(2)}) async-start(), calls=%async_computation.7 | async-start | bytes 3244032 | tf_op jit(solution)/shard_map/all_gather | solution.py:632
  116.5 45.9 %collective-permute-start.4 = (bf16[128,2048]{1,0:T(8,128)(2,1)S(1)}, bf16[128,2048]{1,0:T(8,128)(2,1)S(1)}, u32[]{:S(2)}, u32[]{:S(2)}) collective-permute-start(bf16[128,2048]{1,0:T(8,128)(2,1)S(1)} %copy-done.18), channel_id=1, source_target_pairs={{2,0},{3,1},{0,2},{1,3},{6,4},{7,5},{4,6},{5,7},{10,8},{11,9},{8,1... | collective-permute-start | bytes 1572872 | tf_op jit(solution)/shard_map/ppermute | solution.py:101
  118.6 44.6 %collective-permute-start.5 = (bf16[128,2048]{1,0:T(8,128)(2,1)S(1)}, bf16[128,2048]{1,0:T(8,128)(2,1)S(1)}, u32[]{:S(2)}, u32[]{:S(2)}) collective-permute-start(bf16[128,2048]{1,0:T(8,128)(2,1)S(1)} %copy-done.18), channel_id=1, source_target_pairs={{3,0},{0,1},{1,2},{2,3},{7,4},{4,5},{5,6},{6,7},{11,8},{8,9},{9,10... | collective-permute-start | bytes 1572872 | tf_op jit(solution)/shard_map/ppermute | solution.py:101
  192.2 48.1 %collective-permute-start.10 = (bf16[512,2048]{1,0:T(8,128)(2,1)}, bf16[512,2048]{1,0:T(8,128)(2,1)}, u32[]{:S(2)}, u32[]{:S(2)}) collective-permute-start(bf16[512,2048]{1,0:T(8,128)(2,1)} %constant_dynamic-update-slice_fusion.4), channel_id=1, source_target_pairs={{0,8},{4,12},{8,0},{12,4},{16,24},{20,28},{24,16},{28,20},{1,9},{5... | collective-permute-start | bytes 6291464 | tf_op jit(solution)/shard_map/ppermute | solution.py:90
  193.7 46.6 %collective-permute-start.11 = (bf16[512,2048]{1,0:T(8,128)(2,1)}, bf16[512,2048]{1,0:T(8,128)(2,1)}, u32[]{:S(2)}, u32[]{:S(2)}) collective-permute-start(bf16[512,2048]{1,0:T(8,128)(2,1)} %constant_dynamic-update-slice_fusion.4), channel_id=1, source_target_pairs={{0,16},{4,20},{8,24},{12,28},{16,0},{20,4},{24,8},{28,12},{1,17},{... | collective-permute-start | bytes 6291464 | tf_op jit(solution)/shard_map/ppermute | solution.py:90
  194.3 46.0 %collective-permute-start.9 = (bf16[512,2048]{1,0:T(8,128)(2,1)}, bf16[512,2048]{1,0:T(8,128)(2,1)}, u32[]{:S(2)}, u32[]{:S(2)}) collective-permute-start(bf16[512,2048]{1,0:T(8,128)(2,1)} %constant_dynamic-update-slice_fusion.4), channel_id=1, source_target_pairs={{0,4},{4,0},{8,12},{12,8},{16,20},{20,16},{24,28},{28,24},{1,5},{5... | collective-permute-start | bytes 6291464 | tf_op jit(solution)/shard_map/ppermute | solution.py:90
  247.3 50.0 %collective-permute-start.16 = (bf16[512,2048]{1,0:T(8,128)(2,1)}, bf16[512,2048]{1,0:T(8,128)(2,1)S(1)}, u32[]{:S(2)}, u32[]{:S(2)}) collective-permute-start(bf16[512,2048]{1,0:T(8,128)(2,1)} %collective-permute-done.11), channel_id=1, source_target_pairs={{0,4},{4,0},{8,12},{12,8},{16,20},{20,16},{24,28},{28,24},{1,5},{5... | collective-permute-start | bytes 6291464 | tf_op jit(solution)/shard_map/ppermute | solution.py:90
  247.3 51.6 %collective-permute-start.15 = (bf16[512,2048]{1,0:T(8,128)(2,1)}, bf16[512,2048]{1,0:T(8,128)(2,1)S(1)}, u32[]{:S(2)}, u32[]{:S(2)}) collective-permute-start(bf16[512,2048]{1,0:T(8,128)(2,1)} %collective-permute-done.10), channel_id=1, source_target_pairs={{0,4},{4,0},{8,12},{12,8},{16,20},{20,16},{24,28},{28,24},{1,5},{5... | collective-permute-start | bytes 6291464 | tf_op jit(solution)/shard_map/ppermute | solution.py:90
  253.7 43.0 %collective-permute-start.17 = (bf16[256,2048]{1,0:T(8,128)(2,1)S(1)}, bf16[256,2048]{1,0:T(8,128)(2,1)S(1)}, u32[]{:S(2)}, u32[]{:S(2)}) collective-permute-start(bf16[256,2048]{1,0:T(8,128)(2,1)S(1)} %get-tuple-element.110.refs_4_), channel_id=1, source_target_pairs={{0,16},{4,20},{8,24},{12,28},{16,0},{20,4},{24,8},{28,12},{1,17},{... | collective-permute-start | bytes 3145736 | tf_op jit(solution)/shard_map/ppermute | solution.py:90
  259.7 37.1 %collective-permute-start.18 = (bf16[256,2048]{1,0:T(8,128)(2,1)S(1)}, bf16[256,2048]{1,0:T(8,128)(2,1)S(1)}, u32[]{:S(2)}, u32[]{:S(2)}) collective-permute-start(bf16[256,2048]{1,0:T(8,128)(2,1)S(1)} %get-tuple-element.111.refs_5_), channel_id=1, source_target_pairs={{0,8},{4,12},{8,0},{12,4},{16,24},{20,28},{24,16},{28,20},{1,9},{5... | collective-permute-start | bytes 3145736 | tf_op jit(solution)/shard_map/ppermute | solution.py:90
  301.9 34.4 %collective-permute-start.27 = (bf16[512,2048]{1,0:T(8,128)(2,1)}, bf16[512,2048]{1,0:T(8,128)(2,1)}, u32[]{:S(2)}, u32[]{:S(2)}) collective-permute-start(bf16[512,2048]{1,0:T(8,128)(2,1)} %pad_maximum_fusion.2), channel_id=1, source_target_pairs={{0,4},{4,0},{8,12},{12,8},{16,20},{20,16},{24,28},{28,24},{1,5},{5... | collective-permute-start | bytes 6291464 | tf_op jit(solution)/shard_map/ppermute | solution.py:90
  316.0 44.7 %collective-permute-start.35 = (bf16[256,2048]{1,0:T(8,128)(2,1)}, bf16[256,2048]{1,0:T(8,128)(2,1)}, u32[]{:S(2)}, u32[]{:S(2)}) collective-permute-start(bf16[256,2048]{1,0:T(8,128)(2,1)} %get-tuple-element.305.refs_1_), channel_id=1, source_target_pairs={{0,8},{4,12},{8,0},{12,4},{16,24},{20,28},{24,16},{28,20},{1,9},{5... | collective-permute-start | bytes 3145736 | tf_op jit(solution)/shard_map/ppermute | solution.py:90
  317.4 44.7 %collective-permute-start.36 = (bf16[256,2048]{1,0:T(8,128)(2,1)}, bf16[256,2048]{1,0:T(8,128)(2,1)}, u32[]{:S(2)}, u32[]{:S(2)}) collective-permute-start(bf16[256,2048]{1,0:T(8,128)(2,1)} %get-tuple-element.306.refs_0_), channel_id=1, source_target_pairs={{0,16},{4,20},{8,24},{12,28},{16,0},{20,4},{24,8},{28,12},{1,17},{... | collective-permute-start | bytes 3145736 | tf_op jit(solution)/shard_map/ppermute | solution.py:90
  335.4 73.9 %collective-permute-start.22 = (bf16[256,2048]{1,0:T(8,128)(2,1)}, bf16[256,2048]{1,0:T(8,128)(2,1)}, u32[]{:S(2)}, u32[]{:S(2)}) collective-permute-start(bf16[256,2048]{1,0:T(8,128)(2,1)} %collective-permute-done.21.refs_0_), channel_id=1, source_target_pairs={{0,16},{4,20},{8,24},{12,28},{16,0},{20,4},{24,8},{28,12},{1,17},{... | collective-permute-start | bytes 3145736 | tf_op jit(solution)/shard_map/ppermute | solution.py:90
  360.7 48.9 %collective-permute-start.24 = (bf16[256,2048]{1,0:T(8,128)(2,1)S(1)}, bf16[256,2048]{1,0:T(8,128)(2,1)}, u32[]{:S(2)}, u32[]{:S(2)}) collective-permute-start(bf16[256,2048]{1,0:T(8,128)(2,1)S(1)} %collective-permute-done.23.refs_1_), channel_id=1, source_target_pairs={{0,8},{4,12},{8,0},{12,4},{16,24},{20,28},{24,16},{28,20},{1,9},{5... | collective-permute-start | bytes 3145736 | tf_op jit(solution)/shard_map/ppermute | solution.py:90
  362.7 47.2 %collective-permute-start.31 = (bf16[2,256,2048]{2,1,0:T(8,128)(2,1)}, bf16[2,256,2048]{2,1,0:T(8,128)(2,1)}, u32[]{:S(2)}, u32[]{:S(2)}) collective-permute-start(bf16[2,256,2048]{2,1,0:T(8,128)(2,1)} %get-tuple-element.109), channel_id=1, source_target_pairs={{0,4},{4,0},{8,12},{12,8},{16,20},{20,16},{24,28},{28,24},{1,5},{5... | collective-permute-start | bytes 6291464 | tf_op jit(solution)/shard_map/ppermute | solution.py:90
  409.2 433.2 %reduce-scatter.7.cloned.1.call-start = ((), (), s32[]{:S(2)}) async-start(), calls=%async_computation.9 | async-start | bytes 2359296 | tf_op jit(solution)/shard_map/reduce_scatter | solution.py:822
  480.0 48.7 %collective-permute-start.40 = (bf16[256,2048]{1,0:T(8,128)(2,1)}, bf16[256,2048]{1,0:T(8,128)(2,1)S(1)}, u32[]{:S(2)}, u32[]{:S(2)}) collective-permute-start(bf16[256,2048]{1,0:T(8,128)(2,1)} %get-tuple-element.135), channel_id=1, source_target_pairs={{0,8},{4,12},{8,0},{12,4},{16,24},{20,28},{24,16},{28,20},{1,9},{5... | collective-permute-start | bytes 3145736 | tf_op jit(solution)/shard_map/ppermute | solution.py:90
  480.8 60.5 %collective-permute-start.44 = (bf16[256,2048]{1,0:T(8,128)(2,1)}, bf16[256,2048]{1,0:T(8,128)(2,1)S(1)}, u32[]{:S(2)}, u32[]{:S(2)}) collective-permute-start(bf16[256,2048]{1,0:T(8,128)(2,1)} %get-tuple-element.152), channel_id=1, source_target_pairs={{0,16},{4,20},{8,24},{12,28},{16,0},{20,4},{24,8},{28,12},{1,17},{... | collective-permute-start | bytes 3145736 | tf_op jit(solution)/shard_map/ppermute | solution.py:90
  485.0 55.8 %collective-permute-start.43 = (bf16[256,2048]{1,0:T(8,128)(2,1)S(1)}, bf16[256,2048]{1,0:T(8,128)(2,1)S(1)}, u32[]{:S(2)}, u32[]{:S(2)}) collective-permute-start(bf16[256,2048]{1,0:T(8,128)(2,1)S(1)} %add_convert_fusion.2), channel_id=1, source_target_pairs={{0,16},{4,20},{8,24},{12,28},{16,0},{20,4},{24,8},{28,12},{1,17},{... | collective-permute-start | bytes 3145736 | tf_op jit(solution)/shard_map/ppermute | solution.py:90
  498.5 42.8 %collective-permute-start.46 = (bf16[256,2048]{1,0:T(8,128)(2,1)S(1)}, bf16[256,2048]{1,0:T(8,128)(2,1)S(1)}, u32[]{:S(2)}, u32[]{:S(2)}) collective-permute-start(bf16[256,2048]{1,0:T(8,128)(2,1)S(1)} %add_convert_fusion), channel_id=1, source_target_pairs={{0,8},{4,12},{8,0},{12,4},{16,24},{20,28},{24,16},{28,20},{1,9},{5... | collective-permute-start | bytes 3145736 | tf_op jit(solution)/shard_map/ppermute | solution.py:90
  548.8 37.4 %collective-permute-start.61 = (bf16[128,2048]{1,0:T(8,128)(2,1)S(1)}, bf16[128,2048]{1,0:T(8,128)(2,1)S(1)}, u32[]{:S(2)}, u32[]{:S(2)}) collective-permute-start(bf16[128,2048]{1,0:T(8,128)(2,1)S(1)} %get-tuple-element.295), channel_id=1, source_target_pairs={{0,2},{1,3},{2,0},{3,1},{4,6},{5,7},{6,4},{7,5},{8,10},{9,11},{10,... | collective-permute-start | bytes 1572872 | tf_op jit(solution)/shard_map/ppermute | solution.py:111
  550.9 35.2 %collective-permute-start.62 = (bf16[128,2048]{1,0:T(8,128)(2,1)S(1)}, bf16[128,2048]{1,0:T(8,128)(2,1)S(1)}, u32[]{:S(2)}, u32[]{:S(2)}) collective-permute-start(bf16[128,2048]{1,0:T(8,128)(2,1)S(1)} %get-tuple-element.294), channel_id=1, source_target_pairs={{0,3},{1,0},{2,1},{3,2},{4,7},{5,4},{6,5},{7,6},{8,11},{9,8},{10,9... | collective-permute-start | bytes 1572872 | tf_op jit(solution)/shard_map/ppermute | solution.py:111
  597.4 47.3 %collective-permute-start.64 = (bf16[128,2048]{1,0:T(8,128)(2,1)S(1)}, bf16[128,2048]{1,0:T(8,128)(2,1)S(1)}, u32[]{:S(2)}, u32[]{:S(2)}) collective-permute-start(bf16[128,2048]{1,0:T(8,128)(2,1)S(1)} %fusion.118), channel_id=1, source_target_pairs={{2,0},{3,1},{0,2},{1,3},{6,4},{7,5},{4,6},{5,7},{10,8},{11,9},{8,1... | collective-permute-start | bytes 1572872 | tf_op jit(solution)/shard_map/ppermute | solution.py:101
  600.0 44.6 %collective-permute-start.65 = (bf16[128,2048]{1,0:T(8,128)(2,1)S(1)}, bf16[128,2048]{1,0:T(8,128)(2,1)S(1)}, u32[]{:S(2)}, u32[]{:S(2)}) collective-permute-start(bf16[128,2048]{1,0:T(8,128)(2,1)S(1)} %fusion.118), channel_id=1, source_target_pairs={{3,0},{0,1},{1,2},{2,3},{7,4},{4,5},{5,6},{6,7},{11,8},{8,9},{9,10... | collective-permute-start | bytes 1572872 | tf_op jit(solution)/shard_map/ppermute | solution.py:101
  648.9 195.3 %reduce-scatter.11.cloned.1.call-start = ((), (), s32[]{:S(2)}) async-start(), calls=%async_computation.11 | async-start | bytes 3244032 | tf_op jit(solution)/shard_map/reduce_scatter | solution.py:822
  649.5 222.1 %reduce-scatter.9.cloned.1.call-start = ((), (), s32[]{:S(2)}) async-start(), calls=%async_computation.10 | async-start | bytes 6488064 | tf_op jit(solution)/shard_map/reduce_scatter | solution.py:822
  650.2 241.5 %reduce-scatter.5.cloned.1.call-start = ((), (), s32[]{:S(2)}) async-start(), calls=%async_computation.8 | async-start | bytes 7667712 | tf_op jit(solution)/shard_map/reduce_scatter | solution.py:822
  657.7 40.7 %collective-permute-start.48 = (bf16[2,256,2048]{2,1,0:T(8,128)(2,1)}, bf16[2,256,2048]{2,1,0:T(8,128)(2,1)}, u32[]{:S(2)}, u32[]{:S(2)}) collective-permute-start(bf16[2,256,2048]{2,1,0:T(8,128)(2,1)} %get-tuple-element.274), channel_id=1, source_target_pairs={{0,4},{4,0},{8,12},{12,8},{16,20},{20,16},{24,28},{28,24},{1,5},{5... | collective-permute-start | bytes 6291464 | tf_op jit(solution)/shard_map/ppermute | solution.py:90
  657.7 40.6 %collective-permute-start.51 = (bf16[2,256,2048]{2,1,0:T(8,128)(2,1)}, bf16[2,256,2048]{2,1,0:T(8,128)(2,1)}, u32[]{:S(2)}, u32[]{:S(2)}) collective-permute-start(bf16[2,256,2048]{2,1,0:T(8,128)(2,1)} %get-tuple-element.272), channel_id=1, source_target_pairs={{0,4},{4,0},{8,12},{12,8},{16,20},{20,16},{24,28},{28,24},{1,5},{5... | collective-permute-start | bytes 6291464 | tf_op jit(solution)/shard_map/ppermute | solution.py:90
  697.9 48.1 %collective-permute-start.50 = (bf16[2,256,2048]{2,1,0:T(8,128)(2,1)}, bf16[2,256,2048]{2,1,0:T(8,128)(2,1)}, u32[]{:S(2)}, u32[]{:S(2)}) collective-permute-start(bf16[2,256,2048]{2,1,0:T(8,128)(2,1)} %get-tuple-element.273), channel_id=1, source_target_pairs={{0,4},{4,0},{8,12},{12,8},{16,20},{20,16},{24,28},{28,24},{1,5},{5... | collective-permute-start | bytes 6291464 | tf_op jit(solution)/shard_map/ppermute | solution.py:90
  704.6 42.9 %collective-permute-start.52 = (bf16[256,2048]{1,0:T(8,128)(2,1)}, bf16[256,2048]{1,0:T(8,128)(2,1)}, u32[]{:S(2)}, u32[]{:S(2)}) collective-permute-start(bf16[256,2048]{1,0:T(8,128)(2,1)} %get-tuple-element.270), channel_id=1, source_target_pairs={{0,8},{4,12},{8,0},{12,4},{16,24},{20,28},{24,16},{28,20},{1,9},{5... | collective-permute-start | bytes 3145736 | tf_op jit(solution)/shard_map/ppermute | solution.py:90
  705.9 42.1 %collective-permute-start.55 = (bf16[256,2048]{1,0:T(8,128)(2,1)}, bf16[256,2048]{1,0:T(8,128)(2,1)}, u32[]{:S(2)}, u32[]{:S(2)}) collective-permute-start(bf16[256,2048]{1,0:T(8,128)(2,1)} %get-tuple-element.269), channel_id=1, source_target_pairs={{0,16},{4,20},{8,24},{12,28},{16,0},{20,4},{24,8},{28,12},{1,17},{... | collective-permute-start | bytes 3145736 | tf_op jit(solution)/shard_map/ppermute | solution.py:90
  742.2 45.2 %collective-permute-start.47 = (bf16[2,256,2048]{2,1,0:T(8,128)(2,1)}, bf16[2,256,2048]{2,1,0:T(8,128)(2,1)S(1)}, u32[]{:S(2)}, u32[]{:S(2)}) collective-permute-start(bf16[2,256,2048]{2,1,0:T(8,128)(2,1)} %get-tuple-element.271), channel_id=1, source_target_pairs={{0,4},{4,0},{8,12},{12,8},{16,20},{20,16},{24,28},{28,24},{1,5},{5... | collective-permute-start | bytes 6291464 | tf_op jit(solution)/shard_map/ppermute | solution.py:90
  746.0 41.5 %collective-permute-start.49 = (bf16[256,2048]{1,0:T(8,128)(2,1)}, bf16[256,2048]{1,0:T(8,128)(2,1)S(1)}, u32[]{:S(2)}, u32[]{:S(2)}) collective-permute-start(bf16[256,2048]{1,0:T(8,128)(2,1)} %get-tuple-element.263), channel_id=1, source_target_pairs={{0,8},{4,12},{8,0},{12,4},{16,24},{20,28},{24,16},{28,20},{1,9},{5... | collective-permute-start | bytes 3145736 | tf_op jit(solution)/shard_map/ppermute | solution.py:90
  747.5 43.2 %collective-permute-start.54 = (bf16[256,2048]{1,0:T(8,128)(2,1)}, bf16[256,2048]{1,0:T(8,128)(2,1)S(1)}, u32[]{:S(2)}, u32[]{:S(2)}) collective-permute-start(bf16[256,2048]{1,0:T(8,128)(2,1)} %get-tuple-element.264), channel_id=1, source_target_pairs={{0,16},{4,20},{8,24},{12,28},{16,0},{20,4},{24,8},{28,12},{1,17},{... | collective-permute-start | bytes 3145736 | tf_op jit(solution)/shard_map/ppermute | solution.py:90
  752.3 55.3 %collective-permute-start.53 = (bf16[256,2048]{1,0:T(8,128)(2,1)S(1)}, bf16[256,2048]{1,0:T(8,128)(2,1)S(1)}, u32[]{:S(2)}, u32[]{:S(2)}) collective-permute-start(bf16[256,2048]{1,0:T(8,128)(2,1)S(1)} %get-tuple-element.265), channel_id=1, source_target_pairs={{0,16},{4,20},{8,24},{12,28},{16,0},{20,4},{24,8},{28,12},{1,17},{... | collective-permute-start | bytes 3145736 | tf_op jit(solution)/shard_map/ppermute | solution.py:90
  753.8 53.8 %collective-permute-start.56 = (bf16[256,2048]{1,0:T(8,128)(2,1)S(1)}, bf16[256,2048]{1,0:T(8,128)(2,1)S(1)}, u32[]{:S(2)}, u32[]{:S(2)}) collective-permute-start(bf16[256,2048]{1,0:T(8,128)(2,1)S(1)} %get-tuple-element.266), channel_id=1, source_target_pairs={{0,8},{4,12},{8,0},{12,4},{16,24},{20,28},{24,16},{28,20},{1,9},{5... | collective-permute-start | bytes 3145736 | tf_op jit(solution)/shard_map/ppermute | solution.py:90
  787.5 52.4 %collective-permute-start.67 = (bf16[128,2048]{1,0:T(8,128)(2,1)S(1)}, bf16[128,2048]{1,0:T(8,128)(2,1)S(1)}, u32[]{:S(2)}, u32[]{:S(2)}) collective-permute-start(bf16[128,2048]{1,0:T(8,128)(2,1)S(1)} %get-tuple-element.292), channel_id=1, source_target_pairs={{0,2},{1,3},{2,0},{3,1},{4,6},{5,7},{6,4},{7,5},{8,10},{9,11},{10,... | collective-permute-start | bytes 1572872 | tf_op jit(solution)/shard_map/ppermute | solution.py:111
  790.6 49.3 %collective-permute-start.68 = (bf16[128,2048]{1,0:T(8,128)(2,1)S(1)}, bf16[128,2048]{1,0:T(8,128)(2,1)S(1)}, u32[]{:S(2)}, u32[]{:S(2)}) collective-permute-start(bf16[128,2048]{1,0:T(8,128)(2,1)S(1)} %get-tuple-element.291), channel_id=1, source_target_pairs={{0,3},{1,0},{2,1},{3,2},{4,7},{5,4},{6,5},{7,6},{8,11},{9,8},{10,9... | collective-permute-start | bytes 1572872 | tf_op jit(solution)/shard_map/ppermute | solution.py:111
  817.8 48.9 %collective-permute-start.58 = (bf16[128,2048]{1,0:T(8,128)(2,1)}, bf16[128,2048]{1,0:T(8,128)(2,1)}, u32[]{:S(2)}, u32[]{:S(2)}) collective-permute-start(bf16[128,2048]{1,0:T(8,128)(2,1)} %get-tuple-element.298), channel_id=1, source_target_pairs={{0,2},{1,3},{2,0},{3,1},{4,6},{5,7},{6,4},{7,5},{8,10},{9,11},{10,... | collective-permute-start | bytes 1572872 | tf_op jit(solution)/shard_map/ppermute | solution.py:111
  820.4 46.3 %collective-permute-start.59 = (bf16[128,2048]{1,0:T(8,128)(2,1)}, bf16[128,2048]{1,0:T(8,128)(2,1)}, u32[]{:S(2)}, u32[]{:S(2)}) collective-permute-start(bf16[128,2048]{1,0:T(8,128)(2,1)} %get-tuple-element.297), channel_id=1, source_target_pairs={{0,3},{1,0},{2,1},{3,2},{4,7},{5,4},{6,5},{7,6},{8,11},{9,8},{10,9... | collective-permute-start | bytes 1572872 | tf_op jit(solution)/shard_map/ppermute | solution.py:111
  (152 other events, 2245.8 us)
Sparse Core Ops, SparseCore 0:
  13.9 50.4 all-gather.4
  66.2 28.1 all-gather.6
  96.9 44.3 all-gather.8
  409.3 29.7 all-gather.10
  649.0 41.7 reduce-scatter.6
  694.5 51.9 reduce-scatter.10
  749.9 73.6 reduce-scatter.8
  827.5 64.2 reduce-scatter.4

commit v3 on v2

--- a/solution.py
+++ b/solution.py
@@ -16,6 +16,12 @@
 SEQ = 512
 HALF = 256
 QUARTET = 4
+BOX_UNITS = [
+    [(0, 0), (0, 1), (1, 0), (1, 1)],
+    [(2, 0), (4, 0), (3, 0), (5, 0)],
+    [(2, 1), (4, 1), (3, 1), (5, 1)],
+    [(6, 0), (6, 1), (7, 0), (7, 1)],
+]
 
 
 EPSILON = 1e-06
@@ -90,8 +96,8 @@
     return lax.ppermute(values, axis_name, [(i, i ^ bit) for i in range(count)])
 
 
-def after(values, *earlier):
-    return lax.optimization_barrier((values,) + earlier)[0]
+def tie(*values):
+    return lax.optimization_barrier(values)
 
 
 def column_gather(rows):
@@ -154,11 +160,11 @@
 
 def expert_front_kernel(step, experts, cap, aliased, *refs):
     count = QUARTET
-    x_in, dy_in = refs[:count], refs[count : 2 * count]
-    gate_up_in, down_in, slot_row_ref, weight_row_ref, slot_col_ref = refs[
-        2 * count : 2 * count + 5
-    ]
-    base = 2 * count + 5 + aliased
+    x_in = refs[:count]
+    where_ref, dy_in, gate_up_in, down_in, slot_row_ref, weight_row_ref, slot_col_ref = refs[
+        count : count + 7
+    ]
+    base = count + 7 + aliased
     dx_out = refs[base : base + 2]
     x_all, d_all, hid_all, dgu_all = refs[base + 2 : base + 6]
     (xb, db, gate_up, down, xs, ds, dxs, dxo, hid, dgu, sem_in, sem_w, sem_out, sem_dx) = refs[
@@ -169,7 +175,12 @@
     tile = min(1024, width)
     x_copies = [pltpu.make_async_copy(x_in[q], xb.at[q], sem_in.at[q]) for q in range(count)]
     d_copies = [
-        pltpu.make_async_copy(dy_in[q], db.at[q], sem_in.at[count + q]) for q in range(count)
+        pltpu.make_async_copy(
+            dy_in.at[pl.ds(pl.multiple_of(where_ref[q] * HALF, HALF), HALF)],
+            db.at[q],
+            sem_in.at[count + q],
+        )
+        for q in range(count)
     ]
     w_copies = [
         pltpu.make_async_copy(gate_up_in, gate_up, sem_w.at[0]),
@@ -255,7 +266,7 @@
         copy.wait()
 
 
-def expert_front(step, steps, x_parts, dy_parts, gate_up, down, tables, kept, cap):
+def expert_front(step, steps, x_parts, where, dy_all, gate_up, down, tables, kept, cap):
     experts, wide, width = gate_up.shape
     pad = wide // 2
     slots = QUARTET * cap
@@ -270,9 +281,13 @@
     results = pl.pallas_call(
         functools.partial(expert_front_kernel, step, experts, cap, len(kept)),
         out_shape=[pair_shape] * 2 + kept_shapes,
-        in_specs=[any_spec] * (2 * QUARTET + 2) + [vmem_spec] * 3 + [any_spec] * len(kept),
+        in_specs=[any_spec] * QUARTET
+        + [pl.BlockSpec(memory_space=pltpu.SMEM)]
+        + [any_spec] * 3
+        + [vmem_spec] * 3
+        + [any_spec] * len(kept),
         out_specs=[any_spec] * 6,
-        input_output_aliases={2 * QUARTET + 5 + i: 2 + i for i in range(len(kept))},
+        input_output_aliases={QUARTET + 7 + i: 2 + i for i in range(len(kept))},
         scratch_shapes=[
             pltpu.VMEM((QUARTET, HALF, width), BF),
             pltpu.VMEM((QUARTET, HALF, width), BF),
@@ -297,7 +312,7 @@
             transcendentals=slots * experts * pad,
         ),
         name="expert_front",
-    )(*x_parts, *dy_parts, gate_up, down, slot_row, weight_row, slot_col, *kept)
+    )(*x_parts, where, dy_all, gate_up, down, slot_row, weight_row, slot_col, *kept)
     return list(results[:2]), list(results[2:])
 
 
@@ -409,14 +424,652 @@
     )(dgu_all, x_all, hid_all, d_all)
 
 
+def mesh_copy(src, dst, sends, arrivals, number, device):
+    return pltpu.make_async_remote_copy(
+        src_ref=src,
+        dst_ref=dst,
+        send_sem=sends.at[number],
+        recv_sem=arrivals.at[number],
+        device_id=device,
+        device_id_type=pl.DeviceIdType.MESH,
+    )
+
+
+def plane_neighbours():
+    place, column = lax.axis_index("fsdp"), lax.axis_index("tp")
+    core, along, across = place % 2, (place // 2) % 2, place // 4
+    return (
+        (place + 1 - 2 * core, column),
+        (place + 2 - 4 * along, column),
+        (place + 4 - 8 * across, column),
+    )
+
+
+def column_neighbours(count):
+    place, column = lax.axis_index("fsdp"), lax.axis_index("tp")
+    return [(place, (column + s) % count) for s in range(1, count)]
+
+
+def greet(devices):
+    barrier = pltpu.get_barrier_semaphore()
+    for device in devices:
+        pl.semaphore_signal(
+            barrier, inc=1, device_id=device, device_id_type=pl.DeviceIdType.MESH
+        )
+    pl.semaphore_wait(barrier, len(devices))
+
+
+class PlaneGather:
+    def __init__(self, own, others, size, sends, arrivals, base):
+        self.own, self.others, self.size = own, others, size
+        self.sends, self.arrivals, self.base = sends, arrivals, base
+        self.partner, self.along, self.across = plane_neighbours()
+
+    def copies(self, b):
+        half = self.own.shape[1] // 2
+        rows = pl.ds(b * self.size, self.size)
+        left, right = pl.ds(0, half), pl.ds(half, half)
+        other = {r: self.others.at[r - 1] for r in range(1, 8)}
+        plan = [
+            (self.own.at[rows], other[2].at[rows], self.along),
+            (self.own.at[rows], other[4].at[rows], self.across),
+            (self.own.at[rows], other[1].at[rows], self.partner),
+            (other[2].at[rows, left], other[6].at[rows, left], self.across),
+            (other[4].at[rows, right], other[6].at[rows, right], self.along),
+            (other[2].at[rows], other[3].at[rows], self.partner),
+            (other[4].at[rows], other[5].at[rows], self.partner),
+            (other[6].at[rows], other[7].at[rows], self.partner),
+        ]
+        return [
+            mesh_copy(src, dst, self.sends, self.arrivals, self.base + 8 * b + i, device)
+            for i, (src, dst, device) in enumerate(plan)
+        ]
+
+    def start(self, b):
+        for copy in self.copies(b)[:3]:
+            copy.start()
+
+    def forward(self, b):
+        along, across, _, left, right, third, fifth, _ = self.copies(b)
+        along.wait_recv()
+        left.start()
+        third.start()
+        across.wait_recv()
+        right.start()
+        fifth.start()
+
+    def last(self, b):
+        copies = self.copies(b)
+        copies[3].wait_recv()
+        copies[4].wait_recv()
+        copies[7].start()
+
+    def arrived(self, b, numbers):
+        copies = self.copies(b)
+        for i in numbers:
+            copies[i].wait_recv()
+
+    def drain(self, b):
+        for copy in self.copies(b):
+            copy.wait_send()
+
+
+def expert_kernel(experts, cap, columns, size, *refs):
+    (
+        attn_in,
+        tokens_in,
+        cotan_in,
+        gate_up_in,
+        down_in,
+        gain_ref,
+        slot_row_ref,
+        weight_row_ref,
+        slot_col_ref,
+        mixed_out,
+        ffn_all,
+        dx_out,
+        out_all,
+        x_all,
+        d_all,
+        hid_all,
+        dgu_all,
+        x_others,
+        dy_others,
+        theirs,
+        links,
+        attn_v,
+        tokens_v,
+        arrived_v,
+        mixed_v,
+        ffn_v,
+        xb,
+        db,
+        gate_up,
+        down,
+        xs,
+        ds,
+        dxs,
+        others,
+        chip,
+        hid,
+        dgu,
+        stage,
+        sends,
+        arrivals,
+        local,
+        spill,
+    ) = refs
+    count = QUARTET
+    width = xb.shape[2]
+    half_width = width // 2
+    pad = down.shape[1]
+    tile = min(1024, width)
+    blocks = columns
+    partner, along, across = plane_neighbours()
+    column = column_neighbours(columns)
+    number = 0
+
+    def reserve(amount):
+        nonlocal number
+        number += amount
+        return number - amount
+
+    x_gather = PlaneGather(ffn_all, x_others, size, sends, arrivals, reserve(8 * blocks))
+    dy_gather = PlaneGather(cotan_in, dy_others, SEQ, sends, arrivals, reserve(8))
+    rs_base, ag_base = reserve(columns - 1), reserve(columns - 1)
+    pair_base, link_base = reserve(len(BOX_UNITS)), reserve(12)
+
+    greet([partner, along, across] + column)
+    sums = [
+        mesh_copy(
+            attn_in.at[pl.ds(s * size, size)],
+            arrived_v.at[s - 1],
+            sends,
+            arrivals,
+            rs_base + s - 1,
+            column[s - 1],
+        )
+        for s in range(1, columns)
+    ]
+    for copy in sums:
+        copy.start()
+    first = [
+        pltpu.make_async_copy(attn_in.at[pl.ds(0, size)], attn_v, local.at[0]),
+        pltpu.make_async_copy(tokens_in, tokens_v, local.at[1]),
+    ]
+    for copy in first:
+        copy.start()
+    dy_gather.start(0)
+    weights_in = [
+        pltpu.make_async_copy(gate_up_in, gate_up, local.at[2]),
+        pltpu.make_async_copy(down_in, down, local.at[3]),
+    ]
+    for copy in weights_in:
+        copy.start()
+    for copy in first:
+        copy.wait()
+    total = tokens_v[...].astype(F32) + attn_v[...].astype(F32)
+    for s in range(1, columns):
+        sums[s - 1].wait_recv()
+        total = total + arrived_v[s - 1].astype(F32)
+    mixed_v[...] = total
+    inverse = lax.rsqrt(jnp.mean(total * total, axis=1, keepdims=True) + EPSILON)
+    ffn_v[...] = (total * inverse * gain_ref[...]).astype(BF)
+    own_copy = pltpu.make_async_copy(ffn_v, ffn_all.at[pl.ds(0, size)], local.at[0])
+    own_copy.start()
+    mixed_copy = pltpu.make_async_copy(mixed_v, mixed_out, local.at[1])
+    mixed_copy.start()
+    own_copy.wait()
+
+    rows_out = [
+        mesh_copy(
+            ffn_all.at[pl.ds(0, size)],
+            ffn_all.at[pl.ds((columns - s) * size, size)],
+            sends,
+            arrivals,
+            ag_base + s - 1,
+            column[s - 1],
+        )
+        for s in range(1, columns)
+    ]
+    for copy in rows_out:
+        copy.start()
+    x_gather.start(0)
+    dy_gather.forward(0)
+    for b in range(1, blocks):
+        rows_out[columns - b - 1].wait_recv()
+        x_gather.start(b)
+        x_gather.forward(b - 1)
+    for b in range(blocks):
+        x_gather.arrived(b, [2])
+    dy_gather.arrived(0, [2])
+
+    def source(own, gathered, r):
+        return own if r == 0 else gathered.at[r - 1]
+
+    def load(unit):
+        copies = []
+        for q, (r, h) in enumerate(unit):
+            rows = pl.ds(h * HALF, HALF)
+            copies.append(
+                pltpu.make_async_copy(
+                    source(ffn_all, x_others, r).at[rows], xb.at[q], local.at[4 + q]
+                )
+            )
+            copies.append(
+                pltpu.make_async_copy(
+                    source(cotan_in, dy_others, r).at[rows], db.at[q], local.at[8 + q]
+                )
+            )
+        return copies
+
+    def choose_cols(step, q):
+        return jnp.where(select_cols(slot_col_ref[step, q], experts, cap), 1.0, 0.0).astype(BF)
+
+    def combine(step, target):
+        for q in range(count):
+            choose = choose_cols(step, q)
+
+            def gather(n, carry, q=q, choose=choose):
+                cols = pl.ds(pl.multiple_of(n * tile, tile), tile)
+                ref, place = target(q)
+                ref[place + (slice(None), cols)] = dot_plain(choose, dxs[q, :, cols]).astype(BF)
+                return carry
+
+            lax.fori_loop(0, width // tile, gather, 0)
+
+    def spills(step):
+        return [
+            pltpu.make_async_copy(xs, x_all.at[step], spill.at[0]),
+            pltpu.make_async_copy(ds, d_all.at[step], spill.at[1]),
+            pltpu.make_async_copy(hid.at[step], hid_all.at[step], spill.at[2]),
+            pltpu.make_async_copy(dgu, dgu_all.at[step], spill.at[3]),
+        ]
+
+    def pair_copy(step):
+        return mesh_copy(others, theirs.at[step], sends, arrivals, pair_base + step, partner)
+
+    def front(step):
+        copies = load(BOX_UNITS[step])
+        for copy in copies:
+            copy.start()
+        if step == 0:
+            for copy in weights_in:
+                copy.wait()
+        if step > 0:
+            for copy in spills(step - 1):
+                copy.wait()
+        for q in range(count):
+            copies[2 * q].wait()
+            copies[2 * q + 1].wait()
+            hit = select_rows(slot_row_ref[step, q], experts, cap)
+            weights = slot_weights(hit, weight_row_ref[step, q], experts, cap)
+            choose = jnp.where(hit, 1.0, 0.0).astype(BF)
+
+            def spread(n, carry, q=q, choose=choose, weights=weights):
+                cols = pl.ds(pl.multiple_of(n * tile, tile), tile)
+                rows = dot_plain(choose, xb[q, :, cols])
+                grads = dot_plain(choose, db[q, :, cols]) * weights
+                for e in range(experts):
+                    low, high = e * cap, (e + 1) * cap
+                    xs[e, q * cap : (q + 1) * cap, cols] = rows[low:high].astype(BF)
+                    ds[e, q * cap : (q + 1) * cap, cols] = grads[low:high].astype(BF)
+                return carry
+
+            lax.fori_loop(0, width // tile, spread, 0)
+        out_copies = spills(step)
+        out_copies[0].start()
+        out_copies[1].start()
+
+        def one_expert(e, carry):
+            both = dot_rows(xs[e], gate_up[e])
+            gate_pre, up_pre = both[:, :pad], both[:, pad:]
+            d_hidden = dot_rows(ds[e], down[e])
+            sigmoid = jax.nn.sigmoid(gate_pre)
+            silu = gate_pre * sigmoid
+            hid[step, e] = (silu * up_pre).astype(BF)
+            gate_grad = d_hidden * up_pre * (sigmoid * (1.0 + gate_pre * (1.0 - sigmoid)))
+            dgu[e] = jnp.concatenate([gate_grad, d_hidden * silu], axis=1).astype(BF)
+
+            def back(n, inner):
+                cols = pl.ds(pl.multiple_of(n * tile, tile), tile)
+                part = dot_plain(dgu[e], gate_up[e, :, cols]).astype(BF)
+                for q in range(count):
+                    dxs[q, pl.ds(pl.multiple_of(e * cap, cap), cap), cols] = part[
+                        q * cap : (q + 1) * cap
+                    ]
+                return inner
+
+            lax.fori_loop(0, width // tile, back, 0)
+            return carry
+
+        lax.fori_loop(0, experts, one_expert, 0)
+        out_copies[2].start()
+        out_copies[3].start()
+        if step > 0:
+            pair_copy(step - 1).wait_send()
+        combine(step, lambda q: (chip, (step, q)) if q < 2 else (others, (q - 2,)))
+        pair_copy(step).start()
+
+    def add_rows(step, q, cols, landed):
+        fetch = pltpu.make_async_copy(landed, stage.at[:, cols], local.at[12])
+        fetch.start()
+        fetch.wait()
+
+        def some(i, carry):
+            rows = pl.ds(pl.multiple_of(i * 32, 32), 32)
+            chip[step, q, rows, cols] = (
+                chip[step, q, rows, cols].astype(F32) + stage[rows, cols].astype(F32)
+            ).astype(BF)
+            return carry
+
+        lax.fori_loop(0, HALF // 32, some, 0)
+
+    left, right = pl.ds(0, half_width), pl.ds(half_width, half_width)
+
+    def chip_sum(step):
+        pair_copy(step).wait_recv()
+        for h in range(2):
+            add_rows(step, h, pl.ds(0, width), theirs.at[step, h])
+
+    def chip_place(r, h):
+        step = [i for i, unit in enumerate(BOX_UNITS) if (r, h) in unit][0]
+        return step, BOX_UNITS[step].index((r, h))
+
+    def chip_rows(r, h):
+        return chip.at[chip_place(r, h)]
+
+    def link_copy(stage_number, side, h):
+        first_hop, second_hop = (along, across) if side == 0 else (across, along)
+        near, far = (2, 4) if side == 0 else (4, 2)
+        r = (near, 6, far)[stage_number]
+        device = second_hop if stage_number == 2 else first_hop
+        i = (stage_number * 2 + side) * 2 + h
+        return mesh_copy(
+            chip.at[chip_place(r, h) + (pl.ds(0, HALF), (left, right)[side])],
+            links.at[i],
+            sends,
+            arrivals,
+            link_base + i,
+            device,
+        )
+
+    def take_link(stage_number, side, h, r):
+        link_copy(stage_number, side, h).wait_recv()
+        i = (stage_number * 2 + side) * 2 + h
+        add_rows(*chip_place(r, h), (left, right)[side], links.at[i])
+
+    def out_part(step):
+        weights = [
+            slot_weights(
+                select_rows(slot_row_ref[step, q], experts, cap),
+                weight_row_ref[step, q],
+                experts,
+                cap,
+            )
+            for q in range(count)
+        ]
+        for e in range(experts):
+
+            def one_tile(n, carry, e=e):
+                cols = pl.ds(pl.multiple_of(n * tile, tile), tile)
+                rows = dot_plain(hid[step, e], down[e, :, cols])
+                for q in range(count):
+                    dxs[q, e * cap : (e + 1) * cap, cols] = (
+                        rows[q * cap : (q + 1) * cap] * weights[q][e * cap : (e + 1) * cap]
+                    ).astype(BF)
+                return carry
+
+            lax.fori_loop(0, width // tile, one_tile, 0)
+        if step > 0:
+            out_copy(step - 1).wait()
+        combine(step, lambda q: (db, (q,)))
+        out_copy(step).start()
+
+    def out_copy(step):
+        return pltpu.make_async_copy(db, out_all.at[step], local.at[13])
+
+    middle = blocks // 2
+    front(0)
+    x_gather.forward(blocks - 1)
+    dy_gather.last(0)
+    for b in range(middle):
+        x_gather.arrived(b, [5, 6])
+    dy_gather.arrived(0, [5, 6])
+    front(1)
+    for b in range(blocks):
+        x_gather.last(b)
+    for b in range(middle, blocks):
+        x_gather.arrived(b, [5, 6])
+    chip_sum(0)
+    front(2)
+    chip_sum(1)
+    for side in range(2):
+        link_copy(0, side, 0).start()
+    for b in range(blocks):
+        x_gather.arrived(b, [7])
+    dy_gather.arrived(0, [7])
+    front(3)
+    chip_sum(2)
+    for side in range(2):
+        link_copy(0, side, 1).start()
+    for copy in spills(3):
+        copy.wait()
+    out_part(0)
+    chip_sum(3)
+    for h in range(2):
+        for side in range(2):
+            link_copy(1, side, h).start()
+    out_part(1)
+    for h in range(2):
+        for side in range(2):
+            take_link(1, side, h, (4, 2)[side])
+            link_copy(2, side, h).start()
+    out_part(2)
+    out_part(3)
+    for h in range(2):
+        for side in range(2):
+            take_link(0, side, h, 0)
+        for side in range(2):
+            take_link(2, side, h, 0)
+        done = pltpu.make_async_copy(
+            chip_rows(0, h), dx_out.at[pl.ds(h * HALF, HALF)], local.at[14 + h]
+        )
+        done.start()
+    for h in range(2):
+        pltpu.make_async_copy(
+            chip_rows(0, h), dx_out.at[pl.ds(h * HALF, HALF)], local.at[14 + h]
+        ).wait()
+    out_copy(3).wait()
+    mixed_copy.wait()
+
+    for b in range(blocks):
+        x_gather.drain(b)
+    dy_gather.drain(0)
+    for copy in sums + rows_out:
+        copy.wait_send()
+    pair_copy(3).wait_send()
+    for stage_number in range(3):
+        for side in range(2):
+            for h in range(2):
+                link_copy(stage_number, side, h).wait_send()
+
+
+def expert_call(attn_part, tokens, cotan_all, gate_up, down, gain, tables, cap):
+    columns = lax.axis_size("tp")
+    size, width = tokens.shape
+    experts, wide, _ = gate_up.shape
+    pad = wide // 2
+    slots = QUARTET * cap
+    steps = len(BOX_UNITS)
+    anywhere = pl.BlockSpec(memory_space=pl.ANY)
+    held = pl.BlockSpec(memory_space=pltpu.VMEM)
+
+    def array(*dims, kind=BF):
+        return jax.ShapeDtypeStruct(dims, kind)
+
+    copies = 8 * columns + 8 + 2 * (columns - 1) + steps + 12
+    results = pl.pallas_call(
+        functools.partial(expert_kernel, experts, cap, columns, size),
+        out_shape=[
+            array(size, width, kind=F32),
+            array(SEQ, width),
+            array(SEQ, width),
+            array(steps, QUARTET, HALF, width),
+            array(steps, experts, slots, width),
+            array(steps, experts, slots, width),
+            array(steps, experts, slots, pad),
+            array(steps, experts, slots, wide),
+            array(7, SEQ, width),
+            array(7, SEQ, width),
+            array(steps, 2, HALF, width),
+            array(12, HALF, width // 2),
+        ],
+        in_specs=[anywhere] * 5 + [held] * 4,
+        out_specs=[anywhere] * 12,
+        scratch_shapes=[
+            pltpu.VMEM((size, width), BF),
+            pltpu.VMEM((size, width), BF),
+            pltpu.VMEM((columns - 1, size, width), BF),
+            pltpu.VMEM((size, width), F32),
+            pltpu.VMEM((size, width), BF),
+            pltpu.VMEM((QUARTET, HALF, width), BF),
+            pltpu.VMEM((QUARTET, HALF, width), BF),
+            pltpu.VMEM((experts, wide, width), BF),
+            pltpu.VMEM((experts, pad, width), BF),
+            pltpu.VMEM((experts, slots, width), BF),
+            pltpu.VMEM((experts, slots, width), BF),
+            pltpu.VMEM((QUARTET, experts * cap, width), BF),
+            pltpu.VMEM((2, HALF, width), BF),
+            pltpu.VMEM((steps, 2, HALF, width), BF),
+            pltpu.VMEM((steps, experts, slots, pad), BF),
+            pltpu.VMEM((experts, slots, wide), BF),
+            pltpu.VMEM((HALF, width), BF),
+            pltpu.SemaphoreType.DMA((copies,)),
+            pltpu.SemaphoreType.DMA((copies,)),
+            pltpu.SemaphoreType.DMA((16,)),
+            pltpu.SemaphoreType.DMA((4,)),
+        ],
+        compiler_params=pltpu.CompilerParams(
+            collective_id=1, has_side_effects=True, vmem_limit_bytes=67_043_328
+        ),
+        cost_estimate=pl.CostEstimate(
+            flops=steps
+            * (2 * slots * experts * width * pad * 6 + 8 * QUARTET * HALF * experts * cap * width),
+            bytes_accessed=60 * SEQ * width,
+            transcendentals=0,
+        ),
+        name="experts",
+    )(attn_part, tokens, cotan_all, gate_up, down, gain, *tables)
+    return results[:8]
+
+
+def first_kernel(columns, size, *refs):
+    (
+        tokens_in,
+        packed_in,
+        tokens_all,
+        packed_all,
+        tokens_v,
+        packed_v,
+        sends,
+        arrivals,
+        local,
+    ) = refs
+    partner, along, across = plane_neighbours()
+    column = column_neighbours(columns)
+    place = lax.axis_index("fsdp")
+    rows = packed_in.shape[0]
+    top, bottom = pl.ds(0, rows // 2), pl.ds(rows // 2, rows // 2)
+    opposite = along[0] + across[0] - place
+    greet([partner, along, across] + column)
+    plan = [
+        (packed_in, packed_all.at[place], along),
+        (packed_in, packed_all.at[place], across),
+        (packed_in, packed_all.at[place], partner),
+        (packed_all.at[along[0], top], packed_all.at[along[0], top], across),
+        (packed_all.at[across[0], bottom], packed_all.at[across[0], bottom], along),
+        (packed_all.at[along[0]], packed_all.at[along[0]], partner),
+        (packed_all.at[across[0]], packed_all.at[across[0]], partner),
+        (packed_all.at[opposite], packed_all.at[opposite], partner),
+    ]
+    copies = [
+        mesh_copy(src, dst, sends, arrivals, i, device) for i, (src, dst, device) in enumerate(plan)
+    ]
+    rows_out = [
+        mesh_copy(
+            tokens_in,
+            tokens_all.at[pl.ds((columns - s) * size, size)],
+            sends,
+            arrivals,
+            7 + s,
+            column[s - 1],
+        )
+        for s in range(1, columns)
+    ]
+    for copy in copies[:3] + rows_out:
+        copy.start()
+    here = [
+        pltpu.make_async_copy(tokens_in, tokens_v, local.at[0]),
+        pltpu.make_async_copy(packed_in, packed_v, local.at[1]),
+    ]
+    for copy in here:
+        copy.start()
+    for copy in here:
+        copy.wait()
+    there = [
+        pltpu.make_async_copy(tokens_v, tokens_all.at[pl.ds(0, size)], local.at[0]),
+        pltpu.make_async_copy(packed_v, packed_all.at[place], local.at[1]),
+    ]
+    for copy in there:
+        copy.start()
+    copies[0].wait_recv()
+    copies[3].start()
+    copies[5].start()
+    copies[1].wait_recv()
+    copies[4].start()
+    copies[6].start()
+    copies[3].wait_recv()
+    copies[4].wait_recv()
+    copies[7].start()
+    for i in (2, 5, 6, 7):
+        copies[i].wait_recv()
+    for copy in rows_out:
+        copy.wait_recv()
+    for copy in there:
+        copy.wait()
+    for copy in copies + rows_out:
+        copy.wait_send()
+
+
+def first_call(tokens, packed):
+    columns = lax.axis_size("tp")
+    size, width = tokens.shape
+    anywhere = pl.BlockSpec(memory_space=pl.ANY)
+    copies = 8 + columns - 1
+    return pl.pallas_call(
+        functools.partial(first_kernel, columns, size),
+        out_shape=[
+            jax.ShapeDtypeStruct((columns * size, width), BF),
+            jax.ShapeDtypeStruct((8,) + packed.shape, BF),
+        ],
+        in_specs=[anywhere] * 2,
+        out_specs=[anywhere] * 2,
+        scratch_shapes=[
+            pltpu.VMEM((size, width), BF),
+            pltpu.VMEM(packed.shape, BF),
+            pltpu.SemaphoreType.DMA((copies,)),
+            pltpu.SemaphoreType.DMA((copies,)),
+            pltpu.SemaphoreType.DMA((2,)),
+        ],
+        compiler_params=pltpu.CompilerParams(collective_id=2, has_side_effects=True),
+        name="first_gather",
+    )(tokens, packed)
+
+
 def plane_units(count):
     if count == 8:
-        return [
-            [(0, 0), (0, 1), (1, 0), (1, 1)],
-            [(2, 0), (4, 1), (3, 0), (5, 1)],
-            [(2, 1), (4, 0), (3, 1), (5, 0)],
-            [(6, 0), (6, 1), (7, 0), (7, 1)],
-        ]
+        return BOX_UNITS
     return [[(2 * i + j // 2, j % 2) for j in range(4)] for i in range(count // 2)]
 
 
@@ -425,52 +1078,10 @@
 
 
 def plane_gather(rows, count):
-    blocks = {}
-    if count == 8:
-        other = partner(rows)
-        for h in (0, 1):
-            blocks[0, h] = rows[h * HALF : (h + 1) * HALF]
-            blocks[1, h] = other[h * HALF : (h + 1) * HALF]
-        blocks[2, 0] = swap(blocks[0, 0], "fsdp", 2)
-        blocks[4, 1] = swap(blocks[0, 1], "fsdp", 4)
-        blocks[2, 1] = swap(blocks[0, 1], "fsdp", 2)
-        blocks[4, 0] = swap(blocks[0, 0], "fsdp", 4)
-        blocks[6, 0] = swap(blocks[2, 0], "fsdp", 4)
-        blocks[6, 1] = swap(blocks[4, 1], "fsdp", 2)
-        for r in (2, 4, 6):
-            for h in (0, 1):
-                blocks[r + 1, h] = partner(blocks[r, h])
-        return blocks
     gathered = lax.all_gather(rows, "fsdp", axis=0)
-    for r in range(count):
-        blocks[r, 0] = gathered[r, :HALF]
-        blocks[r, 1] = gathered[r, HALF:]
-    return blocks
-
-
-def whole_gather_first(rows, count):
-    if count == 8:
-        return [rows, partner(rows), swap(rows, "fsdp", 2), swap(rows, "fsdp", 4)]
-    gathered = lax.all_gather(rows, "fsdp", axis=0)
-    return [gathered[r] for r in range(count)]
-
-
-def whole_gather_rest(first, count):
-    blocks = {}
-    if count == 8:
-        whole = {0: first[0], 1: first[1], 2: first[2], 4: first[3]}
-        blocks[6, 0] = swap(whole[2][:HALF], "fsdp", 4)
-        blocks[6, 1] = swap(whole[4][HALF:], "fsdp", 2)
-        whole[3] = partner(whole[2])
-        whole[5] = partner(whole[4])
-        for h in (0, 1):
-            blocks[7, h] = partner(blocks[6, h])
-    else:
-        whole = dict(enumerate(first))
-    for r, rows in whole.items():
-        for h in (0, 1):
-            blocks[r, h] = rows[h * HALF : (h + 1) * HALF]
-    return blocks
+    return {
+        (r, h): gathered[r, h * HALF : (h + 1) * HALF] for r in range(count) for h in (0, 1)
+    }
 
 
 def add_pairs(left, right):
@@ -483,13 +1094,20 @@
 
 
 def plane_scatter(chip):
-    top = add_pairs(chip[0, 0], swap(chip[2, 0].astype(BF), "fsdp", 2))
-    bottom = add_pairs(chip[0, 1], swap(chip[4, 1].astype(BF), "fsdp", 4))
-    over_top = add_pairs(chip[4, 0], swap(chip[6, 0].astype(BF), "fsdp", 2)).astype(BF)
-    over_bottom = add_pairs(chip[2, 1], swap(chip[6, 1].astype(BF), "fsdp", 4)).astype(BF)
-    top = add_pairs(top, swap(over_top, "fsdp", 4))
-    bottom = add_pairs(bottom, swap(over_bottom, "fsdp", 2))
-    return jnp.concatenate([top, bottom], axis=0)
+    whole = {r: jnp.concatenate([chip[r, 0], chip[r, 1]], axis=0) for r in (0, 2, 4, 6)}
+    half = whole[0].shape[1] // 2
+    left, right = slice(None, half), slice(half, None)
+
+    def send(rows, bit):
+        return swap(rows.astype(BF), "fsdp", bit)
+
+    on_left = add_pairs(whole[4][:, left], send(whole[6][:, left], 2))
+    on_right = add_pairs(whole[2][:, right], send(whole[6][:, right], 4))
+    first = add_pairs(whole[0][:, left], send(whole[2][:, left], 2))
+    second = add_pairs(whole[0][:, right], send(whole[4][:, right], 4))
+    first = add_pairs(first, send(on_left, 4))
+    second = add_pairs(second, send(on_right, 2))
+    return jnp.concatenate([first, second], axis=1)
 
 
 def plane_scatter_whole(pairs, units, count):
@@ -609,7 +1227,13 @@
         [query_proj, latent_proj, gains, latent_up.reshape(shard_rows, -1)], axis=1
     )
     lift_cols = packed.shape[1] - joint - spare
-    packed_all = lax.all_gather(packed, "fsdp", axis=0, tiled=True)
+    paired = fsdp_count == 8
+    if paired:
+        tokens_all, packed_all = first_call(block_in, packed)
+        packed_all = packed_all.reshape(-1, packed.shape[1])
+    else:
+        packed_all = lax.all_gather(packed, "fsdp", axis=0, tiled=True)
+        tokens_all = column_gather(block_in)
     joint_weight = packed_all[:, :joint]
     gain_attn = packed_all[:, joint].astype(F32)
     gain_ffn = packed_all[:, joint + 1].astype(F32)
@@ -620,18 +1244,13 @@
         .astype(F32)
     )
     latent_up_weight = packed_all[:, joint + spare :].reshape(LAT, up_cols)
-    tokens_all = column_gather(block_in)
-    out_weight = lax.all_gather(after(out_proj, packed_all), "fsdp", axis=1, tiled=True)
-    cotan_all = column_gather(after(out_cotan, tokens_all))
+    out_weight = lax.all_gather(out_proj, "fsdp", axis=1, tiled=True)
+    cotan_own, tokens_all = tie(out_cotan, tokens_all)
+    cotan_all = column_gather(cotan_own)
     shared_weight = lax.all_gather(
-        after(jnp.concatenate([shared_gate, shared_up], axis=1), out_weight),
-        "fsdp",
-        axis=0,
-        tiled=True,
-    )
-    shared_down_weight = lax.all_gather(
-        after(shared_down, shared_weight), "fsdp", axis=1, tiled=True
-    )
+        jnp.concatenate([shared_gate, shared_up], axis=1), "fsdp", axis=0, tiled=True
+    )
+    shared_down_weight = lax.all_gather(shared_down, "fsdp", axis=1, tiled=True)
     shared_cols = shared_gate.shape[1]
     tables = expert_tables(expert_ids, expert_wts, local_experts, units, cap)
     hidden_pad = -(-local_hidden // 128) * 128
@@ -690,47 +1309,44 @@
         .reshape(SEQ, heads_local * DV)
         .astype(BF)
     )
-    attended = after(attended, cotan_all)
-    dy_first = whole_gather_first(cotan_all, fsdp_count)
-    attn_rows = column_scatter(jnp.dot(attended, out_weight, preferred_element_type=F32))
-    mixed_rows = block_in.astype(F32) + attn_rows
-    unit_two, inverse_two = norm_parts(mixed_rows)
-    normed_ffn, dy_first, shared_weight = after(
-        ((unit_two * gain_ffn).astype(BF), dy_first, shared_weight)
-    )
-    normed_ffn_all = column_gather(normed_ffn)
-
-    dy_blocks = whole_gather_rest(dy_first, fsdp_count)
-    normed_ffn_all, dy_blocks = after((normed_ffn_all, dy_blocks))
-    x_blocks = plane_gather(normed_ffn_all, fsdp_count)
-    paired = fsdp_count == 8
-    kept = []
-    dx_pairs = []
-    dx_chip = {}
-    for step, unit in enumerate(units):
-        x_list = [x_blocks[key] for key in unit]
-        if paired and step == 2:
-            x_list = after(x_list, dx_pairs[0])
-        if paired and step == 3:
-            x_list, dx_chip = after((x_list, dx_chip))
-        pair, kept = expert_front(
-            step,
-            len(units),
-            x_list,
-            [dy_blocks[key] for key in unit],
+    attn_part = jnp.dot(attended, out_weight, preferred_element_type=F32).astype(BF)
+    if paired:
+        mixed_rows, normed_ffn_all, d_routed_in, out_array, *kept = expert_call(
+            attn_part,
+            block_in,
+            cotan_all,
             routed_gate_up,
             routed_down_pad,
+            gain_ffn[None, :],
             tables,
-            kept,
             cap,
         )
-        dx_pairs.append(pair)
-        if paired:
-            dx_chip.update(chip_sums(unit, pair))
-    near, far = expert_out(kept[2], routed_down_pad, tables, cap)
-    if paired:
-        d_routed_in = plane_scatter(dx_chip)
+        unit_two, inverse_two = norm_parts(mixed_rows)
+        d_routed_in = d_routed_in.astype(F32)
+        near, far = out_array[:, :2], out_array[:, 2:]
     else:
+        mixed_rows = block_in.astype(F32) + column_scatter(attn_part)
+        unit_two, inverse_two = norm_parts(mixed_rows)
+        normed_ffn_all = column_gather((unit_two * gain_ffn).astype(BF))
+        x_blocks = plane_gather(normed_ffn_all, fsdp_count)
+        dy_all = lax.all_gather(cotan_all, "fsdp", axis=0, tiled=True)
+        kept = []
+        dx_pairs = []
+        for step, unit in enumerate(units):
+            pair, kept = expert_front(
+                step,
+                len(units),
+                [x_blocks[key] for key in unit],
+                jnp.array([2 * r + h for r, h in unit], jnp.int32),
+                dy_all,
+                routed_gate_up,
+                routed_down_pad,
+                tables,
+                kept,
+                cap,
+            )
+            dx_pairs.append(pair)
+        near, far = expert_out(kept[2], routed_down_pad, tables, cap)
         d_routed_in = plane_scatter_whole(dx_pairs, units, fsdp_count)
     routed_gate_grad, routed_up_grad, routed_down_grad = expert_grads(kept, local_hidden)
 
@@ -744,14 +1360,12 @@
     shared_part = jnp.dot(normed_ffn_all.T, d_shared, preferred_element_type=F32)
     d_shared_in = jnp.dot(d_shared, shared_weight.T, preferred_element_type=F32)
 
-    d_ffn_rows, shared_part, shared_down_part, near, far = after(
-        (
-            d_shared_in + d_routed_in,
-            shared_part.astype(BF),
-            shared_down_part.astype(BF),
-            near,
-            far,
-        )
+    d_ffn_rows, shared_part, shared_down_part, near, far = tie(
+        d_shared_in + d_routed_in,
+        shared_part.astype(BF),
+        shared_down_part.astype(BF),
+        near,
+        far,
     )
     d_normed_ffn = column_scatter(d_ffn_rows)
     out_pairs = [(near[step], far[step]) for step in range(len(units))]
@@ -762,11 +1376,12 @@
         routed_rows = plane_scatter(out_chip)
     else:
         routed_rows = plane_scatter_whole(out_pairs, units, fsdp_count)
+    ffn_gain_part, d_mixed_norm = norm_back(d_normed_ffn, unit_two, inverse_two, gain_ffn)
+    d_mixed = out_cotan.astype(F32) + d_mixed_norm
+    d_proj_all, routed_rows = tie(column_gather(d_mixed.astype(BF)), routed_rows)
+
     ffn_rows = column_scatter(shared_rows + routed_rows)
     block_out = (mixed_rows + ffn_rows).astype(BF)
-    ffn_gain_part, d_mixed_norm = norm_back(d_normed_ffn, unit_two, inverse_two, gain_ffn)
-    d_mixed = out_cotan.astype(F32) + d_mixed_norm
-    d_proj_all = after(column_gather(d_mixed.astype(BF)), routed_rows)
 
     out_part = jnp.dot(attended.T, d_proj_all, preferred_element_type=F32)
     d_attended = (
@@ -823,18 +1438,22 @@
             part.astype(BF), "fsdp", scatter_dimension=dimension, tiled=True
         )
 
+    shared_down_grad = scatter(shared_down_part, 1)
+    shared_part, shared_down_grad = tie(shared_part, shared_down_grad)
+    shared_grad = scatter(shared_part, 0)
+    out_part, shared_grad = tie(out_part.astype(BF), shared_grad)
+    out_proj_grad = scatter(out_part, 1)
     lift_part = latent_up_part.astype(BF).reshape(model_width, lift_cols)
-    joint_grad = scatter(
-        jnp.concatenate(
-            [
-                joint_part.astype(BF),
-                jnp.zeros((model_width, (-joint) % 128), BF),
-                lift_part,
-            ],
-            axis=1,
-        ),
-        0,
-    )
+    joint_sum = jnp.concatenate(
+        [
+            joint_part.astype(BF),
+            jnp.zeros((model_width, (-joint) % 128), BF),
+            lift_part,
+        ],
+        axis=1,
+    )
+    joint_sum, out_proj_grad = tie(joint_sum, out_proj_grad)
+    joint_grad = scatter(joint_sum, 0)
     query_proj_grad = joint_grad[:, :query_cols].astype(F32)
     latent_grad = joint_grad[:, query_cols:joint].reshape(tp_count, -1, latent_cols)
     latent_proj_grad = column_scatter(
@@ -843,10 +1462,10 @@
     latent_up_grad = (
         joint_grad[:, joint_grad.shape[1] - lift_cols :].reshape(latent_up.shape).astype(F32)
     )
-    out_proj_grad = scatter(out_part, 1).astype(F32)
-    shared_grad = scatter(shared_part, 0).astype(F32)
+    out_proj_grad = out_proj_grad.astype(F32)
+    shared_grad = shared_grad.astype(F32)
     shared_gate_grad, shared_up_grad = shared_grad[:, :shared_cols], shared_grad[:, shared_cols:]
-    shared_down_grad = scatter(shared_down_part, 1).astype(F32)
+    shared_down_grad = shared_down_grad.astype(F32)
     gain_sums = sum_everywhere(
         jnp.concatenate([attn_gain_part, latent_gain_part, ffn_gain_part]).reshape(-1, 128)
     ).reshape(-1)

time: 916 us -> 875 us (0.955)
  Pallas kernels: 150 us -> 341 us
  waiting for transfers between devices: 406 us -> 228 us
  local copies, waits for them, and re-layouts: 102 us -> 73.2 us
  other arithmetic: 77.4 us -> 57 us
  starting transfers between devices: 82.3 us -> 72.3 us
    pallas_call x5 -> x2, Pallas kernels: 117 us -> 308 us  [the longest x1 262 us: expert_call(): pl.pallas_call(functools.partial(expert_kernel, experts, cap, columns, si...]
    ppermute x12 -> x6, waiting for transfers between devices: 132 us -> 8.39 us  [column_gather(): lax.ppermute(rows, 'tp', [((i + s) % count, i) for i in range(count)])]
    all_gather x4 -> x3, waiting for transfers between devices: 67.4 us -> 0.04 us  [the longest x1 0.02 us: per_device(): out_weight = lax.all_gather(out_proj, 'fsdp', axis=1, tiled=True)]
    ppermute x50 -> x18, waiting for transfers between devices: 85.6 us -> 143 us  [swap(): return lax.ppermute(values, axis_name, [(i, i ^ bit) for i in range(count)])]
    ppermute x15 -> x12, waiting for transfers between devices: 103 us -> 56.7 us  [column_scatter(): lax.ppermute(piece, 'tp', [(i, (i + s) % count) for i in range(count)])]
    ppermute x50 -> x18, starting transfers between devices: 31.2 us -> 12.6 us  [swap(): return lax.ppermute(values, axis_name, [(i, i ^ bit) for i in range(count)])]
    convert_element_type x9 -> x5, other arithmetic: 19.6 us -> 2.8 us  [the longest x1 0.91 us: per_device(): shared_down_grad = shared_down_grad.astype(F32)]
    unnamed x242 -> x175, local copies, waits for them, and re-layouts: 26.8 us -> 18.4 us
  transfers between devices with their start and end apart: 85 -> 43, of which waited for: 32 -> 19; matrix products, arithmetic and copies ran while one was open for 24% -> 20% of each run, Pallas kernels for 16% -> 39%
where the time goes in v3:
time: 875 us; the launch traced here: 867 us
  Pallas kernels  341 us (39%)
  waiting for transfers between devices  228 us (26%)
  matrix products  79.2 us (9%)
  local copies, waits for them, and re-layouts  73.2 us (8%)
  starting transfers between devices  72.3 us (8%)
  other arithmetic  57 us (7%)
  between operations  16.2 us (2%)
    pallas_call x1, Pallas kernels, expert_call(): pl.pallas_call(functools.partial(expert_kernel, experts, cap, columns, si...  262 us
    ppermute x18, waiting for transfers between devices, swap(): return lax.ppermute(values, axis_name, [(i, i ^ bit) for i in range(count)])  143 us
    ppermute x12, waiting for transfers between devices, column_scatter(): lax.ppermute(piece, 'tp', [(i, (i + s) % count) for i in range(count)])  56.7 us
    pallas_call x1, Pallas kernels, first_call(): pl.pallas_call(functools.partial(first_kernel, columns, size), out_shape=...  45.7 us
    ppermute x6, starting transfers between devices, column_gather(): lax.ppermute(rows, 'tp', [((i + s) % count, i) for i in range(count)])  34.2 us
    pallas_call x1, Pallas kernels, expert_grads(): pl.pallas_call(expert_grads_kernel, grid=(experts, steps), out_shape=[gra...  33.4 us
    ppermute x12, starting transfers between devices, column_scatter(): lax.ppermute(piece, 'tp', [(i, (i + s) % count) for i in range(count)])  25.2 us
    reduce_scatter x4, waiting for transfers between devices, scatter(): lax.psum_scatter(part.astype(BF), 'fsdp', scatter_dimension=dimension, ti...  19 us
  transfers between devices with their start and end apart: 43, of which 19 were waited for; matrix products, arithmetic and copies ran while one was open for 20% of the time, Pallas kernels for 39%

profile of v3, /device:TPU:0, one launch (start us, length us, event | category | flops | bytes accessed | tf_op | source)
XLA Modules:
  0.0 867.0 jit_solution(3823051622907910363)
XLA Ops:
  12.0 45.7 %first_gather.1 = (bf16[512,2048]{1,0:T(8,128)(2,1)}, bf16[8,256,1664]{2,1,0:T(8,128)(2,1)}) custom-call(bf16[128,2048]{1,0:T(8,128)(2,1)} %refs_1_.1, bf16[256,1664]{1,0:T(8,128)(2,1)} %concatenate.82.refs_1_), custom_call_target="tpu_custom_call" | custom-call | tf_op jit(solution)/shard_map/first_gather/pallas_call | solution.py:1050
  57.7 8.2 collective-permute-start
  70.0 3.1 slice_convert_fusion.2
  73.5 2.5 fusion.12
  76.4 6.0 fusion.6
  86.4 2.7 reshape.497
  99.8 5.9 fusion.3.refs_3_
  112.2 3.3 collective-permute-done.4
  119.0 3.9 pad.17.refs_4_
  124.2 5.0 collective-permute-done.5
  138.3 4.9 convolution_convert_fusion.4.refs_0_
  143.2 261.8 %experts.1 = (f32[128,2048]{1,0:T(8,128)}, bf16[512,2048]{1,0:T(8,128)(2,1)}, bf16[512,2048]{1,0:T(8,128)(2,1)}, bf16[4,4,256,2048]{3,2,1,0:T(8,128)(2,1)}, bf16...) custom-call(bf16[512,2048]{1,0:T(8,128)(2,1)} %convolution_convert_f, ...), custom_call_target="tpu_custom_call" | custom-call | flops 55834574848 | bytes 62914560 | tf_op jit(solution)/shard_map/experts/pallas_call | solution.py:912
  405.0 12.2 %fusion.111 = (bf16[4,2,256,2048]{3,2,1,0:T(8,128)(2,1)}, bf16[4,2,256,2048]{3,2,1,0:T(8,128)(2,1)}) fusion(bf16[4,4,256,2048]{3,2,1,0:T(8,128)(2,1)} %get-tuple-element.50), kind=kLoop, calls=%fused_computation.312 | loop fusion | bytes 33554432 | tf_op jit(solution)/shard_map/slice | solution.py:1326
  417.3 8.4 fusion.120
  425.7 5.8 multiply_convert_fusion.2
  432.4 3.3 convolution_convert_fusion.2
  435.7 7.9 convolution_convert_fusion.1
  443.6 5.7 fusion.47
  449.3 2.7 convert_add_fusion
  452.0 6.6 slice_bitcast_fusion
  459.8 13.2 %collective-permute-start.6 = (bf16[128,2048]{1,0:T(8,128)(2,1)S(1)}, bf16[128,2048]{1,0:T(8,128)(2,1)S(1)}, u32[]{:S(2)}, u32[]{:S(2)}) collective-permute-start(bf16[128,2048]{1,0:T(8,128)(2,1)S(1)} %get-tuple-element.199), channel_id=1, source_target_pairs={{0,1},{1,2},{2,3},{3,0},{4,5},{5,6},{6,7},{7,4},{8,9},{9,10},{10,1... | collective-permute-start | bytes 1572872 | tf_op jit(solution)/shard_map/ppermute | solution.py:117
  473.0 2.4 collective-permute-start.8
  475.7 9.6 %collective-permute-done.6 = bf16[128,2048]{1,0:T(8,128)(2,1)S(1)} collective-permute-done((bf16[128,2048]{1,0:T(8,128)(2,1)S(1)}, bf16[128,2048]{1,0:T(8,128)(2,1)S(1)}, u32[]{:S(2)}, u32[]{:S(2)}) %collective-permute-start.6) | collective-permute-done | bytes 524320 | tf_op jit(solution)/shard_map/ppermute | solution.py:117
  485.3 13.7 %collective-permute-done.7 = bf16[128,2048]{1,0:T(8,128)(2,1)S(1)} collective-permute-done((bf16[128,2048]{1,0:T(8,128)(2,1)S(1)}, bf16[128,2048]{1,0:T(8,128)(2,1)S(1)}, u32[]{:S(2)}, u32[]{:S(2)}) %collective-permute-start.7) | collective-permute-done | bytes 524320 | tf_op jit(solution)/shard_map/ppermute | solution.py:117
  499.0 7.7 collective-permute-done.8
  509.5 2.5 collective-permute-start.10
  512.0 22.8 %collective-permute-start.11 = (bf16[128,2048]{1,0:T(8,128)(2,1)S(1)}, bf16[128,2048]{1,0:T(8,128)(2,1)S(1)}, u32[]{:S(2)}, u32[]{:S(2)}) collective-permute-start(bf16[128,2048]{1,0:T(8,128)(2,1)S(1)} %fusion.108), channel_id=1, source_target_pairs={{3,0},{0,1},{1,2},{2,3},{7,4},{4,5},{5,6},{6,7},{11,8},{8,9},{9,10... | collective-permute-start | bytes 1572872 | tf_op jit(solution)/shard_map/ppermute | solution.py:107
  534.8 3.2 convert_add_fusion.2
  540.9 4.8 convert_add_fusion.4
  546.8 27.0 %collective-permute-done.20 = bf16[512,1024]{1,0:T(8,128)(2,1)S(1)} collective-permute-done((bf16[512,1024]{1,0:T(8,128)(2,1)S(1)}, bf16[512,1024]{1,0:T(8,128)(2,1)S(1)}, u32[]{:S(2)}, u32[]{:S(2)}) %collective-permute-start.20) | collective-permute-done | bytes 1048608 | tf_op jit(solution)/shard_map/ppermute | solution.py:96
  575.4 2.5 collective-permute-start.21
  579.2 8.4 collective-permute-done.9
  589.0 20.7 %collective-permute-done.19 = bf16[512,1024]{1,0:T(8,128)(2,1)S(1)} collective-permute-done((bf16[512,1024]{1,0:T(8,128)(2,1)S(1)}, bf16[512,1024]{1,0:T(8,128)(2,1)S(1)}, u32[]{:S(2)}, u32[]{:S(2)}) %collective-permute-start.19) | collective-permute-done | bytes 1048608 | tf_op jit(solution)/shard_map/ppermute | solution.py:96
  610.9 21.2 %collective-permute-done.21 = bf16[512,1024]{1,0:T(8,128)(2,1)S(1)} collective-permute-done((bf16[512,1024]{1,0:T(8,128)(2,1)S(1)}, bf16[512,1024]{1,0:T(8,128)(2,1)S(1)}, u32[]{:S(2)}, u32[]{:S(2)}) %collective-permute-start.21) | collective-permute-done | bytes 1048608 | tf_op jit(solution)/shard_map/ppermute | solution.py:96
  645.2 3.0 convolution_convert_fusion.5
  648.2 2.5 reshape.507
  654.1 4.3 convolution_convert_fusion.3
  665.6 7.6 convolution_convert_fusion
  673.2 6.8 pad_maximum_fusion
  679.9 17.1 %reduce-scatter.9.cloned.1.call-done = bf16[512,256]{1,0:T(8,128)(2,1)} async-done(((bf16[512,2048]{1,0:T(8,128)(2,1)}), bf16[512,256]{1,0:T(8,128)(2,1)}) %reduce-scatter.9.cloned.1.call-update) | async-done | bytes 262160 | tf_op jit(solution)/shard_map/reduce_scatter | solution.py:1437
  697.3 7.5 fusion.11
  705.0 33.4 %expert_grads.1 = (f32[2,352,2048]{2,1,0:T(8,128)}, f32[2,352,2048]{2,1,0:T(8,128)}, f32[2,352,2048]{2,1,0:T(8,128)}) custom-call(bf16[4,2,512,768]{3,2,1,0:T(8,128)(2,1)} %get-tuple-element.64.dgu, bf16[4,2,512,2048]{3,2,1,0:T(8,128)(2,1)} %get-tuple-element.65.x, bf16[4,2,512,384]{3,2,1,0:T(8,128)(2,1)S(1)} %copy-done, ...), custom_call_target="tpu_custom_call" | custom-call | flops 19327352832 | bytes 60293120 | tf_op jit(solution)/shard_map/expert_grads/pallas_call | solution.py:410
  739.7 3.8 fusion.121
  745.8 2.4 collective-permute-start.26
  752.0 30.7 %collective-permute-done.31 = f32[36,128]{1,0:T(8,128)S(1)} collective-permute-done((f32[36,128]{1,0:T(8,128)S(1)}, f32[36,128]{1,0:T(8,128)S(1)}, u32[]{:S(2)}, u32[]{:S(2)}) %collective-permute-start.31) | collective-permute-done | bytes 18464 | tf_op jit(solution)/shard_map/ppermute | solution.py:96
  783.6 33.3 %collective-permute-done.32 = f32[36,128]{1,0:T(8,128)S(1)} collective-permute-done((f32[36,128]{1,0:T(8,128)S(1)}, f32[36,128]{1,0:T(8,128)S(1)}, u32[]{:S(2)}, u32[]{:S(2)}) %collective-permute-start.32) | collective-permute-done | bytes 18464 | tf_op jit(solution)/shard_map/ppermute | solution.py:96
  819.6 13.1 %collective-permute-done.23 = bf16[128,2048]{1,0:T(8,128)(2,1)S(1)} collective-permute-done((bf16[128,2048]{1,0:T(8,128)(2,1)S(1)}, bf16[128,2048]{1,0:T(8,128)(2,1)S(1)}, u32[]{:S(2)}, u32[]{:S(2)}) %collective-permute-start.23) | collective-permute-done | bytes 524320 | tf_op jit(solution)/shard_map/ppermute | solution.py:117
  832.6 9.4 %collective-permute-done.24 = bf16[128,2048]{1,0:T(8,128)(2,1)S(1)} collective-permute-done((bf16[128,2048]{1,0:T(8,128)(2,1)S(1)}, bf16[128,2048]{1,0:T(8,128)(2,1)S(1)}, u32[]{:S(2)}, u32[]{:S(2)}) %collective-permute-start.24) | collective-permute-done | bytes 524320 | tf_op jit(solution)/shard_map/ppermute | solution.py:117
  (399 shorter events, 110.4 us)
Async XLA Ops:
  7.2 131.0 %all-gather.4.cloned.1.call-start = ((), (), s32[]{:S(2)}) async-start(), calls=%async_computation.4 | async-start | bytes 2359296 | tf_op jit(solution)/shard_map/all_gather | solution.py:1247
  8.0 409.3 %all-gather.6.cloned.1.call-start = ((), (), s32[]{:S(2)}) async-start(), calls=%async_computation.5 | async-start | bytes 6488064 | tf_op jit(solution)/shard_map/all_gather | solution.py:1250
  10.0 47.6 %copy-start.6 = (bf16[128,2048]{1,0:T(8,128)(2,1)S(1)}, bf16[128,2048]{1,0:T(8,128)(2,1)}, u32[]{:S(2)}) copy-start(bf16[128,2048]{1,0:T(8,128)(2,1)} %param.19) | copy-start | bytes 1572868
  10.1 415.7 %all-gather.8.cloned.1.call-start = ((), (), s32[]{:S(2)}) async-start(), calls=%async_computation.6 | async-start | bytes 3244032 | tf_op jit(solution)/shard_map/all_gather | solution.py:1253
  10.3 56.2 %copy-start.13 = (s32[512,6]{0,1:T(8,128)S(1)}, s32[512,6]{0,1:T(8,128)}, u32[]{:S(2)}) copy-start(s32[512,6]{0,1:T(8,128)} %param.21) | copy-start | bytes 36868
  10.8 57.2 %copy-start.14 = (f32[512,6]{0,1:T(8,128)S(1)}, f32[512,6]{0,1:T(8,128)}, u32[]{:S(2)}) copy-start(f32[512,6]{0,1:T(8,128)} %param.22) | copy-start | bytes 36868
  57.7 77.3 %collective-permute-start = (bf16[128,2048]{1,0:T(8,128)(2,1)S(1)}, bf16[128,2048]{1,0:T(8,128)(2,1)}, u32[]{:S(2)}, u32[]{:S(2)}) collective-permute-start(bf16[128,2048]{1,0:T(8,128)(2,1)S(1)} %copy-done.6), channel_id=1, source_target_pairs={{1,0},{2,1},{3,2},{0,3},{5,4},{6,5},{7,6},{4,7},{9,8},{10,9},{11,1... | collective-permute-start | bytes 1572872 | tf_op jit(solution)/shard_map/ppermute | solution.py:107
  65.9 70.2 %collective-permute-start.1 = (bf16[128,2048]{1,0:T(8,128)(2,1)S(1)}, bf16[128,2048]{1,0:T(8,128)(2,1)}, u32[]{:S(2)}, u32[]{:S(2)}) collective-permute-start(bf16[128,2048]{1,0:T(8,128)(2,1)S(1)} %copy-done.6), channel_id=1, source_target_pairs={{2,0},{3,1},{0,2},{1,3},{6,4},{7,5},{4,6},{5,7},{10,8},{11,9},{8,1... | collective-permute-start | bytes 1572872 | tf_op jit(solution)/shard_map/ppermute | solution.py:107
  65.9 71.3 %collective-permute-start.2 = (bf16[128,2048]{1,0:T(8,128)(2,1)S(1)}, bf16[128,2048]{1,0:T(8,128)(2,1)}, u32[]{:S(2)}, u32[]{:S(2)}) collective-permute-start(bf16[128,2048]{1,0:T(8,128)(2,1)S(1)} %copy-done.6), channel_id=1, source_target_pairs={{3,0},{0,1},{1,2},{2,3},{7,4},{4,5},{5,6},{6,7},{11,8},{8,9},{9,10... | collective-permute-start | bytes 1572872 | tf_op jit(solution)/shard_map/ppermute | solution.py:107
  69.9 39.6 %collective-permute-start.3 = (f32[32,512]{1,0:T(8,128)S(1)}, f32[32,512]{1,0:T(8,128)S(1)}, u32[]{:S(2)}, u32[]{:S(2)}) collective-permute-start(f32[32,512]{1,0:T(8,128)S(1)} %pad_maximum_fusion.23), channel_id=1, source_target_pairs={{0,4},{4,0},{8,12},{12,8},{16,20},{20,16},{24,28},{28,24},{1,5},{5... | collective-permute-start | bytes 196616 | tf_op jit(solution)/shard_map/ppermute | solution.py:96
  69.9 439.2 %reduce-scatter.5.cloned.1.call-start = ((), (), s32[]{:S(2)}) async-start(), calls=%async_computation.7 | async-start | bytes 3244032 | tf_op jit(solution)/shard_map/reduce_scatter | solution.py:1437
  109.5 6.0 collective-permute-start.4
  115.5 13.6 %collective-permute-start.5 = (f32[128,512]{1,0:T(8,128)S(1)}, f32[128,512]{1,0:T(8,128)S(1)}, u32[]{:S(2)}, u32[]{:S(2)}) collective-permute-start(f32[128,512]{1,0:T(8,128)S(1)} %pad_maximum_fusion.18), channel_id=1, source_target_pairs={{0,16},{4,20},{8,24},{12,28},{16,0},{20,4},{24,8},{28,12},{1,17},{... | collective-permute-start | bytes 786440 | tf_op jit(solution)/shard_map/ppermute | solution.py:96
  452.0 206.4 %reduce-scatter.7.cloned.1.call-start = ((), (), s32[]{:S(2)}) async-start(), calls=%async_computation.8 | async-start | bytes 6488064 | tf_op jit(solution)/shard_map/reduce_scatter | solution.py:1437
  458.6 53.4 %collective-permute-start.16 = (bf16[2,256,2048]{2,1,0:T(8,128)(2,1)}, bf16[2,256,2048]{2,1,0:T(8,128)(2,1)}, u32[]{:S(2)}, u32[]{:S(2)}) collective-permute-start(bf16[2,256,2048]{2,1,0:T(8,128)(2,1)} %get-tuple-element.175), channel_id=1, source_target_pairs={{0,4},{4,0},{8,12},{12,8},{16,20},{20,16},{24,28},{28,24},{1,5},{5... | collective-permute-start | bytes 6291464 | tf_op jit(solution)/shard_map/ppermute | solution.py:96
  459.6 47.1 %copy-start.54 = (f32[2048,1]{0,1:T(1,128)S(1)}, f32[2048,1]{0,1:T(1,128)}, u32[]{:S(2)}) copy-start(f32[2048,1]{0,1:T(1,128)} %copy.168) | copy-start | bytes 24580
  459.8 25.5 %collective-permute-start.6 = (bf16[128,2048]{1,0:T(8,128)(2,1)S(1)}, bf16[128,2048]{1,0:T(8,128)(2,1)S(1)}, u32[]{:S(2)}, u32[]{:S(2)}) collective-permute-start(bf16[128,2048]{1,0:T(8,128)(2,1)S(1)} %get-tuple-element.199), channel_id=1, source_target_pairs={{0,1},{1,2},{2,3},{3,0},{4,5},{5,6},{6,7},{7,4},{8,9},{9,10},{10,1... | collective-permute-start | bytes 1572872 | tf_op jit(solution)/shard_map/ppermute | solution.py:117
  473.0 26.1 %collective-permute-start.7 = (bf16[128,2048]{1,0:T(8,128)(2,1)S(1)}, bf16[128,2048]{1,0:T(8,128)(2,1)S(1)}, u32[]{:S(2)}, u32[]{:S(2)}) collective-permute-start(bf16[128,2048]{1,0:T(8,128)(2,1)S(1)} %get-tuple-element.201), channel_id=1, source_target_pairs={{0,2},{1,3},{2,0},{3,1},{4,6},{5,7},{6,4},{7,5},{8,10},{9,11},{10,... | collective-permute-start | bytes 1572872 | tf_op jit(solution)/shard_map/ppermute | solution.py:117
  473.0 33.7 %collective-permute-start.8 = (bf16[128,2048]{1,0:T(8,128)(2,1)S(1)}, bf16[128,2048]{1,0:T(8,128)(2,1)S(1)}, u32[]{:S(2)}, u32[]{:S(2)}) collective-permute-start(bf16[128,2048]{1,0:T(8,128)(2,1)S(1)} %get-tuple-element.200), channel_id=1, source_target_pairs={{0,3},{1,0},{2,1},{3,2},{4,7},{5,4},{6,5},{7,6},{8,11},{9,8},{10,9... | collective-permute-start | bytes 1572872 | tf_op jit(solution)/shard_map/ppermute | solution.py:117
  475.6 62.9 %collective-permute-start.12 = (bf16[2,256,2048]{2,1,0:T(8,128)(2,1)}, bf16[2,256,2048]{2,1,0:T(8,128)(2,1)}, u32[]{:S(2)}, u32[]{:S(2)}) collective-permute-start(bf16[2,256,2048]{2,1,0:T(8,128)(2,1)} %get-tuple-element.178), channel_id=1, source_target_pairs={{0,4},{4,0},{8,12},{12,8},{16,20},{20,16},{24,28},{28,24},{1,5},{5... | collective-permute-start | bytes 6291464 | tf_op jit(solution)/shard_map/ppermute | solution.py:96
  485.3 54.1 %collective-permute-start.13 = (bf16[2,256,2048]{2,1,0:T(8,128)(2,1)}, bf16[2,256,2048]{2,1,0:T(8,128)(2,1)}, u32[]{:S(2)}, u32[]{:S(2)}) collective-permute-start(bf16[2,256,2048]{2,1,0:T(8,128)(2,1)} %get-tuple-element.177), channel_id=1, source_target_pairs={{0,4},{4,0},{8,12},{12,8},{16,20},{20,16},{24,28},{28,24},{1,5},{5... | collective-permute-start | bytes 6291464 | tf_op jit(solution)/shard_map/ppermute | solution.py:96
  499.0 41.8 %collective-permute-start.14 = (bf16[2,256,2048]{2,1,0:T(8,128)(2,1)}, bf16[2,256,2048]{2,1,0:T(8,128)(2,1)}, u32[]{:S(2)}, u32[]{:S(2)}) collective-permute-start(bf16[2,256,2048]{2,1,0:T(8,128)(2,1)} %get-tuple-element.176), channel_id=1, source_target_pairs={{0,4},{4,0},{8,12},{12,8},{16,20},{20,16},{24,28},{28,24},{1,5},{5... | collective-permute-start | bytes 6291464 | tf_op jit(solution)/shard_map/ppermute | solution.py:96
  509.1 187.9 %reduce-scatter.9.cloned.1.call-start = ((), (), s32[]{:S(2)}) async-start(), calls=%async_computation.9 | async-start | bytes 2359296 | tf_op jit(solution)/shard_map/reduce_scatter | solution.py:1437
  509.5 68.7 %collective-permute-start.10 = (bf16[128,2048]{1,0:T(8,128)(2,1)S(1)}, bf16[128,2048]{1,0:T(8,128)(2,1)S(1)}, u32[]{:S(2)}, u32[]{:S(2)}) collective-permute-start(bf16[128,2048]{1,0:T(8,128)(2,1)S(1)} %fusion.108), channel_id=1, source_target_pairs={{2,0},{3,1},{0,2},{1,3},{6,4},{7,5},{4,6},{5,7},{10,8},{11,9},{8,1... | collective-permute-start | bytes 1572872 | tf_op jit(solution)/shard_map/ppermute | solution.py:107
  512.0 66.3 %collective-permute-start.11 = (bf16[128,2048]{1,0:T(8,128)(2,1)S(1)}, bf16[128,2048]{1,0:T(8,128)(2,1)S(1)}, u32[]{:S(2)}, u32[]{:S(2)}) collective-permute-start(bf16[128,2048]{1,0:T(8,128)(2,1)S(1)} %fusion.108), channel_id=1, source_target_pairs={{3,0},{0,1},{1,2},{2,3},{7,4},{4,5},{5,6},{6,7},{11,8},{8,9},{9,10... | collective-permute-start | bytes 1572872 | tf_op jit(solution)/shard_map/ppermute | solution.py:107
  538.5 35.4 %collective-permute-start.20 = (bf16[512,1024]{1,0:T(8,128)(2,1)S(1)}, bf16[512,1024]{1,0:T(8,128)(2,1)S(1)}, u32[]{:S(2)}, u32[]{:S(2)}) collective-permute-start(bf16[512,1024]{1,0:T(8,128)(2,1)S(1)} %get-tuple-element.198), channel_id=1, source_target_pairs={{0,16},{4,20},{8,24},{12,28},{16,0},{20,4},{24,8},{28,12},{1,17},{... | collective-permute-start | bytes 3145736 | tf_op jit(solution)/shard_map/ppermute | solution.py:96
  539.4 35.9 %collective-permute-start.17 = (bf16[512,1024]{1,0:T(8,128)(2,1)S(1)}, bf16[512,1024]{1,0:T(8,128)(2,1)S(1)}, u32[]{:S(2)}, u32[]{:S(2)}) collective-permute-start(bf16[512,1024]{1,0:T(8,128)(2,1)S(1)} %get-tuple-element.197), channel_id=1, source_target_pairs={{0,8},{4,12},{8,0},{12,4},{16,24},{20,28},{24,16},{28,20},{1,9},{5... | collective-permute-start | bytes 3145736 | tf_op jit(solution)/shard_map/ppermute | solution.py:96
  545.8 63.8 %collective-permute-start.19 = (bf16[512,1024]{1,0:T(8,128)(2,1)S(1)}, bf16[512,1024]{1,0:T(8,128)(2,1)S(1)}, u32[]{:S(2)}, u32[]{:S(2)}) collective-permute-start(bf16[512,1024]{1,0:T(8,128)(2,1)S(1)} %fusion.24), channel_id=1, source_target_pairs={{0,16},{4,20},{8,24},{12,28},{16,0},{20,4},{24,8},{28,12},{1,17},{... | collective-permute-start | bytes 3145736 | tf_op jit(solution)/shard_map/ppermute | solution.py:96
  573.8 37.1 %collective-permute-start.15 = (bf16[512,1024]{1,0:T(8,128)(2,1)S(1)}, bf16[512,1024]{1,0:T(8,128)(2,1)S(1)}, u32[]{:S(2)}, u32[]{:S(2)}) collective-permute-start(bf16[512,1024]{1,0:T(8,128)(2,1)S(1)} %fusion.18), channel_id=1, source_target_pairs={{0,8},{4,12},{8,0},{12,4},{16,24},{20,28},{24,16},{28,20},{1,9},{5... | collective-permute-start | bytes 3145736 | tf_op jit(solution)/shard_map/ppermute | solution.py:96
  575.4 56.8 %collective-permute-start.21 = (bf16[512,1024]{1,0:T(8,128)(2,1)S(1)}, bf16[512,1024]{1,0:T(8,128)(2,1)S(1)}, u32[]{:S(2)}, u32[]{:S(2)}) collective-permute-start(bf16[512,1024]{1,0:T(8,128)(2,1)S(1)} %fusion.23), channel_id=1, source_target_pairs={{0,8},{4,12},{8,0},{12,4},{16,24},{20,28},{24,16},{28,20},{1,9},{5... | collective-permute-start | bytes 3145736 | tf_op jit(solution)/shard_map/ppermute | solution.py:96
  578.3 53.9 %collective-permute-start.18 = (bf16[512,1024]{1,0:T(8,128)(2,1)S(1)}, bf16[512,1024]{1,0:T(8,128)(2,1)S(1)}, u32[]{:S(2)}, u32[]{:S(2)}) collective-permute-start(bf16[512,1024]{1,0:T(8,128)(2,1)S(1)} %fusion.16), channel_id=1, source_target_pairs={{0,16},{4,20},{8,24},{12,28},{16,0},{20,4},{24,8},{28,12},{1,17},{... | collective-permute-start | bytes 3145736 | tf_op jit(solution)/shard_map/ppermute | solution.py:96
  578.4 9.2 %collective-permute-start.9 = (bf16[128,2048]{1,0:T(8,128)(2,1)S(1)}, bf16[128,2048]{1,0:T(8,128)(2,1)S(1)}, u32[]{:S(2)}, u32[]{:S(2)}) collective-permute-start(bf16[128,2048]{1,0:T(8,128)(2,1)S(1)} %fusion.108), channel_id=1, source_target_pairs={{1,0},{2,1},{3,2},{0,3},{5,4},{6,5},{7,6},{4,7},{9,8},{10,9},{11,1... | collective-permute-start | bytes 1572872 | tf_op jit(solution)/shard_map/ppermute | solution.py:107
  658.4 189.2 %reduce-scatter.11.cloned.1.call-start = ((), (), s32[]{:S(2)}) async-start(), calls=%async_computation.10 | async-start | bytes 7667712 | tf_op jit(solution)/shard_map/reduce_scatter | solution.py:1437
  704.9 33.5 %collective-permute-start.28 = (f32[36,128]{1,0:T(8,128)S(1)}, f32[36,128]{1,0:T(8,128)S(1)}, u32[]{:S(2)}, u32[]{:S(2)}) collective-permute-start(f32[36,128]{1,0:T(8,128)S(1)} %maximum_bitcast_fusion), channel_id=1, source_target_pairs={{0,4},{4,0},{8,12},{12,8},{16,20},{20,16},{24,28},{28,24},{1,5},{5... | collective-permute-start | bytes 55304 | tf_op jit(solution)/shard_map/ppermute | solution.py:96
  738.3 5.2 collective-permute-start.29
  743.5 6.3 collective-permute-start.30
  744.2 72.7 %collective-permute-start.25 = (bf16[128,2048]{1,0:T(8,128)(2,1)S(1)}, bf16[128,2048]{1,0:T(8,128)(2,1)S(1)}, u32[]{:S(2)}, u32[]{:S(2)}) collective-permute-start(bf16[128,2048]{1,0:T(8,128)(2,1)S(1)} %get-tuple-element.191), channel_id=1, source_target_pairs={{0,1},{1,2},{2,3},{3,0},{4,5},{5,6},{6,7},{7,4},{8,9},{9,10},{10,1... | collective-permute-start | bytes 1572872 | tf_op jit(solution)/shard_map/ppermute | solution.py:117
  745.8 73.3 %collective-permute-start.26 = (bf16[128,2048]{1,0:T(8,128)(2,1)S(1)}, bf16[128,2048]{1,0:T(8,128)(2,1)S(1)}, u32[]{:S(2)}, u32[]{:S(2)}) collective-permute-start(bf16[128,2048]{1,0:T(8,128)(2,1)S(1)} %get-tuple-element.193), channel_id=1, source_target_pairs={{0,2},{1,3},{2,0},{3,1},{4,6},{5,7},{6,4},{7,5},{8,10},{9,11},{10,... | collective-permute-start | bytes 1572872 | tf_op jit(solution)/shard_map/ppermute | solution.py:117
  748.2 70.9 %collective-permute-start.27 = (bf16[128,2048]{1,0:T(8,128)(2,1)S(1)}, bf16[128,2048]{1,0:T(8,128)(2,1)S(1)}, u32[]{:S(2)}, u32[]{:S(2)}) collective-permute-start(bf16[128,2048]{1,0:T(8,128)(2,1)S(1)} %get-tuple-element.192), channel_id=1, source_target_pairs={{0,3},{1,0},{2,1},{3,2},{4,7},{5,4},{6,5},{7,6},{8,11},{9,8},{10,9... | collective-permute-start | bytes 1572872 | tf_op jit(solution)/shard_map/ppermute | solution.py:117
  749.8 32.8 %collective-permute-start.31 = (f32[36,128]{1,0:T(8,128)S(1)}, f32[36,128]{1,0:T(8,128)S(1)}, u32[]{:S(2)}, u32[]{:S(2)}) collective-permute-start(f32[36,128]{1,0:T(8,128)S(1)} %add.364), channel_id=1, source_target_pairs={{0,1},{1,0},{2,3},{3,2},{4,5},{5,4},{6,7},{7,6},{8,9},{9,8},{10,11... | collective-permute-start | bytes 55304 | tf_op jit(solution)/shard_map/ppermute | solution.py:96
  751.9 66.2 %copy-start.46 = (bf16[704,256]{1,0:T(8,128)(2,1)S(1)}, bf16[704,256]{1,0:T(8,128)(2,1)}, u32[]{:S(2)}) copy-start(bf16[704,256]{1,0:T(8,128)(2,1)} %reduce-scatter.5.cloned.1.call-done) | copy-start | bytes 1081348
  782.7 34.2 %collective-permute-start.32 = (f32[36,128]{1,0:T(8,128)S(1)}, f32[36,128]{1,0:T(8,128)S(1)}, u32[]{:S(2)}, u32[]{:S(2)}) collective-permute-start(f32[36,128]{1,0:T(8,128)S(1)} %add.365), channel_id=1, source_target_pairs={{0,2},{1,3},{2,0},{3,1},{4,6},{5,7},{6,4},{7,5},{8,10},{9,11},{10,... | collective-permute-start | bytes 55304 | tf_op jit(solution)/shard_map/ppermute | solution.py:96
  783.5 36.1 %collective-permute-start.22 = (bf16[128,2048]{1,0:T(8,128)(2,1)S(1)}, bf16[128,2048]{1,0:T(8,128)(2,1)S(1)}, u32[]{:S(2)}, u32[]{:S(2)}) collective-permute-start(bf16[128,2048]{1,0:T(8,128)(2,1)S(1)} %get-tuple-element.194), channel_id=1, source_target_pairs={{0,1},{1,2},{2,3},{3,0},{4,5},{5,6},{6,7},{7,4},{8,9},{9,10},{10,1... | collective-permute-start | bytes 1572872 | tf_op jit(solution)/shard_map/ppermute | solution.py:117
  816.9 15.7 %collective-permute-start.23 = (bf16[128,2048]{1,0:T(8,128)(2,1)S(1)}, bf16[128,2048]{1,0:T(8,128)(2,1)S(1)}, u32[]{:S(2)}, u32[]{:S(2)}) collective-permute-start(bf16[128,2048]{1,0:T(8,128)(2,1)S(1)} %get-tuple-element.196), channel_id=1, source_target_pairs={{0,2},{1,3},{2,0},{3,1},{4,6},{5,7},{6,4},{7,5},{8,10},{9,11},{10,... | collective-permute-start | bytes 1572872 | tf_op jit(solution)/shard_map/ppermute | solution.py:117
  816.9 25.1 %collective-permute-start.24 = (bf16[128,2048]{1,0:T(8,128)(2,1)S(1)}, bf16[128,2048]{1,0:T(8,128)(2,1)S(1)}, u32[]{:S(2)}, u32[]{:S(2)}) collective-permute-start(bf16[128,2048]{1,0:T(8,128)(2,1)S(1)} %get-tuple-element.195), channel_id=1, source_target_pairs={{0,3},{1,0},{2,1},{3,2},{4,7},{5,4},{6,5},{7,6},{8,11},{9,8},{10,9... | collective-permute-start | bytes 1572872 | tf_op jit(solution)/shard_map/ppermute | solution.py:117
  849.8 7.3 collective-permute-start.33
  851.3 7.7 collective-permute-start.34
  852.4 6.6 collective-permute-start.35
  (77 other events, 525.6 us)
Sparse Core Ops, SparseCore 0:
  10.0 39.4 all-gather.3
  51.9 43.2 all-gather.5
  97.1 36.3 all-gather.7
  452.1 56.9 reduce-scatter.4
  513.4 98.6 reduce-scatter.6
  658.6 38.4 reduce-scatter.8
  700.9 64.5 reduce-scatter.10

commit v4 on v3

--- a/solution.py
+++ b/solution.py
@@ -1067,14 +1067,647 @@
     )(tokens, packed)
 
 
+class PlaneSum:
+    def __init__(self, source, chip, theirs, links, stage, sends, arrivals, base, local):
+        self.source, self.chip, self.theirs, self.links = source, chip, theirs, links
+        self.stage, self.sends, self.arrivals, self.base = stage, sends, arrivals, base
+        self.local = local
+        self.parts, self.rows = chip.shape[1], chip.shape[2]
+        self.partner, self.along, self.across = plane_neighbours()
+
+    def pair(self, i, h):
+        return mesh_copy(
+            self.source(2 * i + 1, h),
+            self.theirs.at[i, h],
+            self.sends,
+            self.arrivals,
+            self.base + i * self.parts + h,
+            self.partner,
+        )
+
+    def mine(self, i, h):
+        return pltpu.make_async_copy(
+            self.source(2 * i, h), self.chip.at[i, h], self.local.at[1 + i * self.parts + h]
+        )
+
+    def begin(self):
+        for i in (3, 1, 2, 0):
+            for h in range(self.parts):
+                self.pair(i, h).start()
+                self.mine(i, h).start()
+
+    def add(self, i, h, start, size, landed):
+        fetch = pltpu.make_async_copy(
+            landed, self.stage.at[pl.ds(start, size)], self.local.at[0]
+        )
+        fetch.start()
+        fetch.wait()
+        some = min(32, size)
+
+        def one(n, carry):
+            rows = pl.ds(pl.multiple_of(start + n * some, some), some)
+            self.chip[i, h, rows, :] = (
+                self.chip[i, h, rows, :].astype(F32) + self.stage[rows, :].astype(F32)
+            ).astype(BF)
+            return carry
+
+        lax.fori_loop(0, size // some, one, 0)
+
+    def on_chip(self, i):
+        for h in range(self.parts):
+            self.mine(i, h).wait()
+            self.pair(i, h).wait_recv()
+            self.add(i, h, 0, self.rows, self.theirs.at[i, h])
+
+    def link(self, stage_number, side, h):
+        first_hop, second_hop = (
+            (self.along, self.across) if side == 0 else (self.across, self.along)
+        )
+        near, far = (1, 2) if side == 0 else (2, 1)
+        i = (near, 3, far)[stage_number]
+        place = (stage_number * 2 + side) * self.parts + h
+        rows = pl.ds(side * (self.rows // 2), self.rows // 2)
+        return mesh_copy(
+            self.chip.at[i, h, rows],
+            self.links.at[place],
+            self.sends,
+            self.arrivals,
+            self.base + 4 * self.parts + place,
+            second_hop if stage_number == 2 else first_hop,
+        )
+
+    def take(self, stage_number, side, h, i):
+        self.link(stage_number, side, h).wait_recv()
+        place = (stage_number * 2 + side) * self.parts + h
+        self.add(i, h, side * (self.rows // 2), self.rows // 2, self.links.at[place])
+
+    def send_first(self):
+        self.on_chip(3)
+        self.send(1)
+        self.on_chip(1)
+        self.on_chip(2)
+        self.send(0)
+        self.on_chip(0)
+
+    def send(self, stage_number):
+        for h in range(self.parts):
+            for side in range(2):
+                self.link(stage_number, side, h).start()
+
+    def send_second(self):
+        for h in range(self.parts):
+            for side in range(2):
+                self.take(1, side, h, (2, 1)[side])
+                self.link(2, side, h).start()
+
+    def finish(self):
+        for stage_number in (0, 2):
+            for h in range(self.parts):
+                for side in range(2):
+                    self.take(stage_number, side, h, 0)
+
+    def drain(self):
+        for h in range(self.parts):
+            for i in range(4):
+                self.pair(i, h).wait_send()
+            for stage_number in range(3):
+                for side in range(2):
+                    self.link(stage_number, side, h).wait_send()
+
+
+def plane_sum_sizes(parts):
+    return 10 * parts, 1 + 4 * parts
+
+
+def plane_sum_space(parts, rows, width):
+    landing = [
+        jax.ShapeDtypeStruct((4, parts, rows, width), BF),
+        jax.ShapeDtypeStruct((6 * parts, rows // 2, width), BF),
+    ]
+    scratch = [pltpu.VMEM((4, parts, rows, width), BF), pltpu.VMEM((rows, width), BF)]
+    return landing, scratch
+
+
+def middle_kernel(columns, size, experts, steps, local_hidden, *refs):
+    (
+        d_ffn_in,
+        mixed_in,
+        cotan_in,
+        gain_ref,
+        out_all,
+        x_all,
+        d_all,
+        hid_all,
+        dgu_all,
+        d_mixed_out,
+        d_proj_all,
+        gain_out,
+        routed_out,
+        gate_grad,
+        up_grad,
+        down_grad,
+        theirs,
+        links,
+        chip,
+        stage,
+        own_v,
+        arrived_v,
+        mixed_v,
+        cotan_v,
+        proj_v,
+        xk,
+        dk,
+        hk,
+        gk,
+        totals,
+        sends,
+        arrivals,
+        local,
+        sum_local,
+        work,
+        written,
+    ) = refs
+    partner, along, across = plane_neighbours()
+    column = column_neighbours(columns)
+    greet([partner, along, across] + column)
+    plane = PlaneSum(
+        lambda r, h: out_all.at[
+            [(s, unit.index((r, h))) for s, unit in enumerate(BOX_UNITS) if (r, h) in unit][0]
+        ],
+        chip,
+        theirs,
+        links,
+        stage,
+        sends,
+        arrivals,
+        0,
+        sum_local,
+    )
+    base = plane_sum_sizes(2)[0]
+    sums = [
+        mesh_copy(
+            d_ffn_in.at[pl.ds(s * size, size)],
+            arrived_v.at[s - 1],
+            sends,
+            arrivals,
+            base + s - 1,
+            column[s - 1],
+        )
+        for s in range(1, columns)
+    ]
+    rows_out = [
+        mesh_copy(
+            d_proj_all.at[pl.ds(0, size)],
+            d_proj_all.at[pl.ds((columns - s) * size, size)],
+            sends,
+            arrivals,
+            base + columns - 1 + s - 1,
+            column[s - 1],
+        )
+        for s in range(1, columns)
+    ]
+    for copy in sums:
+        copy.start()
+    first = [
+        pltpu.make_async_copy(d_ffn_in.at[pl.ds(0, size)], own_v, local.at[0]),
+        pltpu.make_async_copy(mixed_in, mixed_v, local.at[1]),
+        pltpu.make_async_copy(cotan_in, cotan_v, local.at[2]),
+    ]
+    for copy in first:
+        copy.start()
+    plane.begin()
+
+    width = xk.shape[2]
+    pad = hk.shape[2]
+    tile = min(1024, width)
+    jobs = [(e, step) for e in range(experts) for step in range(steps)]
+
+    def fetch(k):
+        e, step = jobs[k]
+        slot = k % 2
+        return [
+            pltpu.make_async_copy(x_all.at[step, e], xk.at[slot], work.at[slot, 0]),
+            pltpu.make_async_copy(d_all.at[step, e], dk.at[slot], work.at[slot, 1]),
+            pltpu.make_async_copy(hid_all.at[step, e], hk.at[slot], work.at[slot, 2]),
+            pltpu.make_async_copy(dgu_all.at[step, e], gk.at[slot], work.at[slot, 3]),
+        ]
+
+    def write(e):
+        return [
+            pltpu.make_async_copy(
+                totals.at[e % 2, i, pl.ds(0, local_hidden)], grad.at[e], written.at[e % 2, i]
+            )
+            for i, grad in enumerate((gate_grad, up_grad, down_grad))
+        ]
+
+    def job(k):
+        e, step = jobs[k]
+        slot, place = k % 2, e % 2
+        if k + 1 < len(jobs):
+            for copy in fetch(k + 1):
+                copy.start()
+        for copy in fetch(k):
+            copy.wait()
+        if step == 0 and e > 1:
+            for copy in write(e - 2):
+                copy.wait()
+
+        def one(n, carry):
+            cols = pl.ds(pl.multiple_of(n * tile, tile), tile)
+            found = [
+                dot_first(gk[slot, :, :pad], xk[slot, :, cols]),
+                dot_first(gk[slot, :, pad:], xk[slot, :, cols]),
+                dot_first(hk[slot], dk[slot, :, cols]),
+            ]
+            for i, value in enumerate(found):
+                if step == 0:
+                    totals[place, i, :, cols] = value
+                else:
+                    totals[place, i, :, cols] += value
+            return carry
+
+        lax.fori_loop(0, width // tile, one, 0)
+        if step == steps - 1:
+            for copy in write(e):
+                copy.start()
+
+    for copy in fetch(0):
+        copy.start()
+    early = len(jobs) // 2
+    late = 3 * len(jobs) // 4
+    for k in range(early):
+        job(k)
+    plane.send_first()
+    for k in range(early, late):
+        job(k)
+
+    for copy in first:
+        copy.wait()
+    total = own_v[...].astype(F32)
+    for s in range(1, columns):
+        sums[s - 1].wait_recv()
+        total = total + arrived_v[s - 1].astype(F32)
+    mixed = mixed_v[...]
+    inverse = lax.rsqrt(jnp.mean(mixed * mixed, axis=1, keepdims=True) + EPSILON)
+    unit = mixed * inverse
+    scaled = total * gain_ref[...]
+    gain_out[...] = jnp.sum(total * unit, axis=0, keepdims=True)
+    back = inverse * (scaled - unit * jnp.mean(scaled * unit, axis=1, keepdims=True))
+    d_mixed = cotan_v[...].astype(F32) + back
+    mixed_v[...] = d_mixed
+    proj_v[...] = d_mixed.astype(BF)
+    own_copy = pltpu.make_async_copy(proj_v, d_proj_all.at[pl.ds(0, size)], local.at[0])
+    own_copy.start()
+    mixed_copy = pltpu.make_async_copy(mixed_v, d_mixed_out, local.at[1])
+    mixed_copy.start()
+    own_copy.wait()
+    for copy in rows_out:
+        copy.start()
+    for k in range(late, len(jobs)):
+        job(k)
+    plane.send_second()
+    plane.finish()
+    done = [
+        pltpu.make_async_copy(
+            chip.at[0, h], routed_out.at[pl.ds(h * HALF, HALF)], sum_local.at[1 + h]
+        )
+        for h in range(2)
+    ]
+    for copy in done:
+        copy.start()
+    for copy in rows_out:
+        copy.wait_recv()
+    for copy in done + [mixed_copy]:
+        copy.wait()
+    for e in range(max(0, experts - 2), experts):
+        for copy in write(e):
+            copy.wait()
+    plane.drain()
+    for copy in sums + rows_out:
+        copy.wait_send()
+
+
+def middle_call(d_ffn, mixed, cotan, gain, out_all, kept, local_hidden):
+    columns = lax.axis_size("tp")
+    size, width = cotan.shape
+    x_all, d_all, hid_all, dgu_all = kept
+    steps, experts, slots, pad = hid_all.shape
+    anywhere = pl.BlockSpec(memory_space=pl.ANY)
+    held = pl.BlockSpec(memory_space=pltpu.VMEM)
+    landing, scratch = plane_sum_space(2, HALF, width)
+    remote, near = plane_sum_sizes(2)
+    remote = remote + 2 * (columns - 1)
+    grad = jax.ShapeDtypeStruct((experts, local_hidden, width), F32)
+    results = pl.pallas_call(
+        functools.partial(middle_kernel, columns, size, experts, steps, local_hidden),
+        out_shape=[
+            jax.ShapeDtypeStruct((size, width), F32),
+            jax.ShapeDtypeStruct((SEQ, width), BF),
+            jax.ShapeDtypeStruct((1, width), F32),
+            jax.ShapeDtypeStruct((SEQ, width), BF),
+            grad,
+            grad,
+            grad,
+        ]
+        + landing,
+        in_specs=[anywhere] * 3 + [held] + [anywhere] * 5,
+        out_specs=[anywhere] * 2 + [held] + [anywhere] * 6,
+        scratch_shapes=scratch
+        + [
+            pltpu.VMEM((size, width), BF),
+            pltpu.VMEM((columns - 1, size, width), BF),
+            pltpu.VMEM((size, width), F32),
+            pltpu.VMEM((size, width), BF),
+            pltpu.VMEM((size, width), BF),
+            pltpu.VMEM((2, slots, width), BF),
+            pltpu.VMEM((2, slots, width), BF),
+            pltpu.VMEM((2, slots, pad), BF),
+            pltpu.VMEM((2, slots, 2 * pad), BF),
+            pltpu.VMEM((2, 3, pad, width), F32),
+            pltpu.SemaphoreType.DMA((remote,)),
+            pltpu.SemaphoreType.DMA((remote,)),
+            pltpu.SemaphoreType.DMA((3,)),
+            pltpu.SemaphoreType.DMA((near,)),
+            pltpu.SemaphoreType.DMA((2, 4)),
+            pltpu.SemaphoreType.DMA((2, 3)),
+        ],
+        compiler_params=pltpu.CompilerParams(
+            collective_id=3, has_side_effects=True, vmem_limit_bytes=67_043_328
+        ),
+        cost_estimate=pl.CostEstimate(
+            flops=2 * 3 * steps * experts * slots * width * pad,
+            bytes_accessed=40 * SEQ * width,
+            transcendentals=0,
+        ),
+        name="middle",
+    )(d_ffn, mixed, cotan, gain, out_all, x_all, d_all, hid_all, dgu_all)
+    return results[:7]
+
+
+def last_kernel(columns, size, latent_start, latent_width, *refs):
+    (
+        d_normed_in,
+        tokens_in,
+        d_mixed_in,
+        gain_ref,
+        joint_in,
+        up_in,
+        out_in,
+        sums_in,
+        grad_out,
+        joint_out,
+        up_out,
+        out_out,
+        latent_out,
+        sums_out,
+        joint_theirs,
+        joint_links,
+        up_theirs,
+        up_links,
+        out_theirs,
+        out_links,
+        joint_chip,
+        joint_stage,
+        up_chip,
+        up_stage,
+        out_chip,
+        out_stage,
+        own_v,
+        arrived_v,
+        tokens_v,
+        mixed_v,
+        running,
+        sums_v,
+        latent_v,
+        sends,
+        arrivals,
+        local,
+        joint_local,
+        up_local,
+        out_local,
+    ) = refs
+    partner, along, across = plane_neighbours()
+    column = column_neighbours(columns)
+    place, row = lax.axis_index("fsdp"), lax.axis_index("tp")
+    core, right, above = place % 2, (place // 2) % 2, place // 4
+
+    def absolute(r):
+        return (
+            (above + r // 4) % 2 * 4 + (right + r // 2 % 2) % 2 * 2 + (core + r % 2) % 2
+        )
+
+    greet([partner, along, across] + column)
+    each = plane_sum_sizes(1)[0]
+    joint_rows, up_rows = joint_chip.shape[2], up_chip.shape[2]
+    out_cols = out_chip.shape[3]
+
+    def by_rows(ref, count):
+        return lambda r, h: ref.at[pl.ds(pl.multiple_of(absolute(r) * count, count), count)]
+
+    joint = PlaneSum(
+        by_rows(joint_in, joint_rows),
+        joint_chip,
+        joint_theirs,
+        joint_links,
+        joint_stage,
+        sends,
+        arrivals,
+        0,
+        joint_local,
+    )
+    up = PlaneSum(
+        by_rows(up_in, up_rows),
+        up_chip,
+        up_theirs,
+        up_links,
+        up_stage,
+        sends,
+        arrivals,
+        each,
+        up_local,
+    )
+    out = PlaneSum(
+        lambda r, h: out_in.at[
+            :, pl.ds(pl.multiple_of(absolute(r) * out_cols, out_cols), out_cols)
+        ],
+        out_chip,
+        out_theirs,
+        out_links,
+        out_stage,
+        sends,
+        arrivals,
+        2 * each,
+        out_local,
+    )
+    base = 3 * each
+    sums = [
+        mesh_copy(
+            d_normed_in.at[pl.ds(s * size, size)],
+            arrived_v.at[s - 1],
+            sends,
+            arrivals,
+            base + s - 1,
+            column[s - 1],
+        )
+        for s in range(1, columns)
+    ]
+    base = base + columns - 1
+    for copy in sums:
+        copy.start()
+    first = [
+        pltpu.make_async_copy(d_normed_in.at[pl.ds(0, size)], own_v, local.at[0]),
+        pltpu.make_async_copy(tokens_in, tokens_v, local.at[1]),
+        pltpu.make_async_copy(d_mixed_in, mixed_v, local.at[2]),
+        pltpu.make_async_copy(sums_in, running.at[0], local.at[3]),
+    ]
+    for copy in first:
+        copy.start()
+    for part in (out, joint, up):
+        part.begin()
+    first[3].wait()
+
+    def small(i, device):
+        return mesh_copy(running.at[i], sums_v.at[i], sends, arrivals, base + i, device)
+
+    hops = [small(i, device) for i, device in enumerate((partner, along, across))]
+    for i, copy in enumerate(hops):
+        copy.start()
+        copy.wait_recv()
+        running[i + 1] = running[i] + sums_v[i]
+    gains = [
+        mesh_copy(running.at[3], sums_v.at[2 + s], sends, arrivals, base + 2 + s, column[s - 1])
+        for s in range(1, columns)
+    ]
+    base = base + 2 + columns
+    for copy in gains:
+        copy.start()
+    for part in (out, joint, up):
+        part.send_first()
+    for part in (out, joint, up):
+        part.send_second()
+    for part in (out, joint, up):
+        part.finish()
+
+    pieces = joint_rows // columns
+    across_columns = [
+        mesh_copy(
+            joint_chip.at[
+                0,
+                0,
+                pl.ds(pl.multiple_of((row + s) % columns * pieces, pieces), pieces),
+                pl.ds(latent_start, latent_width),
+            ],
+            latent_v.at[s - 1],
+            sends,
+            arrivals,
+            base + s - 1,
+            column[s - 1],
+        )
+        for s in range(1, columns)
+    ]
+    for copy in across_columns:
+        copy.start()
+    done = [
+        pltpu.make_async_copy(joint_chip.at[0, 0], joint_out, joint_local.at[1]),
+        pltpu.make_async_copy(up_chip.at[0, 0], up_out, up_local.at[1]),
+        pltpu.make_async_copy(out_chip.at[0, 0], out_out, out_local.at[1]),
+    ]
+    for copy in done:
+        copy.start()
+
+    for copy in first[:3]:
+        copy.wait()
+    total = own_v[...].astype(F32)
+    for s in range(1, columns):
+        sums[s - 1].wait_recv()
+        total = total + arrived_v[s - 1].astype(F32)
+    tokens = tokens_v[...].astype(F32)
+    inverse = lax.rsqrt(jnp.mean(tokens * tokens, axis=1, keepdims=True) + EPSILON)
+    unit = tokens * inverse
+    scaled = total * gain_ref[...]
+    mixed_v[...] = mixed_v[...] + inverse * (
+        scaled - unit * jnp.mean(scaled * unit, axis=1, keepdims=True)
+    )
+    grad_copy = pltpu.make_async_copy(mixed_v, grad_out, local.at[0])
+    grad_copy.start()
+    gathered = running[3]
+    for s in range(1, columns):
+        gains[s - 1].wait_recv()
+        gathered = gathered + sums_v[2 + s]
+    sums_out[...] = gathered
+    latent = joint_chip[
+        0,
+        0,
+        pl.ds(pl.multiple_of(row * pieces, pieces), pieces),
+        pl.ds(latent_start, latent_width),
+    ].astype(F32)
+    for s in range(1, columns):
+        across_columns[s - 1].wait_recv()
+        latent = latent + latent_v[s - 1].astype(F32)
+    latent_out[...] = latent
+    for copy in done + [grad_copy]:
+        copy.wait()
+    for part in (out, joint, up):
+        part.drain()
+    for copy in sums + hops + gains + across_columns:
+        copy.wait_send()
+
+
+def last_call(d_normed, tokens, d_mixed, gain, joint, up, out, sums, latent_start, latent_width):
+    columns = lax.axis_size("tp")
+    size, width = tokens.shape
+    anywhere = pl.BlockSpec(memory_space=pl.ANY)
+    held = pl.BlockSpec(memory_space=pltpu.VMEM)
+    shapes = [
+        (joint.shape[0] // 8, joint.shape[1]),
+        (up.shape[0] // 8, up.shape[1]),
+        (out.shape[0], out.shape[1] // 8),
+    ]
+    landing, scratch = [], []
+    for rows, cols in shapes:
+        one = plane_sum_space(1, rows, cols)
+        landing, scratch = landing + one[0], scratch + one[1]
+    remote, near = plane_sum_sizes(1)
+    remote = 3 * remote + 3 * (columns - 1) + 3
+    pieces = shapes[0][0] // columns
+    return pl.pallas_call(
+        functools.partial(last_kernel, columns, size, latent_start, latent_width),
+        out_shape=[jax.ShapeDtypeStruct((size, width), F32)]
+        + [jax.ShapeDtypeStruct(shape, BF) for shape in shapes]
+        + [
+            jax.ShapeDtypeStruct((pieces, latent_width), F32),
+            jax.ShapeDtypeStruct(sums.shape, F32),
+        ]
+        + landing,
+        in_specs=[anywhere] * 3 + [held] + [anywhere] * 4,
+        out_specs=[anywhere] * 4 + [held] * 2 + [anywhere] * 6,
+        scratch_shapes=scratch
+        + [
+            pltpu.VMEM((size, width), BF),
+            pltpu.VMEM((columns - 1, size, width), BF),
+            pltpu.VMEM((size, width), BF),
+            pltpu.VMEM((size, width), F32),
+            pltpu.VMEM((4,) + sums.shape, F32),
+            pltpu.VMEM((2 + columns,) + sums.shape, F32),
+            pltpu.VMEM((columns - 1, pieces, latent_width), BF),
+            pltpu.SemaphoreType.DMA((remote,)),
+            pltpu.SemaphoreType.DMA((remote,)),
+            pltpu.SemaphoreType.DMA((4,)),
+            pltpu.SemaphoreType.DMA((near,)),
+            pltpu.SemaphoreType.DMA((near,)),
+            pltpu.SemaphoreType.DMA((near,)),
+        ],
+        compiler_params=pltpu.CompilerParams(
+            collective_id=4, has_side_effects=True, vmem_limit_bytes=48 * 1024 * 1024
+        ),
+        name="last_sums",
+    )(d_normed, tokens, d_mixed, gain, joint, up, out, sums)[:6]
+
+
 def plane_units(count):
     if count == 8:
         return BOX_UNITS
     return [[(2 * i + j // 2, j % 2) for j in range(4)] for i in range(count // 2)]
-
-
-def partner(block):
-    return swap(block, "fsdp", 1)
 
 
 def plane_gather(rows, count):
@@ -1082,32 +1715,6 @@
     return {
         (r, h): gathered[r, h * HALF : (h + 1) * HALF] for r in range(count) for h in (0, 1)
     }
-
-
-def add_pairs(left, right):
-    return left.astype(F32) + right.astype(F32)
-
-
-def chip_sums(unit, pair):
-    theirs = partner(pair[1])
-    return {unit[h]: add_pairs(pair[0][h], theirs[h]) for h in (0, 1)}
-
-
-def plane_scatter(chip):
-    whole = {r: jnp.concatenate([chip[r, 0], chip[r, 1]], axis=0) for r in (0, 2, 4, 6)}
-    half = whole[0].shape[1] // 2
-    left, right = slice(None, half), slice(half, None)
-
-    def send(rows, bit):
-        return swap(rows.astype(BF), "fsdp", bit)
-
-    on_left = add_pairs(whole[4][:, left], send(whole[6][:, left], 2))
-    on_right = add_pairs(whole[2][:, right], send(whole[6][:, right], 4))
-    first = add_pairs(whole[0][:, left], send(whole[2][:, left], 2))
-    second = add_pairs(whole[0][:, right], send(whole[4][:, right], 4))
-    first = add_pairs(first, send(on_left, 4))
-    second = add_pairs(second, send(on_right, 2))
-    return jnp.concatenate([first, second], axis=1)
 
 
 def plane_scatter_whole(pairs, units, count):
@@ -1323,7 +1930,6 @@
         )
         unit_two, inverse_two = norm_parts(mixed_rows)
         d_routed_in = d_routed_in.astype(F32)
-        near, far = out_array[:, :2], out_array[:, 2:]
     else:
         mixed_rows = block_in.astype(F32) + column_scatter(attn_part)
         unit_two, inverse_two = norm_parts(mixed_rows)
@@ -1348,7 +1954,8 @@
             dx_pairs.append(pair)
         near, far = expert_out(kept[2], routed_down_pad, tables, cap)
         d_routed_in = plane_scatter_whole(dx_pairs, units, fsdp_count)
-    routed_gate_grad, routed_up_grad, routed_down_grad = expert_grads(kept, local_hidden)
+    if not paired:
+        routed_gate_grad, routed_up_grad, routed_down_grad = expert_grads(kept, local_hidden)
 
     shared_pre = jnp.dot(normed_ffn_all, shared_weight, preferred_element_type=F32)
     shared_gate_pre, shared_up_pre = shared_pre[:, :shared_cols], shared_pre[:, shared_cols:]
@@ -1360,26 +1967,32 @@
     shared_part = jnp.dot(normed_ffn_all.T, d_shared, preferred_element_type=F32)
     d_shared_in = jnp.dot(d_shared, shared_weight.T, preferred_element_type=F32)
 
-    d_ffn_rows, shared_part, shared_down_part, near, far = tie(
-        d_shared_in + d_routed_in,
-        shared_part.astype(BF),
-        shared_down_part.astype(BF),
-        near,
-        far,
-    )
-    d_normed_ffn = column_scatter(d_ffn_rows)
-    out_pairs = [(near[step], far[step]) for step in range(len(units))]
     if paired:
-        out_chip = {}
-        for unit, pair in zip(units, out_pairs):
-            out_chip.update(chip_sums(unit, pair))
-        routed_rows = plane_scatter(out_chip)
+        d_ffn_rows, shared_part, shared_down_part = tie(
+            (d_shared_in + d_routed_in).astype(BF),
+            shared_part.astype(BF),
+            shared_down_part.astype(BF),
+        )
+        (
+            d_mixed,
+            d_proj_all,
+            ffn_gain_part,
+            routed_rows,
+            routed_gate_grad,
+            routed_up_grad,
+            routed_down_grad,
+        ) = middle_call(
+            d_ffn_rows, mixed_rows, out_cotan, gain_ffn[None, :], out_array, kept, local_hidden
+        )
+        ffn_gain_part = ffn_gain_part[0]
+        routed_rows = routed_rows.astype(F32)
     else:
+        d_normed_ffn = column_scatter(d_shared_in + d_routed_in)
+        out_pairs = [(near[step], far[step]) for step in range(len(units))]
         routed_rows = plane_scatter_whole(out_pairs, units, fsdp_count)
-    ffn_gain_part, d_mixed_norm = norm_back(d_normed_ffn, unit_two, inverse_two, gain_ffn)
-    d_mixed = out_cotan.astype(F32) + d_mixed_norm
-    d_proj_all, routed_rows = tie(column_gather(d_mixed.astype(BF)), routed_rows)
-
+        ffn_gain_part, d_mixed_norm = norm_back(d_normed_ffn, unit_two, inverse_two, gain_ffn)
+        d_mixed = out_cotan.astype(F32) + d_mixed_norm
+        d_proj_all = column_gather(d_mixed.astype(BF))
     ffn_rows = column_scatter(shared_rows + routed_rows)
     block_out = (mixed_rows + ffn_rows).astype(BF)
 
@@ -1428,47 +2041,58 @@
     joint_part = jnp.dot(normed_all.T, d_joint, preferred_element_type=F32)
     d_normed_part = jnp.dot(d_joint, joint_weight.T, preferred_element_type=F32)
     attn_gain_part = jnp.sum(d_normed_part * unit_all, axis=0)
-    d_normed = column_scatter(d_normed_part)
-    unit_one, inverse_one = norm_parts(block_in.astype(F32))
-    _, d_tokens_norm = norm_back(d_normed, unit_one, inverse_one, gain_attn)
-    block_in_grad = d_mixed + d_tokens_norm
 
     def scatter(part, dimension):
-        return lax.psum_scatter(
-            part.astype(BF), "fsdp", scatter_dimension=dimension, tiled=True
-        )
-
+        return lax.psum_scatter(part.astype(BF), "fsdp", scatter_dimension=dimension, tiled=True)
+
+    gain_parts = jnp.concatenate([attn_gain_part, latent_gain_part, ffn_gain_part]).reshape(
+        -1, 128
+    )
+    joint_part = jnp.pad(joint_part.astype(BF), ((0, 0), (0, (-joint) % 128)))
     shared_down_grad = scatter(shared_down_part, 1)
-    shared_part, shared_down_grad = tie(shared_part, shared_down_grad)
     shared_grad = scatter(shared_part, 0)
-    out_part, shared_grad = tie(out_part.astype(BF), shared_grad)
-    out_proj_grad = scatter(out_part, 1)
-    lift_part = latent_up_part.astype(BF).reshape(model_width, lift_cols)
-    joint_sum = jnp.concatenate(
-        [
-            joint_part.astype(BF),
-            jnp.zeros((model_width, (-joint) % 128), BF),
-            lift_part,
-        ],
-        axis=1,
-    )
-    joint_sum, out_proj_grad = tie(joint_sum, out_proj_grad)
-    joint_grad = scatter(joint_sum, 0)
+    if paired:
+        latent_width = joint_part.shape[1] - query_cols
+        (
+            block_in_grad,
+            joint_grad,
+            latent_up_grad,
+            out_proj_grad,
+            latent_proj_grad,
+            gain_sums,
+        ) = last_call(
+            d_normed_part.astype(BF),
+            block_in,
+            d_mixed,
+            gain_attn[None, :],
+            joint_part,
+            latent_up_part.astype(BF),
+            out_part.astype(BF),
+            gain_parts,
+            query_cols,
+            latent_width,
+        )
+        latent_proj_grad = latent_proj_grad[:, :latent_cols]
+    else:
+        d_normed = column_scatter(d_normed_part)
+        unit_one, inverse_one = norm_parts(block_in.astype(F32))
+        _, d_tokens_norm = norm_back(d_normed, unit_one, inverse_one, gain_attn)
+        block_in_grad = d_mixed + d_tokens_norm
+        out_proj_grad = scatter(out_part, 1)
+        latent_up_grad = scatter(latent_up_part, 0)
+        joint_grad = scatter(joint_part, 0)
+        latent_grad = joint_grad[:, query_cols:joint].reshape(tp_count, -1, latent_cols)
+        latent_proj_grad = column_scatter(
+            jnp.take(latent_grad, places, axis=0).reshape(-1, latent_cols)
+        )
+        gain_sums = sum_everywhere(gain_parts)
+    gain_sums = gain_sums.reshape(-1)
     query_proj_grad = joint_grad[:, :query_cols].astype(F32)
-    latent_grad = joint_grad[:, query_cols:joint].reshape(tp_count, -1, latent_cols)
-    latent_proj_grad = column_scatter(
-        jnp.take(latent_grad, places, axis=0).reshape(-1, latent_cols)
-    )
-    latent_up_grad = (
-        joint_grad[:, joint_grad.shape[1] - lift_cols :].reshape(latent_up.shape).astype(F32)
-    )
+    latent_up_grad = latent_up_grad.astype(F32)
     out_proj_grad = out_proj_grad.astype(F32)
     shared_grad = shared_grad.astype(F32)
     shared_gate_grad, shared_up_grad = shared_grad[:, :shared_cols], shared_grad[:, shared_cols:]
     shared_down_grad = shared_down_grad.astype(F32)
-    gain_sums = sum_everywhere(
-        jnp.concatenate([attn_gain_part, latent_gain_part, ffn_gain_part]).reshape(-1, 128)
-    ).reshape(-1)
     device = fsdp_rank * tp_count + tp_rank
     devices = tp_count * fsdp_count
 

time: 875 us -> 727 us (0.83)
  waiting for transfers between devices: 228 us -> 9.3 us
  Pallas kernels: 341 us -> 482 us
  starting transfers between devices: 72.3 us -> 20 us
  other arithmetic: 57 us -> 38.4 us
    pallas_call x1 -> x2, Pallas kernels: 33.4 us -> 176 us  [the longest x1 117 us: middle_call(): pl.pallas_call(functools.partial(middle_kernel, columns, size, experts, s...]
    ppermute x18 -> x3, waiting for transfers between devices: 143 us -> 8.5 us  [swap(): return lax.ppermute(values, axis_name, [(i, i ^ bit) for i in range(count)])]
    ppermute x12 -> x3, waiting for transfers between devices: 56.7 us -> 0.01 us  [column_scatter(): lax.ppermute(piece, 'tp', [(i, (i + s) % count) for i in range(count)])]
    ppermute x6 -> x3, starting transfers between devices: 34.2 us -> 8.87 us  [column_gather(): lax.ppermute(rows, 'tp', [((i + s) % count, i) for i in range(count)])]
    reduce_scatter x4 -> x2, waiting for transfers between devices: 19 us -> 0.01 us  [scatter(): lax.psum_scatter(part.astype(BF), 'fsdp', scatter_dimension=dimension, ti...]
    ppermute x12 -> x3, starting transfers between devices: 25.2 us -> 7.59 us  [column_scatter(): lax.ppermute(piece, 'tp', [(i, (i + s) % count) for i in range(count)])]
    add x10 -> x0, other arithmetic: 14.9 us -> none  [the longest x3 9.18 us: add_pairs(): return left.astype(F32) + right.astype(F32)]
    unnamed x175 -> x151, local copies, waits for them, and re-layouts: 18.4 us -> 32.7 us
  transfers between devices with their start and end apart: 43 -> 14, of which waited for: 19 -> 2; matrix products, arithmetic and copies ran while one was open for 20% -> 19% of each run, Pallas kernels for 39% -> 67%
where the time goes in v4:
time: 727 us; the launch traced here: 716 us
  Pallas kernels  482 us (66%)
  matrix products  76.8 us (11%)
  local copies, waits for them, and re-layouts  73.7 us (10%)
  other arithmetic  38.4 us (5%)
  starting transfers between devices  20 us (3%)
  between operations  15.4 us (2%)
  waiting for transfers between devices  9.3 us (1%)
    pallas_call x1, Pallas kernels, expert_call(): pl.pallas_call(functools.partial(expert_kernel, experts, cap, columns, si...  261 us
    pallas_call x1, Pallas kernels, middle_call(): pl.pallas_call(functools.partial(middle_kernel, columns, size, experts, s...  117 us
    pallas_call x1, Pallas kernels, last_call(): pl.pallas_call(functools.partial(last_kernel, columns, size, latent_start...  58.4 us
    pallas_call x1, Pallas kernels, first_call(): pl.pallas_call(functools.partial(first_kernel, columns, size), out_shape=...  45.7 us
    unnamed x151, local copies, waits for them, and re-layouts  32.7 us
  transfers between devices with their start and end apart: 14, of which 2 were waited for; matrix products, arithmetic and copies ran while one was open for 19% of the time, Pallas kernels for 67%

profile of v4, /device:TPU:0, one launch (start us, length us, event | category | flops | bytes accessed | tf_op | source)
XLA Modules:
  0.0 715.7 jit_solution(2503156871180192116)
XLA Ops:
  8.0 2.0 pad_maximum_fusion.7
  12.9 45.7 %first_gather.1 = (bf16[512,2048]{1,0:T(8,128)(2,1)}, bf16[8,256,1664]{2,1,0:T(8,128)(2,1)}) custom-call(bf16[128,2048]{1,0:T(8,128)(2,1)} %refs_1_.3, bf16[256,1664]{1,0:T(8,128)(2,1)} %concatenate.61.refs_1_), custom_call_target="tpu_custom_call" | custom-call | tf_op jit(solution)/shard_map/first_gather/pallas_call | solution.py:1050
  58.6 8.2 %collective-permute-start = (bf16[128,2048]{1,0:T(8,128)(2,1)}, bf16[128,2048]{1,0:T(8,128)(2,1)}, u32[]{:S(2)}, u32[]{:S(2)}) collective-permute-start(bf16[128,2048]{1,0:T(8,128)(2,1)} %refs_2_.1), channel_id=1, source_target_pairs={{1,0},{2,1},{3,2},{0,3},{5,4},{6,5},{7,6},{4,7},{9,8},{10,9},{11,1... | collective-permute-start | bytes 1572872 | tf_op jit(solution)/shard_map/ppermute | solution.py:107
  71.5 2.9 fusion.84
  74.8 2.2 fusion.12
  77.0 6.5 fusion.6
  85.1 2.3 slice.332
  87.6 2.7 reshape.414
  90.3 2.3 copy.148
  92.5 2.2 convolution_convert_fusion.6
  95.8 2.3 slice.502
  101.6 1.9 fusion.25
  103.5 2.1 fusion.89
  106.4 6.8 fusion.3.refs_3_
  114.8 1.8 collective-permute-start.4
  117.2 5.6 collective-permute-done.4
  124.3 1.9 constant_dynamic-update-slice_fusion.3
  126.2 2.0 pad.21.refs_4_
  129.5 2.9 collective-permute-done.5
  135.7 2.0 copy.153
  142.3 4.9 convolution_convert_fusion.4.refs_0_
  147.2 260.7 %experts.1 = (f32[128,2048]{1,0:T(8,128)}, bf16[512,2048]{1,0:T(8,128)(2,1)}, bf16[512,2048]{1,0:T(8,128)(2,1)}, bf16[4,4,256,2048]{3,2,1,0:T(8,128)(2,1)}, bf16...) custom-call(bf16[512,2048]{1,0:T(8,128)(2,1)} %convolution_convert_f, ...), custom_call_target="tpu_custom_call" | custom-call | flops 55834574848 | bytes 62914560 | tf_op jit(solution)/shard_map/experts/pallas_call | solution.py:912
  407.9 8.4 %fusion.90 = f32[512,1408]{1,0:T(8,128)} fusion(bf16[512,2048]{1,0:T(8,128)(2,1)} %get-tuple-element.48, bf16[2048,1408]{0,1:T(8,128)(2,1)} %all-gather.6.cloned.1.call-done), kind=kOutput, calls=%fused_computation.238 | convolution fusion | flops 2952790016 | bytes 10747904 | tf_op jit(solution)/shard_map/dot_general | solution.py:1960
  416.4 5.8 multiply_convert_fusion.2
  423.1 3.2 convolution_convert_fusion.2
  426.3 7.9 %convolution_convert_fusion.1 = bf16[2048,1408]{1,0:T(8,128)(2,1)} fusion(bf16[512,2048]{1,0:T(8,128)(2,1)} %get-tuple-element.48, bf16[512,704]{1,0:T(8,128)(2,1)} %get-tuple-element.177, bf16[512,704]{1,0:T(8,128)(2,1)S(1)} %get-tuple-element.176), kind=kOutput, calls=%fused_computation.9 | convolution fusion | flops 2958557184 | bytes 9306112 | tf_op jit(solution)/shard_map/dot_general | solution.py:1967
  434.2 5.8 fusion.24
  440.0 2.1 add_convert_fusion.refs_0_
  442.2 117.3 %middle.1 = (f32[128,2048]{1,0:T(8,128)}, bf16[512,2048]{1,0:T(8,128)(2,1)}, f32[1,2048]{1,0:T(1,128)}, bf16[512,2048]{1,0:T(8,128)(2,1)}, f32[2,352,2048]{2,1,0...) custom-call(bf16[512,2048]{1,0:T(8,128)(2,1)} %add_convert_fusion.re, ...), custom_call_target="tpu_custom_call" | custom-call | flops 19327352832 | bytes 41943040 | tf_op jit(solution)/shard_map/middle/pallas_call | solution.py:1401
  559.5 3.7 convolution_convert_fusion.7
  563.3 2.8 multiply_reduce_fusion
  566.1 4.6 multiply_convert_fusion
  574.3 1.8 fusion.91
  576.2 2.9 fusion.82
  579.2 5.1 collective-permute-start.6
  584.4 2.4 collective-permute-start.8
  590.9 2.7 convolution_convert_fusion.3.refs_6_
  593.6 7.6 %convolution_convert_fusion = bf16[2048,1344]{0,1:T(8,128)(2,1)} fusion(bf16[512,2048]{1,0:T(8,128)(2,1)S(1)} %copy-done.21, f32[2048]{0:T(1024)S(1)} %bitcast.178, f32[512]{0:T(512)S(1)} %copy-done.53, bf16[512,32]{0,1:T(8,128)(2,1)S(1)} %get-tuple-element.193, bf16[512,32]{0,1:T(8,128)(2,1)S(1)} %get-tuple-element.192, ...), kind=kOutput, calls=%fused_computation.8 | convolution fusion | flops 2831024128 | bytes 8988672 | tf_op jit(solution)/shard_map/dot_general | solution.py:2041
  601.3 5.2 fusion.11
  606.4 1.8 convolution_convert_fusion.5.refs_5_
  608.2 8.3 %copy.163 = bf16[2048,1344]{1,0:T(8,128)(2,1)} copy(bf16[2048,1344]{0,1:T(8,128)(2,1)} %convolution_convert_fusion) | data formatting | bytes 11010048 | tf_op jit(solution)/shard_map/convert_element_type | solution.py:2051
  616.5 5.7 pad.22.refs_4_
  622.2 58.4 %last_sums.1 = (f32[128,2048]{1,0:T(8,128)S(1)}, bf16[256,1408]{1,0:T(8,128)(2,1)S(1)}, bf16[64,1024]{1,0:T(8,128)(2,1)S(1)}, bf16[512,256]{1,0:T(8,128)(2,1)S(1...) custom-call(bf16[512,2048]{1,0:T(8,128)(2,1)} %get-tuple-element.179, ...), custom_call_target="tpu_custom_call" | custom-call | tf_op jit(solution)/shard_map/last_sums/pallas_call | solution.py:1673
  684.3 2.7 fusion.21
  687.0 1.9 convert_element_type.233
  694.0 6.0 copy.196
  700.1 6.0 copy.197
  706.1 2.5 copy.198
  (277 shorter events, 45.6 us)
Async XLA Ops:
  7.2 4.4 copy-start.55
  7.2 4.5 copy-start.35
  7.2 135.0 %all-gather.4.cloned.1.call-start = ((), (), s32[]{:S(2)}) async-start(), calls=%async_computation.2 | async-start | bytes 2359296 | tf_op jit(solution)/shard_map/all_gather | solution.py:1854
  8.0 399.9 %all-gather.6.cloned.1.call-start = ((), (), s32[]{:S(2)}) async-start(), calls=%async_computation.3 | async-start | bytes 6488064 | tf_op jit(solution)/shard_map/all_gather | solution.py:1857
  10.0 57.5 %copy-start.10 = (s32[512,6]{0,1:T(8,128)S(1)}, s32[512,6]{0,1:T(8,128)}, u32[]{:S(2)}) copy-start(s32[512,6]{0,1:T(8,128)} %param.21) | copy-start | bytes 36868
  10.0 406.3 %all-gather.8.cloned.1.call-start = ((), (), s32[]{:S(2)}) async-start(), calls=%async_computation.4 | async-start | bytes 3244032 | tf_op jit(solution)/shard_map/all_gather | solution.py:1860
  11.3 57.6 %copy-start.11 = (f32[512,6]{0,1:T(8,128)S(1)}, f32[512,6]{0,1:T(8,128)}, u32[]{:S(2)}) copy-start(f32[512,6]{0,1:T(8,128)} %param.22) | copy-start | bytes 36868
  58.6 80.4 %collective-permute-start = (bf16[128,2048]{1,0:T(8,128)(2,1)}, bf16[128,2048]{1,0:T(8,128)(2,1)}, u32[]{:S(2)}, u32[]{:S(2)}) collective-permute-start(bf16[128,2048]{1,0:T(8,128)(2,1)} %refs_2_.1), channel_id=1, source_target_pairs={{1,0},{2,1},{3,2},{0,3},{5,4},{6,5},{7,6},{4,7},{9,8},{10,9},{11,1... | collective-permute-start | bytes 1572872 | tf_op jit(solution)/shard_map/ppermute | solution.py:107
  66.8 73.2 %collective-permute-start.1 = (bf16[128,2048]{1,0:T(8,128)(2,1)}, bf16[128,2048]{1,0:T(8,128)(2,1)}, u32[]{:S(2)}, u32[]{:S(2)}) collective-permute-start(bf16[128,2048]{1,0:T(8,128)(2,1)} %refs_2_.1), channel_id=1, source_target_pairs={{2,0},{3,1},{0,2},{1,3},{6,4},{7,5},{4,6},{5,7},{10,8},{11,9},{8,1... | collective-permute-start | bytes 1572872 | tf_op jit(solution)/shard_map/ppermute | solution.py:107
  66.8 74.3 %collective-permute-start.2 = (bf16[128,2048]{1,0:T(8,128)(2,1)}, bf16[128,2048]{1,0:T(8,128)(2,1)}, u32[]{:S(2)}, u32[]{:S(2)}) collective-permute-start(bf16[128,2048]{1,0:T(8,128)(2,1)} %refs_2_.1), channel_id=1, source_target_pairs={{3,0},{0,1},{1,2},{2,3},{7,4},{4,5},{5,6},{6,7},{11,8},{8,9},{9,10... | collective-permute-start | bytes 1572872 | tf_op jit(solution)/shard_map/ppermute | solution.py:107
  71.4 43.3 %collective-permute-start.3 = (f32[32,512]{1,0:T(8,128)}, f32[32,512]{1,0:T(8,128)S(1)}, u32[]{:S(2)}, u32[]{:S(2)}) collective-permute-start(f32[32,512]{1,0:T(8,128)} %pad_maximum_fusion.17), channel_id=1, source_target_pairs={{0,4},{4,0},{8,12},{12,8},{16,20},{20,16},{24,28},{28,24},{1,5},{5... | collective-permute-start | bytes 196616 | tf_op jit(solution)/shard_map/ppermute | solution.py:96
  71.4 615.5 %reduce-scatter.5.cloned.1.call-start = ((), (), s32[]{:S(2)}) async-start(), calls=%async_computation.6 | async-start | bytes 3244032 | tf_op jit(solution)/shard_map/reduce_scatter | solution.py:2046
  71.5 27.2 %copy-start.50 = (f32[32]{0:T(128)}, f32[32]{0:T(128)S(1)}, u32[]{:S(2)}) copy-start(f32[32]{0:T(128)S(1)} %multiply_power_fusion) | copy-start | bytes 388
  74.8 8.7 %copy-start.1 = (f32[2048,1]{0,1:T(1,128)}, f32[2048,1]{0,1:T(1,128)S(1)}, u32[]{:S(2)}) copy-start(f32[2048,1]{0,1:T(1,128)S(1)} %copy.179) | copy-start | bytes 24580
  77.0 6.6 copy-start.52
  83.6 15.1 %copy-start.3 = (f32[512,1344]{0,1:T(8,128)}, f32[512,1344]{0,1:T(8,128)S(1)}, u32[]{:S(2)}) copy-start(f32[512,1344]{0,1:T(8,128)S(1)} %fusion.6) | copy-start | bytes 8257540
  87.5 11.3 %copy-start.45 = (f32[512]{0:T(512)}, f32[512]{0:T(512)S(1)}, u32[]{:S(2)}) copy-start(f32[512]{0:T(512)S(1)} %get-tuple-element.247) | copy-start | bytes 6148
  87.5 7.3 %copy-start.43 = (f32[512]{0:T(512)}, f32[512]{0:T(512)S(1)}, u32[]{:S(2)}) copy-start(f32[512]{0:T(512)S(1)} %add_rsqrt_fusion) | copy-start | bytes 6148
  87.6 7.2 %copy-start.41 = (f32[512]{0:T(512)}, f32[512]{0:T(512)S(1)}, u32[]{:S(2)}) copy-start(f32[512]{0:T(512)S(1)} %reshape.425) | copy-start | bytes 6148
  92.5 5.5 copy-start.36
  95.8 7.7 %copy-start.5 = (bf16[512,4,128]{0,2,1:T(8,128)(2,1)}, bf16[512,4,128]{0,2,1:T(8,128)(2,1)S(1)}, u32[]{:S(2)}) copy-start(bf16[512,4,128]{0,2,1:T(8,128)(2,1)S(1)} %slice.338) | copy-start | bytes 1572868
  106.4 6.8 copy-start.7
  106.4 6.8 copy-start.47
  106.4 6.8 copy-start.19
  113.3 13.0 %copy-start.13 = (bf16[2,352,2048]{2,1,0:T(8,128)(2,1)S(1)}, bf16[2,352,2048]{2,1,0:T(8,128)(2,1)}, u32[]{:S(2)}) copy-start(bf16[2,352,2048]{2,1,0:T(8,128)(2,1)} %param.35) | copy-start | bytes 8650756
  114.8 8.0 %collective-permute-start.4 = (f32[64,512]{1,0:T(8,128)S(1)}, f32[64,512]{1,0:T(8,128)S(1)}, u32[]{:S(2)}, u32[]{:S(2)}) collective-permute-start(f32[64,512]{1,0:T(8,128)S(1)} %pad_maximum_fusion.15), channel_id=1, source_target_pairs={{0,8},{4,12},{8,0},{12,4},{16,24},{20,28},{24,16},{28,20},{1,9},{5... | collective-permute-start | bytes 393224 | tf_op jit(solution)/shard_map/ppermute | solution.py:96
  122.8 9.6 %collective-permute-start.5 = (f32[128,512]{1,0:T(8,128)S(1)}, f32[128,512]{1,0:T(8,128)}, u32[]{:S(2)}, u32[]{:S(2)}) collective-permute-start(f32[128,512]{1,0:T(8,128)S(1)} %pad_maximum_fusion.12), channel_id=1, source_target_pairs={{0,16},{4,20},{8,24},{12,28},{16,0},{20,4},{24,8},{28,12},{1,17},{... | collective-permute-start | bytes 786440 | tf_op jit(solution)/shard_map/ppermute | solution.py:96
  128.2 10.8 %copy-start.37 = (bf16[512,2048]{1,0:T(8,128)(2,1)S(1)}, bf16[512,2048]{1,0:T(8,128)(2,1)}, u32[]{:S(2)}) copy-start(bf16[512,2048]{1,0:T(8,128)(2,1)} %constant_dynamic-update-slice_fusion.3) | copy-start | bytes 6291460
  135.7 6.6 copy-start.58
  142.2 5.0 copy-start.38
  407.9 8.5 %copy-start.39 = (bf16[512,2048]{1,0:T(8,128)(2,1)S(1)}, bf16[512,2048]{1,0:T(8,128)(2,1)}, u32[]{:S(2)}) copy-start(bf16[512,2048]{1,0:T(8,128)(2,1)} %copy-done.38) | copy-start | bytes 6291460
  426.3 7.9 %copy-start.63 = (bf16[512,704]{1,0:T(8,128)(2,1)S(1)}, bf16[512,704]{1,0:T(8,128)(2,1)}, u32[]{:S(2)}) copy-start(bf16[512,704]{1,0:T(8,128)(2,1)} %get-tuple-element.177) | copy-start | bytes 2162692
  434.2 5.8 copy-start.24
  442.1 246.8 %reduce-scatter.3.cloned.1.call-start = ((), (), s32[]{:S(2)}) async-start(), calls=%async_computation.5 | async-start | bytes 6488064 | tf_op jit(solution)/shard_map/reduce_scatter | solution.py:2046
  566.1 4.7 copy-start.6
  566.1 4.7 copy-start.17
  579.1 7.8 %copy-start.28 = (f32[512,32]{0,1:T(8,128)S(1)}, f32[512,32]{0,1:T(8,128)}, u32[]{:S(2)}) copy-start(f32[512,32]{0,1:T(8,128)} %copy-done.27) | copy-start | bytes 196612
  579.1 7.8 %copy-start.30 = (f32[512,32]{0,1:T(8,128)S(1)}, f32[512,32]{0,1:T(8,128)}, u32[]{:S(2)}) copy-start(f32[512,32]{0,1:T(8,128)} %copy-done.29) | copy-start | bytes 196612
  579.1 8.0 %copy-start.9 = (f32[4,512,512]{1,2,0:T(8,128)S(1)}, f32[4,512,512]{1,2,0:T(8,128)}, u32[]{:S(2)}) copy-start(f32[4,512,512]{1,2,0:T(8,128)} %copy-done.7) | copy-start | bytes 12582916
  579.2 105.0 %collective-permute-start.6 = (bf16[128,2048]{1,0:T(8,128)(2,1)S(1)}, bf16[128,2048]{1,0:T(8,128)(2,1)S(1)}, u32[]{:S(2)}, u32[]{:S(2)}) collective-permute-start(bf16[128,2048]{1,0:T(8,128)(2,1)S(1)} %get-tuple-element.183), channel_id=1, source_target_pairs={{0,1},{1,2},{2,3},{3,0},{4,5},{5,6},{6,7},{7,4},{8,9},{9,10},{10,1... | collective-permute-start | bytes 1572872 | tf_op jit(solution)/shard_map/ppermute | solution.py:117
  584.4 99.9 %collective-permute-start.7 = (bf16[128,2048]{1,0:T(8,128)(2,1)S(1)}, bf16[128,2048]{1,0:T(8,128)(2,1)}, u32[]{:S(2)}, u32[]{:S(2)}) collective-permute-start(bf16[128,2048]{1,0:T(8,128)(2,1)S(1)} %get-tuple-element.185), channel_id=1, source_target_pairs={{0,2},{1,3},{2,0},{3,1},{4,6},{5,7},{6,4},{7,5},{8,10},{9,11},{10,... | collective-permute-start | bytes 1572872 | tf_op jit(solution)/shard_map/ppermute | solution.py:117
  584.4 99.9 %collective-permute-start.8 = (bf16[128,2048]{1,0:T(8,128)(2,1)S(1)}, bf16[128,2048]{1,0:T(8,128)(2,1)}, u32[]{:S(2)}, u32[]{:S(2)}) collective-permute-start(bf16[128,2048]{1,0:T(8,128)(2,1)S(1)} %get-tuple-element.184), channel_id=1, source_target_pairs={{0,3},{1,0},{2,1},{3,2},{4,7},{5,4},{6,5},{7,6},{8,11},{9,8},{10,9... | collective-permute-start | bytes 1572872 | tf_op jit(solution)/shard_map/ppermute | solution.py:117
  590.9 10.4 %slice-start.2 = ((s8[6815744]{0:T(1024)(128)(4,1)}), s8[4194304]{0:T(1024)(128)(4,1)S(1)}, s32[]{:S(2)}) async-start(s8[6815744]{0:T(1024)(128)(4,1)} %bitcast.195), calls=%async_computation.9 | async-start | bytes 8388608
  593.6 7.6 %slice-start.3 = ((s8[6815744]{0:T(1024)(128)(4,1)}), s8[2621440]{0:T(1024)(128)(4,1)S(1)}, s32[]{:S(2)}) async-start(s8[6815744]{0:T(1024)(128)(4,1)} %bitcast.195), calls=%async_computation.10 | async-start | bytes 5242880
  616.5 5.7 copy-start.49
  616.5 5.7 copy-start
  694.0 12.0 %slice-start = ((s8[5767168]{0:T(1024)(128)(4,1)}), s8[4194304]{0:T(1024)(128)(4,1)S(1)}, s32[]{:S(2)}) async-start(s8[5767168]{0:T(1024)(128)(4,1)} %bitcast.182), calls=%async_computation.7 | async-start | bytes 8388608
  700.1 6.0 slice-start.1
  (34 other events, 76.2 us)
Sparse Core Ops, SparseCore 0:
  9.9 39.8 all-gather.3
  52.3 42.9 all-gather.5
  97.1 33.0 all-gather.7
  442.2 69.4 reduce-scatter.4
  566.2 60.7 reduce-scatter.2

commit v5 on v4

--- a/solution.py
+++ b/solution.py
@@ -16,12 +16,7 @@
 SEQ = 512
 HALF = 256
 QUARTET = 4
-BOX_UNITS = [
-    [(0, 0), (0, 1), (1, 0), (1, 1)],
-    [(2, 0), (4, 0), (3, 0), (5, 0)],
-    [(2, 1), (4, 1), (3, 1), (5, 1)],
-    [(6, 0), (6, 1), (7, 0), (7, 1)],
-]
+RAW_ROWS = 8
 
 
 EPSILON = 1e-06
@@ -101,23 +96,11 @@
 
 
 def column_gather(rows):
-    count = lax.axis_size("tp")
-    pieces = [rows]
-    for s in range(1, count):
-        pieces.append(lax.ppermute(rows, "tp", [((i + s) % count, i) for i in range(count)]))
-    return jnp.concatenate(pieces, axis=0)
+    return lax.all_gather(rows, "tp", axis=0, tiled=True)
 
 
 def column_scatter(values):
-    count = lax.axis_size("tp")
-    size = values.shape[0] // count
-    total = values[:size].astype(F32)
-    for s in range(1, count):
-        piece = values[s * size : (s + 1) * size].astype(BF)
-        total = total + lax.ppermute(
-            piece, "tp", [(i, (i + s) % count) for i in range(count)]
-        ).astype(F32)
-    return total
+    return lax.psum_scatter(values.astype(BF), "tp", scatter_dimension=0, tiled=True).astype(F32)
 
 
 def dot_rows(left, right):
@@ -460,14 +443,14 @@
 
 
 class PlaneGather:
-    def __init__(self, own, others, size, sends, arrivals, base):
-        self.own, self.others, self.size = own, others, size
+    def __init__(self, own, others, rows_of, sends, arrivals, base):
+        self.own, self.others, self.rows_of = own, others, rows_of
         self.sends, self.arrivals, self.base = sends, arrivals, base
         self.partner, self.along, self.across = plane_neighbours()
 
     def copies(self, b):
         half = self.own.shape[1] // 2
-        rows = pl.ds(b * self.size, self.size)
+        rows = self.rows_of(b)
         left, right = pl.ds(0, half), pl.ds(half, half)
         other = {r: self.others.at[r - 1] for r in range(1, 8)}
         plan = [
@@ -514,17 +497,21 @@
             copy.wait_send()
 
 
-def expert_kernel(experts, cap, columns, size, *refs):
+def block_rows(columns, size):
+    row = lax.axis_index("tp")
+    return lambda s: pl.ds(pl.multiple_of((row + s) % columns * size, size), size)
+
+
+def expert_kernel(cap, columns, size, *refs):
     (
         attn_in,
         tokens_in,
         cotan_in,
-        gate_up_in,
+        gate_in,
+        up_in,
         down_in,
         gain_ref,
-        slot_row_ref,
-        weight_row_ref,
-        slot_col_ref,
+        raw_ref,
         mixed_out,
         ffn_all,
         dx_out,
@@ -551,20 +538,25 @@
         dxs,
         others,
         chip,
+        stage,
         hid,
         dgu,
-        stage,
+        slot_table,
+        weight_table,
         sends,
         arrivals,
         local,
+        loads,
+        sum_local,
         spill,
     ) = refs
     count = QUARTET
+    experts, local_hidden = gate_in.shape[:2]
     width = xb.shape[2]
-    half_width = width // 2
     pad = down.shape[1]
     tile = min(1024, width)
-    blocks = columns
+    wide = 2 * cap
+    rows_of = block_rows(columns, size)
     partner, along, across = plane_neighbours()
     column = column_neighbours(columns)
     number = 0
@@ -574,15 +566,27 @@
         number += amount
         return number - amount
 
-    x_gather = PlaneGather(ffn_all, x_others, size, sends, arrivals, reserve(8 * blocks))
-    dy_gather = PlaneGather(cotan_in, dy_others, SEQ, sends, arrivals, reserve(8))
+    x_gather = PlaneGather(ffn_all, x_others, rows_of, sends, arrivals, reserve(8 * columns))
+    dy_gather = PlaneGather(
+        cotan_in, dy_others, lambda b: pl.ds(0, SEQ), sends, arrivals, reserve(8)
+    )
     rs_base, ag_base = reserve(columns - 1), reserve(columns - 1)
-    pair_base, link_base = reserve(len(BOX_UNITS)), reserve(12)
+    plane = PlaneSum(
+        lambda r, h: others.at[r // 2],
+        chip,
+        theirs,
+        links,
+        stage,
+        sends,
+        arrivals,
+        reserve(plane_sum_sizes(columns)[0]),
+        sum_local,
+    )
 
     greet([partner, along, across] + column)
     sums = [
         mesh_copy(
-            attn_in.at[pl.ds(s * size, size)],
+            attn_in.at[rows_of(s)],
             arrived_v.at[s - 1],
             sends,
             arrivals,
@@ -594,18 +598,57 @@
     for copy in sums:
         copy.start()
     first = [
-        pltpu.make_async_copy(attn_in.at[pl.ds(0, size)], attn_v, local.at[0]),
+        pltpu.make_async_copy(attn_in.at[rows_of(0)], attn_v, local.at[0]),
         pltpu.make_async_copy(tokens_in, tokens_v, local.at[1]),
     ]
     for copy in first:
         copy.start()
     dy_gather.start(0)
-    weights_in = [
-        pltpu.make_async_copy(gate_up_in, gate_up, local.at[2]),
-        pltpu.make_async_copy(down_in, down, local.at[3]),
-    ]
+    if pad > local_hidden:
+        rest = pad - local_hidden
+        for e in range(experts):
+            for ref, start in ((gate_up, local_hidden), (gate_up, pad + local_hidden), (down, local_hidden)):
+                ref[e, start : start + rest, :] = jnp.zeros((rest, width), BF)
+    weights_in = []
+    for e in range(experts):
+        weights_in += [
+            pltpu.make_async_copy(
+                gate_in.at[e], gate_up.at[e, pl.ds(0, local_hidden)], local.at[2 + 3 * e]
+            ),
+            pltpu.make_async_copy(
+                up_in.at[e], gate_up.at[e, pl.ds(pad, local_hidden)], local.at[3 + 3 * e]
+            ),
+            pltpu.make_async_copy(
+                down_in.at[e], down.at[e, pl.ds(0, local_hidden)], local.at[4 + 3 * e]
+            ),
+        ]
     for copy in weights_in:
         copy.start()
+
+    earlier = lax.broadcasted_iota(jnp.int32, (size, size), 0)
+    later = lax.broadcasted_iota(jnp.int32, (size, size), 1)
+    before = jnp.where(earlier < later, 1.0, 0.0).astype(BF)
+    own_first = (lax.axis_index("fsdp") * experts).astype(F32)
+    for r in range(8):
+        for e in range(experts):
+            member = jnp.zeros((1, SEQ), F32)
+            weight = jnp.zeros((1, SEQ), F32)
+            for pick in range(TOPK):
+                same = raw_ref[r, pick : pick + 1, :] == own_first + float(e)
+                member = jnp.where(same, 1.0, member)
+                weight = weight + jnp.where(
+                    same, raw_ref[r, RAW_ROWS + pick : RAW_ROWS + pick + 1, :], 0.0
+                )
+            slot_table[r * experts + e : r * experts + e + 1, :] = member
+            weight_table[r * experts + e : r * experts + e + 1, :] = weight
+    second = lax.broadcasted_iota(jnp.int32, (8 * experts, size), 0) // experts % 2
+    shift = second.astype(F32) * float(cap)
+    for b in range(columns):
+        cols = pl.ds(b * size, size)
+        member = slot_table[:, cols]
+        rank = dot_plain(member.astype(BF), before)
+        slot_table[:, cols] = jnp.where(member > 0.5, rank + shift, NO_SLOT)
+
     for copy in first:
         copy.wait()
     total = tokens_v[...].astype(F32) + attn_v[...].astype(F32)
@@ -615,7 +658,7 @@
     mixed_v[...] = total
     inverse = lax.rsqrt(jnp.mean(total * total, axis=1, keepdims=True) + EPSILON)
     ffn_v[...] = (total * inverse * gain_ref[...]).astype(BF)
-    own_copy = pltpu.make_async_copy(ffn_v, ffn_all.at[pl.ds(0, size)], local.at[0])
+    own_copy = pltpu.make_async_copy(ffn_v, ffn_all.at[rows_of(0)], local.at[0])
     own_copy.start()
     mixed_copy = pltpu.make_async_copy(mixed_v, mixed_out, local.at[1])
     mixed_copy.start()
@@ -623,8 +666,8 @@
 
     rows_out = [
         mesh_copy(
-            ffn_all.at[pl.ds(0, size)],
-            ffn_all.at[pl.ds((columns - s) * size, size)],
+            ffn_all.at[rows_of(0)],
+            ffn_all.at[rows_of(0)],
             sends,
             arrivals,
             ag_base + s - 1,
@@ -634,76 +677,83 @@
     ]
     for copy in rows_out:
         copy.start()
-    x_gather.start(0)
-    dy_gather.forward(0)
-    for b in range(1, blocks):
-        rows_out[columns - b - 1].wait_recv()
+
+    def enter(b):
+        if b > 0:
+            rows_out[columns - b - 1].wait_recv()
         x_gather.start(b)
-        x_gather.forward(b - 1)
-    for b in range(blocks):
-        x_gather.arrived(b, [2])
-    dy_gather.arrived(0, [2])
+
+    def ready(b):
+        x_gather.arrived(b, [2, 5, 6, 7])
 
     def source(own, gathered, r):
         return own if r == 0 else gathered.at[r - 1]
 
-    def load(unit):
+    def load(b):
         copies = []
-        for q, (r, h) in enumerate(unit):
-            rows = pl.ds(h * HALF, HALF)
-            copies.append(
-                pltpu.make_async_copy(
-                    source(ffn_all, x_others, r).at[rows], xb.at[q], local.at[4 + q]
+        for r in range(8):
+            place = pl.ds(r % 2 * size, size)
+            for k, (own, gathered, target) in enumerate(
+                ((ffn_all, x_others, xb), (cotan_in, dy_others, db))
+            ):
+                copies.append(
+                    pltpu.make_async_copy(
+                        source(own, gathered, r).at[rows_of(b)],
+                        target.at[r // 2, place],
+                        loads.at[2 * r + k],
+                    )
                 )
+        return copies
+
+    def slots_of(table, b, q):
+        place = pl.ds(pl.multiple_of((lax.axis_index("tp") + b) % columns * size, size), size)
+        rows = []
+        for e in range(experts):
+            low, high = 2 * q * experts + e, (2 * q + 1) * experts + e
+            rows.append(
+                jnp.concatenate([table[low : low + 1, place], table[high : high + 1, place]], axis=1)
             )
-            copies.append(
-                pltpu.make_async_copy(
-                    source(cotan_in, dy_others, r).at[rows], db.at[q], local.at[8 + q]
-                )
+        return jnp.concatenate(rows, axis=0)
+
+    def combine(b, keep):
+        for q in range(count):
+            entries = slots_of(slot_table, b, q)
+            entries = jnp.concatenate(
+                [entries, jnp.full((8 - experts, HALF), NO_SLOT, F32)], axis=0
             )
-        return copies
-
-    def choose_cols(step, q):
-        return jnp.where(select_cols(slot_col_ref[step, q], experts, cap), 1.0, 0.0).astype(BF)
-
-    def combine(step, target):
-        for q in range(count):
-            choose = choose_cols(step, q)
+            hit = select_cols(entries.T, experts, wide)
+            choose = jnp.where(hit, 1.0, 0.0).astype(BF)
 
             def gather(n, carry, q=q, choose=choose):
                 cols = pl.ds(pl.multiple_of(n * tile, tile), tile)
-                ref, place = target(q)
-                ref[place + (slice(None), cols)] = dot_plain(choose, dxs[q, :, cols]).astype(BF)
+                keep(q, cols, dot_plain(choose, dxs[q, :, cols]).astype(BF))
                 return carry
 
             lax.fori_loop(0, width // tile, gather, 0)
 
-    def spills(step):
+    def spills(b):
         return [
-            pltpu.make_async_copy(xs, x_all.at[step], spill.at[0]),
-            pltpu.make_async_copy(ds, d_all.at[step], spill.at[1]),
-            pltpu.make_async_copy(hid.at[step], hid_all.at[step], spill.at[2]),
-            pltpu.make_async_copy(dgu, dgu_all.at[step], spill.at[3]),
+            pltpu.make_async_copy(xs, x_all.at[b], spill.at[0]),
+            pltpu.make_async_copy(ds, d_all.at[b], spill.at[1]),
+            pltpu.make_async_copy(hid.at[b], hid_all.at[b], spill.at[2]),
+            pltpu.make_async_copy(dgu, dgu_all.at[b], spill.at[3]),
         ]
 
-    def pair_copy(step):
-        return mesh_copy(others, theirs.at[step], sends, arrivals, pair_base + step, partner)
-
-    def front(step):
-        copies = load(BOX_UNITS[step])
+    def front(b):
+        copies = load(b)
         for copy in copies:
             copy.start()
-        if step == 0:
+        if b == 0:
             for copy in weights_in:
                 copy.wait()
-        if step > 0:
-            for copy in spills(step - 1):
+        if b > 0:
+            for copy in spills(b - 1):
                 copy.wait()
         for q in range(count):
-            copies[2 * q].wait()
-            copies[2 * q + 1].wait()
-            hit = select_rows(slot_row_ref[step, q], experts, cap)
-            weights = slot_weights(hit, weight_row_ref[step, q], experts, cap)
+            for copy in copies[4 * q : 4 * q + 4]:
+                copy.wait()
+            hit = select_rows(slots_of(slot_table, b, q), experts, wide)
+            weights = slot_weights(hit, slots_of(weight_table, b, q), experts, wide)
             choose = jnp.where(hit, 1.0, 0.0).astype(BF)
 
             def spread(n, carry, q=q, choose=choose, weights=weights):
@@ -711,13 +761,13 @@
                 rows = dot_plain(choose, xb[q, :, cols])
                 grads = dot_plain(choose, db[q, :, cols]) * weights
                 for e in range(experts):
-                    low, high = e * cap, (e + 1) * cap
-                    xs[e, q * cap : (q + 1) * cap, cols] = rows[low:high].astype(BF)
-                    ds[e, q * cap : (q + 1) * cap, cols] = grads[low:high].astype(BF)
+                    low, high = e * wide, (e + 1) * wide
+                    xs[e, q * wide : (q + 1) * wide, cols] = rows[low:high].astype(BF)
+                    ds[e, q * wide : (q + 1) * wide, cols] = grads[low:high].astype(BF)
                 return carry
 
             lax.fori_loop(0, width // tile, spread, 0)
-        out_copies = spills(step)
+        out_copies = spills(b)
         out_copies[0].start()
         out_copies[1].start()
 
@@ -727,7 +777,7 @@
             d_hidden = dot_rows(ds[e], down[e])
             sigmoid = jax.nn.sigmoid(gate_pre)
             silu = gate_pre * sigmoid
-            hid[step, e] = (silu * up_pre).astype(BF)
+            hid[b, e] = (silu * up_pre).astype(BF)
             gate_grad = d_hidden * up_pre * (sigmoid * (1.0 + gate_pre * (1.0 - sigmoid)))
             dgu[e] = jnp.concatenate([gate_grad, d_hidden * silu], axis=1).astype(BF)
 
@@ -735,8 +785,8 @@
                 cols = pl.ds(pl.multiple_of(n * tile, tile), tile)
                 part = dot_plain(dgu[e], gate_up[e, :, cols]).astype(BF)
                 for q in range(count):
-                    dxs[q, pl.ds(pl.multiple_of(e * cap, cap), cap), cols] = part[
-                        q * cap : (q + 1) * cap
+                    dxs[q, pl.ds(pl.multiple_of(e * wide, wide), wide), cols] = part[
+                        q * wide : (q + 1) * wide
                     ]
                 return inner
 
@@ -746,66 +796,25 @@
         lax.fori_loop(0, experts, one_expert, 0)
         out_copies[2].start()
         out_copies[3].start()
-        if step > 0:
-            pair_copy(step - 1).wait_send()
-        combine(step, lambda q: (chip, (step, q)) if q < 2 else (others, (q - 2,)))
-        pair_copy(step).start()
-
-    def add_rows(step, q, cols, landed):
-        fetch = pltpu.make_async_copy(landed, stage.at[:, cols], local.at[12])
-        fetch.start()
-        fetch.wait()
-
-        def some(i, carry):
-            rows = pl.ds(pl.multiple_of(i * 32, 32), 32)
-            chip[step, q, rows, cols] = (
-                chip[step, q, rows, cols].astype(F32) + stage[rows, cols].astype(F32)
-            ).astype(BF)
-            return carry
-
-        lax.fori_loop(0, HALF // 32, some, 0)
-
-    left, right = pl.ds(0, half_width), pl.ds(half_width, half_width)
-
-    def chip_sum(step):
-        pair_copy(step).wait_recv()
-        for h in range(2):
-            add_rows(step, h, pl.ds(0, width), theirs.at[step, h])
-
-    def chip_place(r, h):
-        step = [i for i, unit in enumerate(BOX_UNITS) if (r, h) in unit][0]
-        return step, BOX_UNITS[step].index((r, h))
-
-    def chip_rows(r, h):
-        return chip.at[chip_place(r, h)]
-
-    def link_copy(stage_number, side, h):
-        first_hop, second_hop = (along, across) if side == 0 else (across, along)
-        near, far = (2, 4) if side == 0 else (4, 2)
-        r = (near, 6, far)[stage_number]
-        device = second_hop if stage_number == 2 else first_hop
-        i = (stage_number * 2 + side) * 2 + h
-        return mesh_copy(
-            chip.at[chip_place(r, h) + (pl.ds(0, HALF), (left, right)[side])],
-            links.at[i],
-            sends,
-            arrivals,
-            link_base + i,
-            device,
-        )
-
-    def take_link(stage_number, side, h, r):
-        link_copy(stage_number, side, h).wait_recv()
-        i = (stage_number * 2 + side) * 2 + h
-        add_rows(*chip_place(r, h), (left, right)[side], links.at[i])
-
-    def out_part(step):
+        if b > 0:
+            for i in range(4):
+                plane.pair(i, b - 1).wait_send()
+
+        def keep(q, cols, value):
+            chip[q, b, :, cols] = value[:size]
+            others[q, :, cols] = value[size:]
+
+        combine(b, keep)
+        for i in range(4):
+            plane.pair(i, b).start()
+
+    def out_part(b):
         weights = [
             slot_weights(
-                select_rows(slot_row_ref[step, q], experts, cap),
-                weight_row_ref[step, q],
+                select_rows(slots_of(slot_table, b, q), experts, wide),
+                slots_of(weight_table, b, q),
                 experts,
-                cap,
+                wide,
             )
             for q in range(count)
         ]
@@ -813,119 +822,123 @@
 
             def one_tile(n, carry, e=e):
                 cols = pl.ds(pl.multiple_of(n * tile, tile), tile)
-                rows = dot_plain(hid[step, e], down[e, :, cols])
+                rows = dot_plain(hid[b, e], down[e, :, cols])
                 for q in range(count):
-                    dxs[q, e * cap : (e + 1) * cap, cols] = (
-                        rows[q * cap : (q + 1) * cap] * weights[q][e * cap : (e + 1) * cap]
+                    dxs[q, e * wide : (e + 1) * wide, cols] = (
+                        rows[q * wide : (q + 1) * wide] * weights[q][e * wide : (e + 1) * wide]
                     ).astype(BF)
                 return carry
 
             lax.fori_loop(0, width // tile, one_tile, 0)
-        if step > 0:
-            out_copy(step - 1).wait()
-        combine(step, lambda q: (db, (q,)))
-        out_copy(step).start()
-
-    def out_copy(step):
-        return pltpu.make_async_copy(db, out_all.at[step], local.at[13])
-
-    middle = blocks // 2
+        if b > 0:
+            out_copy(b - 1).wait()
+
+        def keep(q, cols, value):
+            db[q, :, cols] = value
+
+        combine(b, keep)
+        out_copy(b).start()
+
+    def out_copy(b):
+        return pltpu.make_async_copy(db, out_all.at[b], local.at[0])
+
+    def send_sums(b):
+        plane.on_chip(3, [b], False)
+        plane.send(1, [b])
+        plane.on_chip(1, [b], False)
+        plane.on_chip(2, [b], False)
+        plane.send(0, [b])
+        plane.on_chip(0, [b], False)
+
+    final = columns - 1
+    enter(0)
+    dy_gather.forward(0)
+    enter(1)
+    x_gather.forward(0)
+    enter(2)
+    x_gather.forward(1)
+    x_gather.last(0)
+    dy_gather.last(0)
+    ready(0)
+    dy_gather.arrived(0, [2, 5, 6, 7])
     front(0)
-    x_gather.forward(blocks - 1)
-    dy_gather.last(0)
-    for b in range(middle):
-        x_gather.arrived(b, [5, 6])
-    dy_gather.arrived(0, [5, 6])
+    for b in range(3, columns):
+        enter(b)
+    x_gather.forward(2)
+    x_gather.last(1)
+    ready(1)
     front(1)
-    for b in range(blocks):
+    for b in range(2, columns):
+        if b > 2:
+            x_gather.forward(b)
         x_gather.last(b)
-    for b in range(middle, blocks):
-        x_gather.arrived(b, [5, 6])
-    chip_sum(0)
-    front(2)
-    chip_sum(1)
-    for side in range(2):
-        link_copy(0, side, 0).start()
-    for b in range(blocks):
-        x_gather.arrived(b, [7])
-    dy_gather.arrived(0, [7])
-    front(3)
-    chip_sum(2)
-    for side in range(2):
-        link_copy(0, side, 1).start()
-    for copy in spills(3):
+        ready(b)
+        send_sums(b - 2)
+        if b > 2:
+            plane.send_second([b - 3])
+        front(b)
+    send_sums(final - 1)
+    plane.send_second([final - 2])
+    for copy in spills(final):
         copy.wait()
     out_part(0)
-    chip_sum(3)
-    for h in range(2):
-        for side in range(2):
-            link_copy(1, side, h).start()
+    send_sums(final)
+    plane.send_second([final - 1])
     out_part(1)
-    for h in range(2):
-        for side in range(2):
-            take_link(1, side, h, (4, 2)[side])
-            link_copy(2, side, h).start()
-    out_part(2)
-    out_part(3)
-    for h in range(2):
-        for side in range(2):
-            take_link(0, side, h, 0)
-        for side in range(2):
-            take_link(2, side, h, 0)
-        done = pltpu.make_async_copy(
-            chip_rows(0, h), dx_out.at[pl.ds(h * HALF, HALF)], local.at[14 + h]
-        )
-        done.start()
-    for h in range(2):
-        pltpu.make_async_copy(
-            chip_rows(0, h), dx_out.at[pl.ds(h * HALF, HALF)], local.at[14 + h]
-        ).wait()
-    out_copy(3).wait()
+    plane.send_second([final])
+    for b in range(2, columns):
+        out_part(b)
+    plane.finish(range(columns))
+    done = [
+        pltpu.make_async_copy(chip.at[0, b], dx_out.at[rows_of(b)], loads.at[b])
+        for b in range(columns)
+    ]
+    for copy in done:
+        copy.start()
+    for copy in done:
+        copy.wait()
+    out_copy(final).wait()
     mixed_copy.wait()
 
-    for b in range(blocks):
+    for b in range(columns):
         x_gather.drain(b)
     dy_gather.drain(0)
     for copy in sums + rows_out:
         copy.wait_send()
-    pair_copy(3).wait_send()
-    for stage_number in range(3):
-        for side in range(2):
-            for h in range(2):
-                link_copy(stage_number, side, h).wait_send()
-
-
-def expert_call(attn_part, tokens, cotan_all, gate_up, down, gain, tables, cap):
+    plane.drain(final)
+
+
+def expert_call(attn_part, tokens, cotan_all, gate, up, down, gain, raw, cap):
     columns = lax.axis_size("tp")
     size, width = tokens.shape
-    experts, wide, _ = gate_up.shape
-    pad = wide // 2
-    slots = QUARTET * cap
-    steps = len(BOX_UNITS)
+    experts, local_hidden, _ = gate.shape
+    pad = -(-local_hidden // 128) * 128
+    slots = 8 * cap
     anywhere = pl.BlockSpec(memory_space=pl.ANY)
     held = pl.BlockSpec(memory_space=pltpu.VMEM)
 
     def array(*dims, kind=BF):
         return jax.ShapeDtypeStruct(dims, kind)
 
-    copies = 8 * columns + 8 + 2 * (columns - 1) + steps + 12
+    landing, scratch = plane_sum_space(columns, size, width)
+    remote, near = plane_sum_sizes(columns)
+    remote = remote + 8 * columns + 8 + 2 * (columns - 1)
     results = pl.pallas_call(
-        functools.partial(expert_kernel, experts, cap, columns, size),
+        functools.partial(expert_kernel, cap, columns, size),
         out_shape=[
             array(size, width, kind=F32),
             array(SEQ, width),
             array(SEQ, width),
-            array(steps, QUARTET, HALF, width),
-            array(steps, experts, slots, width),
-            array(steps, experts, slots, width),
-            array(steps, experts, slots, pad),
-            array(steps, experts, slots, wide),
+            array(columns, QUARTET, HALF, width),
+            array(columns, experts, slots, width),
+            array(columns, experts, slots, width),
+            array(columns, experts, slots, pad),
+            array(columns, experts, slots, 2 * pad),
             array(7, SEQ, width),
             array(7, SEQ, width),
-            array(steps, 2, HALF, width),
-            array(12, HALF, width // 2),
-        ],
-        in_specs=[anywhere] * 5 + [held] * 4,
+        ]
+        + landing,
+        in_specs=[anywhere] * 6 + [held] * 2,
         out_specs=[anywhere] * 12,
         scratch_shapes=[
             pltpu.VMEM((size, width), BF),
@@ -935,136 +948,171 @@
             pltpu.VMEM((size, width), BF),
             pltpu.VMEM((QUARTET, HALF, width), BF),
             pltpu.VMEM((QUARTET, HALF, width), BF),
-            pltpu.VMEM((experts, wide, width), BF),
+            pltpu.VMEM((experts, 2 * pad, width), BF),
             pltpu.VMEM((experts, pad, width), BF),
             pltpu.VMEM((experts, slots, width), BF),
             pltpu.VMEM((experts, slots, width), BF),
-            pltpu.VMEM((QUARTET, experts * cap, width), BF),
-            pltpu.VMEM((2, HALF, width), BF),
-            pltpu.VMEM((steps, 2, HALF, width), BF),
-            pltpu.VMEM((steps, experts, slots, pad), BF),
-            pltpu.VMEM((experts, slots, wide), BF),
-            pltpu.VMEM((HALF, width), BF),
-            pltpu.SemaphoreType.DMA((copies,)),
-            pltpu.SemaphoreType.DMA((copies,)),
+            pltpu.VMEM((QUARTET, 2 * experts * cap, width), BF),
+            pltpu.VMEM((4, size, width), BF),
+        ]
+        + scratch
+        + [
+            pltpu.VMEM((columns, experts, slots, pad), BF),
+            pltpu.VMEM((experts, slots, 2 * pad), BF),
+            pltpu.VMEM((8 * experts, SEQ), F32),
+            pltpu.VMEM((8 * experts, SEQ), F32),
+            pltpu.SemaphoreType.DMA((remote,)),
+            pltpu.SemaphoreType.DMA((remote,)),
+            pltpu.SemaphoreType.DMA((2 + 3 * experts,)),
             pltpu.SemaphoreType.DMA((16,)),
+            pltpu.SemaphoreType.DMA((near,)),
             pltpu.SemaphoreType.DMA((4,)),
         ],
         compiler_params=pltpu.CompilerParams(
             collective_id=1, has_side_effects=True, vmem_limit_bytes=67_043_328
         ),
         cost_estimate=pl.CostEstimate(
-            flops=steps
-            * (2 * slots * experts * width * pad * 6 + 8 * QUARTET * HALF * experts * cap * width),
+            flops=16 * SEQ * experts * cap * width * 8,
             bytes_accessed=60 * SEQ * width,
             transcendentals=0,
         ),
         name="experts",
-    )(attn_part, tokens, cotan_all, gate_up, down, gain, *tables)
+    )(attn_part, tokens, cotan_all, gate, up, down, gain, raw)
     return results[:8]
 
 
-def first_kernel(columns, size, *refs):
-    (
-        tokens_in,
-        packed_in,
-        tokens_all,
-        packed_all,
-        tokens_v,
-        packed_v,
-        sends,
-        arrivals,
-        local,
-    ) = refs
+def first_kernel(columns, size, kinds, *refs):
+    amount = len(kinds)
+    tokens_in, own_in = refs[0], refs[1 : 1 + amount]
+    tokens_all, alls = refs[1 + amount], refs[2 + amount : 2 + 2 * amount]
+    tokens_v, held = refs[2 + 2 * amount], refs[3 + 2 * amount : 3 + 3 * amount]
+    sends, arrivals, local = refs[3 + 3 * amount :]
     partner, along, across = plane_neighbours()
     column = column_neighbours(columns)
+    rows_of = block_rows(columns, size)
     place = lax.axis_index("fsdp")
-    rows = packed_in.shape[0]
-    top, bottom = pl.ds(0, rows // 2), pl.ds(rows // 2, rows // 2)
-    opposite = along[0] + across[0] - place
+    devices = {
+        0: place,
+        1: partner[0],
+        2: along[0],
+        4: across[0],
+        6: along[0] + across[0] - place,
+    }
     greet([partner, along, across] + column)
-    plan = [
-        (packed_in, packed_all.at[place], along),
-        (packed_in, packed_all.at[place], across),
-        (packed_in, packed_all.at[place], partner),
-        (packed_all.at[along[0], top], packed_all.at[along[0], top], across),
-        (packed_all.at[across[0], bottom], packed_all.at[across[0], bottom], along),
-        (packed_all.at[along[0]], packed_all.at[along[0]], partner),
-        (packed_all.at[across[0]], packed_all.at[across[0]], partner),
-        (packed_all.at[opposite], packed_all.at[opposite], partner),
-    ]
-    copies = [
-        mesh_copy(src, dst, sends, arrivals, i, device) for i, (src, dst, device) in enumerate(plan)
-    ]
     rows_out = [
         mesh_copy(
             tokens_in,
-            tokens_all.at[pl.ds((columns - s) * size, size)],
+            tokens_all.at[rows_of(0)],
             sends,
             arrivals,
-            7 + s,
+            8 * amount + s - 1,
             column[s - 1],
         )
         for s in range(1, columns)
     ]
-    for copy in copies[:3] + rows_out:
+    for copy in rows_out:
         copy.start()
-    here = [
-        pltpu.make_async_copy(tokens_in, tokens_v, local.at[0]),
-        pltpu.make_async_copy(packed_in, packed_v, local.at[1]),
-    ]
+    plans = []
+    for k, kind in enumerate(kinds):
+        own, everything = own_in[k], alls[k]
+        rows, cols = own.shape
+        top, bottom = pl.ds(0, rows // 2), pl.ds(rows // 2, rows // 2)
+        whole = pl.ds(0, rows)
+
+        def spot(r, hop, part, kind=kind, everything=everything, cols=cols):
+            if kind == "relative":
+                return everything.at[r ^ hop, part]
+            if kind == "rows":
+                return everything.at[devices[r], part]
+            start = pl.multiple_of(devices[r] * cols, cols)
+            return everything.at[part, pl.ds(start, cols)]
+
+        plan = [
+            (own, spot(0, 2, whole), along),
+            (own, spot(0, 4, whole), across),
+            (own, spot(0, 1, whole), partner),
+            (spot(2, 0, top), spot(2, 4, top), across),
+            (spot(4, 0, bottom), spot(4, 2, bottom), along),
+            (spot(2, 0, whole), spot(2, 1, whole), partner),
+            (spot(4, 0, whole), spot(4, 1, whole), partner),
+            (spot(6, 0, whole), spot(6, 1, whole), partner),
+        ]
+        plans.append(
+            [
+                mesh_copy(src, dst, sends, arrivals, 8 * k + i, device)
+                for i, (src, dst, device) in enumerate(plan)
+            ]
+        )
+    for copies in plans:
+        for copy in copies[:3]:
+            copy.start()
+    here = [pltpu.make_async_copy(tokens_in, tokens_v, local.at[0])]
+    there = [pltpu.make_async_copy(tokens_v, tokens_all.at[rows_of(0)], local.at[0])]
+    for k, kind in enumerate(kinds):
+        rows, cols = own_in[k].shape
+        if kind == "relative":
+            spot_here = alls[k].at[0]
+        elif kind == "rows":
+            spot_here = alls[k].at[place]
+        else:
+            spot_here = alls[k].at[:, pl.ds(pl.multiple_of(place * cols, cols), cols)]
+        here.append(pltpu.make_async_copy(own_in[k], held[k], local.at[1 + k]))
+        there.append(pltpu.make_async_copy(held[k], spot_here, local.at[1 + k]))
     for copy in here:
         copy.start()
     for copy in here:
         copy.wait()
-    there = [
-        pltpu.make_async_copy(tokens_v, tokens_all.at[pl.ds(0, size)], local.at[0]),
-        pltpu.make_async_copy(packed_v, packed_all.at[place], local.at[1]),
-    ]
     for copy in there:
         copy.start()
-    copies[0].wait_recv()
-    copies[3].start()
-    copies[5].start()
-    copies[1].wait_recv()
-    copies[4].start()
-    copies[6].start()
-    copies[3].wait_recv()
-    copies[4].wait_recv()
-    copies[7].start()
-    for i in (2, 5, 6, 7):
-        copies[i].wait_recv()
+    for copies in plans:
+        copies[0].wait_recv()
+        copies[3].start()
+        copies[5].start()
+        copies[1].wait_recv()
+        copies[4].start()
+        copies[6].start()
+    for copies in plans:
+        copies[3].wait_recv()
+        copies[4].wait_recv()
+        copies[7].start()
+    for copies in plans:
+        for i in (2, 5, 6, 7):
+            copies[i].wait_recv()
     for copy in rows_out:
         copy.wait_recv()
     for copy in there:
         copy.wait()
-    for copy in copies + rows_out:
-        copy.wait_send()
-
-
-def first_call(tokens, packed):
+    for copies in plans + [rows_out]:
+        for copy in copies:
+            copy.wait_send()
+
+
+def first_call(tokens, owns, kinds):
     columns = lax.axis_size("tp")
     size, width = tokens.shape
     anywhere = pl.BlockSpec(memory_space=pl.ANY)
-    copies = 8 + columns - 1
+    copies = 8 * len(owns) + columns - 1
+
+    def gathered(own, kind):
+        rows, cols = own.shape
+        return (rows, 8 * cols) if kind == "columns" else (8, rows, cols)
+
     return pl.pallas_call(
-        functools.partial(first_kernel, columns, size),
-        out_shape=[
-            jax.ShapeDtypeStruct((columns * size, width), BF),
-            jax.ShapeDtypeStruct((8,) + packed.shape, BF),
-        ],
-        in_specs=[anywhere] * 2,
-        out_specs=[anywhere] * 2,
-        scratch_shapes=[
-            pltpu.VMEM((size, width), BF),
-            pltpu.VMEM(packed.shape, BF),
+        functools.partial(first_kernel, columns, size, kinds),
+        out_shape=[jax.ShapeDtypeStruct((columns * size, width), BF)]
+        + [jax.ShapeDtypeStruct(gathered(own, kind), own.dtype) for own, kind in zip(owns, kinds)],
+        in_specs=[anywhere] * (1 + len(owns)),
+        out_specs=[anywhere] * (1 + len(owns)),
+        scratch_shapes=[pltpu.VMEM((size, width), BF)]
+        + [pltpu.VMEM(own.shape, own.dtype) for own in owns]
+        + [
             pltpu.SemaphoreType.DMA((copies,)),
             pltpu.SemaphoreType.DMA((copies,)),
-            pltpu.SemaphoreType.DMA((2,)),
+            pltpu.SemaphoreType.DMA((1 + len(owns),)),
         ],
         compiler_params=pltpu.CompilerParams(collective_id=2, has_side_effects=True),
         name="first_gather",
-    )(tokens, packed)
+    )(tokens, *owns)
 
 
 class PlaneSum:
@@ -1113,9 +1161,10 @@
 
         lax.fori_loop(0, size // some, one, 0)
 
-    def on_chip(self, i):
-        for h in range(self.parts):
-            self.mine(i, h).wait()
+    def on_chip(self, i, parts=None, fetched=True):
+        for h in range(self.parts) if parts is None else parts:
+            if fetched:
+                self.mine(i, h).wait()
             self.pair(i, h).wait_recv()
             self.add(i, h, 0, self.rows, self.theirs.at[i, h])
 
@@ -1149,27 +1198,28 @@
         self.send(0)
         self.on_chip(0)
 
-    def send(self, stage_number):
-        for h in range(self.parts):
+    def send(self, stage_number, parts=None):
+        for h in range(self.parts) if parts is None else parts:
             for side in range(2):
                 self.link(stage_number, side, h).start()
 
-    def send_second(self):
-        for h in range(self.parts):
+    def send_second(self, parts=None):
+        for h in range(self.parts) if parts is None else parts:
             for side in range(2):
                 self.take(1, side, h, (2, 1)[side])
                 self.link(2, side, h).start()
 
-    def finish(self):
-        for stage_number in (0, 2):
-            for h in range(self.parts):
+    def finish(self, parts=None):
+        for h in range(self.parts) if parts is None else parts:
+            for stage_number in (0, 2):
                 for side in range(2):
                     self.take(stage_number, side, h, 0)
 
-    def drain(self):
+    def drain(self, first_part=0):
         for h in range(self.parts):
             for i in range(4):
-                self.pair(i, h).wait_send()
+                if h >= first_part:
+                    self.pair(i, h).wait_send()
             for stage_number in range(3):
                 for side in range(2):
                     self.link(stage_number, side, h).wait_send()
@@ -1231,9 +1281,7 @@
     column = column_neighbours(columns)
     greet([partner, along, across] + column)
     plane = PlaneSum(
-        lambda r, h: out_all.at[
-            [(s, unit.index((r, h))) for s, unit in enumerate(BOX_UNITS) if (r, h) in unit][0]
-        ],
+        lambda r, h: out_all.at[h, r // 2, pl.ds(r % 2 * size, size)],
         chip,
         theirs,
         links,
@@ -1243,10 +1291,11 @@
         0,
         sum_local,
     )
-    base = plane_sum_sizes(2)[0]
+    base = plane_sum_sizes(columns)[0]
+    rows_of = block_rows(columns, size)
     sums = [
         mesh_copy(
-            d_ffn_in.at[pl.ds(s * size, size)],
+            d_ffn_in.at[rows_of(s)],
             arrived_v.at[s - 1],
             sends,
             arrivals,
@@ -1257,8 +1306,8 @@
     ]
     rows_out = [
         mesh_copy(
-            d_proj_all.at[pl.ds(0, size)],
-            d_proj_all.at[pl.ds((columns - s) * size, size)],
+            d_proj_all.at[rows_of(0)],
+            d_proj_all.at[rows_of(0)],
             sends,
             arrivals,
             base + columns - 1 + s - 1,
@@ -1269,7 +1318,7 @@
     for copy in sums:
         copy.start()
     first = [
-        pltpu.make_async_copy(d_ffn_in.at[pl.ds(0, size)], own_v, local.at[0]),
+        pltpu.make_async_copy(d_ffn_in.at[rows_of(0)], own_v, local.at[0]),
         pltpu.make_async_copy(mixed_in, mixed_v, local.at[1]),
         pltpu.make_async_copy(cotan_in, cotan_v, local.at[2]),
     ]
@@ -1356,7 +1405,7 @@
     d_mixed = cotan_v[...].astype(F32) + back
     mixed_v[...] = d_mixed
     proj_v[...] = d_mixed.astype(BF)
-    own_copy = pltpu.make_async_copy(proj_v, d_proj_all.at[pl.ds(0, size)], local.at[0])
+    own_copy = pltpu.make_async_copy(proj_v, d_proj_all.at[rows_of(0)], local.at[0])
     own_copy.start()
     mixed_copy = pltpu.make_async_copy(mixed_v, d_mixed_out, local.at[1])
     mixed_copy.start()
@@ -1368,10 +1417,8 @@
     plane.send_second()
     plane.finish()
     done = [
-        pltpu.make_async_copy(
-            chip.at[0, h], routed_out.at[pl.ds(h * HALF, HALF)], sum_local.at[1 + h]
-        )
-        for h in range(2)
+        pltpu.make_async_copy(chip.at[0, h], routed_out.at[rows_of(h)], sum_local.at[1 + h])
+        for h in range(columns)
     ]
     for copy in done:
         copy.start()
@@ -1394,8 +1441,8 @@
     steps, experts, slots, pad = hid_all.shape
     anywhere = pl.BlockSpec(memory_space=pl.ANY)
     held = pl.BlockSpec(memory_space=pltpu.VMEM)
-    landing, scratch = plane_sum_space(2, HALF, width)
-    remote, near = plane_sum_sizes(2)
+    landing, scratch = plane_sum_space(columns, size, width)
+    remote, near = plane_sum_sizes(columns)
     remote = remote + 2 * (columns - 1)
     grad = jax.ShapeDtypeStruct((experts, local_hidden, width), F32)
     results = pl.pallas_call(
@@ -1540,9 +1587,10 @@
         out_local,
     )
     base = 3 * each
+    rows_of = block_rows(columns, size)
     sums = [
         mesh_copy(
-            d_normed_in.at[pl.ds(s * size, size)],
+            d_normed_in.at[rows_of(s)],
             arrived_v.at[s - 1],
             sends,
             arrivals,
@@ -1555,7 +1603,7 @@
     for copy in sums:
         copy.start()
     first = [
-        pltpu.make_async_copy(d_normed_in.at[pl.ds(0, size)], own_v, local.at[0]),
+        pltpu.make_async_copy(d_normed_in.at[rows_of(0)], own_v, local.at[0]),
         pltpu.make_async_copy(tokens_in, tokens_v, local.at[1]),
         pltpu.make_async_copy(d_mixed_in, mixed_v, local.at[2]),
         pltpu.make_async_copy(sums_in, running.at[0], local.at[3]),
@@ -1705,8 +1753,6 @@
 
 
 def plane_units(count):
-    if count == 8:
-        return BOX_UNITS
     return [[(2 * i + j // 2, j % 2) for j in range(4)] for i in range(count // 2)]
 
 
@@ -1742,14 +1788,7 @@
 def expert_tables(expert_ids, expert_wts, local_experts, units, cap):
     fsdp_count = lax.axis_size("fsdp")
     fsdp_rank = lax.axis_index("fsdp")
-    tp_count = lax.axis_size("tp")
     expert_count = local_experts * fsdp_count
-    places = (lax.axis_index("tp") + jnp.arange(tp_count, dtype=jnp.int32)) % tp_count
-
-    def reorder(rows):
-        return jnp.take(rows.reshape(tp_count, -1, TOPK), places, axis=0).reshape(SEQ, TOPK)
-
-    expert_ids, expert_wts = reorder(expert_ids), reorder(expert_wts)
     names = jnp.arange(expert_count, dtype=jnp.int32)[:, None]
     member = jnp.zeros((expert_count, SEQ), jnp.bool_)
     weight = jnp.zeros((expert_count, SEQ), F32)
@@ -1765,11 +1804,7 @@
     ).reshape(expert_count, SEQ)
     slot = jnp.where(member, rank, NO_SLOT)
     table = jnp.concatenate([slot, weight], axis=0)
-    if fsdp_count == 8:
-        for bit in (1, 2, 4):
-            table = jnp.concatenate([table, swap(table, "fsdp", bit)], axis=0)
-    else:
-        table = lax.all_gather(table, "fsdp", axis=0, tiled=True)
+    table = lax.all_gather(table, "fsdp", axis=0, tiled=True)
     table = table.reshape(fsdp_count, 2, fsdp_count, local_experts, 2, HALF)
     table = lax.dynamic_index_in_dim(table, fsdp_rank, axis=2, keepdims=False)
     slot_steps, weight_steps = [], []
@@ -1809,6 +1844,7 @@
     expert_count = local_experts * fsdp_count
     cap_rows = tok_rows * TOPK * 4 // (3 * expert_count)
     cap = cap_rows * (HALF // tok_rows)
+    paired = fsdp_count == 8 and tok_rows * 2 == HALF
     heads_local = H // tp_count
     head_width = NOPE + ROPE
     score_scale = head_width ** (-0.5)
@@ -1816,7 +1852,6 @@
     latent_cols = latent_proj.shape[1]
     up_cols = latent_up.shape[1]
     out_rows = out_proj.shape[0]
-    units = plane_units(fsdp_count)
 
     joint = query_cols + latent_cols
     spare = (-joint) % 128
@@ -1830,18 +1865,30 @@
         ],
         axis=1,
     )
-    packed = jnp.concatenate(
-        [query_proj, latent_proj, gains, latent_up.reshape(shard_rows, -1)], axis=1
-    )
-    lift_cols = packed.shape[1] - joint - spare
-    paired = fsdp_count == 8
+    packed = jnp.concatenate([query_proj, latent_proj, gains], axis=1)
+    shared_weight = lax.all_gather(
+        jnp.concatenate([shared_gate, shared_up], axis=1), "fsdp", axis=0, tiled=True
+    )
     if paired:
-        tokens_all, packed_all = first_call(block_in, packed)
+        low, high = (0, RAW_ROWS - TOPK), (0, 0)
+        raw = jnp.concatenate(
+            [jnp.pad(expert_ids.T.astype(F32), (low, high)), jnp.pad(expert_wts.T, (low, high))]
+        )
+        tokens_all, packed_all, latent_up_weight, out_weight, raw = first_call(
+            block_in,
+            [packed, latent_up, out_proj, raw],
+            ("rows", "rows", "columns", "relative"),
+        )
         packed_all = packed_all.reshape(-1, packed.shape[1])
+        latent_up_weight = latent_up_weight.reshape(LAT, up_cols)
     else:
         packed_all = lax.all_gather(packed, "fsdp", axis=0, tiled=True)
+        latent_up_weight = lax.all_gather(latent_up, "fsdp", axis=0, tiled=True)
+        out_weight = lax.all_gather(out_proj, "fsdp", axis=1, tiled=True)
         tokens_all = column_gather(block_in)
-    joint_weight = packed_all[:, :joint]
+    cotan_own, tokens_all = tie(out_cotan, tokens_all)
+    cotan_all = column_gather(cotan_own)
+    shared_down_weight = lax.all_gather(shared_down, "fsdp", axis=1, tiled=True)
     gain_attn = packed_all[:, joint].astype(F32)
     gain_ffn = packed_all[:, joint + 1].astype(F32)
     gain_latent = (
@@ -1850,32 +1897,15 @@
         .reshape(LAT)
         .astype(F32)
     )
-    latent_up_weight = packed_all[:, joint + spare :].reshape(LAT, up_cols)
-    out_weight = lax.all_gather(out_proj, "fsdp", axis=1, tiled=True)
-    cotan_own, tokens_all = tie(out_cotan, tokens_all)
-    cotan_all = column_gather(cotan_own)
-    shared_weight = lax.all_gather(
-        jnp.concatenate([shared_gate, shared_up], axis=1), "fsdp", axis=0, tiled=True
-    )
-    shared_down_weight = lax.all_gather(shared_down, "fsdp", axis=1, tiled=True)
     shared_cols = shared_gate.shape[1]
-    tables = expert_tables(expert_ids, expert_wts, local_experts, units, cap)
-    hidden_pad = -(-local_hidden // 128) * 128
-    lift = ((0, 0), (0, hidden_pad - local_hidden), (0, 0))
-    routed_gate_up = jnp.concatenate([jnp.pad(routed_gate, lift), jnp.pad(routed_up, lift)], axis=1)
-    routed_down_pad = jnp.pad(routed_down, lift)
 
     unit_all, inverse_all = norm_parts(tokens_all.astype(F32))
     normed_all = (unit_all * gain_attn).astype(BF)
-    joint_rows = jnp.dot(normed_all, joint_weight, preferred_element_type=F32)
+    joint_rows = jnp.dot(normed_all, packed_all, preferred_element_type=F32)
     queries = joint_rows[:, :query_cols].reshape(SEQ, heads_local, head_width)
-    latent = joint_rows[:, query_cols:]
+    latent = joint_rows[:, query_cols:joint]
     unit_lat, inverse_lat = norm_parts(latent[:, :LAT])
-    places = (tp_rank + jnp.arange(tp_count, dtype=jnp.int32)) % tp_count
-    positions = (
-        places[:, None] * tok_rows + jnp.arange(tok_rows, dtype=jnp.int32)[None, :]
-    ).reshape(SEQ)
-    segments = jnp.take(segment_ids.reshape(tp_count, tok_rows), places, axis=0).reshape(SEQ)
+    positions = jnp.arange(SEQ, dtype=jnp.int32)
     cosine, sine_part = rope_tables(positions, ROPE)
     compressed_all = (unit_lat * gain_latent).astype(BF)
     key_rope_all = rotate(latent[:, LAT:], cosine, sine_part).astype(BF)
@@ -1900,7 +1930,7 @@
     )
     values = key_value[:, :, NOPE:]
     allowed = (positions[None, :] <= positions[:, None]) & (
-        segments[None, :] == segments[:, None]
+        segment_ids[None, :] == segment_ids[:, None]
     )
     raw_scores = (
         jnp.einsum("qhd,khd->hqk", query_cat, key_cat, preferred_element_type=F32) * score_scale
@@ -1922,15 +1952,24 @@
             attn_part,
             block_in,
             cotan_all,
-            routed_gate_up,
-            routed_down_pad,
+            routed_gate,
+            routed_up,
+            routed_down,
             gain_ffn[None, :],
-            tables,
-            cap,
+            raw,
+            cap_rows,
         )
         unit_two, inverse_two = norm_parts(mixed_rows)
         d_routed_in = d_routed_in.astype(F32)
     else:
+        units = plane_units(fsdp_count)
+        tables = expert_tables(expert_ids, expert_wts, local_experts, units, cap)
+        hidden_pad = -(-local_hidden // 128) * 128
+        lift = ((0, 0), (0, hidden_pad - local_hidden), (0, 0))
+        routed_gate_up = jnp.concatenate(
+            [jnp.pad(routed_gate, lift), jnp.pad(routed_up, lift)], axis=1
+        )
+        routed_down_pad = jnp.pad(routed_down, lift)
         mixed_rows = block_in.astype(F32) + column_scatter(attn_part)
         unit_two, inverse_two = norm_parts(mixed_rows)
         normed_ffn_all = column_gather((unit_two * gain_ffn).astype(BF))
@@ -2037,9 +2076,9 @@
     d_latent = jnp.concatenate(
         [d_latent_main, unrotate(d_key_rope, cosine, sine_part)], axis=1
     ).astype(BF)
-    d_joint = jnp.concatenate([d_queries, d_latent], axis=1)
+    d_joint = jnp.concatenate([d_queries, d_latent, jnp.zeros((SEQ, spare), BF)], axis=1)
     joint_part = jnp.dot(normed_all.T, d_joint, preferred_element_type=F32)
-    d_normed_part = jnp.dot(d_joint, joint_weight.T, preferred_element_type=F32)
+    d_normed_part = jnp.dot(d_joint, packed_all.T, preferred_element_type=F32)
     attn_gain_part = jnp.sum(d_normed_part * unit_all, axis=0)
 
     def scatter(part, dimension):
@@ -2048,7 +2087,7 @@
     gain_parts = jnp.concatenate([attn_gain_part, latent_gain_part, ffn_gain_part]).reshape(
         -1, 128
     )
-    joint_part = jnp.pad(joint_part.astype(BF), ((0, 0), (0, (-joint) % 128)))
+    joint_part = joint_part.astype(BF)
     shared_down_grad = scatter(shared_down_part, 1)
     shared_grad = scatter(shared_part, 0)
     if paired:
@@ -2081,10 +2120,7 @@
         out_proj_grad = scatter(out_part, 1)
         latent_up_grad = scatter(latent_up_part, 0)
         joint_grad = scatter(joint_part, 0)
-        latent_grad = joint_grad[:, query_cols:joint].reshape(tp_count, -1, latent_cols)
-        latent_proj_grad = column_scatter(
-            jnp.take(latent_grad, places, axis=0).reshape(-1, latent_cols)
-        )
+        latent_proj_grad = column_scatter(joint_grad[:, query_cols:joint])
         gain_sums = sum_everywhere(gain_parts)
     gain_sums = gain_sums.reshape(-1)
     query_proj_grad = joint_grad[:, :query_cols].astype(F32)

time: 727 us -> 765 us (1.052)
  waiting for transfers between devices: 9.3 us -> 62.3 us
  Pallas kernels: 482 us -> 525 us
  local copies, waits for them, and re-layouts: 73.7 us -> 47 us
  starting transfers between devices: 20 us -> 0.24 us
  other arithmetic: 38.4 us -> 21.9 us
    pallas_call x2, Pallas kernels: 306 us -> 358 us  [the longest x1 312 us: expert_call(): pl.pallas_call(functools.partial(expert_kernel, cap, columns, size), out_...]
    reduce_scatter x2, waiting for transfers between devices: 0.01 us -> 46 us  [scatter(): lax.psum_scatter(part.astype(BF), 'fsdp', scatter_dimension=dimension, ti...]
    ppermute x9 -> x0, starting transfers between devices: 19.8 us -> none  [the longest x3 8.87 us: column_gather(): lax.ppermute(rows, 'tp', [((i + s) % count, i) for i in range(count)])]
    pallas_call x1, Pallas kernels: 117 us -> 99 us  [middle_call(): pl.pallas_call(functools.partial(middle_kernel, columns, size, experts, s...]
    all_gather x1, waiting for transfers between devices: 0.02 us -> 14.5 us  [column_gather(): return lax.all_gather(rows, 'tp', axis=0, tiled=True)]
    pallas_call x1, Pallas kernels: 58.4 us -> 68 us  [last_call(): pl.pallas_call(functools.partial(last_kernel, columns, size, latent_start...]
    ppermute x9 -> x0, waiting for transfers between devices: 8.51 us -> none  [the longest x3 8.5 us: swap(): return lax.ppermute(values, axis_name, [(i, i ^ bit) for i in range(count)])]
    convert_element_type x1 -> x0, local copies, waits for them, and re-layouts: 8.32 us -> none  [per_device(): joint_part = jnp.pad(joint_part.astype(BF), ((0, 0), (0, -joint % 128)))]
  transfers between devices with their start and end apart: 14 -> 6, of which waited for: 2 -> 2; matrix products, arithmetic and copies ran while one was open for 19% -> 11% of each run, Pallas kernels for 67% -> 51%
where the time goes in v5:
time: 765 us; the launch traced here: 750 us
  Pallas kernels  525 us (69%)
  matrix products  78.2 us (10%)
  waiting for transfers between devices  62.3 us (8%)
  local copies, waits for them, and re-layouts  47 us (6%)
  other arithmetic  21.9 us (3%)
  between operations  15.4 us (2%)
    pallas_call x1, Pallas kernels, expert_call(): pl.pallas_call(functools.partial(expert_kernel, cap, columns, size), out_...  312 us
    pallas_call x1, Pallas kernels, middle_call(): pl.pallas_call(functools.partial(middle_kernel, columns, size, experts, s...  99 us
    pallas_call x1, Pallas kernels, last_call(): pl.pallas_call(functools.partial(last_kernel, columns, size, latent_start...  68 us
    pallas_call x1, Pallas kernels, first_call(): pl.pallas_call(functools.partial(first_kernel, columns, size, kinds), out...  46.2 us
    reduce_scatter x2, waiting for transfers between devices, scatter(): lax.psum_scatter(part.astype(BF), 'fsdp', scatter_dimension=dimension, ti...  46 us
    unnamed x128, local copies, waits for them, and re-layouts  30.9 us
  transfers between devices with their start and end apart: 6, of which 2 were waited for; matrix products, arithmetic and copies ran while one was open for 11% of the time, Pallas kernels for 51%

profile of v5, /device:TPU:0, one launch (start us, length us, event | category | flops | bytes accessed | tf_op | source)
XLA Modules:
  0.0 750.3 jit_solution(6131865156014506515)
XLA Ops:
  7.2 1.2 copy.112
  11.5 1.3 select_maximum_fusion.refs_4_
  12.8 1.9 concatenate.43.refs_1_
  14.8 46.2 %first_gather.1 = (bf16[512,2048]{1,0:T(8,128)(2,1)}, bf16[8,256,1408]{2,1,0:T(8,128)(2,1)}, bf16[8,64,1024]{2,1,0:T(8,128)(2,1)}, bf16[512,2048]{1,0:T(8,128)(2,1)}, f32[8,16,512]{2,1,0:T(8,128)}) custom-call(bf16[128,2048]{1,0:T(8,128)(2,1)} %refs_1_.3, bf16[256,1408]{1,0:T(8,128)(2,1)} %concatenate.43.refs_1_, bf16[64,1024]{1,0:T(8,128)(2,1)} %refs_2_.2, ...), custom_call_target="tpu_custom_call" | custom-call | tf_op jit(solution)/shard_map/first_gather/pallas_call | solution.py:1100
  62.9 2.7 fusion.47
  65.9 2.1 fusion.5
  68.6 6.5 fusion.16
  75.8 2.7 copy.118
  78.5 3.1 convolution_convert_fusion.6
  81.9 1.3 slice.123
  83.1 2.0 copy.119
  86.2 1.3 copy.148
  87.6 2.0 fusion.14
  89.9 2.1 fusion.51
  92.5 1.6 copy-done.8
  94.2 1.0 copy-done.45
  95.2 2.6 convolution_convert_fusion.4.refs_0_
  98.4 14.5 %all-gather.4.cloned.1.call-done.refs_2_ = bf16[512,2048]{1,0:T(8,128)(2,1)} async-done(((bf16[128,2048]{1,0:T(8,128)(2,1)}), bf16[512,2048]{1,0:T(8,128)(2,1)}) %all-gather.4.cloned.1.call-update) | async-done | bytes 2097168 | tf_op jit(solution)/shard_map/all_gather | solution.py:99
  112.9 312.0 %experts.1 = (f32[128,2048]{1,0:T(8,128)}, bf16[512,2048]{1,0:T(8,128)(2,1)}, bf16[512,2048]{1,0:T(8,128)(2,1)}, bf16[4,4,256,2048]{3,2,1,0:T(8,128)(2,1)}, bf16...) custom-call(bf16[512,2048]{1,0:T(8,128)(2,1)} %convolution_convert_f, ...), custom_call_target="tpu_custom_call" | custom-call | flops 17179869184 | bytes 62914560 | tf_op jit(solution)/shard_map/experts/pallas_call | solution.py:926
  425.0 8.4 %fusion.52 = f32[512,1408]{1,0:T(8,128)} fusion(bf16[512,2048]{1,0:T(8,128)(2,1)} %get-tuple-element.54, bf16[2048,1408]{0,1:T(8,128)(2,1)} %all-gather.6.cloned.1.call-done), kind=kOutput, calls=%fused_computation.117 | convolution fusion | flops 2952790016 | bytes 10747904 | tf_op jit(solution)/shard_map/dot_general | solution.py:1999
  433.4 5.1 multiply_convert_fusion.2
  439.6 5.4 convolution_convert_fusion.1
  445.1 3.3 convolution_convert_fusion.2
  448.4 8.5 %add_convert_fusion.1.refs_0_ = bf16[512,2048]{1,0:T(8,128)(2,1)} fusion(bf16[512,2048]{1,0:T(8,128)(2,1)} %get-tuple-element.55, bf16[2048,1408]{0,1:T(8,128)(2,1)} %all-gather.6.cloned.1.call-done, bf16[512,704]{1,0:T(8,128)(2,1)} %copy-done.54, bf16[512,704]{1,0:T(8,128)(2,1)} %copy-done.53), kind=kOutput, calls=%fused_computation.13 | convolution fusion | flops 2958819328 | bytes 11403264 | tf_op jit(solution)/shard_map/dot_general | solution.py:2007
  456.9 99.0 %middle.1 = (f32[128,2048]{1,0:T(8,128)}, bf16[512,2048]{1,0:T(8,128)(2,1)}, f32[1,2048]{1,0:T(1,128)}, bf16[512,2048]{1,0:T(8,128)(2,1)}, f32[2,352,2048]{2,1,0...) custom-call(bf16[512,2048]{1,0:T(8,128)(2,1)} %add_convert_fusion.1., ...), custom_call_target="tpu_custom_call" | custom-call | flops 19327352832 | bytes 41943040 | tf_op jit(solution)/shard_map/middle/pallas_call | solution.py:1448
  555.8 5.9 add_convert_fusion
  563.0 1.0 copy-done.46
  564.0 3.0 convolution_convert_fusion.7
  568.3 1.2 multiply_convert_fusion
  572.1 1.5 copy-done.4
  575.0 1.0 multiply_convert_fusion.4
  576.0 2.0 copy.132
  578.1 2.3 multiply_bitcast_fusion.1
  581.6 1.1 slice_reduce_fusion
  583.4 8.0 %fusion.4 = (f32[2048]{0:T(1024)S(1)}, bf16[512,2048]{1,0:T(8,128)(2,1)}) fusion(bf16[512,2048]{1,0:T(8,128)(2,1)S(1)} %copy-done.15, f32[512]{0:T(512)S(1)} %copy-done.44, bf16[512,1408]{0,1:T(8,128)(2,1)S(1)} %broadcast_dynamic-update-slice_fusion, bf16[2048,1408]{1,0:T(8,128)(2,1)} %bitcast.80), kind=kOutput, calls=%fused_computation.8 | convolution fusion | flops 2958030848 | bytes 11413504 | tf_op jit(solution)/shard_map/dot_general | solution.py:2081
  591.5 1.9 convolution_convert_fusion.5.refs_5_
  593.4 2.6 convolution_convert_fusion.3.refs_6_
  596.0 5.7 convolution_convert_fusion.refs_4_
  601.7 68.0 %last_sums.1 = (f32[128,2048]{1,0:T(8,128)S(1)}, bf16[256,1408]{1,0:T(8,128)(2,1)S(1)}, bf16[64,1024]{1,0:T(8,128)(2,1)S(1)}, bf16[512,256]{1,0:T(8,128)(2,1)S(1...) custom-call(bf16[512,2048]{1,0:T(8,128)(2,1)} %get-tuple-element.145, ...), custom_call_target="tpu_custom_call" | custom-call | tf_op jit(solution)/shard_map/last_sums/pallas_call | solution.py:1721
  673.3 2.0 add_convert_fusion.2
  675.3 1.9 convert_element_type.289
  677.2 46.0 %reduce-scatter.6.cloned.1.call-done = bf16[256,1408]{1,0:T(8,128)(2,1)} async-done(((bf16[2048,1408]{1,0:T(8,128)(2,1)}), bf16[256,1408]{1,0:T(8,128)(2,1)}) %reduce-scatter.6.cloned.1.call-update) | async-done | bytes 720912 | tf_op jit(solution)/shard_map/reduce_scatter | solution.py:2085
  723.2 1.3 fusion.49
  724.5 1.1 copy.134
  725.6 1.1 copy.135
  728.4 6.0 copy.162
  734.4 6.0 copy.163
  740.4 2.5 copy.164
  (178 shorter events, 23.7 us)
Async XLA Ops:
  7.2 105.7 %all-gather.4.cloned.1.call-start = ((), (), s32[]{:S(2)}) async-start(), calls=%async_computation.3 | async-start | bytes 2621440 | tf_op jit(solution)/shard_map/all_gather | solution.py:99
  9.2 51.9 %copy-start.29 = (bf16[256,704]{0,1:T(8,128)(2,1)S(1)}, bf16[256,704]{0,1:T(8,128)(2,1)}, u32[]{:S(2)}) copy-start(bf16[256,704]{0,1:T(8,128)(2,1)} %param.31) | copy-start | bytes 1081348
  9.2 51.9 %copy-start.30 = (bf16[256,704]{0,1:T(8,128)(2,1)S(1)}, bf16[256,704]{0,1:T(8,128)(2,1)}, u32[]{:S(2)}) copy-start(bf16[256,704]{0,1:T(8,128)(2,1)} %param.30) | copy-start | bytes 1081348
  61.0 363.9 %all-gather.6.cloned.1.call-start = ((), (), s32[]{:S(2)}) async-start(), calls=%async_computation.4 | async-start | bytes 6488064 | tf_op jit(solution)/shard_map/all_gather | solution.py:1869
  62.0 371.4 %all-gather.8.cloned.1.call-start = ((), (), s32[]{:S(2)}) async-start(), calls=%async_computation.5 | async-start | bytes 3244032 | tf_op jit(solution)/shard_map/all_gather | solution.py:1891
  62.8 610.5 %reduce-scatter.4.cloned.1.call-start = ((), (), s32[]{:S(2)}) async-start(), calls=%async_computation.6 | async-start | bytes 2621440 | tf_op jit(solution)/shard_map/reduce_scatter | solution.py:103
  62.8 18.7 %copy-start.31 = (f32[512]{0:T(512)}, f32[512]{0:T(512)S(1)}, u32[]{:S(2)}) copy-start(f32[512]{0:T(512)S(1)} %iota_convert_fusion) | copy-start | bytes 6148
  62.8 18.7 %copy-start.41 = (f32[32]{0:T(128)}, f32[32]{0:T(128)S(1)}, u32[]{:S(2)}) copy-start(f32[32]{0:T(128)S(1)} %multiply_power_fusion) | copy-start | bytes 388
  65.9 9.2 %copy-start.1 = (f32[2048,1]{0,1:T(1,128)}, f32[2048,1]{0,1:T(1,128)S(1)}, u32[]{:S(2)}) copy-start(f32[2048,1]{0,1:T(1,128)S(1)} %copy.150) | copy-start | bytes 24580
  75.1 6.8 copy-start.3
  75.7 2.8 copy-start.35
  75.8 2.7 copy-start.33
  81.8 5.6 copy-start.21
  81.8 5.6 copy-start.23
  85.2 4.4 copy-start.6
  87.5 2.1 copy-start.25
  87.5 2.1 copy-start.27
  87.6 2.1 copy-start.12
  87.6 2.1 copy-start.39
  92.0 2.1 copy-start.8
  92.0 2.1 copy-start.37
  92.0 3.1 copy-start.45
  94.2 3.6 copy-start.48
  425.0 8.5 %copy-start.47 = (bf16[512,2048]{1,0:T(8,128)(2,1)S(1)}, bf16[512,2048]{1,0:T(8,128)(2,1)}, u32[]{:S(2)}) copy-start(bf16[512,2048]{1,0:T(8,128)(2,1)} %all-gather.4.cloned.1.call-done.refs_2_) | copy-start | bytes 6291460
  433.4 6.2 copy-start.52
  438.5 6.6 copy-start.51
  561.8 113.5 %reduce-scatter.8.cloned.1.call-start = ((), (), s32[]{:S(2)}) async-start(), calls=%async_computation.8 | async-start | bytes 3244032 | tf_op jit(solution)/shard_map/reduce_scatter | solution.py:2085
  562.4 160.9 %reduce-scatter.6.cloned.1.call-start = ((), (), s32[]{:S(2)}) async-start(), calls=%async_computation.7 | async-start | bytes 6488064 | tf_op jit(solution)/shard_map/reduce_scatter | solution.py:2085
  564.0 3.2 copy-start.9
  564.0 3.5 copy-start.14
  564.0 3.5 copy-start.38
  570.9 2.7 copy-start.4
  572.0 2.1 copy-start.36
  572.0 2.9 copy-start.10
  575.0 3.1 copy-start.7
  578.1 2.4 copy-start.22
  578.1 2.4 copy-start.24
  580.6 2.1 copy-start.32
  580.6 2.1 copy-start.42
  580.7 2.7 copy-start.15
  580.7 2.7 copy-start.44
  583.4 8.1 %copy-start.40 = (f32[1,2048]{1,0:T(1,128)S(1)}, f32[1,2048]{1,0:T(1,128)}, u32[]{:S(2)}) copy-start(f32[1,2048]{1,0:T(1,128)} %get-tuple-element.65) | copy-start | bytes 24580
  583.4 8.1 %copy-start.11 = (bf16[512,4,256]{0,2,1:T(8,128)(2,1)S(1)}, bf16[512,4,256]{0,2,1:T(8,128)(2,1)}, u32[]{:S(2)}) copy-start(bf16[512,4,256]{0,2,1:T(8,128)(2,1)} %copy-done.10) | copy-start | bytes 3145732
  593.4 2.6 copy-start.2
  596.0 5.7 copy-start
  669.6 3.7 copy-start.19
  728.4 12.0 %slice-start = ((s8[5767168]{0:T(1024)(128)(4,1)}), s8[4194304]{0:T(1024)(128)(4,1)S(1)}, s32[]{:S(2)}) async-start(s8[5767168]{0:T(1024)(128)(4,1)} %bitcast.68), calls=%async_computation.9 | async-start | bytes 8388608
  734.4 6.0 slice-start.1
  (15 other events, 21.3 us)
Sparse Core Ops, SparseCore 0:
  61.1 51.6 all-gather.3
  115.3 66.5 all-gather.5
  183.8 43.4 all-gather.7
  561.9 42.1 reduce-scatter.3
  607.7 53.2 reduce-scatter.7
  664.8 58.3 reduce-scatter.5

commit v6 on v5

--- a/solution.py
+++ b/solution.py
@@ -442,6 +442,198 @@
     pl.semaphore_wait(barrier, len(devices))
 
 
+class ColumnGather:
+    def __init__(self, blocks, rows_of, sends, arrivals, base):
+        self.blocks, self.rows_of = blocks, rows_of
+        self.sends, self.arrivals, self.base = sends, arrivals, base
+        self.row = lax.axis_index("tp")
+        self.column = column_neighbours(4)
+
+    def direct(self, s):
+        place = self.blocks.at[self.rows_of(0)]
+        return mesh_copy(
+            place, place, self.sends, self.arrivals, self.base + s - 1, self.column[s - 1]
+        )
+
+    def start(self):
+        @pl.when(self.row < 3)
+        def _():
+            self.direct(1).start()
+
+        @pl.when(self.row > 0)
+        def _():
+            self.direct(3).start()
+
+        self.direct(2).start()
+
+    def wait(self, b):
+        self.direct(4 - b).wait_recv()
+        if b == 2:
+
+            @pl.when(self.row == 1)
+            def _():
+                self.relay(3).start()
+
+            @pl.when(self.row == 2)
+            def _():
+                self.relay(1).start()
+
+    def relay(self, s):
+        place = self.blocks.at[self.rows_of(2)]
+        return pltpu.make_async_remote_copy(
+            src_ref=place,
+            dst_ref=place,
+            send_sem=self.sends.at[self.base + 3],
+            recv_sem=self.arrivals.at[self.base + 3 - s],
+            device_id=self.column[s - 1],
+            device_id_type=pl.DeviceIdType.MESH,
+        )
+
+    def drain(self):
+        @pl.when(self.row < 3)
+        def _():
+            self.direct(1).wait_send()
+
+        @pl.when(self.row > 0)
+        def _():
+            self.direct(3).wait_send()
+
+        self.direct(2).wait_send()
+
+        @pl.when(self.row == 1)
+        def _():
+            self.relay(3).wait_send()
+
+        @pl.when(self.row == 2)
+        def _():
+            self.relay(1).wait_send()
+
+
+class ColumnSum:
+    def __init__(self, parts, rows_of, landed, relayed, sends, arrivals, base):
+        self.parts, self.rows_of, self.landed, self.relayed = parts, rows_of, landed, relayed
+        self.sends, self.arrivals, self.base = sends, arrivals, base
+        self.row = lax.axis_index("tp")
+        self.column = column_neighbours(4)
+
+    def direct(self, s):
+        return mesh_copy(
+            self.parts.at[self.rows_of(s)],
+            self.landed.at[s - 1],
+            self.sends,
+            self.arrivals,
+            self.base + s - 1,
+            self.column[s - 1],
+        )
+
+    def first_leg(self, s):
+        return mesh_copy(
+            self.parts.at[self.rows_of(4 - s)],
+            self.relayed.at[0],
+            self.sends,
+            self.arrivals,
+            self.base + 3,
+            self.column[s - 1],
+        )
+
+    def own_part(self, local):
+        return pltpu.make_async_copy(self.parts.at[self.rows_of(2)], self.relayed.at[1], local)
+
+    def second_leg(self):
+        return mesh_copy(
+            self.relayed.at[1],
+            self.landed.at[1],
+            self.sends,
+            self.arrivals,
+            self.base + 1,
+            self.column[1],
+        )
+
+    def start(self, local):
+        @pl.when(self.row == 0)
+        def _():
+            self.first_leg(1).start()
+
+        @pl.when(self.row == 3)
+        def _():
+            self.first_leg(3).start()
+
+        @pl.when((self.row == 1) | (self.row == 2))
+        def _():
+            self.own_part(local).start()
+
+        @pl.when(self.row < 3)
+        def _():
+            self.direct(1).start()
+
+        @pl.when(self.row > 0)
+        def _():
+            self.direct(3).start()
+
+        @pl.when((self.row == 0) | (self.row == 3))
+        def _():
+            self.direct(2).start()
+
+    def middle(self, local):
+        @pl.when((self.row == 1) | (self.row == 2))
+        def _():
+            self.own_part(local).wait()
+            self.first_leg(1).wait_recv()
+
+            def some(i, carry):
+                rows = pl.ds(pl.multiple_of(i * 32, 32), 32)
+                self.relayed[1, rows, :] = (
+                    self.relayed[0, rows, :].astype(F32) + self.relayed[1, rows, :].astype(F32)
+                ).astype(BF)
+                return carry
+
+            lax.fori_loop(0, self.relayed.shape[1] // 32, some, 0)
+            self.second_leg().start()
+
+    def clear(self):
+        @pl.when(self.row == 0)
+        def _():
+            self.landed[0] = jnp.zeros(self.landed.shape[1:], BF)
+
+        @pl.when(self.row == 3)
+        def _():
+            self.landed[2] = jnp.zeros(self.landed.shape[1:], BF)
+
+    def total(self, own):
+        @pl.when(self.row > 0)
+        def _():
+            self.direct(1).wait_recv()
+
+        @pl.when(self.row < 3)
+        def _():
+            self.direct(3).wait_recv()
+
+        self.direct(2).wait_recv()
+        total = own.astype(F32)
+        for s in range(3):
+            total = total + self.landed[s].astype(F32)
+        return total
+
+    def drain(self):
+        @pl.when(self.row == 0)
+        def _():
+            self.first_leg(1).wait_send()
+
+        @pl.when(self.row == 3)
+        def _():
+            self.first_leg(3).wait_send()
+
+        @pl.when(self.row < 3)
+        def _():
+            self.direct(1).wait_send()
+
+        @pl.when(self.row > 0)
+        def _():
+            self.direct(3).wait_send()
+
+        self.direct(2).wait_send()
+
+
 class PlaneGather:
     def __init__(self, own, others, rows_of, sends, arrivals, base):
         self.own, self.others, self.rows_of = own, others, rows_of
@@ -527,6 +719,7 @@
         attn_v,
         tokens_v,
         arrived_v,
+        relayed_v,
         mixed_v,
         ffn_v,
         xb,
@@ -551,6 +744,7 @@
         spill,
     ) = refs
     count = QUARTET
+    previous, following = {2: 0, 1: 2, 3: 1}, {0: 2, 2: 1, 1: 3}
     experts, local_hidden = gate_in.shape[:2]
     width = xb.shape[2]
     pad = down.shape[1]
@@ -570,7 +764,8 @@
     dy_gather = PlaneGather(
         cotan_in, dy_others, lambda b: pl.ds(0, SEQ), sends, arrivals, reserve(8)
     )
-    rs_base, ag_base = reserve(columns - 1), reserve(columns - 1)
+    gather = ColumnGather(ffn_all, rows_of, sends, arrivals, reserve(4))
+    summed = ColumnSum(attn_in, rows_of, arrived_v, relayed_v, sends, arrivals, reserve(4))
     plane = PlaneSum(
         lambda r, h: others.at[r // 2],
         chip,
@@ -584,19 +779,7 @@
     )
 
     greet([partner, along, across] + column)
-    sums = [
-        mesh_copy(
-            attn_in.at[rows_of(s)],
-            arrived_v.at[s - 1],
-            sends,
-            arrivals,
-            rs_base + s - 1,
-            column[s - 1],
-        )
-        for s in range(1, columns)
-    ]
-    for copy in sums:
-        copy.start()
+    summed.start(local.at[2])
     first = [
         pltpu.make_async_copy(attn_in.at[rows_of(0)], attn_v, local.at[0]),
         pltpu.make_async_copy(tokens_in, tokens_v, local.at[1]),
@@ -613,17 +796,20 @@
     for e in range(experts):
         weights_in += [
             pltpu.make_async_copy(
-                gate_in.at[e], gate_up.at[e, pl.ds(0, local_hidden)], local.at[2 + 3 * e]
+                gate_in.at[e], gate_up.at[e, pl.ds(0, local_hidden)], local.at[3 + 3 * e]
             ),
             pltpu.make_async_copy(
-                up_in.at[e], gate_up.at[e, pl.ds(pad, local_hidden)], local.at[3 + 3 * e]
+                up_in.at[e], gate_up.at[e, pl.ds(pad, local_hidden)], local.at[4 + 3 * e]
             ),
             pltpu.make_async_copy(
-                down_in.at[e], down.at[e, pl.ds(0, local_hidden)], local.at[4 + 3 * e]
+                down_in.at[e], down.at[e, pl.ds(0, local_hidden)], local.at[5 + 3 * e]
             ),
         ]
     for copy in weights_in:
         copy.start()
+
+    summed.clear()
+    summed.middle(local.at[2])
 
     earlier = lax.broadcasted_iota(jnp.int32, (size, size), 0)
     later = lax.broadcasted_iota(jnp.int32, (size, size), 1)
@@ -651,10 +837,7 @@
 
     for copy in first:
         copy.wait()
-    total = tokens_v[...].astype(F32) + attn_v[...].astype(F32)
-    for s in range(1, columns):
-        sums[s - 1].wait_recv()
-        total = total + arrived_v[s - 1].astype(F32)
+    total = summed.total(attn_v[...]) + tokens_v[...].astype(F32)
     mixed_v[...] = total
     inverse = lax.rsqrt(jnp.mean(total * total, axis=1, keepdims=True) + EPSILON)
     ffn_v[...] = (total * inverse * gain_ref[...]).astype(BF)
@@ -664,23 +847,11 @@
     mixed_copy.start()
     own_copy.wait()
 
-    rows_out = [
-        mesh_copy(
-            ffn_all.at[rows_of(0)],
-            ffn_all.at[rows_of(0)],
-            sends,
-            arrivals,
-            ag_base + s - 1,
-            column[s - 1],
-        )
-        for s in range(1, columns)
-    ]
-    for copy in rows_out:
-        copy.start()
+    gather.start()
 
     def enter(b):
         if b > 0:
-            rows_out[columns - b - 1].wait_recv()
+            gather.wait(b)
         x_gather.start(b)
 
     def ready(b):
@@ -689,21 +860,16 @@
     def source(own, gathered, r):
         return own if r == 0 else gathered.at[r - 1]
 
-    def load(b):
-        copies = []
-        for r in range(8):
-            place = pl.ds(r % 2 * size, size)
-            for k, (own, gathered, target) in enumerate(
-                ((ffn_all, x_others, xb), (cotan_in, dy_others, db))
-            ):
-                copies.append(
-                    pltpu.make_async_copy(
-                        source(own, gathered, r).at[rows_of(b)],
-                        target.at[r // 2, place],
-                        loads.at[2 * r + k],
-                    )
-                )
-        return copies
+    def load(b, k):
+        own, gathered, target = ((ffn_all, x_others, xb), (cotan_in, dy_others, db))[k]
+        return [
+            pltpu.make_async_copy(
+                source(own, gathered, r).at[rows_of(b)],
+                target.at[r // 2, pl.ds(r % 2 * size, size)],
+                loads.at[8 * k + r],
+            )
+            for r in range(8)
+        ]
 
     def slots_of(table, b, q):
         place = pl.ds(pl.multiple_of((lax.axis_index("tp") + b) % columns * size, size), size)
@@ -740,17 +906,17 @@
         ]
 
     def front(b):
-        copies = load(b)
-        for copy in copies:
+        x_load, dy_load = load(b, 0), load(b, 1)
+        for copy in x_load + (dy_load if b == 0 else []):
             copy.start()
         if b == 0:
             for copy in weights_in:
                 copy.wait()
         if b > 0:
-            for copy in spills(b - 1):
+            for copy in spills(previous[b]):
                 copy.wait()
         for q in range(count):
-            for copy in copies[4 * q : 4 * q + 4]:
+            for copy in x_load[2 * q : 2 * q + 2] + dy_load[2 * q : 2 * q + 2]:
                 copy.wait()
             hit = select_rows(slots_of(slot_table, b, q), experts, wide)
             weights = slot_weights(hit, slots_of(weight_table, b, q), experts, wide)
@@ -767,6 +933,9 @@
                 return carry
 
             lax.fori_loop(0, width // tile, spread, 0)
+        if b in following:
+            for copy in load(following[b], 1):
+                copy.start()
         out_copies = spills(b)
         out_copies[0].start()
         out_copies[1].start()
@@ -798,7 +967,7 @@
         out_copies[3].start()
         if b > 0:
             for i in range(4):
-                plane.pair(i, b - 1).wait_send()
+                plane.pair(i, previous[b]).wait_send()
 
         def keep(q, cols, value):
             chip[q, b, :, cols] = value[:size]
@@ -842,69 +1011,65 @@
     def out_copy(b):
         return pltpu.make_async_copy(db, out_all.at[b], local.at[0])
 
-    def send_sums(b):
-        plane.on_chip(3, [b], False)
-        plane.send(1, [b])
-        plane.on_chip(1, [b], False)
-        plane.on_chip(2, [b], False)
-        plane.send(0, [b])
-        plane.on_chip(0, [b], False)
-
     final = columns - 1
     enter(0)
     dy_gather.forward(0)
+    enter(2)
+    x_gather.forward(0)
     enter(1)
-    x_gather.forward(0)
-    enter(2)
-    x_gather.forward(1)
     x_gather.last(0)
     dy_gather.last(0)
     ready(0)
     dy_gather.arrived(0, [2, 5, 6, 7])
     front(0)
-    for b in range(3, columns):
-        enter(b)
     x_gather.forward(2)
+    enter(3)
+    x_gather.forward(1)
+    x_gather.last(2)
+    ready(2)
     x_gather.last(1)
+    front(2)
+    x_gather.forward(3)
     ready(1)
+    plane.send_first([0], False)
     front(1)
-    for b in range(2, columns):
-        if b > 2:
-            x_gather.forward(b)
-        x_gather.last(b)
-        ready(b)
-        send_sums(b - 2)
-        if b > 2:
-            plane.send_second([b - 3])
-        front(b)
-    send_sums(final - 1)
-    plane.send_second([final - 2])
-    for copy in spills(final):
+    x_gather.last(3)
+    ready(3)
+    plane.send_first([2], False)
+    plane.send_second([0])
+    front(3)
+    plane.send_first([1], False)
+    plane.send_second([2])
+    for copy in spills(3):
         copy.wait()
     out_part(0)
-    send_sums(final)
-    plane.send_second([final - 1])
+    plane.send_first([3], False)
+    plane.send_second([1])
+    done = {}
+
+    def close(b):
+        plane.finish([b])
+        done[b] = pltpu.make_async_copy(chip.at[0, b], dx_out.at[rows_of(b)], loads.at[b])
+        done[b].start()
+
     out_part(1)
-    plane.send_second([final])
-    for b in range(2, columns):
-        out_part(b)
-    plane.finish(range(columns))
-    done = [
-        pltpu.make_async_copy(chip.at[0, b], dx_out.at[rows_of(b)], loads.at[b])
-        for b in range(columns)
-    ]
-    for copy in done:
-        copy.start()
-    for copy in done:
-        copy.wait()
+    plane.send_second([3])
+    close(0)
+    out_part(2)
+    close(2)
+    out_part(3)
+    close(1)
+    close(3)
+    for b in range(columns):
+        done[b].wait()
     out_copy(final).wait()
     mixed_copy.wait()
 
     for b in range(columns):
         x_gather.drain(b)
     dy_gather.drain(0)
-    for copy in sums + rows_out:
-        copy.wait_send()
+    gather.drain()
+    summed.drain()
     plane.drain(final)
 
 
@@ -922,7 +1087,7 @@
 
     landing, scratch = plane_sum_space(columns, size, width)
     remote, near = plane_sum_sizes(columns)
-    remote = remote + 8 * columns + 8 + 2 * (columns - 1)
+    remote = remote + 8 * columns + 8 + 8
     results = pl.pallas_call(
         functools.partial(expert_kernel, cap, columns, size),
         out_shape=[
@@ -944,6 +1109,7 @@
             pltpu.VMEM((size, width), BF),
             pltpu.VMEM((size, width), BF),
             pltpu.VMEM((columns - 1, size, width), BF),
+            pltpu.VMEM((2, size, width), BF),
             pltpu.VMEM((size, width), F32),
             pltpu.VMEM((size, width), BF),
             pltpu.VMEM((QUARTET, HALF, width), BF),
@@ -963,7 +1129,7 @@
             pltpu.VMEM((8 * experts, SEQ), F32),
             pltpu.SemaphoreType.DMA((remote,)),
             pltpu.SemaphoreType.DMA((remote,)),
-            pltpu.SemaphoreType.DMA((2 + 3 * experts,)),
+            pltpu.SemaphoreType.DMA((3 + 3 * experts,)),
             pltpu.SemaphoreType.DMA((16,)),
             pltpu.SemaphoreType.DMA((near,)),
             pltpu.SemaphoreType.DMA((4,)),
@@ -999,19 +1165,14 @@
         6: along[0] + across[0] - place,
     }
     greet([partner, along, across] + column)
-    rows_out = [
-        mesh_copy(
-            tokens_in,
-            tokens_all.at[rows_of(0)],
-            sends,
-            arrivals,
-            8 * amount + s - 1,
-            column[s - 1],
-        )
-        for s in range(1, columns)
-    ]
-    for copy in rows_out:
-        copy.start()
+    here = [pltpu.make_async_copy(tokens_in, tokens_v, local.at[0])]
+    there = [pltpu.make_async_copy(tokens_v, tokens_all.at[rows_of(0)], local.at[0])]
+    here[0].start()
+    here[0].wait()
+    there[0].start()
+    there[0].wait()
+    gather = ColumnGather(tokens_all, rows_of, sends, arrivals, 8 * amount)
+    gather.start()
     plans = []
     for k, kind in enumerate(kinds):
         own, everything = own_in[k], alls[k]
@@ -1046,8 +1207,7 @@
     for copies in plans:
         for copy in copies[:3]:
             copy.start()
-    here = [pltpu.make_async_copy(tokens_in, tokens_v, local.at[0])]
-    there = [pltpu.make_async_copy(tokens_v, tokens_all.at[rows_of(0)], local.at[0])]
+    here, there = [], []
     for k, kind in enumerate(kinds):
         rows, cols = own_in[k].shape
         if kind == "relative":
@@ -1071,6 +1231,7 @@
         copies[1].wait_recv()
         copies[4].start()
         copies[6].start()
+    gather.wait(2)
     for copies in plans:
         copies[3].wait_recv()
         copies[4].wait_recv()
@@ -1078,11 +1239,12 @@
     for copies in plans:
         for i in (2, 5, 6, 7):
             copies[i].wait_recv()
-    for copy in rows_out:
-        copy.wait_recv()
+    gather.wait(1)
+    gather.wait(3)
     for copy in there:
         copy.wait()
-    for copies in plans + [rows_out]:
+    gather.drain()
+    for copies in plans:
         for copy in copies:
             copy.wait_send()
 
@@ -1091,7 +1253,7 @@
     columns = lax.axis_size("tp")
     size, width = tokens.shape
     anywhere = pl.BlockSpec(memory_space=pl.ANY)
-    copies = 8 * len(owns) + columns - 1
+    copies = 8 * len(owns) + 4
 
     def gathered(own, kind):
         rows, cols = own.shape
@@ -1135,7 +1297,7 @@
 
     def mine(self, i, h):
         return pltpu.make_async_copy(
-            self.source(2 * i, h), self.chip.at[i, h], self.local.at[1 + i * self.parts + h]
+            self.source(2 * i, h), self.chip.at[i, h], self.local.at[4 + i * self.parts + h]
         )
 
     def begin(self):
@@ -1144,29 +1306,39 @@
                 self.pair(i, h).start()
                 self.mine(i, h).start()
 
-    def add(self, i, h, start, size, landed):
-        fetch = pltpu.make_async_copy(
-            landed, self.stage.at[pl.ds(start, size)], self.local.at[0]
-        )
-        fetch.start()
-        fetch.wait()
+    def fetch(self, landed, slot):
+        size = landed.shape[0]
+        return pltpu.make_async_copy(
+            landed, self.stage.at[slot, pl.ds(0, size)], self.local.at[slot]
+        )
+
+    def add(self, i, h, start, size, slot):
         some = min(32, size)
 
         def one(n, carry):
             rows = pl.ds(pl.multiple_of(start + n * some, some), some)
+            from_rows = pl.ds(pl.multiple_of(n * some, some), some)
             self.chip[i, h, rows, :] = (
-                self.chip[i, h, rows, :].astype(F32) + self.stage[rows, :].astype(F32)
+                self.chip[i, h, rows, :].astype(F32) + self.stage[slot, from_rows, :].astype(F32)
             ).astype(BF)
             return carry
 
         lax.fori_loop(0, size // some, one, 0)
 
-    def on_chip(self, i, parts=None, fetched=True):
+    def send_first(self, parts=None, fetched=True):
         for h in range(self.parts) if parts is None else parts:
-            if fetched:
-                self.mine(i, h).wait()
-            self.pair(i, h).wait_recv()
-            self.add(i, h, 0, self.rows, self.theirs.at[i, h])
+            for i in (3, 1, 2, 0):
+                self.pair(i, h).wait_recv()
+                self.fetch(self.theirs.at[i, h], i).start()
+            for i in (3, 1, 2, 0):
+                if fetched:
+                    self.mine(i, h).wait()
+                self.fetch(self.theirs.at[i, h], i).wait()
+                self.add(i, h, 0, self.rows, i)
+                if i == 3:
+                    self.send(1, [h])
+                if i == 2:
+                    self.send(0, [h])
 
     def link(self, stage_number, side, h):
         first_hop, second_hop = (
@@ -1185,18 +1357,8 @@
             second_hop if stage_number == 2 else first_hop,
         )
 
-    def take(self, stage_number, side, h, i):
-        self.link(stage_number, side, h).wait_recv()
-        place = (stage_number * 2 + side) * self.parts + h
-        self.add(i, h, side * (self.rows // 2), self.rows // 2, self.links.at[place])
-
-    def send_first(self):
-        self.on_chip(3)
-        self.send(1)
-        self.on_chip(1)
-        self.on_chip(2)
-        self.send(0)
-        self.on_chip(0)
+    def landed(self, stage_number, side, h):
+        return self.links.at[(stage_number * 2 + side) * self.parts + h]
 
     def send(self, stage_number, parts=None):
         for h in range(self.parts) if parts is None else parts:
@@ -1204,16 +1366,28 @@
                 self.link(stage_number, side, h).start()
 
     def send_second(self, parts=None):
+        half = self.rows // 2
         for h in range(self.parts) if parts is None else parts:
             for side in range(2):
-                self.take(1, side, h, (2, 1)[side])
+                self.link(1, side, h).wait_recv()
+                self.fetch(self.landed(1, side, h), side).start()
+            for side in range(2):
+                self.fetch(self.landed(1, side, h), side).wait()
+                self.add((2, 1)[side], h, side * half, half, side)
                 self.link(2, side, h).start()
 
     def finish(self, parts=None):
+        half = self.rows // 2
         for h in range(self.parts) if parts is None else parts:
             for stage_number in (0, 2):
                 for side in range(2):
-                    self.take(stage_number, side, h, 0)
+                    self.link(stage_number, side, h).wait_recv()
+                    self.fetch(self.landed(stage_number, side, h), stage_number + side).start()
+            for stage_number in (0, 2):
+                for side in range(2):
+                    slot = stage_number + side
+                    self.fetch(self.landed(stage_number, side, h), slot).wait()
+                    self.add(0, h, side * half, half, slot)
 
     def drain(self, first_part=0):
         for h in range(self.parts):
@@ -1226,7 +1400,7 @@
 
 
 def plane_sum_sizes(parts):
-    return 10 * parts, 1 + 4 * parts
+    return 10 * parts, 4 + 4 * parts
 
 
 def plane_sum_space(parts, rows, width):
@@ -1234,7 +1408,7 @@
         jax.ShapeDtypeStruct((4, parts, rows, width), BF),
         jax.ShapeDtypeStruct((6 * parts, rows // 2, width), BF),
     ]
-    scratch = [pltpu.VMEM((4, parts, rows, width), BF), pltpu.VMEM((rows, width), BF)]
+    scratch = [pltpu.VMEM((4, parts, rows, width), BF), pltpu.VMEM((4, rows, width), BF)]
     return landing, scratch
 
 
@@ -1262,6 +1436,7 @@
         stage,
         own_v,
         arrived_v,
+        relayed_v,
         mixed_v,
         cotan_v,
         proj_v,
@@ -1293,30 +1468,9 @@
     )
     base = plane_sum_sizes(columns)[0]
     rows_of = block_rows(columns, size)
-    sums = [
-        mesh_copy(
-            d_ffn_in.at[rows_of(s)],
-            arrived_v.at[s - 1],
-            sends,
-            arrivals,
-            base + s - 1,
-            column[s - 1],
-        )
-        for s in range(1, columns)
-    ]
-    rows_out = [
-        mesh_copy(
-            d_proj_all.at[rows_of(0)],
-            d_proj_all.at[rows_of(0)],
-            sends,
-            arrivals,
-            base + columns - 1 + s - 1,
-            column[s - 1],
-        )
-        for s in range(1, columns)
-    ]
-    for copy in sums:
-        copy.start()
+    summed = ColumnSum(d_ffn_in, rows_of, arrived_v, relayed_v, sends, arrivals, base)
+    gather = ColumnGather(d_proj_all, rows_of, sends, arrivals, base + 4)
+    summed.start(local.at[3])
     first = [
         pltpu.make_async_copy(d_ffn_in.at[rows_of(0)], own_v, local.at[0]),
         pltpu.make_async_copy(mixed_in, mixed_v, local.at[1]),
@@ -1325,6 +1479,7 @@
     for copy in first:
         copy.start()
     plane.begin()
+    summed.clear()
 
     width = xk.shape[2]
     pad = hk.shape[2]
@@ -1382,9 +1537,12 @@
 
     for copy in fetch(0):
         copy.start()
+    for k in range(2):
+        job(k)
+    summed.middle(local.at[3])
     early = len(jobs) // 2
     late = 3 * len(jobs) // 4
-    for k in range(early):
+    for k in range(2, early):
         job(k)
     plane.send_first()
     for k in range(early, late):
@@ -1392,10 +1550,7 @@
 
     for copy in first:
         copy.wait()
-    total = own_v[...].astype(F32)
-    for s in range(1, columns):
-        sums[s - 1].wait_recv()
-        total = total + arrived_v[s - 1].astype(F32)
+    total = summed.total(own_v[...])
     mixed = mixed_v[...]
     inverse = lax.rsqrt(jnp.mean(mixed * mixed, axis=1, keepdims=True) + EPSILON)
     unit = mixed * inverse
@@ -1410,28 +1565,28 @@
     mixed_copy = pltpu.make_async_copy(mixed_v, d_mixed_out, local.at[1])
     mixed_copy.start()
     own_copy.wait()
-    for copy in rows_out:
-        copy.start()
+    gather.start()
     for k in range(late, len(jobs)):
         job(k)
     plane.send_second()
+    gather.wait(2)
     plane.finish()
     done = [
-        pltpu.make_async_copy(chip.at[0, h], routed_out.at[rows_of(h)], sum_local.at[1 + h])
+        pltpu.make_async_copy(chip.at[0, h], routed_out.at[rows_of(h)], sum_local.at[4 + h])
         for h in range(columns)
     ]
     for copy in done:
         copy.start()
-    for copy in rows_out:
-        copy.wait_recv()
+    gather.wait(1)
+    gather.wait(3)
     for copy in done + [mixed_copy]:
         copy.wait()
     for e in range(max(0, experts - 2), experts):
         for copy in write(e):
             copy.wait()
     plane.drain()
-    for copy in sums + rows_out:
-        copy.wait_send()
+    gather.drain()
+    summed.drain()
 
 
 def middle_call(d_ffn, mixed, cotan, gain, out_all, kept, local_hidden):
@@ -1443,7 +1598,7 @@
     held = pl.BlockSpec(memory_space=pltpu.VMEM)
     landing, scratch = plane_sum_space(columns, size, width)
     remote, near = plane_sum_sizes(columns)
-    remote = remote + 2 * (columns - 1)
+    remote = remote + 8
     grad = jax.ShapeDtypeStruct((experts, local_hidden, width), F32)
     results = pl.pallas_call(
         functools.partial(middle_kernel, columns, size, experts, steps, local_hidden),
@@ -1463,6 +1618,7 @@
         + [
             pltpu.VMEM((size, width), BF),
             pltpu.VMEM((columns - 1, size, width), BF),
+            pltpu.VMEM((2, size, width), BF),
             pltpu.VMEM((size, width), F32),
             pltpu.VMEM((size, width), BF),
             pltpu.VMEM((size, width), BF),
@@ -1473,7 +1629,7 @@
             pltpu.VMEM((2, 3, pad, width), F32),
             pltpu.SemaphoreType.DMA((remote,)),
             pltpu.SemaphoreType.DMA((remote,)),
-            pltpu.SemaphoreType.DMA((3,)),
+            pltpu.SemaphoreType.DMA((4,)),
             pltpu.SemaphoreType.DMA((near,)),
             pltpu.SemaphoreType.DMA((2, 4)),
             pltpu.SemaphoreType.DMA((2, 3)),
@@ -1521,6 +1677,7 @@
         out_stage,
         own_v,
         arrived_v,
+        relayed_v,
         tokens_v,
         mixed_v,
         running,
@@ -1588,20 +1745,9 @@
     )
     base = 3 * each
     rows_of = block_rows(columns, size)
-    sums = [
-        mesh_copy(
-            d_normed_in.at[rows_of(s)],
-            arrived_v.at[s - 1],
-            sends,
-            arrivals,
-            base + s - 1,
-            column[s - 1],
-        )
-        for s in range(1, columns)
-    ]
-    base = base + columns - 1
-    for copy in sums:
-        copy.start()
+    summed = ColumnSum(d_normed_in, rows_of, arrived_v, relayed_v, sends, arrivals, base)
+    base = base + 4
+    summed.start(local.at[4])
     first = [
         pltpu.make_async_copy(d_normed_in.at[rows_of(0)], own_v, local.at[0]),
         pltpu.make_async_copy(tokens_in, tokens_v, local.at[1]),
@@ -1612,6 +1758,7 @@
         copy.start()
     for part in (out, joint, up):
         part.begin()
+    summed.clear()
     first[3].wait()
 
     def small(i, device):
@@ -1629,6 +1776,7 @@
     base = base + 2 + columns
     for copy in gains:
         copy.start()
+    summed.middle(local.at[4])
     for part in (out, joint, up):
         part.send_first()
     for part in (out, joint, up):
@@ -1656,19 +1804,16 @@
     for copy in across_columns:
         copy.start()
     done = [
-        pltpu.make_async_copy(joint_chip.at[0, 0], joint_out, joint_local.at[1]),
-        pltpu.make_async_copy(up_chip.at[0, 0], up_out, up_local.at[1]),
-        pltpu.make_async_copy(out_chip.at[0, 0], out_out, out_local.at[1]),
+        pltpu.make_async_copy(joint_chip.at[0, 0], joint_out, joint_local.at[4]),
+        pltpu.make_async_copy(up_chip.at[0, 0], up_out, up_local.at[4]),
+        pltpu.make_async_copy(out_chip.at[0, 0], out_out, out_local.at[4]),
     ]
     for copy in done:
         copy.start()
 
     for copy in first[:3]:
         copy.wait()
-    total = own_v[...].astype(F32)
-    for s in range(1, columns):
-        sums[s - 1].wait_recv()
-        total = total + arrived_v[s - 1].astype(F32)
+    total = summed.total(own_v[...])
     tokens = tokens_v[...].astype(F32)
     inverse = lax.rsqrt(jnp.mean(tokens * tokens, axis=1, keepdims=True) + EPSILON)
     unit = tokens * inverse
@@ -1697,7 +1842,8 @@
         copy.wait()
     for part in (out, joint, up):
         part.drain()
-    for copy in sums + hops + gains + across_columns:
+    summed.drain()
+    for copy in hops + gains + across_columns:
         copy.wait_send()
 
 
@@ -1716,7 +1862,7 @@
         one = plane_sum_space(1, rows, cols)
         landing, scratch = landing + one[0], scratch + one[1]
     remote, near = plane_sum_sizes(1)
-    remote = 3 * remote + 3 * (columns - 1) + 3
+    remote = 3 * remote + 2 * (columns - 1) + 7
     pieces = shapes[0][0] // columns
     return pl.pallas_call(
         functools.partial(last_kernel, columns, size, latent_start, latent_width),
@@ -1733,6 +1879,7 @@
         + [
             pltpu.VMEM((size, width), BF),
             pltpu.VMEM((columns - 1, size, width), BF),
+            pltpu.VMEM((2, size, width), BF),
             pltpu.VMEM((size, width), BF),
             pltpu.VMEM((size, width), F32),
             pltpu.VMEM((4,) + sums.shape, F32),
@@ -1740,7 +1887,7 @@
             pltpu.VMEM((columns - 1, pieces, latent_width), BF),
             pltpu.SemaphoreType.DMA((remote,)),
             pltpu.SemaphoreType.DMA((remote,)),
-            pltpu.SemaphoreType.DMA((4,)),
+            pltpu.SemaphoreType.DMA((5,)),
             pltpu.SemaphoreType.DMA((near,)),
             pltpu.SemaphoreType.DMA((near,)),
             pltpu.SemaphoreType.DMA((near,)),
@@ -1844,7 +1991,7 @@
     expert_count = local_experts * fsdp_count
     cap_rows = tok_rows * TOPK * 4 // (3 * expert_count)
     cap = cap_rows * (HALF // tok_rows)
-    paired = fsdp_count == 8 and tok_rows * 2 == HALF
+    paired = fsdp_count == 8 and tp_count == 4 and tok_rows * 2 == HALF
     heads_local = H // tp_count
     head_width = NOPE + ROPE
     score_scale = head_width ** (-0.5)
@@ -1886,7 +2033,7 @@
         latent_up_weight = lax.all_gather(latent_up, "fsdp", axis=0, tiled=True)
         out_weight = lax.all_gather(out_proj, "fsdp", axis=1, tiled=True)
         tokens_all = column_gather(block_in)
-    cotan_own, tokens_all = tie(out_cotan, tokens_all)
+    cotan_own, tokens_all, shared_weight = tie(out_cotan, tokens_all, shared_weight)
     cotan_all = column_gather(cotan_own)
     shared_down_weight = lax.all_gather(shared_down, "fsdp", axis=1, tiled=True)
     gain_attn = packed_all[:, joint].astype(F32)
@@ -1898,6 +2045,9 @@
         .astype(F32)
     )
     shared_cols = shared_gate.shape[1]
+
+    def scatter(part, dimension):
+        return lax.psum_scatter(part.astype(BF), "fsdp", scatter_dimension=dimension, tiled=True)
 
     unit_all, inverse_all = norm_parts(tokens_all.astype(F32))
     normed_all = (unit_all * gain_attn).astype(BF)
@@ -2032,6 +2182,8 @@
         ffn_gain_part, d_mixed_norm = norm_back(d_normed_ffn, unit_two, inverse_two, gain_ffn)
         d_mixed = out_cotan.astype(F32) + d_mixed_norm
         d_proj_all = column_gather(d_mixed.astype(BF))
+    shared_grad = scatter(shared_part, 0)
+    d_proj_all, shared_grad = tie(d_proj_all, shared_grad)
     ffn_rows = column_scatter(shared_rows + routed_rows)
     block_out = (mixed_rows + ffn_rows).astype(BF)
 
@@ -2081,15 +2233,11 @@
     d_normed_part = jnp.dot(d_joint, packed_all.T, preferred_element_type=F32)
     attn_gain_part = jnp.sum(d_normed_part * unit_all, axis=0)
 
-    def scatter(part, dimension):
-        return lax.psum_scatter(part.astype(BF), "fsdp", scatter_dimension=dimension, tiled=True)
-
     gain_parts = jnp.concatenate([attn_gain_part, latent_gain_part, ffn_gain_part]).reshape(
         -1, 128
     )
     joint_part = joint_part.astype(BF)
     shared_down_grad = scatter(shared_down_part, 1)
-    shared_grad = scatter(shared_part, 0)
     if paired:
         latent_width = joint_part.shape[1] - query_cols
         (

time: 765 us -> 823 us (1.076)
  waiting for transfers between devices: 62.3 us -> 162 us
  Pallas kernels: 525 us -> 503 us
    reduce_scatter x2, waiting for transfers between devices: 46 us -> 107 us  [scatter(): lax.psum_scatter(part.astype(BF), 'fsdp', scatter_dimension=dimension, ti...]
    reduce_scatter x1, waiting for transfers between devices: 0.01 us -> 41.7 us  [column_scatter(): lax.psum_scatter(values.astype(BF), 'tp', scatter_dimension=0, tiled=True)]
    pallas_call x1, Pallas kernels: 312 us -> 276 us  [expert_call(): pl.pallas_call(functools.partial(expert_kernel, cap, columns, size), out_...]
    pallas_call x1, Pallas kernels: 46.2 us -> 71.3 us  [first_call(): pl.pallas_call(functools.partial(first_kernel, columns, size, kinds), out...]
    unnamed x128 -> x144, local copies, waits for them, and re-layouts: 30.9 us -> 28.8 us
  transfers between devices with their start and end apart: 6 -> 6, of which waited for: 2 -> 4; matrix products, arithmetic and copies ran while one was open for 11% -> 5% of each run, Pallas kernels for 51% -> 43%
where the time goes in v6:
time: 823 us; the launch traced here: 813 us
  Pallas kernels  503 us (61%)
  waiting for transfers between devices  162 us (20%)
  matrix products  73.6 us (9%)
  local copies, waits for them, and re-layouts  39.3 us (5%)
  other arithmetic  19.1 us (2%)
  between operations  15.5 us (2%)
    pallas_call x1, Pallas kernels, expert_call(): pl.pallas_call(functools.partial(expert_kernel, cap, columns, size), out_...  276 us
    reduce_scatter x2, waiting for transfers between devices, scatter(): lax.psum_scatter(part.astype(BF), 'fsdp', scatter_dimension=dimension, ti...  107 us
    pallas_call x1, Pallas kernels, middle_call(): pl.pallas_call(functools.partial(middle_kernel, columns, size, experts, s...  94.1 us
    pallas_call x1, Pallas kernels, first_call(): pl.pallas_call(functools.partial(first_kernel, columns, size, kinds), out...  71.3 us
    pallas_call x1, Pallas kernels, last_call(): pl.pallas_call(functools.partial(last_kernel, columns, size, latent_start...  61.3 us
    reduce_scatter x1, waiting for transfers between devices, column_scatter(): lax.psum_scatter(values.astype(BF), 'tp', scatter_dimension=0, tiled=True)  41.7 us
    unnamed x144, local copies, waits for them, and re-layouts  28.8 us
  transfers between devices with their start and end apart: 6, of which 4 were waited for; matrix products, arithmetic and copies ran while one was open for 5% of the time, Pallas kernels for 43%

profile of v6, /device:TPU:0, one launch (start us, length us, event | category | flops | bytes accessed | tf_op | source)
XLA Modules:
  0.0 813.0 jit_solution(2720464280781566320)
XLA Ops:
  7.3 2.1 pad_maximum_fusion.6
  10.1 1.1 concatenate.43.refs_1_
  11.8 71.3 %first_gather.1 = (bf16[512,2048]{1,0:T(8,128)(2,1)}, bf16[8,256,1408]{2,1,0:T(8,128)(2,1)}, bf16[8,64,1024]{2,1,0:T(8,128)(2,1)}, bf16[512,2048]{1,0:T(8,128)(2,1)}, f32[8,16,512]{2,1,0:T(8,128)}) custom-call(bf16[128,2048]{1,0:T(8,128)(2,1)} %refs_1_.3, bf16[256,1408]{1,0:T(8,128)(2,1)} %concatenate.43.refs_1_, bf16[64,1024]{1,0:T(8,128)(2,1)} %refs_2_.2, ...), custom_call_target="tpu_custom_call" | custom-call | tf_op jit(solution)/shard_map/first_gather/pallas_call | solution.py:1262
  83.9 3.0 fusion.47
  87.3 2.5 copy.118
  89.9 0.9 fusion.13
  92.7 5.9 fusion.16
  98.9 1.5 slice.123
  100.7 3.0 copy.119
  103.7 2.2 convolution_convert_fusion.6
  108.1 0.8 fusion.14
  109.0 2.1 fusion.51
  111.7 1.6 copy-done.8
  113.3 0.8 copy-done.56
  114.3 2.6 convolution_convert_fusion.4.refs_0_
  116.9 12.0 %all-gather.6.cloned.1.call-done.refs_2_ = bf16[512,2048]{1,0:T(8,128)(2,1)} async-done(((bf16[128,2048]{1,0:T(8,128)(2,1)}), bf16[512,2048]{1,0:T(8,128)(2,1)}) %all-gather.6.cloned.1.call-update) | async-done | bytes 2097168 | tf_op jit(solution)/shard_map/all_gather | solution.py:99
  128.9 276.1 %experts.1 = (f32[128,2048]{1,0:T(8,128)}, bf16[512,2048]{1,0:T(8,128)(2,1)}, bf16[512,2048]{1,0:T(8,128)(2,1)}, bf16[4,4,256,2048]{3,2,1,0:T(8,128)(2,1)}, bf16...) custom-call(bf16[512,2048]{1,0:T(8,128)(2,1)} %convolution_convert_f, ...), custom_call_target="tpu_custom_call" | custom-call | flops 17179869184 | bytes 62914560 | tf_op jit(solution)/shard_map/experts/pallas_call | solution.py:1091
  405.1 8.4 %fusion.52 = f32[512,1408]{1,0:T(8,128)} fusion(bf16[512,2048]{1,0:T(8,128)(2,1)} %get-tuple-element.57, bf16[2048,1408]{0,1:T(8,128)(2,1)} %all-gather.4.cloned.1.call-done), kind=kOutput, calls=%fused_computation.117 | convolution fusion | flops 2952790016 | bytes 10747904 | tf_op jit(solution)/shard_map/dot_general | solution.py:2149
  413.5 5.1 multiply_convert_fusion.2
  418.6 0.9 copy-done.61
  419.7 5.5 convolution_convert_fusion.1
  425.2 8.5 %add_convert_fusion.1.refs_0_ = bf16[512,2048]{1,0:T(8,128)(2,1)} fusion(bf16[512,2048]{1,0:T(8,128)(2,1)} %get-tuple-element.59, bf16[2048,1408]{0,1:T(8,128)(2,1)} %all-gather.4.cloned.1.call-done, bf16[512,704]{1,0:T(8,128)(2,1)} %copy-done.62, bf16[512,704]{1,0:T(8,128)(2,1)} %copy-done.61), kind=kOutput, calls=%fused_computation.13 | convolution fusion | flops 2958819328 | bytes 11403264 | tf_op jit(solution)/shard_map/dot_general | solution.py:2157
  433.7 3.3 convolution_convert_fusion.2
  436.9 94.1 %middle.1 = (f32[128,2048]{1,0:T(8,128)}, bf16[512,2048]{1,0:T(8,128)(2,1)}, f32[1,2048]{1,0:T(1,128)}, bf16[512,2048]{1,0:T(8,128)(2,1)}, f32[2,352,2048]{2,1,0...) custom-call(bf16[512,2048]{1,0:T(8,128)(2,1)} %add_convert_fusion.1., ...), custom_call_target="tpu_custom_call" | custom-call | flops 19327352832 | bytes 41943040 | tf_op jit(solution)/shard_map/middle/pallas_call | solution.py:1603
  531.1 5.8 add_convert_fusion
  538.1 41.7 %reduce-scatter.4.cloned.1.call-done = bf16[128,2048]{1,0:T(8,128)(2,1)} async-done(((bf16[512,2048]{1,0:T(8,128)(2,1)}), bf16[128,2048]{1,0:T(8,128)(2,1)}) %reduce-scatter.4.cloned.1.call-update) | async-done | bytes 524304 | tf_op jit(solution)/shard_map/reduce_scatter | solution.py:103
  579.8 1.9 add_convert_fusion.2
  581.8 45.9 %reduce-scatter.8.cloned.1.call-done = bf16[704,256]{1,0:T(8,128)(2,1)} async-done(((bf16[704,2048]{1,0:T(8,128)(2,1)}), bf16[704,256]{1,0:T(8,128)(2,1)}) %reduce-scatter.8.cloned.1.call-update) | async-done | bytes 360464 | tf_op jit(solution)/shard_map/reduce_scatter | solution.py:2050
  627.7 1.9 convert_element_type.289
  629.6 61.1 %reduce-scatter.6.cloned.1.call-done = bf16[256,1408]{1,0:T(8,128)(2,1)} async-done(((bf16[2048,1408]{1,0:T(8,128)(2,1)}), bf16[256,1408]{1,0:T(8,128)(2,1)}) %reduce-scatter.6.cloned.1.call-update) | async-done | bytes 720912 | tf_op jit(solution)/shard_map/reduce_scatter | solution.py:2050
  690.7 3.0 convolution_convert_fusion.7
  694.5 0.8 convolution_bitcast_fusion
  695.4 1.2 multiply_convert_fusion
  696.6 0.8 multiply_bitcast_fusion
  700.1 2.6 convolution_convert_fusion.3.refs_6_
  703.4 1.9 convolution_convert_fusion.5.refs_5_
  705.3 1.0 multiply_reduce_fusion.1
  708.4 7.9 fusion.4
  716.3 5.7 convolution_convert_fusion.refs_4_
  722.1 61.3 %last_sums.1 = (f32[128,2048]{1,0:T(8,128)S(1)}, bf16[256,1408]{1,0:T(8,128)(2,1)S(1)}, bf16[64,1024]{1,0:T(8,128)(2,1)S(1)}, bf16[512,256]{1,0:T(8,128)(2,1)S(1...) custom-call(bf16[512,2048]{1,0:T(8,128)(2,1)} %get-tuple-element.151, ...), custom_call_target="tpu_custom_call" | custom-call | tf_op jit(solution)/shard_map/last_sums/pallas_call | solution.py:1867
  783.4 0.9 slice_convert_fusion.3
  784.4 0.8 convert_element_type.287
  786.1 1.1 copy.134
  787.2 1.1 copy.135
  789.5 1.0 copy.160
  791.1 6.0 copy.162
  797.2 6.0 copy.163
  803.2 2.5 copy.164
  (194 shorter events, 18.1 us)
Async XLA Ops:
  7.2 2.3 copy-start.32
  7.2 2.5 copy-start.55
  7.2 2.6 copy-start.50
  7.2 2.7 copy-start.51
  7.2 2.8 copy-start.31
  7.2 3.9 copy-start.40
  7.2 3.9 copy-start.41
  7.3 75.8 %all-gather.4.cloned.1.call-start = ((), (), s32[]{:S(2)}) async-start(), calls=%async_computation.3 | async-start | bytes 6488064 | tf_op jit(solution)/shard_map/all_gather | solution.py:2016
  9.4 119.5 %all-gather.6.cloned.1.call-start = ((), (), s32[]{:S(2)}) async-start(), calls=%async_computation.4 | async-start | bytes 2621440 | tf_op jit(solution)/shard_map/all_gather | solution.py:99
  83.1 330.4 %all-gather.8.cloned.1.call-start = ((), (), s32[]{:S(2)}) async-start(), calls=%async_computation.5 | async-start | bytes 3244032 | tf_op jit(solution)/shard_map/all_gather | solution.py:2038
  83.8 496.0 %reduce-scatter.4.cloned.1.call-start = ((), (), s32[]{:S(2)}) async-start(), calls=%async_computation.6 | async-start | bytes 2621440 | tf_op jit(solution)/shard_map/reduce_scatter | solution.py:103
  83.9 22.2 %copy-start.34 = (f32[512]{0:T(512)}, f32[512]{0:T(512)S(1)}, u32[]{:S(2)}) copy-start(f32[512]{0:T(512)S(1)} %iota_convert_fusion) | copy-start | bytes 6148
  83.9 22.2 %copy-start.46 = (f32[32]{0:T(128)}, f32[32]{0:T(128)S(1)}, u32[]{:S(2)}) copy-start(f32[32]{0:T(128)S(1)} %multiply_power_fusion) | copy-start | bytes 388
  86.9 3.0 copy-start.44
  86.9 4.7 copy-start.15
  87.2 4.9 copy-start.1
  87.2 3.5 copy-start.18
  87.3 16.4 %copy-start.36 = (f32[512]{0:T(512)}, f32[512]{0:T(512)S(1)}, u32[]{:S(2)}) copy-start(f32[512]{0:T(512)S(1)} %reshape.242) | copy-start | bytes 6148
  91.0 1.7 copy-start.16
  98.6 5.1 copy-start.3
  98.9 4.8 copy-start.38
  103.7 2.3 copy-start.7
  105.9 5.3 copy-start.13
  106.0 1.3 copy-start.5
  111.1 2.1 copy-start.8
  111.2 2.1 copy-start.42
  111.2 3.1 copy-start.52
  405.0 8.5 %copy-start.54 = (bf16[512,2048]{1,0:T(8,128)(2,1)S(1)}, bf16[512,2048]{1,0:T(8,128)(2,1)}, u32[]{:S(2)}) copy-start(bf16[512,2048]{1,0:T(8,128)(2,1)} %all-gather.6.cloned.1.call-done.refs_2_) | copy-start | bytes 6291460
  413.5 6.2 copy-start.60
  418.6 15.1 %copy-start.59 = (bf16[512,704]{1,0:T(8,128)(2,1)}, bf16[512,704]{1,0:T(8,128)(2,1)S(1)}, u32[]{:S(2)}) copy-start(bf16[512,704]{1,0:T(8,128)(2,1)S(1)} %get-tuple-element.152) | copy-start | bytes 2162692
  536.9 90.8 %reduce-scatter.8.cloned.1.call-start = ((), (), s32[]{:S(2)}) async-start(), calls=%async_computation.8 | async-start | bytes 3244032 | tf_op jit(solution)/shard_map/reduce_scatter | solution.py:2050
  537.5 42.3 %copy-start.22 = (f32[128,2048]{1,0:T(8,128)S(1)}, f32[128,2048]{1,0:T(8,128)}, u32[]{:S(2)}) copy-start(f32[128,2048]{1,0:T(8,128)} %get-tuple-element.56.refs_1_) | copy-start | bytes 3145732
  537.5 153.1 %reduce-scatter.6.cloned.1.call-start = ((), (), s32[]{:S(2)}) async-start(), calls=%async_computation.7 | async-start | bytes 6488064 | tf_op jit(solution)/shard_map/reduce_scatter | solution.py:2050
  538.1 152.6 %copy-start.53 = (bf16[512,2048]{1,0:T(8,128)(2,1)S(1)}, bf16[512,2048]{1,0:T(8,128)(2,1)}, u32[]{:S(2)}) copy-start(bf16[512,2048]{1,0:T(8,128)(2,1)} %get-tuple-element.53) | copy-start | bytes 6291460
  690.7 3.0 copy-start.9
  690.7 3.1 copy-start.14
  690.7 3.1 copy-start.43
  698.3 1.8 copy-start.58
  700.1 2.7 copy-start.4
  702.8 2.5 copy-start.21
  706.8 1.6 copy-start.17
  706.8 1.6 copy-start.49
  708.4 7.9 copy-start.2
  716.3 5.7 copy-start.45
  716.3 5.7 copy-start
  783.4 2.5 copy-start.10
  791.1 12.0 %slice-start = ((s8[5767168]{0:T(1024)(128)(4,1)}), s8[4194304]{0:T(1024)(128)(4,1)S(1)}, s32[]{:S(2)}) async-start(s8[5767168]{0:T(1024)(128)(4,1)} %bitcast.68), calls=%async_computation.9 | async-start | bytes 8388608
  797.2 6.0 slice-start.1
  (23 other events, 20.7 us)
Sparse Core Ops, SparseCore 0:
  10.5 70.6 all-gather.3
  83.2 45.6 all-gather.5
  130.8 42.1 all-gather.7
  537.0 42.7 reduce-scatter.3
  583.4 44.2 reduce-scatter.7
  631.6 59.0 reduce-scatter.5

commit v7 on v6

--- a/solution.py
+++ b/solution.py
@@ -694,6 +694,35 @@
     return lambda s: pl.ds(pl.multiple_of((row + s) % columns * size, size), size)
 
 
+def slots_of(table, experts, columns, size, b, q):
+    place = pl.ds(pl.multiple_of((lax.axis_index("tp") + b) % columns * size, size), size)
+    rows = []
+    for e in range(experts):
+        low, high = 2 * q * experts + e, (2 * q + 1) * experts + e
+        rows.append(
+            jnp.concatenate([table[low : low + 1, place], table[high : high + 1, place]], axis=1)
+        )
+    return jnp.concatenate(rows, axis=0)
+
+
+def token_sums(table, experts, columns, size, wide, b, slots, keep):
+    width = slots.shape[2]
+    tile = min(1024, width)
+    for q in range(QUARTET):
+        entries = slots_of(table, experts, columns, size, b, q)
+        entries = jnp.concatenate(
+            [entries, jnp.full((8 - experts, HALF), NO_SLOT, F32)], axis=0
+        )
+        choose = jnp.where(select_cols(entries.T, experts, wide), 1.0, 0.0).astype(BF)
+
+        def gather(n, carry, q=q, choose=choose):
+            cols = pl.ds(pl.multiple_of(n * tile, tile), tile)
+            keep(q, cols, dot_plain(choose, slots[q, :, cols]).astype(BF))
+            return carry
+
+        lax.fori_loop(0, width // tile, gather, 0)
+
+
 def expert_kernel(cap, columns, size, *refs):
     (
         attn_in,
@@ -707,7 +736,8 @@
         mixed_out,
         ffn_all,
         dx_out,
-        out_all,
+        slots_out,
+        weights_out,
         x_all,
         d_all,
         hid_all,
@@ -744,7 +774,7 @@
         spill,
     ) = refs
     count = QUARTET
-    previous, following = {2: 0, 1: 2, 3: 1}, {0: 2, 2: 1, 1: 3}
+    previous = {2: 0, 1: 2, 3: 1}
     experts, local_hidden = gate_in.shape[:2]
     width = xb.shape[2]
     pad = down.shape[1]
@@ -761,9 +791,7 @@
         return number - amount
 
     x_gather = PlaneGather(ffn_all, x_others, rows_of, sends, arrivals, reserve(8 * columns))
-    dy_gather = PlaneGather(
-        cotan_in, dy_others, lambda b: pl.ds(0, SEQ), sends, arrivals, reserve(8)
-    )
+    dy_gather = PlaneGather(cotan_in, dy_others, rows_of, sends, arrivals, reserve(8 * columns))
     gather = ColumnGather(ffn_all, rows_of, sends, arrivals, reserve(4))
     summed = ColumnSum(attn_in, rows_of, arrived_v, relayed_v, sends, arrivals, reserve(4))
     plane = PlaneSum(
@@ -786,7 +814,9 @@
     ]
     for copy in first:
         copy.start()
-    dy_gather.start(0)
+    order = (0, 2, 1, 3)
+    for b in order:
+        dy_gather.start(b)
     if pad > local_hidden:
         rest = pad - local_hidden
         for e in range(experts):
@@ -834,6 +864,8 @@
         member = slot_table[:, cols]
         rank = dot_plain(member.astype(BF), before)
         slot_table[:, cols] = jnp.where(member > 0.5, rank + shift, NO_SLOT)
+    slots_out[...] = slot_table[...]
+    weights_out[...] = weight_table[...]
 
     for copy in first:
         copy.wait()
@@ -855,7 +887,10 @@
         x_gather.start(b)
 
     def ready(b):
+        x_gather.last(b)
+        dy_gather.last(b)
         x_gather.arrived(b, [2, 5, 6, 7])
+        dy_gather.arrived(b, [2, 5, 6, 7])
 
     def source(own, gathered, r):
         return own if r == 0 else gathered.at[r - 1]
@@ -871,31 +906,8 @@
             for r in range(8)
         ]
 
-    def slots_of(table, b, q):
-        place = pl.ds(pl.multiple_of((lax.axis_index("tp") + b) % columns * size, size), size)
-        rows = []
-        for e in range(experts):
-            low, high = 2 * q * experts + e, (2 * q + 1) * experts + e
-            rows.append(
-                jnp.concatenate([table[low : low + 1, place], table[high : high + 1, place]], axis=1)
-            )
-        return jnp.concatenate(rows, axis=0)
-
     def combine(b, keep):
-        for q in range(count):
-            entries = slots_of(slot_table, b, q)
-            entries = jnp.concatenate(
-                [entries, jnp.full((8 - experts, HALF), NO_SLOT, F32)], axis=0
-            )
-            hit = select_cols(entries.T, experts, wide)
-            choose = jnp.where(hit, 1.0, 0.0).astype(BF)
-
-            def gather(n, carry, q=q, choose=choose):
-                cols = pl.ds(pl.multiple_of(n * tile, tile), tile)
-                keep(q, cols, dot_plain(choose, dxs[q, :, cols]).astype(BF))
-                return carry
-
-            lax.fori_loop(0, width // tile, gather, 0)
+        token_sums(slot_table, experts, columns, size, wide, b, dxs, keep)
 
     def spills(b):
         return [
@@ -907,7 +919,7 @@
 
     def front(b):
         x_load, dy_load = load(b, 0), load(b, 1)
-        for copy in x_load + (dy_load if b == 0 else []):
+        for copy in x_load + dy_load:
             copy.start()
         if b == 0:
             for copy in weights_in:
@@ -918,8 +930,8 @@
         for q in range(count):
             for copy in x_load[2 * q : 2 * q + 2] + dy_load[2 * q : 2 * q + 2]:
                 copy.wait()
-            hit = select_rows(slots_of(slot_table, b, q), experts, wide)
-            weights = slot_weights(hit, slots_of(weight_table, b, q), experts, wide)
+            hit = select_rows(slots_of(slot_table, experts, columns, size, b, q), experts, wide)
+            weights = slot_weights(hit, slots_of(weight_table, experts, columns, size, b, q), experts, wide)
             choose = jnp.where(hit, 1.0, 0.0).astype(BF)
 
             def spread(n, carry, q=q, choose=choose, weights=weights):
@@ -933,9 +945,6 @@
                 return carry
 
             lax.fori_loop(0, width // tile, spread, 0)
-        if b in following:
-            for copy in load(following[b], 1):
-                copy.start()
         out_copies = spills(b)
         out_copies[0].start()
         out_copies[1].start()
@@ -977,74 +986,31 @@
         for i in range(4):
             plane.pair(i, b).start()
 
-    def out_part(b):
-        weights = [
-            slot_weights(
-                select_rows(slots_of(slot_table, b, q), experts, wide),
-                slots_of(weight_table, b, q),
-                experts,
-                wide,
-            )
-            for q in range(count)
-        ]
-        for e in range(experts):
-
-            def one_tile(n, carry, e=e):
-                cols = pl.ds(pl.multiple_of(n * tile, tile), tile)
-                rows = dot_plain(hid[b, e], down[e, :, cols])
-                for q in range(count):
-                    dxs[q, e * wide : (e + 1) * wide, cols] = (
-                        rows[q * wide : (q + 1) * wide] * weights[q][e * wide : (e + 1) * wide]
-                    ).astype(BF)
-                return carry
-
-            lax.fori_loop(0, width // tile, one_tile, 0)
-        if b > 0:
-            out_copy(b - 1).wait()
-
-        def keep(q, cols, value):
-            db[q, :, cols] = value
-
-        combine(b, keep)
-        out_copy(b).start()
-
-    def out_copy(b):
-        return pltpu.make_async_copy(db, out_all.at[b], local.at[0])
-
-    final = columns - 1
+    dy_gather.forward(0)
     enter(0)
-    dy_gather.forward(0)
+    x_gather.forward(0)
+    dy_gather.forward(2)
     enter(2)
-    x_gather.forward(0)
+    dy_gather.forward(1)
     enter(1)
-    x_gather.last(0)
-    dy_gather.last(0)
+    x_gather.forward(2)
     ready(0)
-    dy_gather.arrived(0, [2, 5, 6, 7])
     front(0)
-    x_gather.forward(2)
+    dy_gather.forward(3)
     enter(3)
     x_gather.forward(1)
-    x_gather.last(2)
     ready(2)
-    x_gather.last(1)
     front(2)
     x_gather.forward(3)
+    plane.send_first([0], False)
     ready(1)
-    plane.send_first([0], False)
     front(1)
-    x_gather.last(3)
-    ready(3)
     plane.send_first([2], False)
     plane.send_second([0])
+    ready(3)
     front(3)
     plane.send_first([1], False)
     plane.send_second([2])
-    for copy in spills(3):
-        copy.wait()
-    out_part(0)
-    plane.send_first([3], False)
-    plane.send_second([1])
     done = {}
 
     def close(b):
@@ -1052,25 +1018,25 @@
         done[b] = pltpu.make_async_copy(chip.at[0, b], dx_out.at[rows_of(b)], loads.at[b])
         done[b].start()
 
-    out_part(1)
+    plane.send_first([3], False)
+    close(0)
+    plane.send_second([1])
+    close(2)
     plane.send_second([3])
-    close(0)
-    out_part(2)
-    close(2)
-    out_part(3)
     close(1)
     close(3)
+    for copy in spills(3):
+        copy.wait()
     for b in range(columns):
         done[b].wait()
-    out_copy(final).wait()
     mixed_copy.wait()
 
     for b in range(columns):
         x_gather.drain(b)
-    dy_gather.drain(0)
+        dy_gather.drain(b)
     gather.drain()
     summed.drain()
-    plane.drain(final)
+    plane.drain(3)
 
 
 def expert_call(attn_part, tokens, cotan_all, gate, up, down, gain, raw, cap):
@@ -1087,14 +1053,15 @@
 
     landing, scratch = plane_sum_space(columns, size, width)
     remote, near = plane_sum_sizes(columns)
-    remote = remote + 8 * columns + 8 + 8
+    remote = remote + 16 * columns + 8
     results = pl.pallas_call(
         functools.partial(expert_kernel, cap, columns, size),
         out_shape=[
             array(size, width, kind=F32),
             array(SEQ, width),
             array(SEQ, width),
-            array(columns, QUARTET, HALF, width),
+            array(8 * experts, SEQ, kind=F32),
+            array(8 * experts, SEQ, kind=F32),
             array(columns, experts, slots, width),
             array(columns, experts, slots, width),
             array(columns, experts, slots, pad),
@@ -1104,7 +1071,7 @@
         ]
         + landing,
         in_specs=[anywhere] * 6 + [held] * 2,
-        out_specs=[anywhere] * 12,
+        out_specs=[anywhere] * 3 + [held] * 2 + [anywhere] * 8,
         scratch_shapes=[
             pltpu.VMEM((size, width), BF),
             pltpu.VMEM((size, width), BF),
@@ -1139,20 +1106,20 @@
         ),
         cost_estimate=pl.CostEstimate(
             flops=16 * SEQ * experts * cap * width * 8,
-            bytes_accessed=60 * SEQ * width,
+            bytes_accessed=800 * SEQ * width,
             transcendentals=0,
         ),
         name="experts",
     )(attn_part, tokens, cotan_all, gate, up, down, gain, raw)
-    return results[:8]
+    return results[:9]
 
 
 def first_kernel(columns, size, kinds, *refs):
     amount = len(kinds)
-    tokens_in, own_in = refs[0], refs[1 : 1 + amount]
-    tokens_all, alls = refs[1 + amount], refs[2 + amount : 2 + 2 * amount]
-    tokens_v, held = refs[2 + 2 * amount], refs[3 + 2 * amount : 3 + 3 * amount]
-    sends, arrivals, local = refs[3 + 3 * amount :]
+    rows_in, own_in = refs[:2], refs[2 : 2 + amount]
+    rows_all, alls = refs[2 + amount : 4 + amount], refs[4 + amount : 4 + 2 * amount]
+    rows_v, held = refs[4 + 2 * amount : 6 + 2 * amount], refs[6 + 2 * amount : 6 + 3 * amount]
+    sends, arrivals, local = refs[6 + 3 * amount :]
     partner, along, across = plane_neighbours()
     column = column_neighbours(columns)
     rows_of = block_rows(columns, size)
@@ -1165,14 +1132,17 @@
         6: along[0] + across[0] - place,
     }
     greet([partner, along, across] + column)
-    here = [pltpu.make_async_copy(tokens_in, tokens_v, local.at[0])]
-    there = [pltpu.make_async_copy(tokens_v, tokens_all.at[rows_of(0)], local.at[0])]
-    here[0].start()
-    here[0].wait()
-    there[0].start()
-    there[0].wait()
-    gather = ColumnGather(tokens_all, rows_of, sends, arrivals, 8 * amount)
-    gather.start()
+    gathers = []
+    for n in range(2):
+        inward = pltpu.make_async_copy(rows_in[n], rows_v[n], local.at[n])
+        inward.start()
+        inward.wait()
+        place_here = rows_all[n].at[rows_of(0)]
+        outward = pltpu.make_async_copy(rows_v[n], place_here, local.at[n])
+        outward.start()
+        outward.wait()
+        gathers.append(ColumnGather(rows_all[n], rows_of, sends, arrivals, 8 * amount + 4 * n))
+        gathers[n].start()
     plans = []
     for k, kind in enumerate(kinds):
         own, everything = own_in[k], alls[k]
@@ -1216,8 +1186,8 @@
             spot_here = alls[k].at[place]
         else:
             spot_here = alls[k].at[:, pl.ds(pl.multiple_of(place * cols, cols), cols)]
-        here.append(pltpu.make_async_copy(own_in[k], held[k], local.at[1 + k]))
-        there.append(pltpu.make_async_copy(held[k], spot_here, local.at[1 + k]))
+        here.append(pltpu.make_async_copy(own_in[k], held[k], local.at[2 + k]))
+        there.append(pltpu.make_async_copy(held[k], spot_here, local.at[2 + k]))
     for copy in here:
         copy.start()
     for copy in here:
@@ -1231,7 +1201,7 @@
         copies[1].wait_recv()
         copies[4].start()
         copies[6].start()
-    gather.wait(2)
+    gathers[0].wait(2)
     for copies in plans:
         copies[3].wait_recv()
         copies[4].wait_recv()
@@ -1239,21 +1209,24 @@
     for copies in plans:
         for i in (2, 5, 6, 7):
             copies[i].wait_recv()
-    gather.wait(1)
-    gather.wait(3)
+    gathers[1].wait(2)
+    for gather in gathers:
+        gather.wait(1)
+        gather.wait(3)
     for copy in there:
         copy.wait()
-    gather.drain()
+    for gather in gathers:
+        gather.drain()
     for copies in plans:
         for copy in copies:
             copy.wait_send()
 
 
-def first_call(tokens, owns, kinds):
+def first_call(tokens, cotan, owns, kinds):
     columns = lax.axis_size("tp")
     size, width = tokens.shape
     anywhere = pl.BlockSpec(memory_space=pl.ANY)
-    copies = 8 * len(owns) + 4
+    copies = 8 * len(owns) + 8
 
     def gathered(own, kind):
         rows, cols = own.shape
@@ -1261,20 +1234,23 @@
 
     return pl.pallas_call(
         functools.partial(first_kernel, columns, size, kinds),
-        out_shape=[jax.ShapeDtypeStruct((columns * size, width), BF)]
+        out_shape=[jax.ShapeDtypeStruct((columns * size, width), BF)] * 2
         + [jax.ShapeDtypeStruct(gathered(own, kind), own.dtype) for own, kind in zip(owns, kinds)],
-        in_specs=[anywhere] * (1 + len(owns)),
-        out_specs=[anywhere] * (1 + len(owns)),
-        scratch_shapes=[pltpu.VMEM((size, width), BF)]
+        in_specs=[anywhere] * (2 + len(owns)),
+        out_specs=[anywhere] * (2 + len(owns)),
+        scratch_shapes=[pltpu.VMEM((size, width), BF)] * 2
         + [pltpu.VMEM(own.shape, own.dtype) for own in owns]
         + [
             pltpu.SemaphoreType.DMA((copies,)),
             pltpu.SemaphoreType.DMA((copies,)),
-            pltpu.SemaphoreType.DMA((1 + len(owns),)),
+            pltpu.SemaphoreType.DMA((2 + len(owns),)),
         ],
         compiler_params=pltpu.CompilerParams(collective_id=2, has_side_effects=True),
+        cost_estimate=pl.CostEstimate(
+            flops=0, bytes_accessed=240 * SEQ * width, transcendentals=0
+        ),
         name="first_gather",
-    )(tokens, *owns)
+    )(tokens, cotan, *owns)
 
 
 class PlaneSum:
@@ -1412,13 +1388,15 @@
     return landing, scratch
 
 
-def middle_kernel(columns, size, experts, steps, local_hidden, *refs):
+def middle_kernel(cap, columns, size, experts, steps, local_hidden, *refs):
     (
         d_ffn_in,
         mixed_in,
         cotan_in,
         gain_ref,
-        out_all,
+        slot_table,
+        weight_table,
+        down_in,
         x_all,
         d_all,
         hid_all,
@@ -1445,6 +1423,10 @@
         hk,
         gk,
         totals,
+        hid,
+        down,
+        parts,
+        others,
         sends,
         arrivals,
         local,
@@ -1456,7 +1438,7 @@
     column = column_neighbours(columns)
     greet([partner, along, across] + column)
     plane = PlaneSum(
-        lambda r, h: out_all.at[h, r // 2, pl.ds(r % 2 * size, size)],
+        lambda r, h: others.at[h % 2, r // 2],
         chip,
         theirs,
         links,
@@ -1478,12 +1460,62 @@
     ]
     for copy in first:
         copy.start()
-    plane.begin()
-    summed.clear()
-
     width = xk.shape[2]
     pad = hk.shape[2]
     tile = min(1024, width)
+    hidden_in = [pltpu.make_async_copy(hid_all.at[b], hid.at[b], local.at[4 + b]) for b in range(columns)]
+    down_copies = [
+        pltpu.make_async_copy(
+            down_in.at[e], down.at[e, pl.ds(0, local_hidden)], local.at[4 + columns + e]
+        )
+        for e in range(experts)
+    ]
+    for copy in down_copies + hidden_in:
+        copy.start()
+    summed.clear()
+    rest = down.shape[1] - local_hidden
+    if rest > 0:
+        for e in range(experts):
+            down[e, local_hidden:, :] = jnp.zeros((rest, down.shape[2]), BF)
+    for copy in down_copies:
+        copy.wait()
+    wide = 2 * cap
+
+    def out_part(b):
+        hidden_in[b].wait()
+        weights = [
+            slot_weights(
+                select_rows(slots_of(slot_table, experts, columns, size, b, q), experts, wide),
+                slots_of(weight_table, experts, columns, size, b, q),
+                experts,
+                wide,
+            )
+            for q in range(QUARTET)
+        ]
+        for e in range(experts):
+
+            def one_tile(n, carry, e=e):
+                cols = pl.ds(pl.multiple_of(n * tile, tile), tile)
+                rows = dot_plain(hid[b, e], down[e, :, cols])
+                for q in range(QUARTET):
+                    parts[q, e * wide : (e + 1) * wide, cols] = (
+                        rows[q * wide : (q + 1) * wide] * weights[q][e * wide : (e + 1) * wide]
+                    ).astype(BF)
+                return carry
+
+            lax.fori_loop(0, width // tile, one_tile, 0)
+        if b > 1:
+            for i in range(4):
+                plane.pair(i, b - 2).wait_send()
+
+        def keep(q, cols, value):
+            chip[q, b, :, cols] = value[:size]
+            others[b % 2, q, :, cols] = value[size:]
+
+        token_sums(slot_table, experts, columns, size, wide, b, parts, keep)
+        for i in range(4):
+            plane.pair(i, b).start()
+
     jobs = [(e, step) for e in range(experts) for step in range(steps)]
 
     def fetch(k):
@@ -1535,18 +1567,18 @@
             for copy in write(e):
                 copy.start()
 
+    out_part(0)
+    out_part(1)
+    summed.middle(local.at[3])
+    plane.send_first([0], False)
+    out_part(2)
+    plane.send_first([1], False)
     for copy in fetch(0):
         copy.start()
-    for k in range(2):
-        job(k)
-    summed.middle(local.at[3])
-    early = len(jobs) // 2
-    late = 3 * len(jobs) // 4
-    for k in range(2, early):
-        job(k)
-    plane.send_first()
-    for k in range(early, late):
-        job(k)
+    out_part(3)
+    plane.send_first([2], False)
+    job(0)
+    plane.send_first([3], False)
 
     for copy in first:
         copy.wait()
@@ -1566,11 +1598,20 @@
     mixed_copy.start()
     own_copy.wait()
     gather.start()
-    for k in range(late, len(jobs)):
+    for b in range(columns):
+        if b + 1 < len(jobs):
+            job(b + 1)
+        plane.send_second([b])
+        if b == 1:
+            gather.wait(2)
+    for b in range(columns):
+        if columns + 1 + b < len(jobs):
+            job(columns + 1 + b)
+        if b < columns - 1:
+            plane.finish([b])
+    for k in range(2 * columns + 1, len(jobs)):
         job(k)
-    plane.send_second()
-    gather.wait(2)
-    plane.finish()
+    plane.finish([columns - 1])
     done = [
         pltpu.make_async_copy(chip.at[0, h], routed_out.at[rows_of(h)], sum_local.at[4 + h])
         for h in range(columns)
@@ -1584,16 +1625,17 @@
     for e in range(max(0, experts - 2), experts):
         for copy in write(e):
             copy.wait()
-    plane.drain()
+    plane.drain(2)
     gather.drain()
     summed.drain()
 
 
-def middle_call(d_ffn, mixed, cotan, gain, out_all, kept, local_hidden):
+def middle_call(d_ffn, mixed, cotan, gain, tables, down, kept, cap):
     columns = lax.axis_size("tp")
     size, width = cotan.shape
     x_all, d_all, hid_all, dgu_all = kept
     steps, experts, slots, pad = hid_all.shape
+    local_hidden = down.shape[1]
     anywhere = pl.BlockSpec(memory_space=pl.ANY)
     held = pl.BlockSpec(memory_space=pltpu.VMEM)
     landing, scratch = plane_sum_space(columns, size, width)
@@ -1601,7 +1643,7 @@
     remote = remote + 8
     grad = jax.ShapeDtypeStruct((experts, local_hidden, width), F32)
     results = pl.pallas_call(
-        functools.partial(middle_kernel, columns, size, experts, steps, local_hidden),
+        functools.partial(middle_kernel, cap, columns, size, experts, steps, local_hidden),
         out_shape=[
             jax.ShapeDtypeStruct((size, width), F32),
             jax.ShapeDtypeStruct((SEQ, width), BF),
@@ -1612,7 +1654,7 @@
             grad,
         ]
         + landing,
-        in_specs=[anywhere] * 3 + [held] + [anywhere] * 5,
+        in_specs=[anywhere] * 3 + [held] * 3 + [anywhere] * 5,
         out_specs=[anywhere] * 2 + [held] + [anywhere] * 6,
         scratch_shapes=scratch
         + [
@@ -1627,9 +1669,13 @@
             pltpu.VMEM((2, slots, pad), BF),
             pltpu.VMEM((2, slots, 2 * pad), BF),
             pltpu.VMEM((2, 3, pad, width), F32),
+            pltpu.VMEM((steps, experts, slots, pad), BF),
+            pltpu.VMEM((experts, pad, width), BF),
+            pltpu.VMEM((QUARTET, 2 * experts * cap, width), BF),
+            pltpu.VMEM((2, 4, size, width), BF),
             pltpu.SemaphoreType.DMA((remote,)),
             pltpu.SemaphoreType.DMA((remote,)),
-            pltpu.SemaphoreType.DMA((4,)),
+            pltpu.SemaphoreType.DMA((4 + columns + experts,)),
             pltpu.SemaphoreType.DMA((near,)),
             pltpu.SemaphoreType.DMA((2, 4)),
             pltpu.SemaphoreType.DMA((2, 3)),
@@ -1639,11 +1685,11 @@
         ),
         cost_estimate=pl.CostEstimate(
             flops=2 * 3 * steps * experts * slots * width * pad,
-            bytes_accessed=40 * SEQ * width,
+            bytes_accessed=300 * SEQ * width,
             transcendentals=0,
         ),
         name="middle",
-    )(d_ffn, mixed, cotan, gain, out_all, x_all, d_all, hid_all, dgu_all)
+    )(d_ffn, mixed, cotan, gain, *tables, down, x_all, d_all, hid_all, dgu_all)
     return results[:7]
 
 
@@ -1895,6 +1941,9 @@
         compiler_params=pltpu.CompilerParams(
             collective_id=4, has_side_effects=True, vmem_limit_bytes=48 * 1024 * 1024
         ),
+        cost_estimate=pl.CostEstimate(
+            flops=0, bytes_accessed=180 * SEQ * width, transcendentals=0
+        ),
         name="last_sums",
     )(d_normed, tokens, d_mixed, gain, joint, up, out, sums)[:6]
 
@@ -2013,19 +2062,34 @@
         axis=1,
     )
     packed = jnp.concatenate([query_proj, latent_proj, gains], axis=1)
-    shared_weight = lax.all_gather(
-        jnp.concatenate([shared_gate, shared_up], axis=1), "fsdp", axis=0, tiled=True
-    )
     if paired:
         low, high = (0, RAW_ROWS - TOPK), (0, 0)
         raw = jnp.concatenate(
             [jnp.pad(expert_ids.T.astype(F32), (low, high)), jnp.pad(expert_wts.T, (low, high))]
         )
-        tokens_all, packed_all, latent_up_weight, out_weight, raw = first_call(
+        (
+            tokens_all,
+            cotan_all,
+            packed_all,
+            latent_up_weight,
+            out_weight,
+            raw,
+            shared_weight,
+            shared_down_weight,
+        ) = first_call(
             block_in,
-            [packed, latent_up, out_proj, raw],
-            ("rows", "rows", "columns", "relative"),
-        )
+            out_cotan,
+            [
+                packed,
+                latent_up,
+                out_proj,
+                raw,
+                jnp.concatenate([shared_gate, shared_up], axis=1),
+                shared_down,
+            ],
+            ("rows", "rows", "columns", "relative", "rows", "columns"),
+        )
+        shared_weight = shared_weight.reshape(model_width, -1)
         packed_all = packed_all.reshape(-1, packed.shape[1])
         latent_up_weight = latent_up_weight.reshape(LAT, up_cols)
     else:
@@ -2033,9 +2097,11 @@
         latent_up_weight = lax.all_gather(latent_up, "fsdp", axis=0, tiled=True)
         out_weight = lax.all_gather(out_proj, "fsdp", axis=1, tiled=True)
         tokens_all = column_gather(block_in)
-    cotan_own, tokens_all, shared_weight = tie(out_cotan, tokens_all, shared_weight)
-    cotan_all = column_gather(cotan_own)
-    shared_down_weight = lax.all_gather(shared_down, "fsdp", axis=1, tiled=True)
+        cotan_all = column_gather(out_cotan)
+        shared_weight = lax.all_gather(
+            jnp.concatenate([shared_gate, shared_up], axis=1), "fsdp", axis=0, tiled=True
+        )
+        shared_down_weight = lax.all_gather(shared_down, "fsdp", axis=1, tiled=True)
     gain_attn = packed_all[:, joint].astype(F32)
     gain_ffn = packed_all[:, joint + 1].astype(F32)
     gain_latent = (
@@ -2098,7 +2164,7 @@
     )
     attn_part = jnp.dot(attended, out_weight, preferred_element_type=F32).astype(BF)
     if paired:
-        mixed_rows, normed_ffn_all, d_routed_in, out_array, *kept = expert_call(
+        mixed_rows, normed_ffn_all, d_routed_in, *kept = expert_call(
             attn_part,
             block_in,
             cotan_all,
@@ -2171,7 +2237,14 @@
             routed_up_grad,
             routed_down_grad,
         ) = middle_call(
-            d_ffn_rows, mixed_rows, out_cotan, gain_ffn[None, :], out_array, kept, local_hidden
+            d_ffn_rows,
+            mixed_rows,
+            out_cotan,
+            gain_ffn[None, :],
+            kept[:2],
+            routed_down,
+            kept[2:],
+            cap_rows,
         )
         ffn_gain_part = ffn_gain_part[0]
         routed_rows = routed_rows.astype(F32)
@@ -2183,8 +2256,11 @@
         d_mixed = out_cotan.astype(F32) + d_mixed_norm
         d_proj_all = column_gather(d_mixed.astype(BF))
     shared_grad = scatter(shared_part, 0)
-    d_proj_all, shared_grad = tie(d_proj_all, shared_grad)
-    ffn_rows = column_scatter(shared_rows + routed_rows)
+    down_own, ffn_rows, shared_grad = tie(
+        shared_down_part.astype(BF), (shared_rows + routed_rows).astype(BF), shared_grad
+    )
+    shared_down_grad = scatter(down_own, 1)
+    ffn_rows = column_scatter(ffn_rows)
     block_out = (mixed_rows + ffn_rows).astype(BF)
 
     out_part = jnp.dot(attended.T, d_proj_all, preferred_element_type=F32)
@@ -2237,7 +2313,6 @@
         -1, 128
     )
     joint_part = joint_part.astype(BF)
-    shared_down_grad = scatter(shared_down_part, 1)
     if paired:
         latent_width = joint_part.shape[1] - query_cols
         (

time: 823 us -> 700 us (0.85)
  waiting for transfers between devices: 162 us -> 0.05 us
  Pallas kernels: 503 us -> 529 us
  local copies, waits for them, and re-layouts: 39.3 us -> 52.5 us
    reduce_scatter x2, waiting for transfers between devices: 107 us -> 0.01 us  [scatter(): lax.psum_scatter(part.astype(BF), 'fsdp', scatter_dimension=dimension, ti...]
    reduce_scatter x1, waiting for transfers between devices: 41.7 us -> 0.01 us  [column_scatter(): lax.psum_scatter(values.astype(BF), 'tp', scatter_dimension=0, tiled=True)]
    pallas_call x1, Pallas kernels: 276 us -> 246 us  [expert_call(): pl.pallas_call(functools.partial(expert_kernel, cap, columns, size), out_...]
    pallas_call x1, Pallas kernels: 71.3 us -> 97.1 us  [first_call(): pl.pallas_call(functools.partial(first_kernel, columns, size, kinds), out...]
    pallas_call x1, Pallas kernels: 94.1 us -> 115 us  [middle_call(): pl.pallas_call(functools.partial(middle_kernel, cap, columns, size, exper...]
    all_gather x3 -> x0, waiting for transfers between devices: 12 us -> none  [the longest x1 12 us: column_gather(): return lax.all_gather(rows, 'tp', axis=0, tiled=True)]
    pallas_call x1, Pallas kernels: 61.3 us -> 70 us  [last_call(): pl.pallas_call(functools.partial(last_kernel, columns, size, latent_start...]
    unnamed x144 -> x142, local copies, waits for them, and re-layouts: 28.8 us -> 37.4 us
  transfers between devices with their start and end apart: 6 -> 3, of which waited for: 4 -> 0; matrix products, arithmetic and copies ran while one was open for 5% -> 7% of each run, Pallas kernels for 43% -> 27%
where the time goes in v7:
time: 700 us; the launch traced here: 690 us
  Pallas kernels  529 us (76%)
  matrix products  70.8 us (10%)
  local copies, waits for them, and re-layouts  52.5 us (8%)
  other arithmetic  22.5 us (3%)
  between operations  14.8 us (2%)
    pallas_call x1, Pallas kernels, expert_call(): pl.pallas_call(functools.partial(expert_kernel, cap, columns, size), out_...  246 us
    pallas_call x1, Pallas kernels, middle_call(): pl.pallas_call(functools.partial(middle_kernel, cap, columns, size, exper...  115 us
    pallas_call x1, Pallas kernels, first_call(): pl.pallas_call(functools.partial(first_kernel, columns, size, kinds), out...  97.1 us
    pallas_call x1, Pallas kernels, last_call(): pl.pallas_call(functools.partial(last_kernel, columns, size, latent_start...  70 us
    unnamed x142, local copies, waits for them, and re-layouts  37.4 us
  transfers between devices with their start and end apart: 3, of which 0 were waited for; matrix products, arithmetic and copies ran while one was open for 7% of the time, Pallas kernels for 27%

profile of v7, /device:TPU:0, one launch (start us, length us, event | category | flops | bytes accessed | tf_op | source)
XLA Modules:
  0.0 689.6 jit_solution(7095102289635037147)
XLA Ops:
  7.8 1.2 copy.122
  9.0 1.2 copy.123
  10.2 1.2 copy.118
  11.7 1.1 pad_maximum_fusion.6.refs_6_
  13.4 1.1 concatenate.43.refs_2_
  14.5 97.1 %first_gather.1 = (bf16[512,2048]{1,0:T(8,128)(2,1)}, bf16[512,2048]{1,0:T(8,128)(2,1)}, bf16[8,256,1408]{2,1,0:T(8,128)(2,1)}, bf16[8,64,1024]{2,1,0:T(8,128)(2...) custom-call(bf16[128,2048]{1,0:T(8,128)(2,1)} %refs_1_.5, ...), custom_call_target="tpu_custom_call" | custom-call | bytes 251658240 | tf_op jit(solution)/shard_map/first_gather/pallas_call | solution.py:1235
  111.6 2.2 fusion.47
  114.2 2.1 fusion.5
  116.3 6.5 fusion.16
  123.8 1.3 slice.123
  125.3 1.1 copy.154
  126.3 1.1 copy.155
  127.4 3.0 copy.127
  130.6 2.3 copy.126
  132.8 2.1 convolution_convert_fusion.6
  135.9 1.5 slice.196
  138.9 1.2 subtract_convert_fusion.1
  142.3 2.1 fusion.51
  144.9 1.6 copy-done.8
  147.6 2.6 convolution_convert_fusion.4.refs_0_
  150.2 246.4 %experts.1 = (f32[128,2048]{1,0:T(8,128)}, bf16[512,2048]{1,0:T(8,128)(2,1)}, bf16[512,2048]{1,0:T(8,128)(2,1)}, f32[16,512]{1,0:T(8,128)}, f32[16,512]{1,0:T(8,...) custom-call(bf16[512,2048]{1,0:T(8,128)(2,1)} %convolution_convert_f, ...), custom_call_target="tpu_custom_call" | custom-call | flops 17179869184 | bytes 838860800 | tf_op jit(solution)/shard_map/experts/pallas_call | solution.py:1057
  396.6 6.7 fusion.52
  403.4 2.2 multiply_convert_fusion.3
  406.5 3.2 convolution_convert_fusion.2
  409.7 5.3 convolution_convert_fusion.1
  415.0 8.1 %add_convert_fusion.1.refs_0_ = bf16[512,2048]{1,0:T(8,128)(2,1)} fusion(bf16[512,2048]{1,0:T(8,128)(2,1)} %get-tuple-element.61, bf16[2048,1408]{1,0:T(8,128)(2,1)} %bitcast.85, bf16[512,704]{0,1:T(8,128)(2,1)S(1)} %get-tuple-element.153, bf16[512,704]{0,1:T(8,128)(2,1)S(1)} %get-tuple-element.152), kind=kOutput, calls=%fused_computation.13 | convolution fusion | flops 2958819328 | bytes 11403264 | tf_op jit(solution)/shard_map/dot_general | solution.py:2223
  423.2 115.2 %middle.1 = (f32[128,2048]{1,0:T(8,128)}, bf16[512,2048]{1,0:T(8,128)(2,1)}, f32[1,2048]{1,0:T(1,128)}, bf16[512,2048]{1,0:T(8,128)(2,1)}, f32[2,352,2048]{2,1,0...) custom-call(bf16[512,2048]{1,0:T(8,128)(2,1)} %add_convert_fusion.1., ...), custom_call_target="tpu_custom_call" | custom-call | flops 19327352832 | bytes 314572800 | tf_op jit(solution)/shard_map/middle/pallas_call | solution.py:1645
  538.4 5.9 add_convert_fusion
  544.3 1.5 copy-done.53
  545.9 3.0 convolution_convert_fusion.7
  549.8 1.2 multiply_convert_fusion
  553.6 1.5 copy-done.4
  557.5 2.0 copy.140
  559.6 2.3 multiply_bitcast_fusion.1
  563.1 1.3 constant_dynamic-update-slice_fusion.1
  564.5 1.1 slice_reduce_fusion
  566.3 8.0 %fusion.4 = (f32[2048]{0:T(1024)S(1)}, bf16[512,2048]{1,0:T(8,128)(2,1)}) fusion(bf16[512,2048]{1,0:T(8,128)(2,1)S(1)} %copy-done.17, f32[512]{0:T(512)S(1)} %copy-done.48, bf16[512,1408]{0,1:T(8,128)(2,1)S(1)} %broadcast_dynamic-update-slice_fusion, bf16[2048,1408]{1,0:T(8,128)(2,1)} %bitcast.81), kind=kOutput, calls=%fused_computation.8 | convolution fusion | flops 2958030848 | bytes 11413504 | tf_op jit(solution)/shard_map/dot_general | solution.py:2309
  574.3 1.9 convolution_convert_fusion.5.refs_5_
  576.3 2.6 convolution_convert_fusion.3.refs_6_
  578.9 5.7 convolution_convert_fusion.refs_4_
  584.6 70.0 %last_sums.1 = (f32[128,2048]{1,0:T(8,128)S(1)}, bf16[256,1408]{1,0:T(8,128)(2,1)S(1)}, bf16[64,1024]{1,0:T(8,128)(2,1)S(1)}, bf16[512,256]{1,0:T(8,128)(2,1)S(1...) custom-call(bf16[512,2048]{1,0:T(8,128)(2,1)} %get-tuple-element.155, ...), custom_call_target="tpu_custom_call" | custom-call | bytes 188743680 | tf_op jit(solution)/shard_map/last_sums/pallas_call | solution.py:1913
  659.4 2.3 copy.142
  661.7 1.1 copy.143
  662.8 1.9 add_convert_fusion.2
  664.8 1.9 convert_element_type.289
  668.3 6.0 copy.170
  674.3 6.0 copy.171
  680.3 2.5 copy.172
  (183 shorter events, 24.1 us)
Async XLA Ops:
  7.2 4.1 copy-start.55
  7.2 4.3 copy-start.49
  7.2 4.4 copy-start.50
  7.2 4.5 copy-start.39
  7.2 5.5 copy-start.40
  7.2 6.2 copy-start.32
  7.2 537.0 %reduce-scatter.4.cloned.1.call-start = ((), (), s32[]{:S(2)}) async-start(), calls=%async_computation.3 | async-start | bytes 6488064 | tf_op jit(solution)/shard_map/reduce_scatter | solution.py:2116
  7.3 131.2 %copy-start.33 = (f32[512]{0:T(512)}, f32[512]{0:T(512)S(1)}, u32[]{:S(2)}) copy-start(f32[512]{0:T(512)S(1)} %iota_convert_fusion) | copy-start | bytes 6148
  114.2 8.6 %copy-start.1 = (f32[2048,1]{0,1:T(1,128)}, f32[2048,1]{0,1:T(1,128)S(1)}, u32[]{:S(2)}) copy-start(f32[2048,1]{0,1:T(1,128)S(1)} %copy.158) | copy-start | bytes 24580
  116.3 6.5 copy-start.47
  122.8 10.0 %copy-start.3 = (f32[512,1408]{1,0:T(8,128)}, f32[512,1408]{1,0:T(8,128)S(1)}, u32[]{:S(2)}) copy-start(f32[512,1408]{1,0:T(8,128)S(1)} %fusion.16) | copy-start | bytes 8650756
  130.4 4.5 copy-start.37
  130.5 4.4 copy-start.35
  132.8 4.6 copy-start.43
  135.9 2.6 copy-start.45
  135.9 6.3 copy-start.6
  137.4 4.8 copy-start.19
  142.3 2.2 copy-start.15
  144.4 2.1 copy-start.8
  144.4 2.1 copy-start.41
  144.5 3.1 copy-start.52
  146.6 3.6 copy-start.56
  396.6 6.7 copy-start.51
  396.6 6.7 copy-start.54
  406.5 3.2 copy-start.60
  423.2 239.6 %reduce-scatter.6.cloned.1.call-start = ((), (), s32[]{:S(2)}) async-start(), calls=%async_computation.4 | async-start | bytes 2621440 | tf_op jit(solution)/shard_map/reduce_scatter | solution.py:103
  544.3 120.5 %reduce-scatter.8.cloned.1.call-start = ((), (), s32[]{:S(2)}) async-start(), calls=%async_computation.5 | async-start | bytes 3244032 | tf_op jit(solution)/shard_map/reduce_scatter | solution.py:2116
  545.9 3.0 copy-start.9
  545.9 3.1 copy-start.16
  545.9 3.1 copy-start.42
  552.4 2.7 copy-start.4
  553.5 2.0 copy-start.38
  553.5 2.9 copy-start.10
  556.5 3.1 copy-start.7
  559.6 2.4 copy-start.25
  559.6 2.4 copy-start.27
  563.0 2.5 copy-start.34
  563.0 2.5 copy-start.46
  563.0 3.2 copy-start.17
  563.1 3.2 copy-start.48
  566.3 8.1 %copy-start.44 = (f32[1,2048]{1,0:T(1,128)S(1)}, f32[1,2048]{1,0:T(1,128)}, u32[]{:S(2)}) copy-start(f32[1,2048]{1,0:T(1,128)} %get-tuple-element.75) | copy-start | bytes 24580
  566.3 8.1 %copy-start.11 = (bf16[512,4,256]{0,2,1:T(8,128)(2,1)S(1)}, bf16[512,4,256]{0,2,1:T(8,128)(2,1)}, u32[]{:S(2)}) copy-start(bf16[512,4,256]{0,2,1:T(8,128)(2,1)} %copy-done.10) | copy-start | bytes 3145732
  576.3 2.6 copy-start.2
  578.9 5.7 copy-start
  654.6 3.7 copy-start.12
  659.4 3.4 copy-start.21
  668.3 12.0 %slice-start = ((s8[5767168]{0:T(1024)(128)(4,1)}), s8[4194304]{0:T(1024)(128)(4,1)S(1)}, s32[]{:S(2)}) async-start(s8[5767168]{0:T(1024)(128)(4,1)} %bitcast.69), calls=%async_computation.6 | async-start | bytes 8388608
  674.3 6.0 slice-start.1
  (18 other events, 23.4 us)
Sparse Core Ops, SparseCore 0:
  423.3 81.8 reduce-scatter.3
  544.4 42.8 reduce-scatter.5
  590.7 54.1 reduce-scatter.7

commit v8 on v7

--- a/solution.py
+++ b/solution.py
@@ -723,11 +723,18 @@
         lax.fori_loop(0, width // tile, gather, 0)
 
 
+def plane_place(r):
+    place = lax.axis_index("fsdp")
+    core, along, across = place % 2, (place // 2) % 2, place // 4
+    return (across + r // 4) % 2 * 4 + (along + r // 2 % 2) % 2 * 2 + (core + r % 2) % 2
+
+
 def expert_kernel(cap, columns, size, *refs):
     (
         attn_in,
         tokens_in,
         cotan_in,
+        cotan_left,
         gate_in,
         up_in,
         down_in,
@@ -895,16 +902,27 @@
     def source(own, gathered, r):
         return own if r == 0 else gathered.at[r - 1]
 
+    half = width // 2
+    left, right = pl.ds(0, half), pl.ds(half, half)
+
     def load(b, k):
-        own, gathered, target = ((ffn_all, x_others, xb), (cotan_in, dy_others, db))[k]
-        return [
-            pltpu.make_async_copy(
-                source(own, gathered, r).at[rows_of(b)],
-                target.at[r // 2, pl.ds(r % 2 * size, size)],
-                loads.at[8 * k + r],
-            )
-            for r in range(8)
-        ]
+        copies = []
+        for r in range(8):
+            place = pl.ds(r % 2 * size, size)
+            if k == 0:
+                plan = [(source(ffn_all, x_others, r).at[rows_of(b)], xb.at[r // 2, place])]
+            else:
+                start = plane_place(r) * SEQ + (lax.axis_index("tp") + b) % columns * size
+                plan = [
+                    (source(cotan_in, dy_others, r).at[rows_of(b)], db.at[r // 2, place, right]),
+                    (
+                        cotan_left.at[pl.ds(pl.multiple_of(start, size), size)],
+                        db.at[r // 2, place, left],
+                    ),
+                ]
+            for n, (src, dst) in enumerate(plan):
+                copies.append(pltpu.make_async_copy(src, dst, loads.at[8 * (k + n) + r]))
+        return copies
 
     def combine(b, keep):
         token_sums(slot_table, experts, columns, size, wide, b, dxs, keep)
@@ -928,7 +946,7 @@
             for copy in spills(previous[b]):
                 copy.wait()
         for q in range(count):
-            for copy in x_load[2 * q : 2 * q + 2] + dy_load[2 * q : 2 * q + 2]:
+            for copy in x_load[2 * q : 2 * q + 2] + dy_load[4 * q : 4 * q + 4]:
                 copy.wait()
             hit = select_rows(slots_of(slot_table, experts, columns, size, b, q), experts, wide)
             weights = slot_weights(hit, slots_of(weight_table, experts, columns, size, b, q), experts, wide)
@@ -1039,7 +1057,7 @@
     plane.drain(3)
 
 
-def expert_call(attn_part, tokens, cotan_all, gate, up, down, gain, raw, cap):
+def expert_call(attn_part, tokens, cotan_right, cotan_left, gate, up, down, gain, raw, cap):
     columns = lax.axis_size("tp")
     size, width = tokens.shape
     experts, local_hidden, _ = gate.shape
@@ -1067,10 +1085,10 @@
             array(columns, experts, slots, pad),
             array(columns, experts, slots, 2 * pad),
             array(7, SEQ, width),
-            array(7, SEQ, width),
+            array(7, SEQ, width // 2),
         ]
         + landing,
-        in_specs=[anywhere] * 6 + [held] * 2,
+        in_specs=[anywhere] * 7 + [held] * 2,
         out_specs=[anywhere] * 3 + [held] * 2 + [anywhere] * 8,
         scratch_shapes=[
             pltpu.VMEM((size, width), BF),
@@ -1097,7 +1115,7 @@
             pltpu.SemaphoreType.DMA((remote,)),
             pltpu.SemaphoreType.DMA((remote,)),
             pltpu.SemaphoreType.DMA((3 + 3 * experts,)),
-            pltpu.SemaphoreType.DMA((16,)),
+            pltpu.SemaphoreType.DMA((24,)),
             pltpu.SemaphoreType.DMA((near,)),
             pltpu.SemaphoreType.DMA((4,)),
         ],
@@ -1110,7 +1128,7 @@
             transcendentals=0,
         ),
         name="experts",
-    )(attn_part, tokens, cotan_all, gate, up, down, gain, raw)
+    )(attn_part, tokens, cotan_right, cotan_left, gate, up, down, gain, raw)
     return results[:9]
 
 
@@ -1234,11 +1252,11 @@
 
     return pl.pallas_call(
         functools.partial(first_kernel, columns, size, kinds),
-        out_shape=[jax.ShapeDtypeStruct((columns * size, width), BF)] * 2
+        out_shape=[jax.ShapeDtypeStruct((columns * size, rows.shape[1]), BF) for rows in (tokens, cotan)]
         + [jax.ShapeDtypeStruct(gathered(own, kind), own.dtype) for own, kind in zip(owns, kinds)],
         in_specs=[anywhere] * (2 + len(owns)),
         out_specs=[anywhere] * (2 + len(owns)),
-        scratch_shapes=[pltpu.VMEM((size, width), BF)] * 2
+        scratch_shapes=[pltpu.VMEM(rows.shape, BF) for rows in (tokens, cotan)]
         + [pltpu.VMEM(own.shape, own.dtype) for own in owns]
         + [
             pltpu.SemaphoreType.DMA((copies,)),
@@ -1738,21 +1756,14 @@
     ) = refs
     partner, along, across = plane_neighbours()
     column = column_neighbours(columns)
-    place, row = lax.axis_index("fsdp"), lax.axis_index("tp")
-    core, right, above = place % 2, (place // 2) % 2, place // 4
-
-    def absolute(r):
-        return (
-            (above + r // 4) % 2 * 4 + (right + r // 2 % 2) % 2 * 2 + (core + r % 2) % 2
-        )
-
+    row = lax.axis_index("tp")
     greet([partner, along, across] + column)
     each = plane_sum_sizes(1)[0]
     joint_rows, up_rows = joint_chip.shape[2], up_chip.shape[2]
     out_cols = out_chip.shape[3]
 
     def by_rows(ref, count):
-        return lambda r, h: ref.at[pl.ds(pl.multiple_of(absolute(r) * count, count), count)]
+        return lambda r, h: ref.at[pl.ds(pl.multiple_of(plane_place(r) * count, count), count)]
 
     joint = PlaneSum(
         by_rows(joint_in, joint_rows),
@@ -1778,7 +1789,7 @@
     )
     out = PlaneSum(
         lambda r, h: out_in.at[
-            :, pl.ds(pl.multiple_of(absolute(r) * out_cols, out_cols), out_cols)
+            :, pl.ds(pl.multiple_of(plane_place(r) * out_cols, out_cols), out_cols)
         ],
         out_chip,
         out_theirs,
@@ -2067,29 +2078,19 @@
         raw = jnp.concatenate(
             [jnp.pad(expert_ids.T.astype(F32), (low, high)), jnp.pad(expert_wts.T, (low, high))]
         )
-        (
-            tokens_all,
-            cotan_all,
-            packed_all,
-            latent_up_weight,
-            out_weight,
-            raw,
-            shared_weight,
-            shared_down_weight,
-        ) = first_call(
+        half = model_width // 2
+        cotan_left = lax.all_gather(out_cotan[:, :half], ("fsdp", "tp"), axis=0, tiled=True)
+        tokens_all, cotan_right, packed_all, latent_up_weight, out_weight, raw = first_call(
             block_in,
-            out_cotan,
-            [
-                packed,
-                latent_up,
-                out_proj,
-                raw,
-                jnp.concatenate([shared_gate, shared_up], axis=1),
-                shared_down,
-            ],
-            ("rows", "rows", "columns", "relative", "rows", "columns"),
-        )
-        shared_weight = shared_weight.reshape(model_width, -1)
+            out_cotan[:, half:],
+            [packed, latent_up, out_proj, raw],
+            ("rows", "rows", "columns", "relative"),
+        )
+        shared_own, down_own, cotan_right = tie(
+            jnp.concatenate([shared_gate, shared_up], axis=1), shared_down, cotan_right
+        )
+        own_left = lax.dynamic_slice_in_dim(cotan_left, fsdp_rank * SEQ, SEQ, axis=0)
+        cotan_all = jnp.concatenate([own_left, cotan_right], axis=1)
         packed_all = packed_all.reshape(-1, packed.shape[1])
         latent_up_weight = latent_up_weight.reshape(LAT, up_cols)
     else:
@@ -2098,10 +2099,9 @@
         out_weight = lax.all_gather(out_proj, "fsdp", axis=1, tiled=True)
         tokens_all = column_gather(block_in)
         cotan_all = column_gather(out_cotan)
-        shared_weight = lax.all_gather(
-            jnp.concatenate([shared_gate, shared_up], axis=1), "fsdp", axis=0, tiled=True
-        )
-        shared_down_weight = lax.all_gather(shared_down, "fsdp", axis=1, tiled=True)
+        shared_own, down_own = jnp.concatenate([shared_gate, shared_up], axis=1), shared_down
+    shared_weight = lax.all_gather(shared_own, "fsdp", axis=0, tiled=True)
+    shared_down_weight = lax.all_gather(down_own, "fsdp", axis=1, tiled=True)
     gain_attn = packed_all[:, joint].astype(F32)
     gain_ffn = packed_all[:, joint + 1].astype(F32)
     gain_latent = (
@@ -2167,7 +2167,8 @@
         mixed_rows, normed_ffn_all, d_routed_in, *kept = expert_call(
             attn_part,
             block_in,
-            cotan_all,
+            cotan_right,
+            cotan_left,
             routed_gate,
             routed_up,
             routed_down,

time: 700 us -> 702 us (level)
    unnamed x142 -> x140, local copies, waits for them, and re-layouts: 37.4 us -> 32.7 us
  transfers between devices with their start and end apart: 3 -> 6, of which waited for: 0 -> 0; matrix products, arithmetic and copies ran while one was open for 7% -> 14% of each run, Pallas kernels for 27% -> 76%
where the time goes in v8:
time: 702 us; the launch traced here: 692 us
  Pallas kernels  525 us (75%)
  matrix products  76.7 us (11%)
  local copies, waits for them, and re-layouts  51.6 us (7%)
  other arithmetic  21.4 us (3%)
  between operations  15.4 us (2%)
    pallas_call x1, Pallas kernels, expert_call(): pl.pallas_call(functools.partial(expert_kernel, cap, columns, size), out_...  240 us
    pallas_call x1, Pallas kernels, middle_call(): pl.pallas_call(functools.partial(middle_kernel, cap, columns, size, exper...  116 us
    pallas_call x1, Pallas kernels, first_call(): pl.pallas_call(functools.partial(first_kernel, columns, size, kinds), out...  99.6 us
    pallas_call x1, Pallas kernels, last_call(): pl.pallas_call(functools.partial(last_kernel, columns, size, latent_start...  69.8 us
    unnamed x140, local copies, waits for them, and re-layouts  32.7 us
  transfers between devices with their start and end apart: 6, of which 0 were waited for; matrix products, arithmetic and copies ran while one was open for 14% of the time, Pallas kernels for 76%

profile of v8, /device:TPU:0, one launch (start us, length us, event | category | flops | bytes accessed | tf_op | source)
XLA Modules:
  0.0 691.7 jit_solution(15922734679625791986)
XLA Ops:
  7.3 1.9 fusion.53
  9.2 1.2 copy.112
  12.8 1.1 concatenate.46.refs_2_
  14.5 99.6 %first_gather.1 = (bf16[512,2048]{1,0:T(8,128)(2,1)}, bf16[512,1024]{1,0:T(8,128)(2,1)}, bf16[8,256,1408]{2,1,0:T(8,128)(2,1)}, bf16[8,64,1024]{2,1,0:T(8,128)(2...) custom-call(bf16[128,2048]{1,0:T(8,128)(2,1)} %refs_1_.3, bf16[128,1024]{1,0:T(8,128)(2,1)} %get-tuple-element.168.refs_1_, ...), custom_call_target="tpu_custom_call" | custom-call | bytes 251658240 | tf_op jit(solution)/shard_map/first_gather/pallas_call | solution.py:1253
  116.4 2.4 fusion.50
  119.1 2.1 fusion.5
  121.2 6.5 fusion.17
  127.7 1.0 fusion.51
  128.7 1.3 slice.131
  130.2 1.1 copy.146
  131.3 1.1 copy.147
  132.3 3.0 copy.119
  135.5 2.3 copy.118
  137.8 2.2 convolution_convert_fusion.6
  142.7 2.1 fusion.55
  145.4 1.7 copy-done.9
  147.1 1.0 copy-done.53
  148.1 2.6 convolution_convert_fusion.4.refs_0_
  151.3 2.3 constant_dynamic-slice_fusion
  153.6 239.7 %experts.1 = (f32[128,2048]{1,0:T(8,128)}, bf16[512,2048]{1,0:T(8,128)(2,1)}, bf16[512,2048]{1,0:T(8,128)(2,1)}, f32[16,512]{1,0:T(8,128)}, f32[16,512]{1,0:T(8,...) custom-call(bf16[512,2048]{1,0:T(8,128)(2,1)} %convolution_convert_f, ...), custom_call_target="tpu_custom_call" | custom-call | flops 17179869184 | bytes 838860800 | tf_op jit(solution)/shard_map/experts/pallas_call | solution.py:1075
  393.3 8.2 %fusion.56 = f32[512,1408]{0,1:T(8,128)} fusion(bf16[512,2048]{1,0:T(8,128)(2,1)} %get-tuple-element.61, bf16[2048,1408]{0,1:T(8,128)(2,1)} %all-gather.8.cloned.1.call-done), kind=kOutput, calls=%fused_computation.123 | convolution fusion | flops 2952790016 | bytes 10747904 | tf_op jit(solution)/shard_map/dot_general | solution.py:2216
  401.5 4.8 multiply_convert_fusion.3
  407.2 3.3 convolution_convert_fusion.2
  410.5 7.8 %convolution_convert_fusion.1 = bf16[2048,1408]{1,0:T(8,128)(2,1)} fusion(bf16[512,2048]{1,0:T(8,128)(2,1)} %get-tuple-element.61, bf16[512,704]{0,1:T(8,128)(2,1)S(1)} %get-tuple-element.155, bf16[512,704]{0,1:T(8,128)(2,1)S(1)} %get-tuple-element.154), kind=kOutput, calls=%fused_computation.2 | convolution fusion | flops 2958557184 | bytes 9306112 | tf_op jit(solution)/shard_map/dot_general | solution.py:2223
  418.3 7.3 %add_convert_fusion.1.refs_0_ = bf16[512,2048]{1,0:T(8,128)(2,1)} fusion(bf16[512,2048]{1,0:T(8,128)(2,1)S(1)} %copy-done.59, bf16[2048,1408]{0,1:T(8,128)(2,1)} %all-gather.8.cloned.1.call-done, bf16[512,704]{0,1:T(8,128)(2,1)S(1)} %get-tuple-element.155, bf16[512,704]{0,1:T(8,128)(2,1)S(1)} %get-tuple-element.154), kind=kOutput, calls=%fused_computation.13 | convolution fusion | flops 2958819328 | bytes 11403264 | tf_op jit(solution)/shard_map/dot_general | solution.py:2224
  426.0 116.0 %middle.1 = (f32[128,2048]{1,0:T(8,128)}, bf16[512,2048]{1,0:T(8,128)(2,1)}, f32[1,2048]{1,0:T(1,128)}, bf16[512,2048]{1,0:T(8,128)(2,1)}, f32[2,352,2048]{2,1,0...) custom-call(bf16[512,2048]{1,0:T(8,128)(2,1)} %add_convert_fusion.1., ...), custom_call_target="tpu_custom_call" | custom-call | flops 19327352832 | bytes 314572800 | tf_op jit(solution)/shard_map/middle/pallas_call | solution.py:1663
  542.1 5.9 add_convert_fusion
  548.0 1.5 copy-done.54
  549.6 3.0 convolution_convert_fusion.7
  553.5 1.2 multiply_convert_fusion
  557.2 1.5 copy-done.4
  560.2 1.0 multiply_convert_fusion.4
  561.2 2.0 copy.132
  563.3 2.3 multiply_bitcast_fusion.1
  566.7 1.3 constant_dynamic-update-slice_fusion.1
  568.1 1.1 slice_reduce_fusion
  570.0 8.0 %fusion.4 = (f32[2048]{0:T(1024)S(1)}, bf16[512,2048]{1,0:T(8,128)(2,1)}) fusion(bf16[512,2048]{1,0:T(8,128)(2,1)S(1)} %copy-done.18, f32[512]{0:T(512)S(1)} %copy-done.52, bf16[512,1408]{0,1:T(8,128)(2,1)S(1)} %broadcast_dynamic-update-slice_fusion, bf16[2048,1408]{1,0:T(8,128)(2,1)} %bitcast.78), kind=kOutput, calls=%fused_computation.8 | convolution fusion | flops 2958030848 | bytes 11413504 | tf_op jit(solution)/shard_map/dot_general | solution.py:2310
  578.0 1.9 convolution_convert_fusion.5.refs_5_
  579.9 2.6 convolution_convert_fusion.3.refs_6_
  582.5 5.7 convolution_convert_fusion.refs_4_
  588.2 69.8 %last_sums.1 = (f32[128,2048]{1,0:T(8,128)S(1)}, bf16[256,1408]{1,0:T(8,128)(2,1)S(1)}, bf16[64,1024]{1,0:T(8,128)(2,1)S(1)}, bf16[512,256]{1,0:T(8,128)(2,1)S(1...) custom-call(bf16[512,2048]{1,0:T(8,128)(2,1)} %get-tuple-element.157, ...), custom_call_target="tpu_custom_call" | custom-call | bytes 188743680 | tf_op jit(solution)/shard_map/last_sums/pallas_call | solution.py:1924
  662.0 1.1 copy.134
  663.1 1.1 copy.135
  664.4 1.9 add_convert_fusion.2
  666.4 1.9 convert_element_type.289
  669.9 6.0 copy.162
  675.9 6.0 copy.163
  681.9 2.5 copy.164
  (192 shorter events, 23.2 us)
Async XLA Ops:
  7.2 5.6 copy-start.34
  7.2 6.7 copy-start.43
  7.2 6.7 copy-start.44
  7.2 144.1 %all-gather.4.cloned.1.call-start = ((), (), s32[]{:S(2)}) async-start(), calls=%async_computation.3 | async-start | bytes 8650752 | tf_op jit(solution)/shard_map/all_gather | solution.py:2082
  9.2 384.1 %all-gather.8.cloned.1.call-start = ((), (), s32[]{:S(2)}) async-start(), calls=%async_computation.5 | async-start | bytes 6488064 | tf_op jit(solution)/shard_map/all_gather | solution.py:2103
  10.4 103.7 %copy-start.35 = (bf16[256,704]{0,1:T(8,128)(2,1)S(1)}, bf16[256,704]{0,1:T(8,128)(2,1)}, u32[]{:S(2)}) copy-start(bf16[256,704]{0,1:T(8,128)(2,1)} %param.31) | copy-start | bytes 1081348
  10.4 103.7 %copy-start.36 = (bf16[256,704]{0,1:T(8,128)(2,1)S(1)}, bf16[256,704]{0,1:T(8,128)(2,1)}, u32[]{:S(2)}) copy-start(bf16[256,704]{0,1:T(8,128)(2,1)} %param.30) | copy-start | bytes 1081348
  115.1 286.5 %all-gather.6.cloned.1.call-start = ((), (), s32[]{:S(2)}) async-start(), calls=%async_computation.4 | async-start | bytes 3244032 | tf_op jit(solution)/shard_map/all_gather | solution.py:2104
  115.8 432.2 %reduce-scatter.4.cloned.1.call-start = ((), (), s32[]{:S(2)}) async-start(), calls=%async_computation.6 | async-start | bytes 6488064 | tf_op jit(solution)/shard_map/reduce_scatter | solution.py:2116
  115.8 24.1 %copy-start.37 = (f32[512]{0:T(512)}, f32[512]{0:T(512)S(1)}, u32[]{:S(2)}) copy-start(f32[512]{0:T(512)S(1)} %iota_convert_fusion) | copy-start | bytes 6148
  119.1 8.6 %copy-start.1 = (f32[2048,1]{0,1:T(1,128)}, f32[2048,1]{0,1:T(1,128)S(1)}, u32[]{:S(2)}) copy-start(f32[2048,1]{0,1:T(1,128)S(1)} %copy.150) | copy-start | bytes 24580
  121.2 6.5 copy-start.51
  127.7 10.0 %copy-start.3 = (f32[512,1408]{1,0:T(8,128)}, f32[512,1408]{1,0:T(8,128)S(1)}, u32[]{:S(2)}) copy-start(f32[512,1408]{1,0:T(8,128)S(1)} %fusion.17) | copy-start | bytes 8650756
  135.4 4.6 copy-start.41
  135.5 4.5 copy-start.39
  137.8 2.2 copy-start.49
  137.8 3.3 copy-start.8
  142.7 2.2 copy-start.16
  144.9 2.2 copy-start.9
  144.9 2.2 copy-start.45
  144.9 3.2 copy-start.53
  147.1 3.7 copy-start.56
  393.3 8.2 %copy-start.22 = (bf16[512,1024]{1,0:T(8,128)(2,1)S(1)}, bf16[512,1024]{1,0:T(8,128)(2,1)}, u32[]{:S(2)}) copy-start(bf16[512,1024]{1,0:T(8,128)(2,1)} %constant_dynamic-slice_fusion) | copy-start | bytes 3145732
  393.3 8.2 %copy-start.55 = (bf16[512,1024]{1,0:T(8,128)(2,1)S(1)}, bf16[512,1024]{1,0:T(8,128)(2,1)}, u32[]{:S(2)}) copy-start(bf16[512,1024]{1,0:T(8,128)(2,1)} %get-tuple-element.57.refs_2_) | copy-start | bytes 3145732
  410.5 7.8 %copy-start.59 = (bf16[512,2048]{1,0:T(8,128)(2,1)S(1)}, bf16[512,2048]{1,0:T(8,128)(2,1)}, u32[]{:S(2)}) copy-start(bf16[512,2048]{1,0:T(8,128)(2,1)} %get-tuple-element.63) | copy-start | bytes 6291460
  425.6 238.6 %reduce-scatter.6.cloned.1.call-start = ((), (), s32[]{:S(2)}) async-start(), calls=%async_computation.7 | async-start | bytes 2621440 | tf_op jit(solution)/shard_map/reduce_scatter | solution.py:103
  548.0 118.4 %reduce-scatter.8.cloned.1.call-start = ((), (), s32[]{:S(2)}) async-start(), calls=%async_computation.8 | async-start | bytes 3244032 | tf_op jit(solution)/shard_map/reduce_scatter | solution.py:2116
  549.5 3.0 copy-start.10
  549.5 3.1 copy-start.17
  549.5 3.1 copy-start.46
  556.1 2.7 copy-start.4
  557.2 2.0 copy-start.40
  557.2 2.0 copy-start.42
  557.2 2.9 copy-start.11
  560.1 3.1 copy-start.7
  563.3 2.4 copy-start.27
  563.3 2.4 copy-start.29
  566.7 2.5 copy-start.38
  566.7 2.5 copy-start.50
  566.7 3.2 copy-start.18
  566.7 3.2 copy-start.52
  569.9 8.1 %copy-start.48 = (f32[1,2048]{1,0:T(1,128)S(1)}, f32[1,2048]{1,0:T(1,128)}, u32[]{:S(2)}) copy-start(f32[1,2048]{1,0:T(1,128)} %get-tuple-element.77) | copy-start | bytes 24580
  569.9 8.1 %copy-start.12 = (bf16[512,4,256]{0,2,1:T(8,128)(2,1)S(1)}, bf16[512,4,256]{0,2,1:T(8,128)(2,1)}, u32[]{:S(2)}) copy-start(bf16[512,4,256]{0,2,1:T(8,128)(2,1)} %copy-done.11) | copy-start | bytes 3145732
  579.9 2.6 copy-start.2
  582.5 5.7 copy-start
  658.1 3.7 copy-start.13
  669.9 12.0 %slice-start = ((s8[5767168]{0:T(1024)(128)(4,1)}), s8[4194304]{0:T(1024)(128)(4,1)S(1)}, s32[]{:S(2)}) async-start(s8[5767168]{0:T(1024)(128)(4,1)} %bitcast.66), calls=%async_computation.9 | async-start | bytes 8388608
  675.9 6.0 slice-start.1
  (21 other events, 26.6 us)
Sparse Core Ops, SparseCore 0:
  11.5 107.7 all-gather.3
  121.8 50.3 all-gather.7
  174.0 42.5 all-gather.5
  425.7 82.4 reduce-scatter.3
  548.1 43.0 reduce-scatter.5
  594.4 53.2 reduce-scatter.7

commit v9 on v7

--- a/solution.py
+++ b/solution.py
@@ -443,8 +443,9 @@
 
 
 class ColumnGather:
-    def __init__(self, blocks, rows_of, sends, arrivals, base):
+    def __init__(self, blocks, rows_of, sends, arrivals, base, own=None):
         self.blocks, self.rows_of = blocks, rows_of
+        self.own = blocks.at[rows_of(0)] if own is None else own
         self.sends, self.arrivals, self.base = sends, arrivals, base
         self.row = lax.axis_index("tp")
         self.column = column_neighbours(4)
@@ -452,7 +453,7 @@
     def direct(self, s):
         place = self.blocks.at[self.rows_of(0)]
         return mesh_copy(
-            place, place, self.sends, self.arrivals, self.base + s - 1, self.column[s - 1]
+            self.own, place, self.sends, self.arrivals, self.base + s - 1, self.column[s - 1]
         )
 
     def start(self):
@@ -764,6 +765,7 @@
         stage,
         hid,
         dgu,
+        d_hidden,
         slot_table,
         weight_table,
         sends,
@@ -814,8 +816,7 @@
     ]
     for copy in first:
         copy.start()
-    order = (0, 2, 1, 3)
-    for b in order:
+    for b in (0, 2, 1):
         dy_gather.start(b)
     if pad > local_hidden:
         rest = pad - local_hidden
@@ -867,6 +868,150 @@
     slots_out[...] = slot_table[...]
     weights_out[...] = weight_table[...]
 
+    def enter(b):
+        if b > 0:
+            gather.wait(b)
+        x_gather.start(b)
+
+    def ready(b):
+        x_gather.last(b)
+        x_gather.arrived(b, [2, 5, 6, 7])
+
+    def source(own, gathered, r):
+        return own if r == 0 else gathered.at[r - 1]
+
+    def load(b, k):
+        own, gathered, target = ((ffn_all, x_others, xb), (cotan_in, dy_others, db))[k]
+        return [
+            pltpu.make_async_copy(
+                source(own, gathered, r).at[rows_of(b)],
+                target.at[r // 2, pl.ds(r % 2 * size, size)],
+                loads.at[8 * k + r],
+            )
+            for r in range(8)
+        ]
+
+    def combine(b, keep):
+        token_sums(slot_table, experts, columns, size, wide, b, dxs, keep)
+
+    def spills(b):
+        return [
+            pltpu.make_async_copy(xs, x_all.at[b], spill.at[0]),
+            pltpu.make_async_copy(hid.at[b], hid_all.at[b], spill.at[1]),
+            pltpu.make_async_copy(dgu, dgu_all.at[b], spill.at[2]),
+        ]
+
+    def d_spill(b):
+        return pltpu.make_async_copy(ds, d_all.at[b], spill.at[3])
+
+    def choice(b, q):
+        return select_rows(
+            slots_of(slot_table, experts, columns, size, b, q), experts, wide
+        )
+
+    def spread(q, source_rows, target, weights, hit):
+        choose = jnp.where(hit, 1.0, 0.0).astype(BF)
+
+        def one(n, carry):
+            cols = pl.ds(pl.multiple_of(n * tile, tile), tile)
+            rows = dot_plain(choose, source_rows[q, :, cols])
+            if weights is not None:
+                rows = rows * weights
+            for e in range(experts):
+                target[e, q * wide : (q + 1) * wide, cols] = rows[
+                    e * wide : (e + 1) * wide
+                ].astype(BF)
+            return carry
+
+        lax.fori_loop(0, width // tile, one, 0)
+
+    def back(b):
+        dy_gather.last(b)
+        dy_gather.arrived(b, [2, 5, 6, 7])
+        copies = load(b, 1)
+        for copy in copies:
+            copy.start()
+        if b == 0:
+            for copy in weights_in:
+                copy.wait()
+        else:
+            d_spill(previous[b]).wait()
+        for q in range(count):
+            for copy in copies[2 * q : 2 * q + 2]:
+                copy.wait()
+            hit = choice(b, q)
+            spread(
+                q,
+                db,
+                ds,
+                slot_weights(
+                    hit, slots_of(weight_table, experts, columns, size, b, q), experts, wide
+                ),
+                hit,
+            )
+        d_spill(b).start()
+
+        def one_expert(e, carry):
+            d_hidden[b, e] = dot_rows(ds[e], down[e])
+            return carry
+
+        lax.fori_loop(0, experts, one_expert, 0)
+
+    def front(b):
+        copies = load(b, 0)
+        for copy in copies:
+            copy.start()
+        if b > 0:
+            for copy in spills(previous[b]):
+                copy.wait()
+        for q in range(count):
+            for copy in copies[2 * q : 2 * q + 2]:
+                copy.wait()
+            spread(q, xb, xs, None, choice(b, q))
+        out_copies = spills(b)
+        out_copies[0].start()
+
+        def one_expert(e, carry):
+            both = dot_rows(xs[e], gate_up[e])
+            gate_pre, up_pre = both[:, :pad], both[:, pad:]
+            d_hid = d_hidden[b, e]
+            sigmoid = jax.nn.sigmoid(gate_pre)
+            silu = gate_pre * sigmoid
+            hid[b, e] = (silu * up_pre).astype(BF)
+            gate_grad = d_hid * up_pre * (sigmoid * (1.0 + gate_pre * (1.0 - sigmoid)))
+            dgu[e] = jnp.concatenate([gate_grad, d_hid * silu], axis=1).astype(BF)
+
+            def inward(n, inner):
+                cols = pl.ds(pl.multiple_of(n * tile, tile), tile)
+                part = dot_plain(dgu[e], gate_up[e, :, cols]).astype(BF)
+                for q in range(count):
+                    dxs[q, pl.ds(pl.multiple_of(e * wide, wide), wide), cols] = part[
+                        q * wide : (q + 1) * wide
+                    ]
+                return inner
+
+            lax.fori_loop(0, width // tile, inward, 0)
+            return carry
+
+        lax.fori_loop(0, experts, one_expert, 0)
+        out_copies[1].start()
+        out_copies[2].start()
+        if b > 0:
+            for i in range(4):
+                plane.pair(i, previous[b]).wait_send()
+
+        def keep(q, cols, value):
+            chip[q, b, :, cols] = value[:size]
+            others[q, :, cols] = value[size:]
+
+        combine(b, keep)
+        for i in range(4):
+            plane.pair(i, b).start()
+
+    dy_gather.forward(0)
+    dy_gather.forward(2)
+    back(0)
+
     for copy in first:
         copy.wait()
     total = summed.total(attn_v[...]) + tokens_v[...].astype(F32)
@@ -880,131 +1025,27 @@
     own_copy.wait()
 
     gather.start()
-
-    def enter(b):
-        if b > 0:
-            gather.wait(b)
-        x_gather.start(b)
-
-    def ready(b):
-        x_gather.last(b)
-        dy_gather.last(b)
-        x_gather.arrived(b, [2, 5, 6, 7])
-        dy_gather.arrived(b, [2, 5, 6, 7])
-
-    def source(own, gathered, r):
-        return own if r == 0 else gathered.at[r - 1]
-
-    def load(b, k):
-        own, gathered, target = ((ffn_all, x_others, xb), (cotan_in, dy_others, db))[k]
-        return [
-            pltpu.make_async_copy(
-                source(own, gathered, r).at[rows_of(b)],
-                target.at[r // 2, pl.ds(r % 2 * size, size)],
-                loads.at[8 * k + r],
-            )
-            for r in range(8)
-        ]
-
-    def combine(b, keep):
-        token_sums(slot_table, experts, columns, size, wide, b, dxs, keep)
-
-    def spills(b):
-        return [
-            pltpu.make_async_copy(xs, x_all.at[b], spill.at[0]),
-            pltpu.make_async_copy(ds, d_all.at[b], spill.at[1]),
-            pltpu.make_async_copy(hid.at[b], hid_all.at[b], spill.at[2]),
-            pltpu.make_async_copy(dgu, dgu_all.at[b], spill.at[3]),
-        ]
-
-    def front(b):
-        x_load, dy_load = load(b, 0), load(b, 1)
-        for copy in x_load + dy_load:
-            copy.start()
-        if b == 0:
-            for copy in weights_in:
-                copy.wait()
-        if b > 0:
-            for copy in spills(previous[b]):
-                copy.wait()
-        for q in range(count):
-            for copy in x_load[2 * q : 2 * q + 2] + dy_load[2 * q : 2 * q + 2]:
-                copy.wait()
-            hit = select_rows(slots_of(slot_table, experts, columns, size, b, q), experts, wide)
-            weights = slot_weights(hit, slots_of(weight_table, experts, columns, size, b, q), experts, wide)
-            choose = jnp.where(hit, 1.0, 0.0).astype(BF)
-
-            def spread(n, carry, q=q, choose=choose, weights=weights):
-                cols = pl.ds(pl.multiple_of(n * tile, tile), tile)
-                rows = dot_plain(choose, xb[q, :, cols])
-                grads = dot_plain(choose, db[q, :, cols]) * weights
-                for e in range(experts):
-                    low, high = e * wide, (e + 1) * wide
-                    xs[e, q * wide : (q + 1) * wide, cols] = rows[low:high].astype(BF)
-                    ds[e, q * wide : (q + 1) * wide, cols] = grads[low:high].astype(BF)
-                return carry
-
-            lax.fori_loop(0, width // tile, spread, 0)
-        out_copies = spills(b)
-        out_copies[0].start()
-        out_copies[1].start()
-
-        def one_expert(e, carry):
-            both = dot_rows(xs[e], gate_up[e])
-            gate_pre, up_pre = both[:, :pad], both[:, pad:]
-            d_hidden = dot_rows(ds[e], down[e])
-            sigmoid = jax.nn.sigmoid(gate_pre)
-            silu = gate_pre * sigmoid
-            hid[b, e] = (silu * up_pre).astype(BF)
-            gate_grad = d_hidden * up_pre * (sigmoid * (1.0 + gate_pre * (1.0 - sigmoid)))
-            dgu[e] = jnp.concatenate([gate_grad, d_hidden * silu], axis=1).astype(BF)
-
-            def back(n, inner):
-                cols = pl.ds(pl.multiple_of(n * tile, tile), tile)
-                part = dot_plain(dgu[e], gate_up[e, :, cols]).astype(BF)
-                for q in range(count):
-                    dxs[q, pl.ds(pl.multiple_of(e * wide, wide), wide), cols] = part[
-                        q * wide : (q + 1) * wide
-                    ]
-                return inner
-
-            lax.fori_loop(0, width // tile, back, 0)
-            return carry
-
-        lax.fori_loop(0, experts, one_expert, 0)
-        out_copies[2].start()
-        out_copies[3].start()
-        if b > 0:
-            for i in range(4):
-                plane.pair(i, previous[b]).wait_send()
-
-        def keep(q, cols, value):
-            chip[q, b, :, cols] = value[:size]
-            others[q, :, cols] = value[size:]
-
-        combine(b, keep)
-        for i in range(4):
-            plane.pair(i, b).start()
-
-    dy_gather.forward(0)
     enter(0)
+    back(2)
     x_gather.forward(0)
-    dy_gather.forward(2)
     enter(2)
-    dy_gather.forward(1)
     enter(1)
     x_gather.forward(2)
+    dy_gather.forward(1)
+    dy_gather.start(3)
     ready(0)
     front(0)
-    dy_gather.forward(3)
     enter(3)
     x_gather.forward(1)
     ready(2)
     front(2)
     x_gather.forward(3)
+    dy_gather.forward(3)
     plane.send_first([0], False)
+    back(1)
     ready(1)
     front(1)
+    back(3)
     plane.send_first([2], False)
     plane.send_second([0])
     ready(3)
@@ -1025,7 +1066,7 @@
     plane.send_second([3])
     close(1)
     close(3)
-    for copy in spills(3):
+    for copy in spills(3) + [d_spill(3)]:
         copy.wait()
     for b in range(columns):
         done[b].wait()
@@ -1092,6 +1133,7 @@
         + [
             pltpu.VMEM((columns, experts, slots, pad), BF),
             pltpu.VMEM((experts, slots, 2 * pad), BF),
+            pltpu.VMEM((columns, experts, slots, pad), F32),
             pltpu.VMEM((8 * experts, SEQ), F32),
             pltpu.VMEM((8 * experts, SEQ), F32),
             pltpu.SemaphoreType.DMA((remote,)),
@@ -1132,17 +1174,12 @@
         6: along[0] + across[0] - place,
     }
     greet([partner, along, across] + column)
-    gathers = []
-    for n in range(2):
-        inward = pltpu.make_async_copy(rows_in[n], rows_v[n], local.at[n])
-        inward.start()
-        inward.wait()
-        place_here = rows_all[n].at[rows_of(0)]
-        outward = pltpu.make_async_copy(rows_v[n], place_here, local.at[n])
-        outward.start()
-        outward.wait()
-        gathers.append(ColumnGather(rows_all[n], rows_of, sends, arrivals, 8 * amount + 4 * n))
-        gathers[n].start()
+    gathers = [
+        ColumnGather(rows_all[n], rows_of, sends, arrivals, 8 * amount + 4 * n, rows_in[n])
+        for n in range(2)
+    ]
+    for gather in gathers:
+        gather.start()
     plans = []
     for k, kind in enumerate(kinds):
         own, everything = own_in[k], alls[k]
@@ -1177,7 +1214,10 @@
     for copies in plans:
         for copy in copies[:3]:
             copy.start()
-    here, there = [], []
+    here = [pltpu.make_async_copy(rows_in[n], rows_v[n], local.at[n]) for n in range(2)]
+    there = [
+        pltpu.make_async_copy(rows_v[n], rows_all[n].at[rows_of(0)], local.at[n]) for n in range(2)
+    ]
     for k, kind in enumerate(kinds):
         rows, cols = own_in[k].shape
         if kind == "relative":
@@ -1194,14 +1234,15 @@
         copy.wait()
     for copy in there:
         copy.start()
-    for copies in plans:
+    for n, copies in enumerate(plans):
         copies[0].wait_recv()
         copies[3].start()
         copies[5].start()
         copies[1].wait_recv()
         copies[4].start()
         copies[6].start()
-    gathers[0].wait(2)
+        if n == amount - 3:
+            gathers[0].wait(2)
     for copies in plans:
         copies[3].wait_recv()
         copies[4].wait_recv()

time: 700 us -> 707 us (1.010)
  Pallas kernels: 529 us -> 537 us
    pallas_call x1, Pallas kernels: 246 us -> 259 us  [expert_call(): pl.pallas_call(functools.partial(expert_kernel, cap, columns, size), out_...]
  transfers between devices with their start and end apart: 3 -> 3, of which waited for: 0 -> 0; matrix products, arithmetic and copies ran while one was open for 7% -> 7% of each run, Pallas kernels for 27% -> 26%
where the time goes in v9:
time: 707 us; the launch traced here: 697 us
  Pallas kernels  537 us (76%)
  matrix products  70.4 us (10%)
  local copies, waits for them, and re-layouts  52.7 us (7%)
  other arithmetic  22.5 us (3%)
  between operations  14.9 us (2%)
    pallas_call x1, Pallas kernels, expert_call(): pl.pallas_call(functools.partial(expert_kernel, cap, columns, size), out_...  259 us
    pallas_call x1, Pallas kernels, middle_call(): pl.pallas_call(functools.partial(middle_kernel, cap, columns, size, exper...  115 us
    pallas_call x1, Pallas kernels, first_call(): pl.pallas_call(functools.partial(first_kernel, columns, size, kinds), out...  93.4 us
    pallas_call x1, Pallas kernels, last_call(): pl.pallas_call(functools.partial(last_kernel, columns, size, latent_start...  69.3 us
    unnamed x142, local copies, waits for them, and re-layouts  37.7 us
  transfers between devices with their start and end apart: 3, of which 0 were waited for; matrix products, arithmetic and copies ran while one was open for 7% of the time, Pallas kernels for 26%

profile of v9, /device:TPU:0, one launch (start us, length us, event | category | flops | bytes accessed | tf_op | source)
XLA Modules:
  0.0 697.4 jit_solution(10514628472877441086)
XLA Ops:
  7.8 1.2 copy.122
  9.0 1.2 copy.123
  10.2 1.2 copy.118
  11.7 1.1 pad_maximum_fusion.6.refs_6_
  13.4 1.1 concatenate.43.refs_2_
  14.5 93.4 %first_gather.1 = (bf16[512,2048]{1,0:T(8,128)(2,1)}, bf16[512,2048]{1,0:T(8,128)(2,1)}, bf16[8,256,1408]{2,1,0:T(8,128)(2,1)}, bf16[8,64,1024]{2,1,0:T(8,128)(2...) custom-call(bf16[128,2048]{1,0:T(8,128)(2,1)} %refs_1_.5, ...), custom_call_target="tpu_custom_call" | custom-call | bytes 251658240 | tf_op jit(solution)/shard_map/first_gather/pallas_call | solution.py:1276
  107.9 2.2 fusion.47
  110.5 2.1 fusion.5
  112.6 6.5 fusion.16
  120.1 1.3 slice.123
  121.6 1.1 copy.154
  122.6 1.1 copy.155
  123.7 3.0 copy.127
  126.8 2.3 copy.126
  129.1 2.1 convolution_convert_fusion.6
  132.2 1.5 slice.196
  135.2 1.2 subtract_convert_fusion.1
  138.6 2.1 fusion.51
  141.2 1.6 copy-done.8
  143.9 2.6 convolution_convert_fusion.4.refs_0_
  146.5 258.5 %experts.1 = (f32[128,2048]{1,0:T(8,128)}, bf16[512,2048]{1,0:T(8,128)(2,1)}, bf16[512,2048]{1,0:T(8,128)(2,1)}, f32[16,512]{1,0:T(8,128)}, f32[16,512]{1,0:T(8,...) custom-call(bf16[512,2048]{1,0:T(8,128)(2,1)} %convolution_convert_f, ...), custom_call_target="tpu_custom_call" | custom-call | flops 17179869184 | bytes 838860800 | tf_op jit(solution)/shard_map/experts/pallas_call | solution.py:1098
  405.0 6.7 fusion.52
  411.8 2.2 multiply_convert_fusion.3
  414.9 3.2 convolution_convert_fusion.2
  418.1 5.3 convolution_convert_fusion.1
  423.4 7.7 %add_convert_fusion.1.refs_0_ = bf16[512,2048]{1,0:T(8,128)(2,1)} fusion(bf16[512,2048]{1,0:T(8,128)(2,1)} %get-tuple-element.61, bf16[2048,1408]{1,0:T(8,128)(2,1)} %bitcast.85, bf16[512,704]{0,1:T(8,128)(2,1)S(1)} %get-tuple-element.153, bf16[512,704]{0,1:T(8,128)(2,1)S(1)} %get-tuple-element.152), kind=kOutput, calls=%fused_computation.13 | convolution fusion | flops 2958819328 | bytes 11403264 | tf_op jit(solution)/shard_map/dot_general | solution.py:2264
  431.2 115.4 %middle.1 = (f32[128,2048]{1,0:T(8,128)}, bf16[512,2048]{1,0:T(8,128)(2,1)}, f32[1,2048]{1,0:T(1,128)}, bf16[512,2048]{1,0:T(8,128)(2,1)}, f32[2,352,2048]{2,1,0...) custom-call(bf16[512,2048]{1,0:T(8,128)(2,1)} %add_convert_fusion.1., ...), custom_call_target="tpu_custom_call" | custom-call | flops 19327352832 | bytes 314572800 | tf_op jit(solution)/shard_map/middle/pallas_call | solution.py:1686
  546.7 5.9 add_convert_fusion
  552.6 1.5 copy-done.53
  554.1 3.0 convolution_convert_fusion.7
  558.3 1.2 multiply_convert_fusion
  562.1 1.5 copy-done.4
  566.0 2.1 copy.140
  568.1 2.3 multiply_bitcast_fusion.1
  571.6 1.4 constant_dynamic-update-slice_fusion.1
  573.0 1.1 slice_reduce_fusion
  574.8 8.0 %fusion.4 = (f32[2048]{0:T(1024)S(1)}, bf16[512,2048]{1,0:T(8,128)(2,1)}) fusion(bf16[512,2048]{1,0:T(8,128)(2,1)S(1)} %copy-done.17, f32[512]{0:T(512)S(1)} %copy-done.48, bf16[512,1408]{0,1:T(8,128)(2,1)S(1)} %broadcast_dynamic-update-slice_fusion, bf16[2048,1408]{1,0:T(8,128)(2,1)} %bitcast.81), kind=kOutput, calls=%fused_computation.8 | convolution fusion | flops 2958030848 | bytes 11413504 | tf_op jit(solution)/shard_map/dot_general | solution.py:2350
  582.8 1.9 convolution_convert_fusion.5.refs_5_
  584.8 2.6 convolution_convert_fusion.3.refs_6_
  587.4 5.7 convolution_convert_fusion.refs_4_
  593.1 69.3 %last_sums.1 = (f32[128,2048]{1,0:T(8,128)S(1)}, bf16[256,1408]{1,0:T(8,128)(2,1)S(1)}, bf16[64,1024]{1,0:T(8,128)(2,1)S(1)}, bf16[512,256]{1,0:T(8,128)(2,1)S(1...) custom-call(bf16[512,2048]{1,0:T(8,128)(2,1)} %get-tuple-element.155, ...), custom_call_target="tpu_custom_call" | custom-call | bytes 188743680 | tf_op jit(solution)/shard_map/last_sums/pallas_call | solution.py:1954
  667.1 2.3 copy.142
  669.4 1.1 copy.143
  670.6 1.9 add_convert_fusion.2
  672.5 1.9 convert_element_type.289
  676.0 6.0 copy.170
  682.1 6.0 copy.171
  688.1 2.5 copy.172
  (183 shorter events, 24.4 us)
Async XLA Ops:
  7.2 4.1 copy-start.55
  7.2 4.3 copy-start.49
  7.2 4.4 copy-start.50
  7.2 4.5 copy-start.39
  7.2 5.5 copy-start.40
  7.2 6.2 copy-start.32
  7.2 545.3 %reduce-scatter.4.cloned.1.call-start = ((), (), s32[]{:S(2)}) async-start(), calls=%async_computation.3 | async-start | bytes 6488064 | tf_op jit(solution)/shard_map/reduce_scatter | solution.py:2157
  7.3 127.5 %copy-start.33 = (f32[512]{0:T(512)}, f32[512]{0:T(512)S(1)}, u32[]{:S(2)}) copy-start(f32[512]{0:T(512)S(1)} %iota_convert_fusion) | copy-start | bytes 6148
  110.5 8.6 %copy-start.1 = (f32[2048,1]{0,1:T(1,128)}, f32[2048,1]{0,1:T(1,128)S(1)}, u32[]{:S(2)}) copy-start(f32[2048,1]{0,1:T(1,128)S(1)} %copy.158) | copy-start | bytes 24580
  112.6 6.5 copy-start.47
  119.1 10.0 %copy-start.3 = (f32[512,1408]{1,0:T(8,128)}, f32[512,1408]{1,0:T(8,128)S(1)}, u32[]{:S(2)}) copy-start(f32[512,1408]{1,0:T(8,128)S(1)} %fusion.16) | copy-start | bytes 8650756
  126.7 4.5 copy-start.37
  126.8 4.4 copy-start.35
  129.1 4.6 copy-start.43
  132.2 2.6 copy-start.45
  132.2 6.3 copy-start.6
  133.7 4.8 copy-start.19
  138.6 2.2 copy-start.15
  140.7 2.1 copy-start.8
  140.7 2.1 copy-start.41
  140.7 3.1 copy-start.52
  142.9 3.6 copy-start.56
  405.0 6.7 copy-start.51
  405.0 6.7 copy-start.54
  414.9 3.2 copy-start.60
  431.2 239.4 %reduce-scatter.6.cloned.1.call-start = ((), (), s32[]{:S(2)}) async-start(), calls=%async_computation.4 | async-start | bytes 2621440 | tf_op jit(solution)/shard_map/reduce_scatter | solution.py:103
  552.5 120.0 %reduce-scatter.8.cloned.1.call-start = ((), (), s32[]{:S(2)}) async-start(), calls=%async_computation.5 | async-start | bytes 3244032 | tf_op jit(solution)/shard_map/reduce_scatter | solution.py:2157
  554.1 3.0 copy-start.9
  554.1 3.4 copy-start.16
  554.1 3.4 copy-start.42
  560.9 2.7 copy-start.4
  562.0 2.1 copy-start.38
  562.0 2.9 copy-start.10
  565.0 3.1 copy-start.7
  568.1 2.4 copy-start.25
  568.1 2.4 copy-start.27
  571.6 2.6 copy-start.34
  571.6 2.6 copy-start.46
  571.6 3.2 copy-start.17
  571.6 3.2 copy-start.48
  574.8 8.0 %copy-start.44 = (f32[1,2048]{1,0:T(1,128)S(1)}, f32[1,2048]{1,0:T(1,128)}, u32[]{:S(2)}) copy-start(f32[1,2048]{1,0:T(1,128)} %get-tuple-element.75) | copy-start | bytes 24580
  574.8 8.0 %copy-start.11 = (bf16[512,4,256]{0,2,1:T(8,128)(2,1)S(1)}, bf16[512,4,256]{0,2,1:T(8,128)(2,1)}, u32[]{:S(2)}) copy-start(bf16[512,4,256]{0,2,1:T(8,128)(2,1)} %copy-done.10) | copy-start | bytes 3145732
  584.8 2.6 copy-start.2
  587.4 5.7 copy-start
  662.4 3.7 copy-start.12
  667.1 3.4 copy-start.21
  676.0 12.0 %slice-start = ((s8[5767168]{0:T(1024)(128)(4,1)}), s8[4194304]{0:T(1024)(128)(4,1)S(1)}, s32[]{:S(2)}) async-start(s8[5767168]{0:T(1024)(128)(4,1)} %bitcast.69), calls=%async_computation.6 | async-start | bytes 8388608
  682.1 6.0 slice-start.1
  (18 other events, 23.5 us)
Sparse Core Ops, SparseCore 0:
  431.3 80.9 reduce-scatter.3
  552.7 42.1 reduce-scatter.5
  598.2 54.1 reduce-scatter.7

commit v10 on v7

--- a/solution.py
+++ b/solution.py
@@ -443,8 +443,9 @@
 
 
 class ColumnGather:
-    def __init__(self, blocks, rows_of, sends, arrivals, base):
+    def __init__(self, blocks, rows_of, sends, arrivals, base, own=None):
         self.blocks, self.rows_of = blocks, rows_of
+        self.own = blocks.at[rows_of(0)] if own is None else own
         self.sends, self.arrivals, self.base = sends, arrivals, base
         self.row = lax.axis_index("tp")
         self.column = column_neighbours(4)
@@ -452,7 +453,7 @@
     def direct(self, s):
         place = self.blocks.at[self.rows_of(0)]
         return mesh_copy(
-            place, place, self.sends, self.arrivals, self.base + s - 1, self.column[s - 1]
+            self.own, place, self.sends, self.arrivals, self.base + s - 1, self.column[s - 1]
         )
 
     def start(self):
@@ -1116,10 +1117,10 @@
 
 def first_kernel(columns, size, kinds, *refs):
     amount = len(kinds)
-    rows_in, own_in = refs[:2], refs[2 : 2 + amount]
-    rows_all, alls = refs[2 + amount : 4 + amount], refs[4 + amount : 4 + 2 * amount]
-    rows_v, held = refs[4 + 2 * amount : 6 + 2 * amount], refs[6 + 2 * amount : 6 + 3 * amount]
-    sends, arrivals, local = refs[6 + 3 * amount :]
+    tokens_in, own_in = refs[0], refs[1 : 1 + amount]
+    tokens_all, alls = refs[1 + amount], refs[2 + amount : 2 + 2 * amount]
+    tokens_v, held = refs[2 + 2 * amount], refs[3 + 2 * amount : 3 + 3 * amount]
+    sends, arrivals, local = refs[3 + 3 * amount :]
     partner, along, across = plane_neighbours()
     column = column_neighbours(columns)
     rows_of = block_rows(columns, size)
@@ -1132,17 +1133,8 @@
         6: along[0] + across[0] - place,
     }
     greet([partner, along, across] + column)
-    gathers = []
-    for n in range(2):
-        inward = pltpu.make_async_copy(rows_in[n], rows_v[n], local.at[n])
-        inward.start()
-        inward.wait()
-        place_here = rows_all[n].at[rows_of(0)]
-        outward = pltpu.make_async_copy(rows_v[n], place_here, local.at[n])
-        outward.start()
-        outward.wait()
-        gathers.append(ColumnGather(rows_all[n], rows_of, sends, arrivals, 8 * amount + 4 * n))
-        gathers[n].start()
+    gather = ColumnGather(tokens_all, rows_of, sends, arrivals, 8 * amount, tokens_in)
+    gather.start()
     plans = []
     for k, kind in enumerate(kinds):
         own, everything = own_in[k], alls[k]
@@ -1177,7 +1169,8 @@
     for copies in plans:
         for copy in copies[:3]:
             copy.start()
-    here, there = [], []
+    here = [pltpu.make_async_copy(tokens_in, tokens_v, local.at[0])]
+    there = [pltpu.make_async_copy(tokens_v, tokens_all.at[rows_of(0)], local.at[0])]
     for k, kind in enumerate(kinds):
         rows, cols = own_in[k].shape
         if kind == "relative":
@@ -1186,22 +1179,23 @@
             spot_here = alls[k].at[place]
         else:
             spot_here = alls[k].at[:, pl.ds(pl.multiple_of(place * cols, cols), cols)]
-        here.append(pltpu.make_async_copy(own_in[k], held[k], local.at[2 + k]))
-        there.append(pltpu.make_async_copy(held[k], spot_here, local.at[2 + k]))
+        here.append(pltpu.make_async_copy(own_in[k], held[k], local.at[1 + k]))
+        there.append(pltpu.make_async_copy(held[k], spot_here, local.at[1 + k]))
     for copy in here:
         copy.start()
     for copy in here:
         copy.wait()
     for copy in there:
         copy.start()
-    for copies in plans:
+    for n, copies in enumerate(plans):
         copies[0].wait_recv()
         copies[3].start()
         copies[5].start()
         copies[1].wait_recv()
         copies[4].start()
         copies[6].start()
-    gathers[0].wait(2)
+        if n == amount - 2:
+            gather.wait(2)
     for copies in plans:
         copies[3].wait_recv()
         copies[4].wait_recv()
@@ -1209,24 +1203,21 @@
     for copies in plans:
         for i in (2, 5, 6, 7):
             copies[i].wait_recv()
-    gathers[1].wait(2)
-    for gather in gathers:
-        gather.wait(1)
-        gather.wait(3)
+    gather.wait(1)
+    gather.wait(3)
     for copy in there:
         copy.wait()
-    for gather in gathers:
-        gather.drain()
+    gather.drain()
     for copies in plans:
         for copy in copies:
             copy.wait_send()
 
 
-def first_call(tokens, cotan, owns, kinds):
+def first_call(tokens, owns, kinds):
     columns = lax.axis_size("tp")
     size, width = tokens.shape
     anywhere = pl.BlockSpec(memory_space=pl.ANY)
-    copies = 8 * len(owns) + 8
+    copies = 8 * len(owns) + 4
 
     def gathered(own, kind):
         rows, cols = own.shape
@@ -1234,23 +1225,23 @@
 
     return pl.pallas_call(
         functools.partial(first_kernel, columns, size, kinds),
-        out_shape=[jax.ShapeDtypeStruct((columns * size, width), BF)] * 2
+        out_shape=[jax.ShapeDtypeStruct((columns * size, width), BF)]
         + [jax.ShapeDtypeStruct(gathered(own, kind), own.dtype) for own, kind in zip(owns, kinds)],
-        in_specs=[anywhere] * (2 + len(owns)),
-        out_specs=[anywhere] * (2 + len(owns)),
-        scratch_shapes=[pltpu.VMEM((size, width), BF)] * 2
+        in_specs=[anywhere] * (1 + len(owns)),
+        out_specs=[anywhere] * (1 + len(owns)),
+        scratch_shapes=[pltpu.VMEM((size, width), BF)]
         + [pltpu.VMEM(own.shape, own.dtype) for own in owns]
         + [
             pltpu.SemaphoreType.DMA((copies,)),
             pltpu.SemaphoreType.DMA((copies,)),
-            pltpu.SemaphoreType.DMA((2 + len(owns),)),
+            pltpu.SemaphoreType.DMA((1 + len(owns),)),
         ],
         compiler_params=pltpu.CompilerParams(collective_id=2, has_side_effects=True),
         cost_estimate=pl.CostEstimate(
             flops=0, bytes_accessed=240 * SEQ * width, transcendentals=0
         ),
         name="first_gather",
-    )(tokens, cotan, *owns)
+    )(tokens, *owns)
 
 
 class PlaneSum:
@@ -2062,6 +2053,7 @@
         axis=1,
     )
     packed = jnp.concatenate([query_proj, latent_proj, gains], axis=1)
+    cotan_all = column_gather(out_cotan)
     if paired:
         low, high = (0, RAW_ROWS - TOPK), (0, 0)
         raw = jnp.concatenate(
@@ -2069,7 +2061,6 @@
         )
         (
             tokens_all,
-            cotan_all,
             packed_all,
             latent_up_weight,
             out_weight,
@@ -2078,7 +2069,6 @@
             shared_down_weight,
         ) = first_call(
             block_in,
-            out_cotan,
             [
                 packed,
                 latent_up,
@@ -2097,7 +2087,6 @@
         latent_up_weight = lax.all_gather(latent_up, "fsdp", axis=0, tiled=True)
         out_weight = lax.all_gather(out_proj, "fsdp", axis=1, tiled=True)
         tokens_all = column_gather(block_in)
-        cotan_all = column_gather(out_cotan)
         shared_weight = lax.all_gather(
             jnp.concatenate([shared_gate, shared_up], axis=1), "fsdp", axis=0, tiled=True
         )

time: 700 us -> 682 us (0.974)
  Pallas kernels: 529 us -> 514 us
    pallas_call x1, Pallas kernels: 97.1 us -> 82.1 us  [first_call(): pl.pallas_call(functools.partial(first_kernel, columns, size, kinds), out...]
  transfers between devices with their start and end apart: 3 -> 4, of which waited for: 0 -> 0; matrix products, arithmetic and copies ran while one was open for 7% -> 13% of each run, Pallas kernels for 27% -> 40%
where the time goes in v10:
time: 682 us; the launch traced here: 671 us
  Pallas kernels  514 us (75%)
  matrix products  73.6 us (11%)
  local copies, waits for them, and re-layouts  46.8 us (7%)
  other arithmetic  21.4 us (3%)
  between operations  14.9 us (2%)
    pallas_call x1, Pallas kernels, expert_call(): pl.pallas_call(functools.partial(expert_kernel, cap, columns, size), out_...  247 us
    pallas_call x1, Pallas kernels, middle_call(): pl.pallas_call(functools.partial(middle_kernel, cap, columns, size, exper...  115 us
    pallas_call x1, Pallas kernels, first_call(): pl.pallas_call(functools.partial(first_kernel, columns, size, kinds), out...  82.1 us
    pallas_call x1, Pallas kernels, last_call(): pl.pallas_call(functools.partial(last_kernel, columns, size, latent_start...  69.8 us
    unnamed x142, local copies, waits for them, and re-layouts  33.9 us
  transfers between devices with their start and end apart: 4, of which 0 were waited for; matrix products, arithmetic and copies ran while one was open for 13% of the time, Pallas kernels for 40%

profile of v10, /device:TPU:0, one launch (start us, length us, event | category | flops | bytes accessed | tf_op | source)
XLA Modules:
  0.0 671.5 jit_solution(13852881434953621916)
XLA Ops:
  8.0 1.2 copy.122
  9.2 1.2 copy.123
  11.0 1.1 pad_maximum_fusion.6.refs_5_
  12.7 1.1 concatenate.43.refs_1_
  13.8 82.1 %first_gather.1 = (bf16[512,2048]{1,0:T(8,128)(2,1)}, bf16[8,256,1408]{2,1,0:T(8,128)(2,1)}, bf16[8,64,1024]{2,1,0:T(8,128)(2,1)}, bf16[512,2048]{1,0:T(8,128)(2...) custom-call(bf16[128,2048]{1,0:T(8,128)(2,1)} %refs_1_.3, ...), custom_call_target="tpu_custom_call" | custom-call | bytes 251658240 | tf_op jit(solution)/shard_map/first_gather/pallas_call | solution.py:1226
  95.9 2.8 fusion.47
  99.0 2.1 fusion.5
  101.1 6.5 fusion.16
  107.9 3.0 copy.126
  110.9 3.1 convolution_convert_fusion.6
  114.7 1.3 slice.123
  116.0 1.1 copy.154
  117.3 1.9 copy.127
  120.2 1.2 copy.156
  122.5 2.0 fusion.14
  124.8 2.1 fusion.51
  127.4 1.6 copy-done.8
  129.1 1.0 copy-done.51
  130.0 2.6 convolution_convert_fusion.4.refs_0_
  133.2 246.7 %experts.1 = (f32[128,2048]{1,0:T(8,128)}, bf16[512,2048]{1,0:T(8,128)(2,1)}, bf16[512,2048]{1,0:T(8,128)(2,1)}, f32[16,512]{1,0:T(8,128)}, f32[16,512]{1,0:T(8,...) custom-call(bf16[512,2048]{1,0:T(8,128)(2,1)} %convolution_convert_f, ...), custom_call_target="tpu_custom_call" | custom-call | flops 17179869184 | bytes 838860800 | tf_op jit(solution)/shard_map/experts/pallas_call | solution.py:1058
  380.0 6.7 fusion.52
  386.8 2.3 multiply_convert_fusion.3
  389.9 5.7 convolution_convert_fusion.1
  395.6 8.3 %add_convert_fusion.1.refs_0_ = bf16[512,2048]{1,0:T(8,128)(2,1)} fusion(bf16[512,2048]{1,0:T(8,128)(2,1)} %get-tuple-element.59, bf16[2048,1408]{1,0:T(8,128)(2,1)} %bitcast.87, bf16[512,704]{0,1:T(8,128)(2,1)} %copy-done.60, bf16[512,704]{0,1:T(8,128)(2,1)S(1)} %get-tuple-element.150), kind=kOutput, calls=%fused_computation.13 | convolution fusion | flops 2958819328 | bytes 11403264 | tf_op jit(solution)/shard_map/dot_general | solution.py:2212
  403.9 3.3 convolution_convert_fusion.2
  407.3 115.2 %middle.1 = (f32[128,2048]{1,0:T(8,128)}, bf16[512,2048]{1,0:T(8,128)(2,1)}, f32[1,2048]{1,0:T(1,128)}, bf16[512,2048]{1,0:T(8,128)(2,1)}, f32[2,352,2048]{2,1,0...) custom-call(bf16[512,2048]{1,0:T(8,128)(2,1)} %add_convert_fusion.1., ...), custom_call_target="tpu_custom_call" | custom-call | flops 19327352832 | bytes 314572800 | tf_op jit(solution)/shard_map/middle/pallas_call | solution.py:1636
  522.5 5.8 add_convert_fusion
  528.4 1.5 copy-done.52
  529.9 3.0 convolution_convert_fusion.7
  533.9 1.2 multiply_convert_fusion
  537.7 1.5 copy-done.4
  540.6 1.0 multiply_convert_fusion.4
  541.6 2.0 copy.140
  543.7 2.3 multiply_bitcast_fusion.1
  547.2 1.3 constant_dynamic-update-slice_fusion.1
  548.6 1.1 slice_reduce_fusion
  550.4 8.0 %fusion.4 = (f32[2048]{0:T(1024)S(1)}, bf16[512,2048]{1,0:T(8,128)(2,1)}) fusion(bf16[512,2048]{1,0:T(8,128)(2,1)S(1)} %copy-done.16, f32[512]{0:T(512)S(1)} %copy-done.47, bf16[512,1408]{0,1:T(8,128)(2,1)S(1)} %broadcast_dynamic-update-slice_fusion, bf16[2048,1408]{1,0:T(8,128)(2,1)} %bitcast.83), kind=kOutput, calls=%fused_computation.8 | convolution fusion | flops 2958030848 | bytes 11413504 | tf_op jit(solution)/shard_map/dot_general | solution.py:2298
  558.4 1.9 convolution_convert_fusion.5.refs_5_
  560.3 2.6 convolution_convert_fusion.3.refs_6_
  563.0 5.7 convolution_convert_fusion.refs_4_
  568.6 69.8 %last_sums.1 = (f32[128,2048]{1,0:T(8,128)S(1)}, bf16[256,1408]{1,0:T(8,128)(2,1)S(1)}, bf16[64,1024]{1,0:T(8,128)(2,1)S(1)}, bf16[512,256]{1,0:T(8,128)(2,1)S(1...) custom-call(bf16[512,2048]{1,0:T(8,128)(2,1)} %get-tuple-element.153, ...), custom_call_target="tpu_custom_call" | custom-call | bytes 188743680 | tf_op jit(solution)/shard_map/last_sums/pallas_call | solution.py:1904
  642.3 1.1 copy.142
  643.4 1.1 copy.143
  644.7 1.9 add_convert_fusion.2
  646.7 1.9 convert_element_type.289
  650.2 6.0 copy.170
  656.2 6.0 copy.171
  662.2 2.5 copy.172
  (186 shorter events, 20.0 us)
Async XLA Ops:
  7.2 3.2 copy-start.31
  7.2 3.4 copy-start.54
  7.2 3.5 copy-start.48
  7.2 3.6 copy-start.49
  7.2 3.7 copy-start.38
  7.2 4.8 copy-start.39
  7.2 126.0 %all-gather.2.cloned.1.call-start = ((), (), s32[]{:S(2)}) async-start(), calls=%async_computation.3 | async-start | bytes 2621440 | tf_op jit(solution)/shard_map/all_gather | solution.py:99
  8.0 4.7 copy-start.30
  8.0 520.4 %reduce-scatter.4.cloned.1.call-start = ((), (), s32[]{:S(2)}) async-start(), calls=%async_computation.4 | async-start | bytes 6488064 | tf_op jit(solution)/shard_map/reduce_scatter | solution.py:2105
  99.0 8.6 %copy-start.1 = (f32[2048,1]{0,1:T(1,128)}, f32[2048,1]{0,1:T(1,128)S(1)}, u32[]{:S(2)}) copy-start(f32[2048,1]{0,1:T(1,128)S(1)} %copy.158) | copy-start | bytes 24580
  101.1 6.5 copy-start.46
  107.7 7.1 %copy-start.3 = (f32[512,1408]{1,0:T(8,128)}, f32[512,1408]{1,0:T(8,128)S(1)}, u32[]{:S(2)}) copy-start(f32[512,1408]{1,0:T(8,128)S(1)} %fusion.16) | copy-start | bytes 8650756
  107.8 6.1 copy-start.36
  107.9 6.0 copy-start.34
  116.0 3.1 copy-start.14
  119.2 5.3 copy-start.6
  121.4 3.1 copy-start.44
  121.5 3.0 copy-start.32
  121.9 2.6 copy-start.26
  121.9 2.6 copy-start.28
  126.9 2.1 copy-start.40
  126.9 3.1 copy-start.51
  129.1 3.6 copy-start.55
  380.0 6.7 %copy-start.50 = (bf16[704,2048]{1,0:T(8,128)(2,1)S(1)}, bf16[704,2048]{1,0:T(8,128)(2,1)}, u32[]{:S(2)}) copy-start(bf16[704,2048]{1,0:T(8,128)(2,1)} %get-tuple-element.56) | copy-start | bytes 8650756
  380.0 6.7 %copy-start.53 = (bf16[512,2048]{1,0:T(8,128)(2,1)S(1)}, bf16[512,2048]{1,0:T(8,128)(2,1)}, u32[]{:S(2)}) copy-start(bf16[512,2048]{1,0:T(8,128)(2,1)} %all-gather.2.cloned.1.call-done.refs_2_) | copy-start | bytes 6291460
  386.7 3.2 copy-start.59
  389.1 14.8 %copy-start.58 = (bf16[512,704]{0,1:T(8,128)(2,1)}, bf16[512,704]{0,1:T(8,128)(2,1)S(1)}, u32[]{:S(2)}) copy-start(bf16[512,704]{0,1:T(8,128)(2,1)S(1)} %get-tuple-element.154) | copy-start | bytes 2162692
  407.2 237.3 %reduce-scatter.6.cloned.1.call-start = ((), (), s32[]{:S(2)}) async-start(), calls=%async_computation.5 | async-start | bytes 2621440 | tf_op jit(solution)/shard_map/reduce_scatter | solution.py:103
  528.4 118.3 %reduce-scatter.8.cloned.1.call-start = ((), (), s32[]{:S(2)}) async-start(), calls=%async_computation.6 | async-start | bytes 3244032 | tf_op jit(solution)/shard_map/reduce_scatter | solution.py:2105
  529.9 3.0 copy-start.9
  529.9 3.2 copy-start.15
  529.9 3.2 copy-start.41
  536.5 2.7 copy-start.4
  537.7 2.9 copy-start.10
  540.6 3.1 copy-start.7
  543.7 2.4 copy-start.23
  543.7 2.4 copy-start.25
  547.1 2.5 copy-start.33
  547.1 2.5 copy-start.45
  547.1 3.2 copy-start.16
  547.2 3.2 copy-start.47
  550.4 8.1 %copy-start.43 = (f32[1,2048]{1,0:T(1,128)S(1)}, f32[1,2048]{1,0:T(1,128)}, u32[]{:S(2)}) copy-start(f32[1,2048]{1,0:T(1,128)} %get-tuple-element.73) | copy-start | bytes 24580
  550.4 8.1 %copy-start.11 = (bf16[512,4,256]{0,2,1:T(8,128)(2,1)S(1)}, bf16[512,4,256]{0,2,1:T(8,128)(2,1)}, u32[]{:S(2)}) copy-start(bf16[512,4,256]{0,2,1:T(8,128)(2,1)} %copy-done.10) | copy-start | bytes 3145732
  560.3 2.6 copy-start.2
  562.9 5.7 copy-start
  638.4 3.7 copy-start.12
  650.2 12.0 %slice-start = ((s8[5767168]{0:T(1024)(128)(4,1)}), s8[4194304]{0:T(1024)(128)(4,1)S(1)}, s32[]{:S(2)}) async-start(s8[5767168]{0:T(1024)(128)(4,1)} %bitcast.71), calls=%async_computation.7 | async-start | bytes 8388608
  656.2 6.0 slice-start.1
  (19 other events, 28.8 us)
Sparse Core Ops, SparseCore 0:
  9.6 76.9 all-gather.1
  407.3 81.6 reduce-scatter.3
  528.5 42.4 reduce-scatter.5
  574.2 54.2 reduce-scatter.7

commit v11 on v10

--- a/solution.py
+++ b/solution.py
@@ -1568,7 +1568,6 @@
         copy.start()
     out_part(3)
     plane.send_first([2], False)
-    job(0)
     plane.send_first([3], False)
 
     for copy in first:
@@ -1589,6 +1588,7 @@
     mixed_copy.start()
     own_copy.wait()
     gather.start()
+    job(0)
     for b in range(columns):
         if b + 1 < len(jobs):
             job(b + 1)
@@ -1793,17 +1793,19 @@
     ]
     for copy in first:
         copy.start()
+    summed.clear()
+    first[3].wait()
+
+    def small(i, device):
+        return mesh_copy(running.at[i], sums_v.at[i], sends, arrivals, base + i, device)
+
+    hops = [small(i, device) for i, device in enumerate((partner, along, across))]
+    hops[0].start()
     for part in (out, joint, up):
         part.begin()
-    summed.clear()
-    first[3].wait()
-
-    def small(i, device):
-        return mesh_copy(running.at[i], sums_v.at[i], sends, arrivals, base + i, device)
-
-    hops = [small(i, device) for i, device in enumerate((partner, along, across))]
     for i, copy in enumerate(hops):
-        copy.start()
+        if i > 0:
+            copy.start()
         copy.wait_recv()
         running[i + 1] = running[i] + sums_v[i]
     gains = [

time: 682 us -> 682 us (level)
  no operation moved by 1% of the time
where the time goes in v11:
time: 682 us; the launch traced here: 671 us
  Pallas kernels  514 us (75%)
  matrix products  73.6 us (11%)
  local copies, waits for them, and re-layouts  46.8 us (7%)
  other arithmetic  21.4 us (3%)
  between operations  14.9 us (2%)
    pallas_call x1, Pallas kernels, expert_call(): pl.pallas_call(functools.partial(expert_kernel, cap, columns, size), out_...  247 us
    pallas_call x1, Pallas kernels, middle_call(): pl.pallas_call(functools.partial(middle_kernel, cap, columns, size, exper...  115 us
    pallas_call x1, Pallas kernels, first_call(): pl.pallas_call(functools.partial(first_kernel, columns, size, kinds), out...  82.1 us
    pallas_call x1, Pallas kernels, last_call(): pl.pallas_call(functools.partial(last_kernel, columns, size, latent_start...  69.8 us
    unnamed x142, local copies, waits for them, and re-layouts  33.9 us
  transfers between devices with their start and end apart: 4, of which 0 were waited for; matrix products, arithmetic and copies ran while one was open for 13% of the time, Pallas kernels for 40%

profile of v11, /device:TPU:0, one launch (start us, length us, event | category | flops | bytes accessed | tf_op | source)
XLA Modules:
  0.0 671.5 jit_solution(9009936988613809218)
XLA Ops:
  8.0 1.2 copy.122
  9.2 1.2 copy.123
  11.0 1.1 pad_maximum_fusion.6.refs_5_
  12.7 1.1 concatenate.43.refs_1_
  13.8 82.1 %first_gather.1 = (bf16[512,2048]{1,0:T(8,128)(2,1)}, bf16[8,256,1408]{2,1,0:T(8,128)(2,1)}, bf16[8,64,1024]{2,1,0:T(8,128)(2,1)}, bf16[512,2048]{1,0:T(8,128)(2...) custom-call(bf16[128,2048]{1,0:T(8,128)(2,1)} %refs_1_.3, ...), custom_call_target="tpu_custom_call" | custom-call | bytes 251658240 | tf_op jit(solution)/shard_map/first_gather/pallas_call | solution.py:1226
  95.9 2.8 fusion.47
  99.0 2.1 fusion.5
  101.1 6.5 fusion.16
  107.9 3.0 copy.126
  110.9 3.1 convolution_convert_fusion.6
  114.7 1.3 slice.123
  116.0 1.1 copy.154
  117.3 1.9 copy.127
  120.2 1.2 copy.156
  122.5 2.0 fusion.14
  124.8 2.1 fusion.51
  127.4 1.6 copy-done.8
  129.1 1.0 copy-done.51
  130.0 2.6 convolution_convert_fusion.4.refs_0_
  133.2 246.7 %experts.1 = (f32[128,2048]{1,0:T(8,128)}, bf16[512,2048]{1,0:T(8,128)(2,1)}, bf16[512,2048]{1,0:T(8,128)(2,1)}, f32[16,512]{1,0:T(8,128)}, f32[16,512]{1,0:T(8,...) custom-call(bf16[512,2048]{1,0:T(8,128)(2,1)} %convolution_convert_f, ...), custom_call_target="tpu_custom_call" | custom-call | flops 17179869184 | bytes 838860800 | tf_op jit(solution)/shard_map/experts/pallas_call | solution.py:1058
  380.0 6.7 fusion.52
  386.8 2.3 multiply_convert_fusion.3
  389.9 5.7 convolution_convert_fusion.1
  395.6 8.3 %add_convert_fusion.1.refs_0_ = bf16[512,2048]{1,0:T(8,128)(2,1)} fusion(bf16[512,2048]{1,0:T(8,128)(2,1)} %get-tuple-element.59, bf16[2048,1408]{1,0:T(8,128)(2,1)} %bitcast.87, bf16[512,704]{0,1:T(8,128)(2,1)} %copy-done.60, bf16[512,704]{0,1:T(8,128)(2,1)S(1)} %get-tuple-element.150), kind=kOutput, calls=%fused_computation.13 | convolution fusion | flops 2958819328 | bytes 11403264 | tf_op jit(solution)/shard_map/dot_general | solution.py:2214
  403.9 3.3 convolution_convert_fusion.2
  407.3 115.2 %middle.1 = (f32[128,2048]{1,0:T(8,128)}, bf16[512,2048]{1,0:T(8,128)(2,1)}, f32[1,2048]{1,0:T(1,128)}, bf16[512,2048]{1,0:T(8,128)(2,1)}, f32[2,352,2048]{2,1,0...) custom-call(bf16[512,2048]{1,0:T(8,128)(2,1)} %add_convert_fusion.1., ...), custom_call_target="tpu_custom_call" | custom-call | flops 19327352832 | bytes 314572800 | tf_op jit(solution)/shard_map/middle/pallas_call | solution.py:1636
  522.5 5.8 add_convert_fusion
  528.4 1.5 copy-done.52
  529.9 3.0 convolution_convert_fusion.7
  533.9 1.2 multiply_convert_fusion
  537.7 1.5 copy-done.4
  540.6 1.0 multiply_convert_fusion.4
  541.6 2.0 copy.140
  543.7 2.3 multiply_bitcast_fusion.1
  547.2 1.3 constant_dynamic-update-slice_fusion.1
  548.6 1.1 slice_reduce_fusion
  550.4 8.0 %fusion.4 = (f32[2048]{0:T(1024)S(1)}, bf16[512,2048]{1,0:T(8,128)(2,1)}) fusion(bf16[512,2048]{1,0:T(8,128)(2,1)S(1)} %copy-done.16, f32[512]{0:T(512)S(1)} %copy-done.47, bf16[512,1408]{0,1:T(8,128)(2,1)S(1)} %broadcast_dynamic-update-slice_fusion, bf16[2048,1408]{1,0:T(8,128)(2,1)} %bitcast.83), kind=kOutput, calls=%fused_computation.8 | convolution fusion | flops 2958030848 | bytes 11413504 | tf_op jit(solution)/shard_map/dot_general | solution.py:2300
  558.4 1.9 convolution_convert_fusion.5.refs_5_
  560.3 2.6 convolution_convert_fusion.3.refs_6_
  563.0 5.7 convolution_convert_fusion.refs_4_
  568.6 69.8 %last_sums.1 = (f32[128,2048]{1,0:T(8,128)S(1)}, bf16[256,1408]{1,0:T(8,128)(2,1)S(1)}, bf16[64,1024]{1,0:T(8,128)(2,1)S(1)}, bf16[512,256]{1,0:T(8,128)(2,1)S(1...) custom-call(bf16[512,2048]{1,0:T(8,128)(2,1)} %get-tuple-element.153, ...), custom_call_target="tpu_custom_call" | custom-call | bytes 188743680 | tf_op jit(solution)/shard_map/last_sums/pallas_call | solution.py:1906
  642.3 1.1 copy.142
  643.4 1.1 copy.143
  644.7 1.9 add_convert_fusion.2
  646.7 1.9 convert_element_type.289
  650.2 6.0 copy.170
  656.2 6.0 copy.171
  662.2 2.5 copy.172
  (186 shorter events, 20.0 us)
Async XLA Ops:
  7.2 3.2 copy-start.31
  7.2 3.4 copy-start.54
  7.2 3.5 copy-start.48
  7.2 3.6 copy-start.49
  7.2 3.7 copy-start.38
  7.2 4.8 copy-start.39
  7.2 126.0 %all-gather.2.cloned.1.call-start = ((), (), s32[]{:S(2)}) async-start(), calls=%async_computation.3 | async-start | bytes 2621440 | tf_op jit(solution)/shard_map/all_gather | solution.py:99
  8.0 4.7 copy-start.30
  8.0 520.4 %reduce-scatter.4.cloned.1.call-start = ((), (), s32[]{:S(2)}) async-start(), calls=%async_computation.4 | async-start | bytes 6488064 | tf_op jit(solution)/shard_map/reduce_scatter | solution.py:2107
  99.0 8.6 %copy-start.1 = (f32[2048,1]{0,1:T(1,128)}, f32[2048,1]{0,1:T(1,128)S(1)}, u32[]{:S(2)}) copy-start(f32[2048,1]{0,1:T(1,128)S(1)} %copy.158) | copy-start | bytes 24580
  101.1 6.5 copy-start.46
  107.7 7.1 %copy-start.3 = (f32[512,1408]{1,0:T(8,128)}, f32[512,1408]{1,0:T(8,128)S(1)}, u32[]{:S(2)}) copy-start(f32[512,1408]{1,0:T(8,128)S(1)} %fusion.16) | copy-start | bytes 8650756
  107.8 6.1 copy-start.36
  107.9 6.0 copy-start.34
  116.0 3.1 copy-start.14
  119.2 5.3 copy-start.6
  121.4 3.1 copy-start.44
  121.5 3.0 copy-start.32
  121.9 2.6 copy-start.26
  121.9 2.6 copy-start.28
  126.9 2.1 copy-start.40
  126.9 3.1 copy-start.51
  129.1 3.6 copy-start.55
  380.0 6.7 %copy-start.50 = (bf16[704,2048]{1,0:T(8,128)(2,1)S(1)}, bf16[704,2048]{1,0:T(8,128)(2,1)}, u32[]{:S(2)}) copy-start(bf16[704,2048]{1,0:T(8,128)(2,1)} %get-tuple-element.56) | copy-start | bytes 8650756
  380.0 6.7 %copy-start.53 = (bf16[512,2048]{1,0:T(8,128)(2,1)S(1)}, bf16[512,2048]{1,0:T(8,128)(2,1)}, u32[]{:S(2)}) copy-start(bf16[512,2048]{1,0:T(8,128)(2,1)} %all-gather.2.cloned.1.call-done.refs_2_) | copy-start | bytes 6291460
  386.7 3.2 copy-start.59
  389.1 14.8 %copy-start.58 = (bf16[512,704]{0,1:T(8,128)(2,1)}, bf16[512,704]{0,1:T(8,128)(2,1)S(1)}, u32[]{:S(2)}) copy-start(bf16[512,704]{0,1:T(8,128)(2,1)S(1)} %get-tuple-element.154) | copy-start | bytes 2162692
  407.2 237.3 %reduce-scatter.6.cloned.1.call-start = ((), (), s32[]{:S(2)}) async-start(), calls=%async_computation.5 | async-start | bytes 2621440 | tf_op jit(solution)/shard_map/reduce_scatter | solution.py:103
  528.4 118.3 %reduce-scatter.8.cloned.1.call-start = ((), (), s32[]{:S(2)}) async-start(), calls=%async_computation.6 | async-start | bytes 3244032 | tf_op jit(solution)/shard_map/reduce_scatter | solution.py:2107
  529.9 3.0 copy-start.9
  529.9 3.2 copy-start.15
  529.9 3.2 copy-start.41
  536.5 2.7 copy-start.4
  537.7 2.9 copy-start.10
  540.6 3.1 copy-start.7
  543.7 2.4 copy-start.23
  543.7 2.4 copy-start.25
  547.1 2.5 copy-start.33
  547.1 2.5 copy-start.45
  547.1 3.2 copy-start.16
  547.2 3.2 copy-start.47
  550.4 8.1 %copy-start.43 = (f32[1,2048]{1,0:T(1,128)S(1)}, f32[1,2048]{1,0:T(1,128)}, u32[]{:S(2)}) copy-start(f32[1,2048]{1,0:T(1,128)} %get-tuple-element.73) | copy-start | bytes 24580
  550.4 8.1 %copy-start.11 = (bf16[512,4,256]{0,2,1:T(8,128)(2,1)S(1)}, bf16[512,4,256]{0,2,1:T(8,128)(2,1)}, u32[]{:S(2)}) copy-start(bf16[512,4,256]{0,2,1:T(8,128)(2,1)} %copy-done.10) | copy-start | bytes 3145732
  560.3 2.6 copy-start.2
  562.9 5.7 copy-start
  638.4 3.7 copy-start.12
  650.2 12.0 %slice-start = ((s8[5767168]{0:T(1024)(128)(4,1)}), s8[4194304]{0:T(1024)(128)(4,1)S(1)}, s32[]{:S(2)}) async-start(s8[5767168]{0:T(1024)(128)(4,1)} %bitcast.71), calls=%async_computation.7 | async-start | bytes 8388608
  656.2 6.0 slice-start.1
  (19 other events, 28.8 us)
Sparse Core Ops, SparseCore 0:
  9.6 76.9 all-gather.1
  407.3 81.6 reduce-scatter.3
  528.5 42.4 reduce-scatter.5
  574.2 53.7 reduce-scatter.7
